TPU v7x, 32 devices: a whole 2x2x4 slice. The times are simulated.
32 devices in a mesh: dp: 8 (over y, x, core), rep: 4 (over z).
Axes of the slice: x: 2, y: 2, z: 4, core: 2. Of those that a mesh axis runs over, the one named last changes fastest.
Arguments:
- inputs: bfloat16 [32, 1044, 512], P(('dp', 'rep')), may hold values from -6 to 6
- segments: int32 [32, 1024], P(('dp', 'rep')), may hold values from 0 to 3, never falling along the last dimension, each value on 1 to 512 neighbouring positions
- cotangent: bfloat16 [32, 1044, 512], P(('dp', 'rep')), may hold values from -6 to 6
- attend_in: float32 [512, 1536], P(('dp', 'rep'))
- attend_out: float32 [512, 512], P(('dp', 'rep'))
- expand: float32 [512, 2048], P(('dp', 'rep'))
- contract: float32 [2048, 512], P(('dp', 'rep'))
- layer_norms: float32 [4, 512], P(None, ('dp', 'rep'))
- moment_in: float32 [512, 1536], P(('dp', 'rep')), may hold values from -512 to 512
- moment_out: float32 [512, 512], P(('dp', 'rep')), may hold values from -112 to 112
- moment_expand: float32 [512, 2048], P(('dp', 'rep')), may hold values from -320 to 320
- moment_contract: float32 [2048, 512], P(('dp', 'rep')), may hold values from -640 to 640
- moment_norms: float32 [4, 512], P(None, ('dp', 'rep')), may hold values from -1024 to 1024
- square_in: float32 [512, 1536], P(('dp', 'rep')), may hold values from 8352 to 33408
- square_out: float32 [512, 512], P(('dp', 'rep')), may hold values from 334 to 1336
- square_expand: float32 [512, 2048], P(('dp', 'rep')), may hold values from 3037 to 12148
- square_contract: float32 [2048, 512], P(('dp', 'rep')), may hold values from 12026 to 48107
- square_norms: float32 [4, 512], P(None, ('dp', 'rep')), may hold values from 33408 to 133632
Outputs:
- outputs: bfloat16 [32, 1044, 512], P(('dp', 'rep'))
- input_gradient: bfloat16 [32, 1044, 512], P(('dp', 'rep'))
- updated_in: float32 [512, 1536], P(('dp', 'rep'))
- updated_out: float32 [512, 512], P(('dp', 'rep'))
- updated_expand: float32 [512, 2048], P(('dp', 'rep'))
- updated_contract: float32 [2048, 512], P(('dp', 'rep'))
- updated_norms: float32 [4, 512], P(None, ('dp', 'rep'))
- momentum_in: float32 [512, 1536], P(('dp', 'rep'))
- momentum_out: float32 [512, 512], P(('dp', 'rep'))
- momentum_expand: float32 [512, 2048], P(('dp', 'rep'))
- momentum_contract: float32 [2048, 512], P(('dp', 'rep'))
- momentum_norms: float32 [4, 512], P(None, ('dp', 'rep'))
- variance_in: float32 [512, 1536], P(('dp', 'rep'))
- variance_out: float32 [512, 512], P(('dp', 'rep'))
- variance_expand: float32 [512, 2048], P(('dp', 'rep'))
- variance_contract: float32 [2048, 512], P(('dp', 'rep'))
- variance_norms: float32 [4, 512], P(None, ('dp', 'rep'))
- trust_table: float32 [3, 5], replicated
Inputs may be any that keep to these rules, and one draw needn't show every extreme that they name: `segments`: along a row the ids never fall; every id occurs, a segment holds at most 512 positions and in every row one holds exactly that many.
All inputs are finite; a program needn't handle non-finite values.
Results may differ from a plain program's by a relative error of at most 0.019.
The roundings to bfloat16 on the way count: a program that leaves them out, or rounds other values in their place, can miss the bound.
Values may be sent and summed in bfloat16 or wider, within the bound.
No kernel may reach another device: no remote copies, remote signals or barrier semaphores. Data moves between devices by JAX's collectives and lax.ppermute only.
A program may use at most 128 MiB of HBM per device.

v0:
```python
from functools import partial
import math

import jax
import jax.numpy as jnp
from jax import lax
from jax.experimental import pallas as pl
from jax.experimental.pallas import tpu as pltpu
from jax.sharding import PartitionSpec as P

HEADS = 8
HEAD_DIM = 64


EPSILON = 1e-05
ADAM_EPSILON = 1e-06
DECAY = 0.01
RATE = 0.5
BETA = 0.5
LANES = 128
HALF = 64
BIG = 1e30
FEATS = 4
TILE = 256
THIN = 32
CHUNK = 352
VMEM = pltpu.MemorySpace.VMEM


def params(mebibytes):
    return pltpu.CompilerParams(vmem_limit_bytes=mebibytes * 1024 * 1024)


def dot(a, b, ca, cb):
    return lax.dot_general(a, b, (((ca,), (cb,)), ((), ())), preferred_element_type=jnp.float32)


def normalize(values):
    center = values - jnp.mean(values, axis=-1, keepdims=True)
    scale = lax.rsqrt(jnp.mean(center * center, axis=-1, keepdims=True) + EPSILON)
    return center * scale, scale


def core_index():
    return lax.rem(lax.axis_index("dp"), 2)


def plane_index():
    return lax.div(lax.axis_index("dp"), 2)


def block_at(m, other, rows):
    core = core_index()
    side = 1 - core if other else core
    return pl.multiple_of((2 * (plane_index() ^ m) + side) * rows, rows)


def assemble(pieces, full_ref, columns):
    plane = len(pieces) // 2
    for i, piece in enumerate(pieces):
        at = block_at(i % plane, i >= plane, piece.shape[0])
        full_ref[pl.ds(at, piece.shape[0]), :] = piece[:, columns]


def assemble_deep(pieces, full_ref, first, reps):
    plane = len(pieces) // 2
    width = full_ref.shape[1]
    for i, piece in enumerate(pieces):
        rows = piece.shape[0] // reps
        at = block_at(i % plane, i >= plane, 4 * piece.shape[0])
        for z in range(reps):
            for j in range(4):
                source = piece[z * rows : (z + 1) * rows, first + j * width : first + (j + 1) * width]
                full_ref[pl.ds(at + (4 * z + j) * rows, rows), :] = source


def split_rows(full_ref, keep_ref, send_ref, lanes):
    plane, rows, _ = keep_ref.shape
    core = core_index()
    for p in range(plane):
        at = pl.multiple_of((2 * p + core) * rows, rows)
        keep_ref[p, :, lanes] = full_ref[pl.ds(at, rows), :].astype(keep_ref.dtype)
        at = pl.multiple_of((2 * p + 1 - core) * rows, rows)
        send_ref[p, :, lanes] = full_ref[pl.ds(at, rows), :].astype(jnp.bfloat16)


def split_deep(full_ref, keep_ref, send_ref, first, reps):
    plane, rows, _ = keep_ref.shape
    width = full_ref.shape[1]
    core = core_index()
    each = rows // reps
    for p in range(plane):
        for side, target in ((core, keep_ref), (1 - core, send_ref)):
            base = pl.multiple_of((2 * p + side) * 4 * rows, 4 * rows)
            for z in range(reps):
                for j in range(4):
                    source = full_ref[pl.ds(base + (4 * z + j) * each, each), :]
                    columns = slice(first + j * width, first + (j + 1) * width)
                    target[p, z * each : (z + 1) * each, columns] = source.astype(target.dtype)


def row_chunks(rows, size):
    return [(at, min(size, rows - at)) for at in range(0, rows, size)]


def windows(rows):
    half = (rows - THIN) // 2
    span = half + THIN
    spans = [(at, TILE, 0, span) for at in range(0, half, TILE)]
    spans.append((half, THIN, 0, rows))
    return spans + [(at, TILE, half, span) for at in range(span, rows, TILE)]


def arrange_kernel(inputs, cotangent, segments, x, dy, labels, begin, room):
    tokens = segments.shape[1]
    half = tokens // 2
    memory = inputs.shape[0] - tokens
    segment = segments[...].astype(jnp.float32)
    ahead = pltpu.roll(jnp.broadcast_to(segment, (8, tokens)), tokens - half + 1, 1)[:1]
    lane = lax.broadcasted_iota(jnp.int32, (1, tokens), 1)
    fits = (segment == ahead) & (lane <= half)
    start = jnp.sum(jnp.where(fits, lane.astype(jnp.float32), 0.0), axis=1, keepdims=True)
    begin[...] = jnp.broadcast_to(start, begin.shape)
    row = lax.broadcasted_iota(jnp.int32, (half, LANES), 0).astype(jnp.float32)
    early = row < start
    thin = lax.broadcasted_iota(jnp.int32, (THIN, LANES), 0) < memory
    for source, target in ((inputs, x), (cotangent, dy)):
        for at in range(0, inputs.shape[1], LANES):
            columns = slice(at, at + LANES)
            room[: inputs.shape[0]] = source[:, columns].astype(jnp.float32)
            left, right = room[memory : memory + half], room[memory + half : memory + tokens]
            target[:half, columns] = jnp.where(early, right, left).astype(target.dtype)
            target[half : half + THIN, columns] = jnp.where(thin, room[:THIN], 0.0).astype(target.dtype)
            target[half + THIN :, columns] = jnp.where(early, left, right).astype(target.dtype)
    left = jnp.transpose(jnp.broadcast_to(segment[:, :half], (LANES, half)))
    right = jnp.transpose(jnp.broadcast_to(segment[:, half:], (LANES, half)))
    labels[:half] = jnp.where(early, right, left).astype(jnp.int32)
    labels[half : half + THIN] = jnp.where(thin, -1, -2)
    labels[half + THIN :] = jnp.where(early, left, right).astype(jnp.int32)


def arrange(inputs, cotangent, segments):
    width = inputs.shape[1]
    rows = segments.shape[1] + THIN
    return pl.pallas_call(
        arrange_kernel,
        out_shape=(
            jax.ShapeDtypeStruct((rows, width), inputs.dtype),
            jax.ShapeDtypeStruct((rows, width), inputs.dtype),
            jax.ShapeDtypeStruct((rows, LANES), jnp.int32),
            jax.ShapeDtypeStruct((8, LANES), jnp.float32),
        ),
        in_specs=[pl.BlockSpec(memory_space=VMEM)] * 3,
        out_specs=[pl.BlockSpec(memory_space=VMEM)] * 4,
        scratch_shapes=[pltpu.VMEM((rows, LANES), jnp.float32)],
        compiler_params=params(8),
        name="arrange",
    )(inputs, cotangent, segments)


def arrange_back_kernel(begin, first, second, first_out, second_out, room):
    rows = first_out.shape[0]
    half = (first.shape[0] - THIN) // 2
    memory = rows - 2 * half
    row = lax.broadcasted_iota(jnp.int32, (half, LANES), 0).astype(jnp.float32)
    early = row < begin[:1]
    for source, target in ((first, first_out), (second, second_out)):
        for at in range(0, first.shape[1], LANES):
            columns = slice(at, at + LANES)
            left = source[:half, columns].astype(jnp.float32)
            right = source[half + THIN :, columns].astype(jnp.float32)
            room[:THIN] = source[half : half + THIN, columns].astype(jnp.float32)
            room[memory : memory + half] = jnp.where(early, right, left)
            room[memory + half : rows] = jnp.where(early, left, right)
            target[:, columns] = room[:rows].astype(target.dtype)


def arrange_back(begin, first, second, rows):
    width = first.shape[1]
    return pl.pallas_call(
        arrange_back_kernel,
        out_shape=[jax.ShapeDtypeStruct((rows, width), first.dtype)] * 2,
        in_specs=[pl.BlockSpec(memory_space=VMEM)] * 3,
        out_specs=[pl.BlockSpec(memory_space=VMEM)] * 2,
        scratch_shapes=[pltpu.VMEM((first.shape[0], LANES), jnp.float32)],
        compiler_params=params(8),
        name="arrange_back",
    )(begin, first, second)


def attend_kernel(count, x, labels, *refs):
    pieces = refs[:count]
    qx, kx, vx, mixed, gains, weight, qs = refs[count:]
    rows = x.shape[0]
    width = mixed.shape[1]
    assemble(pieces, weight, slice(None))
    gains[...] = jnp.transpose(weight[:, 3 * width :].astype(jnp.float32))[:8]
    gain, bias = gains[0:1], gains[1:2]

    def one_chunk(i, carry):
        span = pl.ds(pl.multiple_of(i * CHUNK, CHUNK), CHUNK)
        normed, _ = normalize(x[span].astype(jnp.float32))
        first = (normed * gain + bias).astype(jnp.bfloat16)
        lane = lax.broadcasted_iota(jnp.int32, (CHUNK, LANES), 1)
        low = lane < HALF
        feature = lane % HALF
        label = labels[span]
        blocked = ((feature < FEATS) & (label >= 0) & (feature != label)) | (feature == FEATS)
        query_side = jnp.where(blocked, -BIG, 0.0)
        marked = ((feature < FEATS) & (feature == label)) | ((feature == FEATS) & (label == -2))
        key_side = jnp.where(marked | (feature > FEATS), 1.0, 0.0)
        sides = (query_side, key_side, jnp.ones_like(key_side))
        for kind, target in enumerate((qs, kx, vx)):
            whole = dot(first, weight[:, kind * width : (kind + 1) * width], 1, 0)
            whole = whole.astype(jnp.bfloat16).astype(jnp.float32)
            for pair in range(width // LANES):
                part = whole[:, pair * LANES : (pair + 1) * LANES]
                if kind == 0:
                    part = part * (1.0 / math.sqrt(HEAD_DIM))
                at = 2 * pair * LANES
                target[span, at : at + LANES] = jnp.where(low, part, sides[kind]).astype(jnp.bfloat16)
                target[span, at + LANES : at + 2 * LANES] = jnp.where(low, sides[kind], part).astype(jnp.bfloat16)
        return carry

    lax.fori_loop(0, rows // CHUNK, one_chunk, 0)

    def one_pair(pair, carry):
        columns = pl.ds(pl.multiple_of(pair * LANES, LANES), LANES)
        for at, size, key_at, key_size in windows(rows):
            span = pl.ds(at, size)
            seen = pl.ds(key_at, key_size)
            lane = lax.broadcasted_iota(jnp.int32, (size, LANES), 1)
            low = lane < HALF
            feature = lane % HALF
            got = []
            for side in range(2):
                head = pl.ds(pl.multiple_of((2 * pair + side) * LANES, LANES), LANES)
                queries = qs[span, head]
                scores = dot(queries, kx[seen, head], 1, 1)
                highest = jnp.max(scores, axis=1, keepdims=True)
                raised = jnp.exp(scores - highest).astype(jnp.bfloat16)
                found = dot(raised, vx[seen, head], 1, 0)
                total = -(highest + jnp.log(found))
                first = total.astype(jnp.bfloat16).astype(jnp.float32)
                second = (total - first).astype(jnp.bfloat16).astype(jnp.float32)
                third = total - first - second
                values = jnp.where(feature == 5, first, jnp.where(feature == 6, second, third))
                place = (feature > FEATS) & (feature < 8) & (low if side else ~low)
                qx[span, head] = jnp.where(place, values, queries.astype(jnp.float32)).astype(jnp.bfloat16)
                got.append(found)
            over = pltpu.roll(jnp.where(low, got[1], got[0]), HALF, 1)
            mixed[span, columns] = (jnp.where(low, got[0], got[1]) / over).astype(jnp.bfloat16)
        return carry

    lax.fori_loop(0, width // LANES, one_pair, 0)


def attend(x, labels, pieces):
    rows, width = x.shape
    wide = jax.ShapeDtypeStruct((rows, 2 * width), jnp.bfloat16)
    depth = len(pieces) * pieces[0].shape[0]
    return pl.pallas_call(
        partial(attend_kernel, len(pieces)),
        out_shape=(
            wide,
            wide,
            wide,
            jax.ShapeDtypeStruct((rows, width), jnp.bfloat16),
            jax.ShapeDtypeStruct((8, width), jnp.float32),
        ),
        in_specs=[pl.BlockSpec(memory_space=VMEM)] * (2 + len(pieces)),
        out_specs=[pl.BlockSpec(memory_space=VMEM)] * 5,
        scratch_shapes=[
            pltpu.VMEM((depth, pieces[0].shape[1]), jnp.bfloat16),
            pltpu.VMEM((rows, 2 * width), jnp.bfloat16),
        ],
        compiler_params=params(16),
        name="attend",
    )(x, labels, *pieces)


def attend_back_kernel(qx, kx, vx, dox, packed, total):
    rows = qx.shape[0]
    width = packed.shape[1] // 3

    def one_pair(pair, carry):
        heads = [pl.ds(pl.multiple_of((2 * pair + side) * LANES, LANES), LANES) for side in range(2)]
        spots = [pl.ds(pl.multiple_of(kind * width + pair * LANES, LANES), LANES) for kind in range(3)]
        total[...] = jnp.zeros_like(total)
        for at, size, query_at, query_size in windows(rows):
            span = pl.ds(at, size)
            seen = pl.ds(query_at, query_size)
            low = lax.broadcasted_iota(jnp.int32, (size, LANES), 1) < HALF
            got = []
            for side in range(2):
                head = heads[side]
                keys = kx[span, head]
                queries = qx[seen, head]
                upstream = dox[seen, head]
                attention = jnp.exp(dot(keys, queries, 1, 1))
                grad = dot(vx[span, head], upstream, 1, 1)
                scores = (attention * grad).astype(jnp.bfloat16)
                got.append((dot(scores, queries, 1, 0), dot(attention.astype(jnp.bfloat16), upstream, 1, 0)))
                total[side, seen] += dot(scores, keys, 0, 0)
            packed[span, spots[1]] = jnp.where(low, got[0][0], got[1][0]).astype(jnp.bfloat16)
            packed[span, spots[2]] = jnp.where(low, got[0][1], got[1][1]).astype(jnp.bfloat16)
        low = lax.broadcasted_iota(jnp.int32, (rows, LANES), 1) < HALF
        packed[:, spots[0]] = (jnp.where(low, total[0], total[1]) * (1.0 / math.sqrt(HEAD_DIM))).astype(jnp.bfloat16)
        return carry

    lax.fori_loop(0, width // LANES, one_pair, 0)


def attend_back(qx, kx, vx, dox):
    rows, wide = qx.shape
    return pl.pallas_call(
        attend_back_kernel,
        out_shape=jax.ShapeDtypeStruct((rows, 3 * wide // 2), jnp.bfloat16),
        in_specs=[pl.BlockSpec(memory_space=VMEM)] * 4,
        out_specs=pl.BlockSpec(memory_space=VMEM),
        scratch_shapes=[pltpu.VMEM((2, rows, LANES), jnp.float32)],
        compiler_params=params(16),
        name="attend_back",
    )(qx, kx, vx, dox)


def norm_back(grad, normed, scale, gain):
    scaled = grad * gain
    return scale * (
        scaled
        - jnp.mean(scaled, axis=-1, keepdims=True)
        - normed * jnp.mean(scaled * normed, axis=-1, keepdims=True)
    )


def feed_kernel(reps, count, deep_count, x, mixed, dy, gains, *refs):
    pieces = refs[:count]
    deep_pieces = refs[count : count + deep_count]
    outputs, dox, middle_grad, keep2, send2, norm_grads, *deep_out = refs[count + deep_count : -7]
    wide, contract, active, hidden_grad, second, middle_low, block = refs[-7:]
    rows, width = x.shape
    hidden = contract.shape[0]
    wide_part = slice(0, width + hidden)
    assemble(pieces, wide, wide_part)
    if deep_count:
        assemble(deep_pieces, contract, slice(None))
    else:
        assemble_deep(pieces, contract, width + hidden, reps)
    gain, bias = gains[2:3], gains[3:4]
    zero = jnp.zeros((1, width), jnp.float32)

    def one_chunk(i, carry):
        gain_sum, bias_sum = carry
        span = pl.ds(pl.multiple_of(i * CHUNK, CHUNK), CHUNK)
        middle = x[span].astype(jnp.float32) + dot(mixed[span], wide[:, :width], 1, 0)
        normed, scale = normalize(middle)
        low = (normed * gain + bias).astype(jnp.bfloat16)
        second[span] = low
        result = middle
        back = jnp.zeros_like(middle)
        for start in range(0, hidden, 512):
            part = slice(start, start + 512)
            from_expand = wide[:, width + start : width + start + 512]
            up = dot(low, from_expand, 1, 0)
            square = up * up
            bend = jnp.tanh(0.7978845608028654 * up * (1.0 + 0.044715 * square))
            half = 0.5 * (1.0 + bend)
            act = (up * half).astype(jnp.bfloat16)
            active[span, part] = act
            slope = half + 0.5 * up * (1.0 - bend * bend) * (0.7978845608028654 * (1.0 + 3 * 0.044715 * square))
            down = (dot(dy[span], contract[part], 1, 1) * slope).astype(jnp.bfloat16)
            hidden_grad[span, part] = down
            result = result + dot(act, contract[part], 1, 0)
            back = back + dot(down, from_expand, 1, 1)
        outputs[span] = result.astype(jnp.bfloat16)
        gain_sum = gain_sum + jnp.sum(back * normed, axis=0, keepdims=True)
        bias_sum = bias_sum + jnp.sum(back, axis=0, keepdims=True)
        grad = dy[span].astype(jnp.float32) + norm_back(back, normed, scale, gain)
        middle_grad[span] = grad
        grad_low = grad.astype(jnp.bfloat16)
        middle_low[span] = grad_low
        mixed_grad = dot(grad_low, wide[:, :width], 1, 1).astype(jnp.bfloat16).astype(jnp.float32)
        lane = lax.broadcasted_iota(jnp.int32, (CHUNK, LANES), 1)
        left = lane < HALF
        feature = lane % HALF
        for pair in range(width // LANES):
            columns = slice(pair * LANES, (pair + 1) * LANES)
            piece = mixed_grad[:, columns]
            product = piece * mixed[span, columns].astype(jnp.float32)
            for side in range(2):
                mine = left if side == 0 else ~left
                delta = -jnp.sum(jnp.where(mine, product, 0.0), axis=1, keepdims=True)
                one = delta.astype(jnp.bfloat16).astype(jnp.float32)
                two = (delta - one).astype(jnp.bfloat16).astype(jnp.float32)
                three = delta - one - two
                extra = jnp.where(feature == 0, one, jnp.where(feature == 1, two, jnp.where(feature == 2, three, 0.0)))
                head = (2 * pair + side) * LANES
                dox[span, head : head + LANES] = jnp.where(mine, piece, extra).astype(jnp.bfloat16)
        return gain_sum, bias_sum

    gain_sum, bias_sum = lax.fori_loop(0, rows // CHUNK, one_chunk, (zero, zero))
    norm_grads[...] = jnp.concatenate([gain_sum, bias_sum, jnp.zeros((6, width), jnp.float32)], axis=0)
    plane = keep2.shape[0]
    deep = hidden // (2 * plane)
    each = 512 // (2 * deep)

    def one_block(i, carry):
        columns = pl.ds(pl.multiple_of(i * 512, 512), 512)
        block[...] = dot(active[:, columns], dy[...], 0, 0)
        planes = pl.ds(i * each, each)
        if deep_count:
            split_rows(block, deep_out[0].at[planes], deep_out[1].at[planes], slice(0, width))
        else:
            split_deep(block, keep2.at[planes], send2.at[planes], width + hidden, reps)
        block[...] = dot(second[...], hidden_grad[:, columns], 0, 0)
        split_rows(block, keep2, send2, pl.ds(pl.multiple_of(width + i * 512, 512), 512))
        return carry

    lax.fori_loop(0, hidden // 512, one_block, 0)
    block[...] = dot(mixed[...], middle_low[...], 0, 0)
    split_rows(block, keep2, send2, slice(0, width))


def feed(reps, x, mixed, dy, gains, pieces, deep_pieces):
    rows, width = x.shape
    plane = len(pieces) // 2
    deep = pieces[0].shape[0]
    columns = pieces[0].shape[1]
    hidden = 4 * width
    out_shape = [
        jax.ShapeDtypeStruct((rows, width), jnp.bfloat16),
        jax.ShapeDtypeStruct((rows, 2 * width), jnp.bfloat16),
        jax.ShapeDtypeStruct((rows, width), jnp.float32),
        jax.ShapeDtypeStruct((plane, deep, columns), jnp.bfloat16),
        jax.ShapeDtypeStruct((plane, deep, columns), jnp.bfloat16),
        jax.ShapeDtypeStruct((8, width), jnp.float32),
    ]
    if deep_pieces:
        out_shape.append(jax.ShapeDtypeStruct((plane, 4 * deep, width), jnp.bfloat16))
        out_shape.append(jax.ShapeDtypeStruct((plane, 4 * deep, width), jnp.bfloat16))
    return pl.pallas_call(
        partial(feed_kernel, reps, len(pieces), len(deep_pieces)),
        out_shape=out_shape,
        in_specs=[pl.BlockSpec(memory_space=VMEM)] * (4 + len(pieces) + len(deep_pieces)),
        out_specs=[pl.BlockSpec(memory_space=VMEM)] * len(out_shape),
        scratch_shapes=[
            pltpu.VMEM((width, width + hidden), jnp.bfloat16),
            pltpu.VMEM((hidden, width), jnp.bfloat16),
            pltpu.VMEM((rows, hidden), jnp.bfloat16),
            pltpu.VMEM((rows, hidden), jnp.bfloat16),
            pltpu.VMEM((rows, width), jnp.bfloat16),
            pltpu.VMEM((rows, width), jnp.bfloat16),
            pltpu.VMEM((width, 512), jnp.float32),
        ],
        compiler_params=params(30),
        name="feed",
    )(x, mixed, dy, gains, *pieces, *deep_pieces)


def project_back_kernel(x, packed, gains, first_norms, second_norms, keep, send, first, block):
    rows, width = x.shape
    gain, bias = gains[0:1], gains[1:2]

    def one_chunk(i, carry):
        span = pl.ds(pl.multiple_of(i * CHUNK, CHUNK), CHUNK)
        normed, _ = normalize(x[span].astype(jnp.float32))
        first[span] = (normed * gain + bias).astype(jnp.bfloat16)
        return carry

    lax.fori_loop(0, rows // CHUNK, one_chunk, 0)

    def one_block(i, carry):
        columns = pl.ds(pl.multiple_of(i * 512, 512), 512)
        block[...] = dot(first[...], packed[:, columns], 0, 0)
        split_rows(block, keep, send, columns)
        return carry

    lax.fori_loop(0, packed.shape[1] // 512, one_block, 0)
    fill = jnp.zeros((LANES - 4, width), jnp.float32)
    norms = jnp.concatenate([first_norms[:2], second_norms[:2], fill], axis=0)
    block[:, :LANES] = jnp.transpose(norms)
    split_rows(block.at[:, :LANES], keep, send, slice(packed.shape[1], packed.shape[1] + LANES))


def project_back(x, packed, gains, first_norms, second_norms, plane, deep):
    rows, width = x.shape
    shape = (plane, deep, packed.shape[1] + LANES)
    return pl.pallas_call(
        project_back_kernel,
        out_shape=(jax.ShapeDtypeStruct(shape, jnp.bfloat16), jax.ShapeDtypeStruct(shape, jnp.bfloat16)),
        in_specs=[pl.BlockSpec(memory_space=VMEM)] * 5,
        out_specs=[pl.BlockSpec(memory_space=VMEM)] * 2,
        scratch_shapes=[pltpu.VMEM((rows, width), jnp.bfloat16), pltpu.VMEM((width, 512), jnp.float32)],
        compiler_params=params(10),
        name="project_back",
    )(x, packed, gains, first_norms, second_norms)


def input_back_kernel(x, packed, gains, middle_grad, *refs):
    pieces = refs[:-3]
    grad_in, norm_grads, weight = refs[-3:]
    rows, width = x.shape
    assemble(pieces, weight, slice(None))
    gain = gains[0:1]
    zero = jnp.zeros((1, width), jnp.float32)

    def one_chunk(i, carry):
        gain_sum, bias_sum = carry
        span = pl.ds(pl.multiple_of(i * CHUNK, CHUNK), CHUNK)
        normed, scale = normalize(x[span].astype(jnp.float32))
        back = dot(packed[span], weight[:, : 3 * width], 1, 1)
        grad_in[span] = (middle_grad[span] + norm_back(back, normed, scale, gain)).astype(jnp.bfloat16)
        gain_sum = gain_sum + jnp.sum(back * normed, axis=0, keepdims=True)
        return gain_sum, bias_sum + jnp.sum(back, axis=0, keepdims=True)

    gain_sum, bias_sum = lax.fori_loop(0, rows // CHUNK, one_chunk, (zero, zero))
    norm_grads[...] = jnp.concatenate([gain_sum, bias_sum, jnp.zeros((6, width), jnp.float32)], axis=0)


def input_back(x, packed, gains, middle_grad, pieces):
    rows, width = x.shape
    return pl.pallas_call(
        input_back_kernel,
        out_shape=(jax.ShapeDtypeStruct((rows, width), jnp.bfloat16), jax.ShapeDtypeStruct((8, width), jnp.float32)),
        in_specs=[pl.BlockSpec(memory_space=VMEM)] * (4 + len(pieces)),
        out_specs=[pl.BlockSpec(memory_space=VMEM)] * 2,
        scratch_shapes=[pltpu.VMEM((width, pieces[0].shape[1]), jnp.bfloat16)],
        compiler_params=params(10),
        name="input_back",
    )(x, packed, gains, middle_grad, *pieces)


def column_kernel(*refs):
    reps = len(refs) - 1
    out = refs[-1]
    z = lax.axis_index("rep")
    rows = refs[0].shape[0]
    got = [ref[...].astype(jnp.float32) for ref in refs[:-1]]
    parts = []
    for j in range(reps):
        part = got[0]
        for k in range(1, reps):
            part = jnp.where(lax.rem(z + reps - k, reps) == j, got[k], part)
        parts.append(part)
    out[...] = jnp.concatenate(parts, axis=0).astype(out.dtype)


def column_of(shards):
    rows, cols = shards[0].shape
    reps = len(shards)
    return pl.pallas_call(
        column_kernel,
        out_shape=jax.ShapeDtypeStruct((reps * rows, cols), shards[0].dtype),
        in_specs=[pl.BlockSpec(memory_space=VMEM)] * reps,
        out_specs=pl.BlockSpec(memory_space=VMEM),
        compiler_params=params(4),
        name="column",
    )(*shards)


def chip_sum_kernel(keep, got, own, *low):
    p = plane_index()
    own[...] = keep[p].astype(jnp.float32) + got[p].astype(jnp.float32)
    for m, ref in enumerate(low, 1):
        ref[...] = (keep[p ^ m].astype(jnp.float32) + got[p ^ m].astype(jnp.float32)).astype(jnp.bfloat16)


def chip_sum(keep, got):
    plane, rows, cols = keep.shape
    block = cols if cols < 2048 else 1536
    part = pl.BlockSpec((rows, block), lambda i: (0, i))
    whole = pl.BlockSpec((plane, rows, block), lambda i: (0, 0, i))
    return pl.pallas_call(
        chip_sum_kernel,
        grid=(cols // block,),
        out_shape=[jax.ShapeDtypeStruct((rows, cols), jnp.float32)]
        + [jax.ShapeDtypeStruct((rows, cols), jnp.bfloat16)] * (plane - 1),
        in_specs=[whole, whole],
        out_specs=[part] * plane,
        compiler_params=params(12),
        name="chip_sum",
    )(keep, got)


def plane_sum_kernel(own, *refs):
    plane = sum(1 for ref in refs if ref.shape == own.shape) + 1
    got, out, low = refs[: plane - 1], refs[plane - 1], refs[plane:]
    reps = len(low) + 1
    rows = out.shape[0]
    z = lax.axis_index("rep")
    total = own[...]
    for ref in got:
        total = total + ref[...].astype(jnp.float32)
    for k, ref in enumerate((out, *low)):
        part = total[:rows]
        for j in range(1, reps):
            part = jnp.where(lax.rem(z + k, reps) == j, total[j * rows : (j + 1) * rows], part)
        ref[...] = part.astype(ref.dtype)


def plane_sum(own, got, reps):
    rows, cols = own.shape
    block = cols if cols < 2048 else 1536
    part = pl.BlockSpec((rows, block), lambda i: (0, i))
    small = pl.BlockSpec((rows // reps, block), lambda i: (0, i))
    return pl.pallas_call(
        plane_sum_kernel,
        grid=(cols // block,),
        out_shape=[jax.ShapeDtypeStruct((rows // reps, cols), jnp.float32)]
        + [jax.ShapeDtypeStruct((rows // reps, cols), jnp.bfloat16)] * (reps - 1),
        in_specs=[part] * (1 + len(got)),
        out_specs=[small] * reps,
        compiler_params=params(10),
        name="plane_sum",
    )(own, *got)


def full_sum(value):
    return jnp.sum(jnp.sum(value, axis=1, keepdims=True), axis=0, keepdims=True)


def turned(columns):
    rows, count = columns.shape
    same = lax.broadcasted_iota(jnp.int32, (rows, rows), 0) == lax.broadcasted_iota(jnp.int32, (rows, rows), 1)
    line = lax.broadcasted_iota(jnp.int32, (count, rows), 0)
    out = jnp.zeros((count, rows), jnp.float32)
    for j in range(count):
        row = jnp.sum(jnp.where(same, columns[:, j : j + 1], 0.0), axis=0, keepdims=True)
        out = jnp.where(line == j, row, out)
    return out


def moments_kernel(pieces_of, first_index, reps, *refs):
    n = len(pieces_of)
    grads, arrays = refs[:reps], refs[reps:]
    total = grads[0][...]
    for ref in grads[1:]:
        total = total + ref[...].astype(jnp.float32)
    weights, firsts, seconds = arrays[:n], arrays[n : 2 * n], arrays[2 * n : 3 * n]
    momenta, variances, directions = arrays[3 * n : 4 * n], arrays[4 * n : 5 * n], arrays[5 * n : 6 * n]
    sums = arrays[6 * n]
    lane = lax.broadcasted_iota(jnp.int32, (1, LANES), 1)
    row = jnp.zeros((1, LANES), jnp.float32)
    for i, parts in enumerate(pieces_of):
        weight_sum = jnp.zeros((1, 1), jnp.float32)
        step_sum = jnp.zeros((1, 1), jnp.float32)
        for at, size, columns in parts:
            rows = slice(at, at + size)
            gradient = total[:, columns[0] : columns[1]]
            if len(columns) > 2:
                gradient = turned(gradient)
            weight = weights[i][rows]
            momentum = BETA * firsts[i][rows] + (1.0 - BETA) * gradient
            variance = BETA * seconds[i][rows] + (1.0 - BETA) * gradient * gradient
            direction = momentum / (jnp.sqrt(variance) + ADAM_EPSILON) + DECAY * weight
            momenta[i][rows] = momentum
            variances[i][rows] = variance
            directions[i][rows] = direction
            weight_sum = weight_sum + full_sum(weight * weight)
            step_sum = step_sum + full_sum(direction * direction)
        row = jnp.where(lane == first_index[i], weight_sum, row)
        row = jnp.where(lane == 5 + first_index[i], step_sum, row)
    sums[...] = row


def moments(pieces_of, first_index, grads, weights, firsts, seconds):
    arrays = [*grads, *weights, *firsts, *seconds]
    shapes = [jax.ShapeDtypeStruct(weight.shape, jnp.float32) for weight in weights]
    outs = pl.pallas_call(
        partial(moments_kernel, pieces_of, first_index, len(grads)),
        out_shape=shapes * 3 + [jax.ShapeDtypeStruct((1, LANES), jnp.float32)],
        in_specs=[pl.BlockSpec(memory_space=VMEM)] * len(arrays),
        out_specs=[pl.BlockSpec(memory_space=VMEM)] * (3 * len(weights) + 1),
        compiler_params=params(8),
        name="moments",
    )(*arrays)
    n = len(weights)
    return outs[:n], outs[n : 2 * n], outs[2 * n : 3 * n], outs[3 * n]


def update_kernel(n, sums, *refs):
    weights, directions, updated, table = refs[:n], refs[n : 2 * n], refs[2 * n : 3 * n], refs[3 * n]
    norms = jnp.sqrt(jnp.sum(sums[...], axis=0, keepdims=True))
    row = lax.broadcasted_iota(jnp.int32, table.shape, 0)
    lane = lax.broadcasted_iota(jnp.int32, table.shape, 1)
    out = jnp.zeros(table.shape, jnp.float32)
    for i in range(n):
        weight_norm = norms[:, i : i + 1]
        step_norm = norms[:, 5 + i : 6 + i]
        ratio = weight_norm / step_norm
        updated[i][...] = weights[i][...] - RATE * ratio * directions[i][...]
        column = jnp.where(row == 0, weight_norm, jnp.where(row == 1, step_norm, ratio))
        out = jnp.where(lane == i, column, out)
    table[...] = out


def update(sums, weights, directions):
    n = len(weights)
    outs = pl.pallas_call(
        partial(update_kernel, n),
        out_shape=[jax.ShapeDtypeStruct(weight.shape, jnp.float32) for weight in weights]
        + [jax.ShapeDtypeStruct((8, LANES), jnp.float32)],
        in_specs=[pl.BlockSpec(memory_space=VMEM)] * (1 + 2 * n),
        out_specs=[pl.BlockSpec(memory_space=VMEM)] * (n + 1),
        compiler_params=params(6),
        name="update",
    )(sums, *weights, *directions)
    return outs[:n], outs[n][:3, :n]


AXES = ("dp", "rep")


class Layout:
    def __init__(self, mesh):
        self.dp = mesh.shape["dp"]
        self.rep = mesh.shape["rep"]
        self.plane = self.dp // 2

    def permute(self, value, move):
        pairs = []
        for p in range(self.plane):
            for c in range(2):
                for z in range(self.rep):
                    q, d, w = move(p, c, z)
                    pairs.append(((p * 2 + c) * self.rep + z, (q * 2 + d) * self.rep + w))
        return lax.ppermute(value, AXES, pairs)

    def to_core(self, value):
        return self.permute(value, lambda p, c, z: (p, 1 - c, z))

    def to_plane(self, value, m):
        return self.permute(value, lambda p, c, z: (p ^ m, c, z))

    def to_rep(self, value, k):
        return self.permute(value, lambda p, c, z: (p, c, (z + k) % self.rep))

    def place(self):
        dp = lax.axis_index("dp")
        return dp // 2, dp % 2, lax.axis_index("rep")


def over_rep(lay, shard):
    return [shard] + [lay.to_rep(shard, k) for k in range(1, lay.rep)]


def over_plane(lay, column):
    return [column] + [lay.to_plane(column, m) for m in range(1, lay.plane)]


def over_core(lay, blocks):
    return blocks + [lay.to_core(block) for block in blocks]


def after(values, others):
    count = len(values)
    return list(lax.optimization_barrier((*values, *others))[:count])


def exchange(lay, value):
    return lax.all_to_all(value, AXES, 0, 0)


def body(
    lay,
    inputs,
    segments,
    cotangent,
    attend_in,
    attend_out,
    expand,
    contract,
    layer_norms,
    moment_in,
    moment_out,
    moment_expand,
    moment_contract,
    moment_norms,
    square_in,
    square_out,
    square_expand,
    square_contract,
    square_norms,
):
    masters = (attend_in, attend_out, expand, contract, layer_norms)
    width = attend_in.shape[1]
    depth = attend_out.shape[1]
    hidden = expand.shape[1]
    own = attend_in.shape[0]
    count = lay.dp * lay.rep
    plain = own % 16 == 0
    norm_rows = jnp.pad(layer_norms.astype(jnp.bfloat16).T, ((0, 0), (0, LANES - 4)))
    shard1 = jnp.concatenate([attend_in.astype(jnp.bfloat16), norm_rows], axis=1)
    column1 = over_rep(lay, shard1)
    rows = inputs.shape[1]
    attend_out_, expand_, contract_ = after([attend_out, expand, contract], [shard1])
    deep = [contract_[j * own : (j + 1) * own] for j in range(4)]
    shard2 = jnp.concatenate([part.astype(jnp.bfloat16) for part in (attend_out_, expand_, *deep)], axis=1)
    (shard2,) = after([shard2], column1[1:])
    column2 = over_rep(lay, shard2)
    inputs_, cotangent_, segments_ = after([inputs[0], cotangent[0], segments], [shard1])
    x, dy, labels, begin = arrange(inputs_, cotangent_, segments_)
    blocks1 = over_plane(lay, column_of(after(column1, [x])))
    blocks2 = over_plane(lay, column_of(after(column2, blocks1)))
    pieces1 = over_core(lay, blocks1)
    *pieces1, x, labels = after([*pieces1, x, labels], blocks2[:1])
    qx, kx, vx, mixed, gains = attend(x, labels, pieces1)
    pieces2 = over_core(lay, after(blocks2, [mixed]))
    deep_pieces = []
    if not plain:
        first = depth + hidden
        for piece in pieces2:
            part = piece[:, first:].reshape(lay.rep, own, 4, depth).transpose(0, 2, 1, 3)
            deep_pieces.append(part.reshape(-1, depth))
    outputs, dox, middle_grad, keep2, send2, second_norms, *deep_out = feed(
        lay.rep, x, mixed, dy, gains, pieces2, deep_pieces
    )
    if not plain:
        keep2, send2 = [
            jnp.concatenate(
                [
                    wide[:, :, : depth + hidden],
                    part.reshape(lay.plane, lay.rep, 4, own, depth).transpose(0, 1, 3, 2, 4).reshape(lay.plane, -1, 4 * depth),
                ],
                axis=2,
            )
            for wide, part in zip((keep2, send2), deep_out)
        ]
    own2, *low2 = chip_sum(keep2, lay.to_core(send2))
    got2 = [lay.to_plane(part, m) for m, part in enumerate(low2, 1)]
    (dox,) = after([dox], low2)
    packed = attend_back(qx, kx, vx, dox)
    input_gradient, first_norms = input_back(x, packed, gains, middle_grad, pieces1)
    own2, *got2 = after([own2, *got2], [first_norms])
    own2, *low2 = plane_sum(own2, got2, lay.rep)
    got2 = [lay.to_rep(part, k) for k, part in enumerate(low2, 1)]
    (packed_,) = after([packed], low2)
    keep1, send1 = project_back(x, packed_, gains, first_norms, second_norms, lay.plane, lay.rep * own)
    own1, *low1 = chip_sum(keep1, lay.to_core(send1))
    got1 = [lay.to_plane(part, m) for m, part in enumerate(low1, 1)]
    outputs, input_gradient = after([outputs, input_gradient], low1)
    outputs, input_gradient = arrange_back(begin, outputs, input_gradient, rows)
    spans = [[(0, own, (0, depth))], [(0, own, (depth, depth + hidden))]]
    spans.append([(j * own, own, (depth + hidden + j * depth, depth + hidden + (j + 1) * depth)) for j in range(4)])
    momenta2, variances2, directions2, sums2 = moments(
        spans, (1, 2, 3), [own2, *got2], masters[1:4],
        (moment_out, moment_expand, moment_contract), (square_out, square_expand, square_contract),
    )
    own1, *got1 = after([own1, *got1], [sums2])
    own1, *low1 = plane_sum(own1, got1, lay.rep)
    got1 = [lay.to_rep(part, k) for k, part in enumerate(low1, 1)]
    momenta1, variances1, directions1, sums1 = moments(
        [[(0, own, (0, width))], [(0, 4, (width, width + 4, True))]], (0, 4), [own1, *got1], (attend_in, layer_norms),
        (moment_in, moment_norms), (square_in, square_norms),
    )
    sums = exchange(lay, jnp.broadcast_to((sums1 + sums2)[None], (count, 1, LANES)))
    directions = (directions1[0], *directions2, directions1[1])
    updated, trust_table = update(sums[:, 0], masters, directions)
    momenta = (momenta1[0], *momenta2, momenta1[1])
    variances = (variances1[0], *variances2, variances1[1])
    return (outputs[None], input_gradient[None], *updated, *momenta, *variances, trust_table)


def solution(mesh):
    placed = (
        P(("dp", "rep"), None, None),
        P(("dp", "rep"), None),
        P(("dp", "rep"), None, None),
        P(("dp", "rep"), None),
        P(("dp", "rep"), None),
        P(("dp", "rep"), None),
        P(("dp", "rep"), None),
        P(None, ("dp", "rep")),
        P(("dp", "rep"), None),
        P(("dp", "rep"), None),
        P(("dp", "rep"), None),
        P(("dp", "rep"), None),
        P(None, ("dp", "rep")),
        P(("dp", "rep"), None),
        P(("dp", "rep"), None),
        P(("dp", "rep"), None),
        P(("dp", "rep"), None),
        P(None, ("dp", "rep")),
    )
    return jax.shard_map(
        partial(body, Layout(mesh)),
        mesh=mesh,
        in_specs=placed,
        out_specs=(
            P(("dp", "rep"), None, None),
            P(("dp", "rep"), None, None),
            P(("dp", "rep"), None),
            P(("dp", "rep"), None),
            P(("dp", "rep"), None),
            P(("dp", "rep"), None),
            P(None, ("dp", "rep")),
            P(("dp", "rep"), None),
            P(("dp", "rep"), None),
            P(("dp", "rep"), None),
            P(("dp", "rep"), None),
            P(None, ("dp", "rep")),
            P(("dp", "rep"), None),
            P(("dp", "rep"), None),
            P(("dp", "rep"), None),
            P(("dp", "rep"), None),
            P(None, ("dp", "rep")),
            P(),
        ),
        check_vma=False,
    )
```

profile of v0, /device:TPU:0, one launch (start us, length us, event | category | flops | bytes accessed | tf_op | source)
XLA Modules:
  0.0 171.8 jit_solution(13675381687078756767)
XLA Ops:
  2.3 5.1 %collective-permute-start.2 = (bf16[16,1664]{1,0:T(8,128)(2,1)S(1)}, bf16[16,1664]{1,0:T(8,128)(2,1)S(1)}, u32[]{:S(2)}, u32[]{:S(2)}) collective-permute-start(bf16[16,1664]{1,0:T(8,128)(2,1)S(1)} %fusion.1.refs_0_), channel_id=1, source_target_pairs={{0,3},{1,0},{2,1},{3,2},{4,7},{5,4},{6,5},{7,6},{8,11},{9,8},{10,9... | collective-permute-start | bytes 159752 | tf_op jit(solution)/shard_map/ppermute | solution.py:727
  11.1 1.4 collective-permute-done.1.refs_2_
  13.4 1.5 collective-permute-start.12
  14.9 1.2 copy-done.2
  16.2 1.2 copy-done.3
  18.1 1.1 arrange.1
  19.3 2.5 %collective-permute-start.5 = (bf16[64,1664]{1,0:T(8,128)(2,1)S(1)}, bf16[64,1664]{1,0:T(8,128)(2,1)S(1)}, u32[]{:S(2)}, u32[]{:S(2)}) collective-permute-start(bf16[64,1664]{1,0:T(8,128)(2,1)S(1)} %column.2.refs_0_), channel_id=1, source_target_pairs={{0,24},{1,25},{2,26},{3,27},{4,28},{5,29},{6,30},{7,31},{8,16},{9,... | collective-permute-start | bytes 638984 | tf_op jit(solution)/shard_map/ppermute | solution.py:727
  23.0 1.7 collective-permute-start.10
  24.7 8.3 %collective-permute-done.11.refs_2_ = bf16[16,4608]{1,0:T(8,128)(2,1)S(1)} collective-permute-done((bf16[16,4608]{1,0:T(8,128)(2,1)S(1)}, bf16[16,4608]{1,0:T(8,128)(2,1)S(1)}, u32[]{:S(2)}, u32[]{:S(2)}) %collective-permute-start.11) | collective-permute-done | bytes 147488 | tf_op jit(solution)/shard_map/ppermute | solution.py:727
  33.3 2.5 %collective-permute-start.15 = (bf16[64,4608]{1,0:T(8,128)(2,1)S(1)}, bf16[64,4608]{1,0:T(8,128)(2,1)S(1)}, u32[]{:S(2)}, u32[]{:S(2)}) collective-permute-start(bf16[64,4608]{1,0:T(8,128)(2,1)S(1)} %column.3.refs_0_), channel_id=1, source_target_pairs={{0,24},{1,25},{2,26},{3,27},{4,28},{5,29},{6,30},{7,31},{8,16},{9,... | collective-permute-start | bytes 1769480 | tf_op jit(solution)/shard_map/ppermute | solution.py:727
  40.1 21.1 %attend.1 = (bf16[1056,1024]{1,0:T(8,128)(2,1)S(1)}, bf16[1056,1024]{1,0:T(8,128)(2,1)S(1)}, bf16[1056,1024]{1,0:T(8,128)(2,1)S(1)}, bf16[1056,512]{1,0:T(8,128)(2,1)S(1)}, f32[8,512]{1,0:T(8,128)S(1)}) custom-call(bf16[1056,512]{1,0:T(8,128)(2,1)S(1)} %get-tuple-element.137.x, s32[1056,128]{1,0:T(8,128)S(1)} %get-tuple-element.138.labels, ...), custom_call_target="tpu_custom_call" | custom-call | tf_op jit(solution)/shard_map/attend/pallas_call | solution.py:262
  66.3 25.9 %feed.1 = (bf16[1056,512]{1,0:T(8,128)(2,1)S(1)}, bf16[1056,1024]{1,0:T(8,128)(2,1)S(1)}, f32[1056,512]{1,0:T(8,128)S(1)}, bf16[4,64,4608]{2,1,0:T(8,128)(2,1)S(...) custom-call(bf16[1056,512]{1,0:T(8,128)(2,1)S(1)} %get-tuple-element.137.x, ...), custom_call_target="tpu_custom_call" | custom-call | tf_op jit(solution)/shard_map/feed/pallas_call | solution.py:441
  92.5 4.3 %collective-permute-done.20.got = bf16[4,64,4608]{2,1,0:T(8,128)(2,1)S(1)} collective-permute-done((bf16[4,64,4608]{2,1,0:T(8,128)(2,1)S(1)}, bf16[4,64,4608]{2,1,0:T(8,128)(2,1)S(1)}, u32[]{:S(2)}, u32[]{:S(2)}) %collective-permute-start.20) | collective-permute-done | bytes 2359328 | tf_op jit(solution)/shard_map/ppermute | solution.py:727
  96.8 1.1 chip_sum.2
  97.9 1.6 collective-permute-start.21
  101.5 18.8 %attend_back.1.packed = bf16[1056,1536]{1,0:T(8,128)(2,1)S(1)} custom-call(bf16[1056,1024]{1,0:T(8,128)(2,1)S(1)} %get-tuple-element.155.qx, bf16[1056,1024]{1,0:T(8,128)(2,1)S(1)} %get-tuple-element.156.kx, bf16[1056,1024]{1,0:T(8,128)(2,1)S(1)} %get-tuple-element.157.vx, bf16[1056,1024]{1,0:T(8,128)(2,1)S(1)} %get-tuple-element.164.dox), custom_call_target="tpu_custom_call" | custom-call | tf_op jit(solution)/shard_map/attend_back/pallas_call | solution.py:316
  120.3 3.2 %input_back.1 = (bf16[1056,512]{1,0:T(8,128)(2,1)S(1)}, f32[8,512]{1,0:T(8,128)S(1)}) custom-call(bf16[1056,512]{1,0:T(8,128)(2,1)S(1)} %get-tuple-element.137.x, bf16[1056,1536]{1,0:T(8,128)(2,1)S(1)} %attend_back.1.packed, f32[8,512]{1,0:T(8,128)S(1)} %get-tuple-element.149.gains, f32[1056,512]{1,0:T(8,128)S(1)} %get-tuple-element.165.middle_grad, ...), custom_call_target="tpu_custom_call" | custom-call | tf_op jit(solution)/shard_map/input_back/pallas_call | solution.py:522
  123.5 3.8 %collective-permute-done.22.refs_1_ = bf16[64,4608]{1,0:T(8,128)(2,1)S(1)} collective-permute-done((bf16[64,4608]{1,0:T(8,128)(2,1)S(1)}, bf16[64,4608]{1,0:T(8,128)(2,1)S(1)}, u32[]{:S(2)}, u32[]{:S(2)}) %collective-permute-start.22) | collective-permute-done | bytes 589856 | tf_op jit(solution)/shard_map/ppermute | solution.py:727
  128.1 3.9 %project_back.1 = (bf16[4,64,1664]{2,1,0:T(8,128)(2,1)S(1)}, bf16[4,64,1664]{2,1,0:T(8,128)(2,1)S(1)}) custom-call(bf16[1056,512]{1,0:T(8,128)(2,1)S(1)} %get-tuple-element.137.x, bf16[1056,1536]{1,0:T(8,128)(2,1)S(1)} %attend_back.1.packed, f32[8,512]{1,0:T(8,128)S(1)} %get-tuple-element.149.gains, f32[8,512]{1,0:T(8,128)S(1)} %get-tuple-element.168.first_norms, ...), custom_call_target="tpu_custom_call" | custom-call | tf_op jit(solution)/shard_map/project_back/pallas_call | solution.py:488
  132.3 2.3 %collective-permute-done.24.got = bf16[4,64,1664]{2,1,0:T(8,128)(2,1)S(1)} collective-permute-done((bf16[4,64,1664]{2,1,0:T(8,128)(2,1)S(1)}, bf16[4,64,1664]{2,1,0:T(8,128)(2,1)S(1)}, u32[]{:S(2)}, u32[]{:S(2)}) %collective-permute-start.24) | collective-permute-done | bytes 852000 | tf_op jit(solution)/shard_map/ppermute | solution.py:727
  135.6 1.1 collective-permute-start.26
  136.8 1.5 collective-permute-start.27
  138.3 1.1 collective-permute-start.29
  140.4 6.4 %collective-permute-done.29.refs_2_ = bf16[16,4608]{1,0:T(8,128)(2,1)S(1)} collective-permute-done((bf16[16,4608]{1,0:T(8,128)(2,1)S(1)}, bf16[16,4608]{1,0:T(8,128)(2,1)S(1)}, u32[]{:S(2)}, u32[]{:S(2)}) %collective-permute-start.29) | collective-permute-done | bytes 147488 | tf_op jit(solution)/shard_map/ppermute | solution.py:727
  146.9 1.8 %collective-permute-done.30.refs_3_ = bf16[16,4608]{1,0:T(8,128)(2,1)S(1)} collective-permute-done((bf16[16,4608]{1,0:T(8,128)(2,1)S(1)}, bf16[16,4608]{1,0:T(8,128)(2,1)S(1)}, u32[]{:S(2)}, u32[]{:S(2)}) %collective-permute-start.30) | collective-permute-done | bytes 147488 | tf_op jit(solution)/shard_map/ppermute | solution.py:727
  150.1 1.7 collective-permute-start.31
  151.7 2.4 %collective-permute-start.32 = (bf16[16,1664]{1,0:T(8,128)(2,1)S(1)}, bf16[16,1664]{1,0:T(8,128)(2,1)S(1)}, u32[]{:S(2)}, u32[]{:S(2)}) collective-permute-start(bf16[16,1664]{1,0:T(8,128)(2,1)S(1)} %get-tuple-element.196), channel_id=1, source_target_pairs={{0,2},{1,3},{2,0},{3,1},{4,6},{5,7},{6,4},{7,5},{8,10},{9,11},{10,... | collective-permute-start | bytes 159752 | tf_op jit(solution)/shard_map/ppermute | solution.py:727
  154.2 2.0 %collective-permute-done.31.refs_1_ = bf16[16,1664]{1,0:T(8,128)(2,1)S(1)} collective-permute-done((bf16[16,1664]{1,0:T(8,128)(2,1)S(1)}, bf16[16,1664]{1,0:T(8,128)(2,1)S(1)}, u32[]{:S(2)}, u32[]{:S(2)}) %collective-permute-start.31) | collective-permute-done | bytes 53280 | tf_op jit(solution)/shard_map/ppermute | solution.py:727
  156.2 1.7 %collective-permute-done.32.refs_2_ = bf16[16,1664]{1,0:T(8,128)(2,1)S(1)} collective-permute-done((bf16[16,1664]{1,0:T(8,128)(2,1)S(1)}, bf16[16,1664]{1,0:T(8,128)(2,1)S(1)}, u32[]{:S(2)}, u32[]{:S(2)}) %collective-permute-start.32) | collective-permute-done | bytes 53280 | tf_op jit(solution)/shard_map/ppermute | solution.py:727
  159.8 3.4 %all-to-all-start = ((f32[32,1,128]{2,1,0:T(1,128)}), f32[32,1,128]{2,1,0:T(1,128)S(1)}, u32[]{:S(2)}, u32[]{:S(2)}) async-start(f32[32,1,128]{2,1,0:T(1,128)} %broadcast_in_dim.17), calls=%async_computation | async-start | bytes 32768 | tf_op jit(solution)/shard_map/all_to_all | solution.py:761
  163.2 2.0 %arrange_back.1 = (bf16[1044,512]{1,0:T(8,128)(2,1)}, bf16[1044,512]{1,0:T(8,128)(2,1)}) custom-call(f32[8,128]{1,0:T(8,128)S(1)} %get-tuple-element.122.begin, bf16[1056,512]{1,0:T(8,128)(2,1)S(1)} %get-tuple-element.183.first, bf16[1056,512]{1,0:T(8,128)(2,1)S(1)} %get-tuple-element.184.second), custom_call_target="tpu_custom_call" | custom-call | tf_op jit(solution)/shard_map/arrange_back/pallas_call | solution.py:180
  165.3 5.1 %all-to-all-done = f32[32,1,128]{2,1,0:T(1,128)S(1)} async-done(((f32[32,1,128]{2,1,0:T(1,128)}), f32[32,1,128]{2,1,0:T(1,128)S(1)}, u32[]{:S(2)}, u32[]{:S(2)}) %all-to-all-start) | async-done | bytes 16416 | tf_op jit(solution)/shard_map/all_to_all | solution.py:761
  (104 shorter events, 27.8 us)
Async XLA Ops:
  2.3 8.8 %collective-permute-start.2 = (bf16[16,1664]{1,0:T(8,128)(2,1)S(1)}, bf16[16,1664]{1,0:T(8,128)(2,1)S(1)}, u32[]{:S(2)}, u32[]{:S(2)}) collective-permute-start(bf16[16,1664]{1,0:T(8,128)(2,1)S(1)} %fusion.1.refs_0_), channel_id=1, source_target_pairs={{0,3},{1,0},{2,1},{3,2},{4,7},{5,4},{6,5},{7,6},{8,11},{9,8},{10,9... | collective-permute-start | bytes 159752 | tf_op jit(solution)/shard_map/ppermute | solution.py:727
  7.5 5.1 %collective-permute-start.1 = (bf16[16,1664]{1,0:T(8,128)(2,1)S(1)}, bf16[16,1664]{1,0:T(8,128)(2,1)S(1)}, u32[]{:S(2)}, u32[]{:S(2)}) collective-permute-start(bf16[16,1664]{1,0:T(8,128)(2,1)S(1)} %fusion.1.refs_0_), channel_id=1, source_target_pairs={{0,2},{1,3},{2,0},{3,1},{4,6},{5,7},{6,4},{7,5},{8,10},{9,11},{10,... | collective-permute-start | bytes 159752 | tf_op jit(solution)/shard_map/ppermute | solution.py:727
  7.5 5.9 %collective-permute-start = (bf16[16,1664]{1,0:T(8,128)(2,1)S(1)}, bf16[16,1664]{1,0:T(8,128)(2,1)S(1)}, u32[]{:S(2)}, u32[]{:S(2)}) collective-permute-start(bf16[16,1664]{1,0:T(8,128)(2,1)S(1)} %fusion.1.refs_0_), channel_id=1, source_target_pairs={{0,1},{1,2},{2,3},{3,0},{4,5},{5,6},{6,7},{7,4},{8,9},{9,10},{10,1... | collective-permute-start | bytes 159752 | tf_op jit(solution)/shard_map/ppermute | solution.py:727
  13.4 9.6 %collective-permute-start.12 = (bf16[16,4608]{1,0:T(8,128)(2,1)S(1)}, bf16[16,4608]{1,0:T(8,128)(2,1)S(1)}, u32[]{:S(2)}, u32[]{:S(2)}) collective-permute-start(bf16[16,4608]{1,0:T(8,128)(2,1)S(1)} %slice_dynamic-update-slice_fusion.refs_0_), channel_id=1, source_target_pairs={{0,3},{1,0},{2,1},{3,2},{4,7},{5,4},{6,5},{7,6},{8,11},{9,8},{10,9... | collective-permute-start | bytes 442376 | tf_op jit(solution)/shard_map/ppermute | solution.py:727
  19.3 13.8 %collective-permute-start.5 = (bf16[64,1664]{1,0:T(8,128)(2,1)S(1)}, bf16[64,1664]{1,0:T(8,128)(2,1)S(1)}, u32[]{:S(2)}, u32[]{:S(2)}) collective-permute-start(bf16[64,1664]{1,0:T(8,128)(2,1)S(1)} %column.2.refs_0_), channel_id=1, source_target_pairs={{0,24},{1,25},{2,26},{3,27},{4,28},{5,29},{6,30},{7,31},{8,16},{9,... | collective-permute-start | bytes 638984 | tf_op jit(solution)/shard_map/ppermute | solution.py:727
  21.8 11.2 %collective-permute-start.4 = (bf16[64,1664]{1,0:T(8,128)(2,1)S(1)}, bf16[64,1664]{1,0:T(8,128)(2,1)S(1)}, u32[]{:S(2)}, u32[]{:S(2)}) collective-permute-start(bf16[64,1664]{1,0:T(8,128)(2,1)S(1)} %column.2.refs_0_), channel_id=1, source_target_pairs={{0,16},{1,17},{2,18},{3,19},{4,20},{5,21},{6,22},{7,23},{8,24},{9,... | collective-permute-start | bytes 638984 | tf_op jit(solution)/shard_map/ppermute | solution.py:727
  22.3 10.7 %collective-permute-start.3 = (bf16[64,1664]{1,0:T(8,128)(2,1)S(1)}, bf16[64,1664]{1,0:T(8,128)(2,1)S(1)}, u32[]{:S(2)}, u32[]{:S(2)}) collective-permute-start(bf16[64,1664]{1,0:T(8,128)(2,1)S(1)} %column.2.refs_0_), channel_id=1, source_target_pairs={{0,8},{1,9},{2,10},{3,11},{4,12},{5,13},{6,14},{7,15},{8,0},{9,1},... | collective-permute-start | bytes 638984 | tf_op jit(solution)/shard_map/ppermute | solution.py:727
  22.8 10.2 %collective-permute-start.11 = (bf16[16,4608]{1,0:T(8,128)(2,1)S(1)}, bf16[16,4608]{1,0:T(8,128)(2,1)S(1)}, u32[]{:S(2)}, u32[]{:S(2)}) collective-permute-start(bf16[16,4608]{1,0:T(8,128)(2,1)S(1)} %slice_dynamic-update-slice_fusion.refs_0_), channel_id=1, source_target_pairs={{0,2},{1,3},{2,0},{3,1},{4,6},{5,7},{6,4},{7,5},{8,10},{9,11},{10,... | collective-permute-start | bytes 442376 | tf_op jit(solution)/shard_map/ppermute | solution.py:727
  23.0 10.0 %collective-permute-start.10 = (bf16[16,4608]{1,0:T(8,128)(2,1)S(1)}, bf16[16,4608]{1,0:T(8,128)(2,1)S(1)}, u32[]{:S(2)}, u32[]{:S(2)}) collective-permute-start(bf16[16,4608]{1,0:T(8,128)(2,1)S(1)} %slice_dynamic-update-slice_fusion.refs_0_), channel_id=1, source_target_pairs={{0,1},{1,2},{2,3},{3,0},{4,5},{5,6},{6,7},{7,4},{8,9},{9,10},{10,1... | collective-permute-start | bytes 442376 | tf_op jit(solution)/shard_map/ppermute | solution.py:727
  33.3 27.9 %collective-permute-start.15 = (bf16[64,4608]{1,0:T(8,128)(2,1)S(1)}, bf16[64,4608]{1,0:T(8,128)(2,1)S(1)}, u32[]{:S(2)}, u32[]{:S(2)}) collective-permute-start(bf16[64,4608]{1,0:T(8,128)(2,1)S(1)} %column.3.refs_0_), channel_id=1, source_target_pairs={{0,24},{1,25},{2,26},{3,27},{4,28},{5,29},{6,30},{7,31},{8,16},{9,... | collective-permute-start | bytes 1769480 | tf_op jit(solution)/shard_map/ppermute | solution.py:727
  35.8 25.8 %collective-permute-start.14 = (bf16[64,4608]{1,0:T(8,128)(2,1)S(1)}, bf16[64,4608]{1,0:T(8,128)(2,1)S(1)}, u32[]{:S(2)}, u32[]{:S(2)}) collective-permute-start(bf16[64,4608]{1,0:T(8,128)(2,1)S(1)} %column.3.refs_0_), channel_id=1, source_target_pairs={{0,16},{1,17},{2,18},{3,19},{4,20},{5,21},{6,22},{7,23},{8,24},{9,... | collective-permute-start | bytes 1769480 | tf_op jit(solution)/shard_map/ppermute | solution.py:727
  36.3 25.4 %collective-permute-start.13 = (bf16[64,4608]{1,0:T(8,128)(2,1)S(1)}, bf16[64,4608]{1,0:T(8,128)(2,1)S(1)}, u32[]{:S(2)}, u32[]{:S(2)}) collective-permute-start(bf16[64,4608]{1,0:T(8,128)(2,1)S(1)} %column.3.refs_0_), channel_id=1, source_target_pairs={{0,8},{1,9},{2,10},{3,11},{4,12},{5,13},{6,14},{7,15},{8,0},{9,1},... | collective-permute-start | bytes 1769480 | tf_op jit(solution)/shard_map/ppermute | solution.py:727
  36.9 1.8 %collective-permute-start.9 = (bf16[64,1664]{1,0:T(8,128)(2,1)S(1)}, bf16[64,1664]{1,0:T(8,128)(2,1)S(1)}, u32[]{:S(2)}, u32[]{:S(2)}) collective-permute-start(bf16[64,1664]{1,0:T(8,128)(2,1)S(1)} %collective-permute-done.5.refs_3_), channel_id=1, source_target_pairs={{0,4},{1,5},{2,6},{3,7},{4,0},{5,1},{6,2},{7,3},{8,12},{9,13},{10,... | collective-permute-start | bytes 638984 | tf_op jit(solution)/shard_map/ppermute | solution.py:727
  61.7 2.0 %collective-permute-start.16 = (bf16[64,4608]{1,0:T(8,128)(2,1)S(1)}, bf16[64,4608]{1,0:T(8,128)(2,1)S(1)}, u32[]{:S(2)}, u32[]{:S(2)}) collective-permute-start(bf16[64,4608]{1,0:T(8,128)(2,1)S(1)} %column.3.refs_0_), channel_id=1, source_target_pairs={{0,4},{1,5},{2,6},{3,7},{4,0},{5,1},{6,2},{7,3},{8,12},{9,13},{10,... | collective-permute-start | bytes 1769480 | tf_op jit(solution)/shard_map/ppermute | solution.py:727
  61.7 2.8 %collective-permute-start.17 = (bf16[64,4608]{1,0:T(8,128)(2,1)S(1)}, bf16[64,4608]{1,0:T(8,128)(2,1)S(1)}, u32[]{:S(2)}, u32[]{:S(2)}) collective-permute-start(bf16[64,4608]{1,0:T(8,128)(2,1)S(1)} %collective-permute-done.13.refs_1_), channel_id=1, source_target_pairs={{0,4},{1,5},{2,6},{3,7},{4,0},{5,1},{6,2},{7,3},{8,12},{9,13},{10,... | collective-permute-start | bytes 1769480 | tf_op jit(solution)/shard_map/ppermute | solution.py:727
  62.3 3.2 %collective-permute-start.18 = (bf16[64,4608]{1,0:T(8,128)(2,1)S(1)}, bf16[64,4608]{1,0:T(8,128)(2,1)S(1)}, u32[]{:S(2)}, u32[]{:S(2)}) collective-permute-start(bf16[64,4608]{1,0:T(8,128)(2,1)S(1)} %collective-permute-done.14.refs_2_), channel_id=1, source_target_pairs={{0,4},{1,5},{2,6},{3,7},{4,0},{5,1},{6,2},{7,3},{8,12},{9,13},{10,... | collective-permute-start | bytes 1769480 | tf_op jit(solution)/shard_map/ppermute | solution.py:727
  62.3 4.0 %collective-permute-start.19 = (bf16[64,4608]{1,0:T(8,128)(2,1)S(1)}, bf16[64,4608]{1,0:T(8,128)(2,1)S(1)}, u32[]{:S(2)}, u32[]{:S(2)}) collective-permute-start(bf16[64,4608]{1,0:T(8,128)(2,1)S(1)} %collective-permute-done.15.refs_3_), channel_id=1, source_target_pairs={{0,4},{1,5},{2,6},{3,7},{4,0},{5,1},{6,2},{7,3},{8,12},{9,13},{10,... | collective-permute-start | bytes 1769480 | tf_op jit(solution)/shard_map/ppermute | solution.py:727
  92.2 4.6 %collective-permute-start.20 = (bf16[4,64,4608]{2,1,0:T(8,128)(2,1)S(1)}, bf16[4,64,4608]{2,1,0:T(8,128)(2,1)S(1)}, u32[]{:S(2)}, u32[]{:S(2)}) collective-permute-start(bf16[4,64,4608]{2,1,0:T(8,128)(2,1)S(1)} %get-tuple-element.160), channel_id=1, source_target_pairs={{0,4},{1,5},{2,6},{3,7},{4,0},{5,1},{6,2},{7,3},{8,12},{9,13},{10,... | collective-permute-start | bytes 7077896 | tf_op jit(solution)/shard_map/ppermute | solution.py:727
  97.9 25.6 %collective-permute-start.21 = (bf16[64,4608]{1,0:T(8,128)(2,1)S(1)}, bf16[64,4608]{1,0:T(8,128)(2,1)S(1)}, u32[]{:S(2)}, u32[]{:S(2)}) collective-permute-start(bf16[64,4608]{1,0:T(8,128)(2,1)S(1)} %get-tuple-element.161), channel_id=1, source_target_pairs={{0,8},{1,9},{2,10},{3,11},{4,12},{5,13},{6,14},{7,15},{8,0},{9,1},... | collective-permute-start | bytes 1769480 | tf_op jit(solution)/shard_map/ppermute | solution.py:727
  99.5 27.8 %collective-permute-start.22 = (bf16[64,4608]{1,0:T(8,128)(2,1)S(1)}, bf16[64,4608]{1,0:T(8,128)(2,1)S(1)}, u32[]{:S(2)}, u32[]{:S(2)}) collective-permute-start(bf16[64,4608]{1,0:T(8,128)(2,1)S(1)} %get-tuple-element.162), channel_id=1, source_target_pairs={{0,16},{1,17},{2,18},{3,19},{4,20},{5,21},{6,22},{7,23},{8,24},{9,... | collective-permute-start | bytes 1769480 | tf_op jit(solution)/shard_map/ppermute | solution.py:727
  100.5 26.8 %collective-permute-start.23 = (bf16[64,4608]{1,0:T(8,128)(2,1)S(1)}, bf16[64,4608]{1,0:T(8,128)(2,1)S(1)}, u32[]{:S(2)}, u32[]{:S(2)}) collective-permute-start(bf16[64,4608]{1,0:T(8,128)(2,1)S(1)} %get-tuple-element.163), channel_id=1, source_target_pairs={{0,24},{1,25},{2,26},{3,27},{4,28},{5,29},{6,30},{7,31},{8,16},{9,... | collective-permute-start | bytes 1769480 | tf_op jit(solution)/shard_map/ppermute | solution.py:727
  132.1 2.4 %collective-permute-start.24 = (bf16[4,64,1664]{2,1,0:T(8,128)(2,1)S(1)}, bf16[4,64,1664]{2,1,0:T(8,128)(2,1)S(1)}, u32[]{:S(2)}, u32[]{:S(2)}) collective-permute-start(bf16[4,64,1664]{2,1,0:T(8,128)(2,1)S(1)} %get-tuple-element.179), channel_id=1, source_target_pairs={{0,4},{1,5},{2,6},{3,7},{4,0},{5,1},{6,2},{7,3},{8,12},{9,13},{10,... | collective-permute-start | bytes 2555912 | tf_op jit(solution)/shard_map/ppermute | solution.py:727
  132.2 8.2 %collective-permute-start.28 = (bf16[16,4608]{1,0:T(8,128)(2,1)S(1)}, bf16[16,4608]{1,0:T(8,128)(2,1)S(1)}, u32[]{:S(2)}, u32[]{:S(2)}) collective-permute-start(bf16[16,4608]{1,0:T(8,128)(2,1)S(1)} %get-tuple-element.173), channel_id=1, source_target_pairs={{0,1},{1,2},{2,3},{3,0},{4,5},{5,6},{6,7},{7,4},{8,9},{9,10},{10,1... | collective-permute-start | bytes 442376 | tf_op jit(solution)/shard_map/ppermute | solution.py:727
  134.7 15.2 %collective-permute-start.25 = (bf16[64,1664]{1,0:T(8,128)(2,1)S(1)}, bf16[64,1664]{1,0:T(8,128)(2,1)S(1)}, u32[]{:S(2)}, u32[]{:S(2)}) collective-permute-start(bf16[64,1664]{1,0:T(8,128)(2,1)S(1)} %get-tuple-element.180), channel_id=1, source_target_pairs={{0,8},{1,9},{2,10},{3,11},{4,12},{5,13},{6,14},{7,15},{8,0},{9,1},... | collective-permute-start | bytes 638984 | tf_op jit(solution)/shard_map/ppermute | solution.py:727
  135.6 14.3 %collective-permute-start.26 = (bf16[64,1664]{1,0:T(8,128)(2,1)S(1)}, bf16[64,1664]{1,0:T(8,128)(2,1)S(1)}, u32[]{:S(2)}, u32[]{:S(2)}) collective-permute-start(bf16[64,1664]{1,0:T(8,128)(2,1)S(1)} %get-tuple-element.181), channel_id=1, source_target_pairs={{0,16},{1,17},{2,18},{3,19},{4,20},{5,21},{6,22},{7,23},{8,24},{9,... | collective-permute-start | bytes 638984 | tf_op jit(solution)/shard_map/ppermute | solution.py:727
  136.8 13.1 %collective-permute-start.27 = (bf16[64,1664]{1,0:T(8,128)(2,1)S(1)}, bf16[64,1664]{1,0:T(8,128)(2,1)S(1)}, u32[]{:S(2)}, u32[]{:S(2)}) collective-permute-start(bf16[64,1664]{1,0:T(8,128)(2,1)S(1)} %get-tuple-element.182), channel_id=1, source_target_pairs={{0,24},{1,25},{2,26},{3,27},{4,28},{5,29},{6,30},{7,31},{8,16},{9,... | collective-permute-start | bytes 638984 | tf_op jit(solution)/shard_map/ppermute | solution.py:727
  138.3 8.6 %collective-permute-start.29 = (bf16[16,4608]{1,0:T(8,128)(2,1)S(1)}, bf16[16,4608]{1,0:T(8,128)(2,1)S(1)}, u32[]{:S(2)}, u32[]{:S(2)}) collective-permute-start(bf16[16,4608]{1,0:T(8,128)(2,1)S(1)} %get-tuple-element.174), channel_id=1, source_target_pairs={{0,2},{1,3},{2,0},{3,1},{4,6},{5,7},{6,4},{7,5},{8,10},{9,11},{10,... | collective-permute-start | bytes 442376 | tf_op jit(solution)/shard_map/ppermute | solution.py:727
  140.4 8.3 %collective-permute-start.30 = (bf16[16,4608]{1,0:T(8,128)(2,1)S(1)}, bf16[16,4608]{1,0:T(8,128)(2,1)S(1)}, u32[]{:S(2)}, u32[]{:S(2)}) collective-permute-start(bf16[16,4608]{1,0:T(8,128)(2,1)S(1)} %get-tuple-element.175), channel_id=1, source_target_pairs={{0,3},{1,0},{2,1},{3,2},{4,7},{5,4},{6,5},{7,6},{8,11},{9,8},{10,9... | collective-permute-start | bytes 442376 | tf_op jit(solution)/shard_map/ppermute | solution.py:727
  150.1 6.2 %collective-permute-start.31 = (bf16[16,1664]{1,0:T(8,128)(2,1)S(1)}, bf16[16,1664]{1,0:T(8,128)(2,1)S(1)}, u32[]{:S(2)}, u32[]{:S(2)}) collective-permute-start(bf16[16,1664]{1,0:T(8,128)(2,1)S(1)} %get-tuple-element.195), channel_id=1, source_target_pairs={{0,1},{1,2},{2,3},{3,0},{4,5},{5,6},{6,7},{7,4},{8,9},{9,10},{10,1... | collective-permute-start | bytes 159752 | tf_op jit(solution)/shard_map/ppermute | solution.py:727
  151.7 6.2 %collective-permute-start.32 = (bf16[16,1664]{1,0:T(8,128)(2,1)S(1)}, bf16[16,1664]{1,0:T(8,128)(2,1)S(1)}, u32[]{:S(2)}, u32[]{:S(2)}) collective-permute-start(bf16[16,1664]{1,0:T(8,128)(2,1)S(1)} %get-tuple-element.196), channel_id=1, source_target_pairs={{0,2},{1,3},{2,0},{3,1},{4,6},{5,7},{6,4},{7,5},{8,10},{9,11},{10,... | collective-permute-start | bytes 159752 | tf_op jit(solution)/shard_map/ppermute | solution.py:727
  154.1 4.3 %collective-permute-start.33 = (bf16[16,1664]{1,0:T(8,128)(2,1)S(1)}, bf16[16,1664]{1,0:T(8,128)(2,1)S(1)}, u32[]{:S(2)}, u32[]{:S(2)}) collective-permute-start(bf16[16,1664]{1,0:T(8,128)(2,1)S(1)} %get-tuple-element.197), channel_id=1, source_target_pairs={{0,3},{1,0},{2,1},{3,2},{4,7},{5,4},{6,5},{7,6},{8,11},{9,8},{10,9... | collective-permute-start | bytes 159752 | tf_op jit(solution)/shard_map/ppermute | solution.py:727
  159.8 10.5 %all-to-all-start = ((f32[32,1,128]{2,1,0:T(1,128)}), f32[32,1,128]{2,1,0:T(1,128)S(1)}, u32[]{:S(2)}, u32[]{:S(2)}) async-start(f32[32,1,128]{2,1,0:T(1,128)} %broadcast_in_dim.17), calls=%async_computation | async-start | bytes 32768 | tf_op jit(solution)/shard_map/all_to_all | solution.py:761
  (21 other events, 215.2 us)
where the time goes:
time: 172 us
  Pallas kernels  81.3 us (47%)
  waiting for transfers between devices  46 us (27%)
  starting transfers between devices  34.7 us (20%)
  local copies, waits for them, and re-layouts  4.55 us (3%)
  other arithmetic  4.19 us (2%)
    ppermute x34, waiting for transfers between devices, permute(): return lax.ppermute(value, AXES, pairs)  41 us
    ppermute x34, starting transfers between devices, permute(): return lax.ppermute(value, AXES, pairs)  31.3 us
    pallas_call x1, Pallas kernels, feed(): pl.pallas_call(partial(feed_kernel, reps, len(pieces), len(deep_pieces)),...  25.9 us
    pallas_call x1, Pallas kernels, attend(): pl.pallas_call(partial(attend_kernel, len(pieces)), out_shape=(wide, wide...  21.1 us
    pallas_call x1, Pallas kernels, attend_back(): pl.pallas_call(attend_back_kernel, out_shape=jax.ShapeDtypeStruct((rows,...  18.8 us
    all_to_all x1, waiting for transfers between devices, exchange(): return lax.all_to_all(value, AXES, 0, 0)  5.06 us
    pallas_call x1, Pallas kernels, project_back(): pl.pallas_call(project_back_kernel, out_shape=(jax.ShapeDtypeStruct(shape...  3.9 us
  transfers between devices with their start and end apart: 35, of which 23 were waited for; matrix products, arithmetic and copies ran while one was open for 2% of the time, Pallas kernels for 28%

commit v1 on v0

--- a/solution.py
+++ b/solution.py
@@ -25,6 +25,7 @@
 THIN = 32
 CHUNK = 352
 VMEM = pltpu.MemorySpace.VMEM
+AXES = ("dp", "rep")
 
 
 def params(mebibytes):
@@ -41,62 +42,95 @@
     return center * scale, scale
 
 
-def core_index():
-    return lax.rem(lax.axis_index("dp"), 2)
-
-
-def plane_index():
-    return lax.div(lax.axis_index("dp"), 2)
-
-
-def block_at(m, other, rows):
-    core = core_index()
-    side = 1 - core if other else core
-    return pl.multiple_of((2 * (plane_index() ^ m) + side) * rows, rows)
-
-
-def assemble(pieces, full_ref, columns):
-    plane = len(pieces) // 2
+class Layout:
+    def __init__(self, mesh):
+        self.dp = mesh.shape["dp"]
+        self.rep = mesh.shape["rep"]
+        self.plane = self.dp // 2
+        self.mixed = self.plane == self.rep
+
+    def pairs(self, move):
+        pairs = []
+        for p in range(self.plane):
+            for c in range(2):
+                for z in range(self.rep):
+                    q, d, w = move(p, c, z)
+                    pairs.append(((p * 2 + c) * self.rep + z, (q * 2 + d) * self.rep + w))
+        return pairs
+
+    def over(self, value, i, first):
+        def move(p, c, z):
+            along_z = (first == (c == 0)) if self.mixed else first
+            return (p, c, (z + i) % self.rep) if along_z else (p ^ i, c, z)
+
+        return lax.ppermute(value, AXES, self.pairs(move))
+
+    def to_core(self, value):
+        return lax.ppermute(value, AXES, self.pairs(lambda p, c, z: (p, 1 - c, z)))
+
+    def core(self):
+        return lax.rem(lax.axis_index("dp"), 2)
+
+    def partner(self, side, i, first, sign):
+        along_z = lax.rem(lax.axis_index("rep") + (sign * i) % self.rep, self.rep)
+        in_plane = lax.div(lax.axis_index("dp"), 2) ^ i
+        if not self.mixed:
+            return along_z if first else in_plane
+        return jnp.where(side == 0, along_z, in_plane) if first else jnp.where(side == 0, in_plane, along_z)
+
+    def device(self, side, second, first):
+        plain = (2 * second + side) * self.rep + first
+        return jnp.where(side == 0, plain, (2 * first + side) * self.rep + second) if self.mixed else plain
+
+
+def row_blocks(lay, side, second, rows):
+    firsts = lay.rep
+    if lay.mixed:
+        return [(j * rows, pl.multiple_of(lay.device(side, second, j) * rows, rows), rows) for j in range(firsts)]
+    return [(0, pl.multiple_of(lay.device(side, second, 0) * rows, firsts * rows), firsts * rows)]
+
+
+def assemble(lay, pieces, full_ref, columns):
+    count = len(pieces) // 2
     for i, piece in enumerate(pieces):
-        at = block_at(i % plane, i >= plane, piece.shape[0])
-        full_ref[pl.ds(at, piece.shape[0]), :] = piece[:, columns]
-
-
-def assemble_deep(pieces, full_ref, first, reps):
-    plane = len(pieces) // 2
+        side = lay.core() if i < count else 1 - lay.core()
+        second = lay.partner(side, i % count, False, -1)
+        for at, to, rows in row_blocks(lay, side, second, piece.shape[0] // lay.rep):
+            full_ref[pl.ds(to, rows), :] = piece[at : at + rows, columns]
+
+
+def assemble_deep(lay, pieces, full_ref, first):
+    count = len(pieces) // 2
     width = full_ref.shape[1]
     for i, piece in enumerate(pieces):
-        rows = piece.shape[0] // reps
-        at = block_at(i % plane, i >= plane, 4 * piece.shape[0])
-        for z in range(reps):
+        side = lay.core() if i < count else 1 - lay.core()
+        second = lay.partner(side, i % count, False, -1)
+        rows = piece.shape[0] // lay.rep
+        for z in range(lay.rep):
+            to = pl.multiple_of(lay.device(side, second, z) * 4 * rows, 4 * rows)
             for j in range(4):
                 source = piece[z * rows : (z + 1) * rows, first + j * width : first + (j + 1) * width]
-                full_ref[pl.ds(at + (4 * z + j) * rows, rows), :] = source
-
-
-def split_rows(full_ref, keep_ref, send_ref, lanes):
-    plane, rows, _ = keep_ref.shape
-    core = core_index()
-    for p in range(plane):
-        at = pl.multiple_of((2 * p + core) * rows, rows)
-        keep_ref[p, :, lanes] = full_ref[pl.ds(at, rows), :].astype(keep_ref.dtype)
-        at = pl.multiple_of((2 * p + 1 - core) * rows, rows)
-        send_ref[p, :, lanes] = full_ref[pl.ds(at, rows), :].astype(jnp.bfloat16)
-
-
-def split_deep(full_ref, keep_ref, send_ref, first, reps):
-    plane, rows, _ = keep_ref.shape
+                full_ref[pl.ds(to + j * rows, rows), :] = source
+
+
+def split_rows(lay, full_ref, keep_ref, send_ref, lanes):
+    for target, side in ((keep_ref, lay.core()), (send_ref, 1 - lay.core())):
+        for second in range(target.shape[0]):
+            for at, source, rows in row_blocks(lay, side, second, target.shape[1] // lay.rep):
+                target[second, at : at + rows, lanes] = full_ref[pl.ds(source, rows), :].astype(target.dtype)
+
+
+def split_deep(lay, full_ref, keep_ref, send_ref, first):
     width = full_ref.shape[1]
-    core = core_index()
-    each = rows // reps
-    for p in range(plane):
-        for side, target in ((core, keep_ref), (1 - core, send_ref)):
-            base = pl.multiple_of((2 * p + side) * 4 * rows, 4 * rows)
-            for z in range(reps):
+    rows = keep_ref.shape[1] // lay.rep
+    for target, side in ((keep_ref, lay.core()), (send_ref, 1 - lay.core())):
+        for second in range(target.shape[0]):
+            for z in range(lay.rep):
+                source = pl.multiple_of(lay.device(side, second, z) * 4 * rows, 4 * rows)
                 for j in range(4):
-                    source = full_ref[pl.ds(base + (4 * z + j) * each, each), :]
+                    part = full_ref[pl.ds(source + j * rows, rows), :]
                     columns = slice(first + j * width, first + (j + 1) * width)
-                    target[p, z * each : (z + 1) * each, columns] = source.astype(target.dtype)
+                    target[second, z * rows : (z + 1) * rows, columns] = part.astype(target.dtype)
 
 
 def row_chunks(rows, size):
@@ -188,12 +222,12 @@
     )(begin, first, second)
 
 
-def attend_kernel(count, x, labels, *refs):
+def attend_kernel(lay, count, x, labels, *refs):
     pieces = refs[:count]
     qx, kx, vx, mixed, gains, weight, qs = refs[count:]
     rows = x.shape[0]
     width = mixed.shape[1]
-    assemble(pieces, weight, slice(None))
+    assemble(lay, pieces, weight, slice(None))
     gains[...] = jnp.transpose(weight[:, 3 * width :].astype(jnp.float32))[:8]
     gain, bias = gains[0:1], gains[1:2]
 
@@ -255,12 +289,12 @@
     lax.fori_loop(0, width // LANES, one_pair, 0)
 
 
-def attend(x, labels, pieces):
+def attend(lay, x, labels, pieces):
     rows, width = x.shape
     wide = jax.ShapeDtypeStruct((rows, 2 * width), jnp.bfloat16)
     depth = len(pieces) * pieces[0].shape[0]
     return pl.pallas_call(
-        partial(attend_kernel, len(pieces)),
+        partial(attend_kernel, lay, len(pieces)),
         out_shape=(
             wide,
             wide,
@@ -333,19 +367,19 @@
     )
 
 
-def feed_kernel(reps, count, deep_count, x, mixed, dy, gains, *refs):
+def feed_kernel(lay, count, deep_count, x, mixed, dy, gains, *refs):
     pieces = refs[:count]
     deep_pieces = refs[count : count + deep_count]
-    outputs, dox, middle_grad, keep2, send2, norm_grads, *deep_out = refs[count + deep_count : -7]
-    wide, contract, active, hidden_grad, second, middle_low, block = refs[-7:]
+    outputs, dox, middle_grad, keep2, send2, norm_grads, *deep_out = refs[count + deep_count : -8]
+    wide, contract, active, hidden_grad, second, middle_low, block, deep_block = refs[-8:]
     rows, width = x.shape
     hidden = contract.shape[0]
     wide_part = slice(0, width + hidden)
-    assemble(pieces, wide, wide_part)
+    assemble(lay, pieces, wide, wide_part)
     if deep_count:
-        assemble(deep_pieces, contract, slice(None))
+        assemble(lay, deep_pieces, contract, slice(None))
     else:
-        assemble_deep(pieces, contract, width + hidden, reps)
+        assemble_deep(lay, pieces, contract, width + hidden)
     gain, bias = gains[2:3], gains[3:4]
     zero = jnp.zeros((1, width), jnp.float32)
 
@@ -400,28 +434,24 @@
 
     gain_sum, bias_sum = lax.fori_loop(0, rows // CHUNK, one_chunk, (zero, zero))
     norm_grads[...] = jnp.concatenate([gain_sum, bias_sum, jnp.zeros((6, width), jnp.float32)], axis=0)
-    plane = keep2.shape[0]
-    deep = hidden // (2 * plane)
-    each = 512 // (2 * deep)
 
     def one_block(i, carry):
         columns = pl.ds(pl.multiple_of(i * 512, 512), 512)
-        block[...] = dot(active[:, columns], dy[...], 0, 0)
-        planes = pl.ds(i * each, each)
-        if deep_count:
-            split_rows(block, deep_out[0].at[planes], deep_out[1].at[planes], slice(0, width))
-        else:
-            split_deep(block, keep2.at[planes], send2.at[planes], width + hidden, reps)
+        deep_block[columns] = dot(active[:, columns], dy[...], 0, 0)
         block[...] = dot(second[...], hidden_grad[:, columns], 0, 0)
-        split_rows(block, keep2, send2, pl.ds(pl.multiple_of(width + i * 512, 512), 512))
+        split_rows(lay, block, keep2, send2, pl.ds(pl.multiple_of(width + i * 512, 512), 512))
         return carry
 
     lax.fori_loop(0, hidden // 512, one_block, 0)
+    if deep_count:
+        split_rows(lay, deep_block, *deep_out, slice(0, width))
+    else:
+        split_deep(lay, deep_block, keep2, send2, width + hidden)
     block[...] = dot(mixed[...], middle_low[...], 0, 0)
-    split_rows(block, keep2, send2, slice(0, width))
-
-
-def feed(reps, x, mixed, dy, gains, pieces, deep_pieces):
+    split_rows(lay, block, keep2, send2, slice(0, width))
+
+
+def feed(lay, x, mixed, dy, gains, pieces, deep_pieces):
     rows, width = x.shape
     plane = len(pieces) // 2
     deep = pieces[0].shape[0]
@@ -439,7 +469,7 @@
         out_shape.append(jax.ShapeDtypeStruct((plane, 4 * deep, width), jnp.bfloat16))
         out_shape.append(jax.ShapeDtypeStruct((plane, 4 * deep, width), jnp.bfloat16))
     return pl.pallas_call(
-        partial(feed_kernel, reps, len(pieces), len(deep_pieces)),
+        partial(feed_kernel, lay, len(pieces), len(deep_pieces)),
         out_shape=out_shape,
         in_specs=[pl.BlockSpec(memory_space=VMEM)] * (4 + len(pieces) + len(deep_pieces)),
         out_specs=[pl.BlockSpec(memory_space=VMEM)] * len(out_shape),
@@ -451,13 +481,14 @@
             pltpu.VMEM((rows, width), jnp.bfloat16),
             pltpu.VMEM((rows, width), jnp.bfloat16),
             pltpu.VMEM((width, 512), jnp.float32),
+            pltpu.VMEM((hidden, width), jnp.float32),
         ],
         compiler_params=params(30),
         name="feed",
     )(x, mixed, dy, gains, *pieces, *deep_pieces)
 
 
-def project_back_kernel(x, packed, gains, first_norms, second_norms, keep, send, first, block):
+def project_back_kernel(lay, x, packed, gains, first_norms, second_norms, keep, send, first, block):
     rows, width = x.shape
     gain, bias = gains[0:1], gains[1:2]
 
@@ -472,21 +503,21 @@
     def one_block(i, carry):
         columns = pl.ds(pl.multiple_of(i * 512, 512), 512)
         block[...] = dot(first[...], packed[:, columns], 0, 0)
-        split_rows(block, keep, send, columns)
+        split_rows(lay, block, keep, send, columns)
         return carry
 
     lax.fori_loop(0, packed.shape[1] // 512, one_block, 0)
     fill = jnp.zeros((LANES - 4, width), jnp.float32)
     norms = jnp.concatenate([first_norms[:2], second_norms[:2], fill], axis=0)
     block[:, :LANES] = jnp.transpose(norms)
-    split_rows(block.at[:, :LANES], keep, send, slice(packed.shape[1], packed.shape[1] + LANES))
-
-
-def project_back(x, packed, gains, first_norms, second_norms, plane, deep):
+    split_rows(lay, block.at[:, :LANES], keep, send, slice(packed.shape[1], packed.shape[1] + LANES))
+
+
+def project_back(lay, x, packed, gains, first_norms, second_norms, own):
     rows, width = x.shape
-    shape = (plane, deep, packed.shape[1] + LANES)
+    shape = (lay.plane, lay.rep * own, packed.shape[1] + LANES)
     return pl.pallas_call(
-        project_back_kernel,
+        partial(project_back_kernel, lay),
         out_shape=(jax.ShapeDtypeStruct(shape, jnp.bfloat16), jax.ShapeDtypeStruct(shape, jnp.bfloat16)),
         in_specs=[pl.BlockSpec(memory_space=VMEM)] * 5,
         out_specs=[pl.BlockSpec(memory_space=VMEM)] * 2,
@@ -496,11 +527,11 @@
     )(x, packed, gains, first_norms, second_norms)
 
 
-def input_back_kernel(x, packed, gains, middle_grad, *refs):
+def input_back_kernel(lay, x, packed, gains, middle_grad, *refs):
     pieces = refs[:-3]
     grad_in, norm_grads, weight = refs[-3:]
     rows, width = x.shape
-    assemble(pieces, weight, slice(None))
+    assemble(lay, pieces, weight, slice(None))
     gain = gains[0:1]
     zero = jnp.zeros((1, width), jnp.float32)
 
@@ -517,10 +548,10 @@
     norm_grads[...] = jnp.concatenate([gain_sum, bias_sum, jnp.zeros((6, width), jnp.float32)], axis=0)
 
 
-def input_back(x, packed, gains, middle_grad, pieces):
+def input_back(lay, x, packed, gains, middle_grad, pieces):
     rows, width = x.shape
     return pl.pallas_call(
-        input_back_kernel,
+        partial(input_back_kernel, lay),
         out_shape=(jax.ShapeDtypeStruct((rows, width), jnp.bfloat16), jax.ShapeDtypeStruct((8, width), jnp.float32)),
         in_specs=[pl.BlockSpec(memory_space=VMEM)] * (4 + len(pieces)),
         out_specs=[pl.BlockSpec(memory_space=VMEM)] * 2,
@@ -530,48 +561,43 @@
     )(x, packed, gains, middle_grad, *pieces)
 
 
-def column_kernel(*refs):
-    reps = len(refs) - 1
+def column_kernel(lay, *refs):
     out = refs[-1]
-    z = lax.axis_index("rep")
-    rows = refs[0].shape[0]
     got = [ref[...].astype(jnp.float32) for ref in refs[:-1]]
     parts = []
-    for j in range(reps):
+    for j in range(len(got)):
         part = got[0]
-        for k in range(1, reps):
-            part = jnp.where(lax.rem(z + reps - k, reps) == j, got[k], part)
+        for i in range(1, len(got)):
+            part = jnp.where(lay.partner(lay.core(), i, True, -1) == j, got[i], part)
         parts.append(part)
     out[...] = jnp.concatenate(parts, axis=0).astype(out.dtype)
 
 
-def column_of(shards):
+def column_of(lay, shards):
     rows, cols = shards[0].shape
-    reps = len(shards)
     return pl.pallas_call(
-        column_kernel,
-        out_shape=jax.ShapeDtypeStruct((reps * rows, cols), shards[0].dtype),
-        in_specs=[pl.BlockSpec(memory_space=VMEM)] * reps,
+        partial(column_kernel, lay),
+        out_shape=jax.ShapeDtypeStruct((len(shards) * rows, cols), shards[0].dtype),
+        in_specs=[pl.BlockSpec(memory_space=VMEM)] * len(shards),
         out_specs=pl.BlockSpec(memory_space=VMEM),
         compiler_params=params(4),
         name="column",
     )(*shards)
 
 
-def chip_sum_kernel(keep, got, own, *low):
-    p = plane_index()
-    own[...] = keep[p].astype(jnp.float32) + got[p].astype(jnp.float32)
-    for m, ref in enumerate(low, 1):
-        ref[...] = (keep[p ^ m].astype(jnp.float32) + got[p ^ m].astype(jnp.float32)).astype(jnp.bfloat16)
-
-
-def chip_sum(keep, got):
+def chip_sum_kernel(lay, keep, got, *outs):
+    for i, ref in enumerate(outs):
+        at = lay.partner(lay.core(), i, False, 1)
+        ref[...] = (keep[at].astype(jnp.float32) + got[at].astype(jnp.float32)).astype(ref.dtype)
+
+
+def chip_sum(lay, keep, got):
     plane, rows, cols = keep.shape
     block = cols if cols < 2048 else 1536
     part = pl.BlockSpec((rows, block), lambda i: (0, i))
     whole = pl.BlockSpec((plane, rows, block), lambda i: (0, 0, i))
     return pl.pallas_call(
-        chip_sum_kernel,
+        partial(chip_sum_kernel, lay),
         grid=(cols // block,),
         out_shape=[jax.ShapeDtypeStruct((rows, cols), jnp.float32)]
         + [jax.ShapeDtypeStruct((rows, cols), jnp.bfloat16)] * (plane - 1),
@@ -582,29 +608,28 @@
     )(keep, got)
 
 
-def plane_sum_kernel(own, *refs):
-    plane = sum(1 for ref in refs if ref.shape == own.shape) + 1
-    got, out, low = refs[: plane - 1], refs[plane - 1], refs[plane:]
-    reps = len(low) + 1
-    rows = out.shape[0]
-    z = lax.axis_index("rep")
+def plane_sum_kernel(lay, own, *refs):
+    got, outs = refs[: lay.plane - 1], refs[lay.plane - 1 :]
+    rows = outs[0].shape[0]
     total = own[...]
     for ref in got:
         total = total + ref[...].astype(jnp.float32)
-    for k, ref in enumerate((out, *low)):
+    for i, ref in enumerate(outs):
+        at = lay.partner(lay.core(), i, True, 1)
         part = total[:rows]
-        for j in range(1, reps):
-            part = jnp.where(lax.rem(z + k, reps) == j, total[j * rows : (j + 1) * rows], part)
+        for j in range(1, lay.rep):
+            part = jnp.where(at == j, total[j * rows : (j + 1) * rows], part)
         ref[...] = part.astype(ref.dtype)
 
 
-def plane_sum(own, got, reps):
+def plane_sum(lay, own, got):
     rows, cols = own.shape
+    reps = lay.rep
     block = cols if cols < 2048 else 1536
     part = pl.BlockSpec((rows, block), lambda i: (0, i))
     small = pl.BlockSpec((rows // reps, block), lambda i: (0, i))
     return pl.pallas_call(
-        plane_sum_kernel,
+        partial(plane_sum_kernel, lay),
         grid=(cols // block,),
         out_shape=[jax.ShapeDtypeStruct((rows // reps, cols), jnp.float32)]
         + [jax.ShapeDtypeStruct((rows // reps, cols), jnp.bfloat16)] * (reps - 1),
@@ -708,44 +733,12 @@
     return outs[:n], outs[n][:3, :n]
 
 
-AXES = ("dp", "rep")
-
-
-class Layout:
-    def __init__(self, mesh):
-        self.dp = mesh.shape["dp"]
-        self.rep = mesh.shape["rep"]
-        self.plane = self.dp // 2
-
-    def permute(self, value, move):
-        pairs = []
-        for p in range(self.plane):
-            for c in range(2):
-                for z in range(self.rep):
-                    q, d, w = move(p, c, z)
-                    pairs.append(((p * 2 + c) * self.rep + z, (q * 2 + d) * self.rep + w))
-        return lax.ppermute(value, AXES, pairs)
-
-    def to_core(self, value):
-        return self.permute(value, lambda p, c, z: (p, 1 - c, z))
-
-    def to_plane(self, value, m):
-        return self.permute(value, lambda p, c, z: (p ^ m, c, z))
-
-    def to_rep(self, value, k):
-        return self.permute(value, lambda p, c, z: (p, c, (z + k) % self.rep))
-
-    def place(self):
-        dp = lax.axis_index("dp")
-        return dp // 2, dp % 2, lax.axis_index("rep")
-
-
-def over_rep(lay, shard):
-    return [shard] + [lay.to_rep(shard, k) for k in range(1, lay.rep)]
-
-
-def over_plane(lay, column):
-    return [column] + [lay.to_plane(column, m) for m in range(1, lay.plane)]
+def over(lay, value, first):
+    return [value] + [lay.over(value, i, first) for i in range(1, lay.rep if first else lay.plane)]
+
+
+def send_over(lay, parts, first):
+    return [lay.over(part, i, first) for i, part in enumerate(parts, 1)]
 
 
 def over_core(lay, blocks):
@@ -791,20 +784,20 @@
     plain = own % 16 == 0
     norm_rows = jnp.pad(layer_norms.astype(jnp.bfloat16).T, ((0, 0), (0, LANES - 4)))
     shard1 = jnp.concatenate([attend_in.astype(jnp.bfloat16), norm_rows], axis=1)
-    column1 = over_rep(lay, shard1)
+    column1 = over(lay, shard1, True)
     rows = inputs.shape[1]
     attend_out_, expand_, contract_ = after([attend_out, expand, contract], [shard1])
     deep = [contract_[j * own : (j + 1) * own] for j in range(4)]
     shard2 = jnp.concatenate([part.astype(jnp.bfloat16) for part in (attend_out_, expand_, *deep)], axis=1)
     (shard2,) = after([shard2], column1[1:])
-    column2 = over_rep(lay, shard2)
-    inputs_, cotangent_, segments_ = after([inputs[0], cotangent[0], segments], [shard1])
-    x, dy, labels, begin = arrange(inputs_, cotangent_, segments_)
-    blocks1 = over_plane(lay, column_of(after(column1, [x])))
-    blocks2 = over_plane(lay, column_of(after(column2, blocks1)))
+    column2 = over(lay, shard2, True)
+    (segments_,) = after([segments], [shard1])
+    x, dy, labels, begin = arrange(inputs[0], cotangent[0], segments_)
+    blocks1 = over(lay, column_of(lay, after(column1, [x])), False)
+    blocks2 = over(lay, column_of(lay, after(column2, blocks1)), False)
     pieces1 = over_core(lay, blocks1)
     *pieces1, x, labels = after([*pieces1, x, labels], blocks2[:1])
-    qx, kx, vx, mixed, gains = attend(x, labels, pieces1)
+    qx, kx, vx, mixed, gains = attend(lay, x, labels, pieces1)
     pieces2 = over_core(lay, after(blocks2, [mixed]))
     deep_pieces = []
     if not plain:
@@ -813,7 +806,7 @@
             part = piece[:, first:].reshape(lay.rep, own, 4, depth).transpose(0, 2, 1, 3)
             deep_pieces.append(part.reshape(-1, depth))
     outputs, dox, middle_grad, keep2, send2, second_norms, *deep_out = feed(
-        lay.rep, x, mixed, dy, gains, pieces2, deep_pieces
+        lay, x, mixed, dy, gains, pieces2, deep_pieces
     )
     if not plain:
         keep2, send2 = [
@@ -826,18 +819,18 @@
             )
             for wide, part in zip((keep2, send2), deep_out)
         ]
-    own2, *low2 = chip_sum(keep2, lay.to_core(send2))
-    got2 = [lay.to_plane(part, m) for m, part in enumerate(low2, 1)]
+    own2, *low2 = chip_sum(lay, keep2, lay.to_core(send2))
+    got2 = send_over(lay, low2, False)
     (dox,) = after([dox], low2)
     packed = attend_back(qx, kx, vx, dox)
-    input_gradient, first_norms = input_back(x, packed, gains, middle_grad, pieces1)
+    input_gradient, first_norms = input_back(lay, x, packed, gains, middle_grad, pieces1)
     own2, *got2 = after([own2, *got2], [first_norms])
-    own2, *low2 = plane_sum(own2, got2, lay.rep)
-    got2 = [lay.to_rep(part, k) for k, part in enumerate(low2, 1)]
+    own2, *low2 = plane_sum(lay, own2, got2)
+    got2 = send_over(lay, low2, True)
     (packed_,) = after([packed], low2)
-    keep1, send1 = project_back(x, packed_, gains, first_norms, second_norms, lay.plane, lay.rep * own)
-    own1, *low1 = chip_sum(keep1, lay.to_core(send1))
-    got1 = [lay.to_plane(part, m) for m, part in enumerate(low1, 1)]
+    keep1, send1 = project_back(lay, x, packed_, gains, first_norms, second_norms, own)
+    own1, *low1 = chip_sum(lay, keep1, lay.to_core(send1))
+    got1 = send_over(lay, low1, False)
     outputs, input_gradient = after([outputs, input_gradient], low1)
     outputs, input_gradient = arrange_back(begin, outputs, input_gradient, rows)
     spans = [[(0, own, (0, depth))], [(0, own, (depth, depth + hidden))]]
@@ -846,9 +839,8 @@
         spans, (1, 2, 3), [own2, *got2], masters[1:4],
         (moment_out, moment_expand, moment_contract), (square_out, square_expand, square_contract),
     )
-    own1, *got1 = after([own1, *got1], [sums2])
-    own1, *low1 = plane_sum(own1, got1, lay.rep)
-    got1 = [lay.to_rep(part, k) for k, part in enumerate(low1, 1)]
+    own1, *low1 = plane_sum(lay, own1, got1)
+    got1 = send_over(lay, low1, True)
     momenta1, variances1, directions1, sums1 = moments(
         [[(0, own, (0, width))], [(0, 4, (width, width + 4, True))]], (0, 4), [own1, *got1], (attend_in, layer_norms),
         (moment_in, moment_norms), (square_in, square_norms),

time: 172 us -> 172 us (level)
  waiting for transfers between devices: 46 us -> 32.3 us
  starting transfers between devices: 34.7 us -> 48.4 us
    ppermute x34, waiting for transfers between devices: 41 us -> 27.2 us  [the longest x24 15.1 us: over(): return lax.ppermute(value, AXES, self.pairs(move))]
    ppermute x34, starting transfers between devices: 31.3 us -> 40.1 us  [the longest x24 37 us: over(): return lax.ppermute(value, AXES, self.pairs(move))]
    all_to_all x1, starting transfers between devices: 3.42 us -> 8.27 us  [exchange(): return lax.all_to_all(value, AXES, 0, 0)]
  transfers between devices with their start and end apart: 35 -> 35, of which waited for: 23 -> 16; matrix products, arithmetic and copies ran while one was open for 2% -> 2% of each run, Pallas kernels for 28% -> 28%
where the time goes in v1:
time: 172 us; the launch traced here: 171 us
  Pallas kernels  81 us (47%)
  starting transfers between devices  48.4 us (28%)
  waiting for transfers between devices  32.3 us (19%)
  local copies, waits for them, and re-layouts  4.54 us (3%)
  other arithmetic  4.19 us (2%)
    ppermute x24, starting transfers between devices, over(): return lax.ppermute(value, AXES, self.pairs(move))  37 us
    pallas_call x1, Pallas kernels, feed(): pl.pallas_call(partial(feed_kernel, lay, len(pieces), len(deep_pieces)),...  25.6 us
    pallas_call x1, Pallas kernels, attend(): pl.pallas_call(partial(attend_kernel, lay, len(pieces)), out_shape=(wide,...  21 us
    pallas_call x1, Pallas kernels, attend_back(): pl.pallas_call(attend_back_kernel, out_shape=jax.ShapeDtypeStruct((rows,...  18.8 us
    ppermute x24, waiting for transfers between devices, over(): return lax.ppermute(value, AXES, self.pairs(move))  15.1 us
    ppermute x10, waiting for transfers between devices, to_core(): return lax.ppermute(value, AXES, self.pairs(lambda p, c, z: (p, 1 - c, z)))  12.1 us
    all_to_all x1, starting transfers between devices, exchange(): return lax.all_to_all(value, AXES, 0, 0)  8.27 us
    all_to_all x1, waiting for transfers between devices, exchange(): return lax.all_to_all(value, AXES, 0, 0)  5.06 us
  transfers between devices with their start and end apart: 35, of which 16 were waited for; matrix products, arithmetic and copies ran while one was open for 2% of the time, Pallas kernels for 28%

profile of v1, /device:TPU:0, one launch (start us, length us, event | category | flops | bytes accessed | tf_op | source)
XLA Modules:
  0.0 171.5 jit_solution(12830185719685427939)
XLA Ops:
  2.3 5.1 %collective-permute-start.2 = (bf16[16,1664]{1,0:T(8,128)(2,1)S(1)}, bf16[16,1664]{1,0:T(8,128)(2,1)S(1)}, u32[]{:S(2)}, u32[]{:S(2)}) collective-permute-start(bf16[16,1664]{1,0:T(8,128)(2,1)S(1)} %fusion.1.refs_0_), channel_id=1, source_target_pairs={{0,3},{1,0},{2,1},{3,2},{4,28},{5,29},{6,30},{7,31},{8,11},{9,8},{... | collective-permute-start | bytes 159752 | tf_op jit(solution)/shard_map/ppermute | solution.py:66
  11.1 1.4 collective-permute-done.1.refs_2_
  14.1 1.2 copy-done.2
  15.3 1.2 copy-done.3
  17.2 1.1 arrange.1
  18.4 2.5 %collective-permute-start.5 = (bf16[64,1664]{1,0:T(8,128)(2,1)S(1)}, bf16[64,1664]{1,0:T(8,128)(2,1)S(1)}, u32[]{:S(2)}, u32[]{:S(2)}) collective-permute-start(bf16[64,1664]{1,0:T(8,128)(2,1)S(1)} %column.2.refs_0_), channel_id=1, source_target_pairs={{0,24},{1,25},{2,26},{3,27},{4,7},{5,4},{6,5},{7,6},{8,16},{9,17},... | collective-permute-start | bytes 638984 | tf_op jit(solution)/shard_map/ppermute | solution.py:66
  23.0 1.4 collective-permute-start.10
  24.4 9.1 %collective-permute-done.11.refs_2_ = bf16[16,4608]{1,0:T(8,128)(2,1)S(1)} collective-permute-done((bf16[16,4608]{1,0:T(8,128)(2,1)S(1)}, bf16[16,4608]{1,0:T(8,128)(2,1)S(1)}, u32[]{:S(2)}, u32[]{:S(2)}) %collective-permute-start.11) | collective-permute-done | bytes 147488 | tf_op jit(solution)/shard_map/ppermute | solution.py:66
  33.8 1.4 collective-permute-start.15
  36.0 1.3 collective-permute-start.13
  40.5 21.0 %attend.1 = (bf16[1056,1024]{1,0:T(8,128)(2,1)S(1)}, bf16[1056,1024]{1,0:T(8,128)(2,1)S(1)}, bf16[1056,1024]{1,0:T(8,128)(2,1)S(1)}, bf16[1056,512]{1,0:T(8,128)(2,1)S(1)}, f32[8,512]{1,0:T(8,128)S(1)}) custom-call(bf16[1056,512]{1,0:T(8,128)(2,1)S(1)} %get-tuple-element.129.x, s32[1056,128]{1,0:T(8,128)S(1)} %get-tuple-element.130.labels, ...), custom_call_target="tpu_custom_call" | custom-call | tf_op jit(solution)/shard_map/attend/pallas_call | solution.py:296
  66.2 25.6 %feed.1 = (bf16[1056,512]{1,0:T(8,128)(2,1)S(1)}, bf16[1056,1024]{1,0:T(8,128)(2,1)S(1)}, f32[1056,512]{1,0:T(8,128)S(1)}, bf16[4,64,4608]{2,1,0:T(8,128)(2,1)S(...) custom-call(bf16[1056,512]{1,0:T(8,128)(2,1)S(1)} %get-tuple-element.129.x, ...), custom_call_target="tpu_custom_call" | custom-call | tf_op jit(solution)/shard_map/feed/pallas_call | solution.py:471
  92.2 4.2 %collective-permute-done.20.got = bf16[4,64,4608]{2,1,0:T(8,128)(2,1)S(1)} collective-permute-done((bf16[4,64,4608]{2,1,0:T(8,128)(2,1)S(1)}, bf16[4,64,4608]{2,1,0:T(8,128)(2,1)S(1)}, u32[]{:S(2)}, u32[]{:S(2)}) %collective-permute-start.20) | collective-permute-done | bytes 2359328 | tf_op jit(solution)/shard_map/ppermute | solution.py:69
  96.4 1.1 chip_sum.2
  98.4 1.1 collective-permute-start.22
  99.4 1.7 collective-permute-start.23
  101.1 18.8 %attend_back.1.packed = bf16[1056,1536]{1,0:T(8,128)(2,1)S(1)} custom-call(bf16[1056,1024]{1,0:T(8,128)(2,1)S(1)} %get-tuple-element.147.qx, bf16[1056,1024]{1,0:T(8,128)(2,1)S(1)} %get-tuple-element.148.kx, bf16[1056,1024]{1,0:T(8,128)(2,1)S(1)} %get-tuple-element.149.vx, bf16[1056,1024]{1,0:T(8,128)(2,1)S(1)} %get-tuple-element.156.dox), custom_call_target="tpu_custom_call" | custom-call | tf_op jit(solution)/shard_map/attend_back/pallas_call | solution.py:350
  119.9 3.2 %input_back.1 = (bf16[1056,512]{1,0:T(8,128)(2,1)S(1)}, f32[8,512]{1,0:T(8,128)S(1)}) custom-call(bf16[1056,512]{1,0:T(8,128)(2,1)S(1)} %get-tuple-element.129.x, bf16[1056,1536]{1,0:T(8,128)(2,1)S(1)} %attend_back.1.packed, f32[8,512]{1,0:T(8,128)S(1)} %get-tuple-element.141.gains, f32[1056,512]{1,0:T(8,128)S(1)} %get-tuple-element.157.middle_grad, ...), custom_call_target="tpu_custom_call" | custom-call | tf_op jit(solution)/shard_map/input_back/pallas_call | solution.py:553
  123.9 3.9 %project_back.1 = (bf16[4,64,1664]{2,1,0:T(8,128)(2,1)S(1)}, bf16[4,64,1664]{2,1,0:T(8,128)(2,1)S(1)}) custom-call(bf16[1056,512]{1,0:T(8,128)(2,1)S(1)} %get-tuple-element.129.x, bf16[1056,1536]{1,0:T(8,128)(2,1)S(1)} %attend_back.1.packed, f32[8,512]{1,0:T(8,128)S(1)} %get-tuple-element.141.gains, f32[8,512]{1,0:T(8,128)S(1)} %get-tuple-element.160.first_norms, ...), custom_call_target="tpu_custom_call" | custom-call | tf_op jit(solution)/shard_map/project_back/pallas_call | solution.py:519
  128.6 2.0 %collective-permute-done.24.got = bf16[4,64,1664]{2,1,0:T(8,128)(2,1)S(1)} collective-permute-done((bf16[4,64,1664]{2,1,0:T(8,128)(2,1)S(1)}, bf16[4,64,1664]{2,1,0:T(8,128)(2,1)S(1)}, u32[]{:S(2)}, u32[]{:S(2)}) %collective-permute-start.24) | collective-permute-done | bytes 852000 | tf_op jit(solution)/shard_map/ppermute | solution.py:69
  130.9 1.3 collective-permute-start.25
  132.7 1.8 %collective-permute-start.27 = (bf16[64,1664]{1,0:T(8,128)(2,1)S(1)}, bf16[64,1664]{1,0:T(8,128)(2,1)S(1)}, u32[]{:S(2)}, u32[]{:S(2)}) collective-permute-start(bf16[64,1664]{1,0:T(8,128)(2,1)S(1)} %get-tuple-element.174), channel_id=1, source_target_pairs={{0,24},{1,25},{2,26},{3,27},{4,7},{5,4},{6,5},{7,6},{8,16},{9,17},... | collective-permute-start | bytes 638984 | tf_op jit(solution)/shard_map/ppermute | solution.py:66
  134.4 3.4 %collective-permute-start.31 = (bf16[16,4608]{1,0:T(8,128)(2,1)S(1)}, bf16[16,4608]{1,0:T(8,128)(2,1)S(1)}, u32[]{:S(2)}, u32[]{:S(2)}) collective-permute-start(bf16[16,4608]{1,0:T(8,128)(2,1)S(1)} %get-tuple-element.165), channel_id=1, source_target_pairs={{0,1},{1,2},{2,3},{3,0},{4,12},{5,13},{6,14},{7,15},{8,9},{9,10},{... | collective-permute-start | bytes 442376 | tf_op jit(solution)/shard_map/ppermute | solution.py:66
  137.9 1.6 collective-permute-start.32
  139.5 2.1 %collective-permute-start.33 = (bf16[16,4608]{1,0:T(8,128)(2,1)S(1)}, bf16[16,4608]{1,0:T(8,128)(2,1)S(1)}, u32[]{:S(2)}, u32[]{:S(2)}) collective-permute-start(bf16[16,4608]{1,0:T(8,128)(2,1)S(1)} %get-tuple-element.167), channel_id=1, source_target_pairs={{0,3},{1,0},{2,1},{3,2},{4,28},{5,29},{6,30},{7,31},{8,11},{9,8},{... | collective-permute-start | bytes 442376 | tf_op jit(solution)/shard_map/ppermute | solution.py:66
  141.8 3.5 %collective-permute-start.28 = (bf16[16,1664]{1,0:T(8,128)(2,1)S(1)}, bf16[16,1664]{1,0:T(8,128)(2,1)S(1)}, u32[]{:S(2)}, u32[]{:S(2)}) collective-permute-start(bf16[16,1664]{1,0:T(8,128)(2,1)S(1)} %get-tuple-element.181), channel_id=1, source_target_pairs={{0,1},{1,2},{2,3},{3,0},{4,12},{5,13},{6,14},{7,15},{8,9},{9,10},{... | collective-permute-start | bytes 159752 | tf_op jit(solution)/shard_map/ppermute | solution.py:66
  145.3 2.9 %collective-permute-start.29 = (bf16[16,1664]{1,0:T(8,128)(2,1)S(1)}, bf16[16,1664]{1,0:T(8,128)(2,1)S(1)}, u32[]{:S(2)}, u32[]{:S(2)}) collective-permute-start(bf16[16,1664]{1,0:T(8,128)(2,1)S(1)} %get-tuple-element.182), channel_id=1, source_target_pairs={{0,2},{1,3},{2,0},{3,1},{4,20},{5,21},{6,22},{7,23},{8,10},{9,11},... | collective-permute-start | bytes 159752 | tf_op jit(solution)/shard_map/ppermute | solution.py:66
  148.4 1.1 moments.3
  149.9 3.3 %collective-permute-done.29.refs_2_ = bf16[16,1664]{1,0:T(8,128)(2,1)S(1)} collective-permute-done((bf16[16,1664]{1,0:T(8,128)(2,1)S(1)}, bf16[16,1664]{1,0:T(8,128)(2,1)S(1)}, u32[]{:S(2)}, u32[]{:S(2)}) %collective-permute-start.29) | collective-permute-done | bytes 53280 | tf_op jit(solution)/shard_map/ppermute | solution.py:66
  154.6 8.3 %all-to-all-start = ((f32[32,1,128]{2,1,0:T(1,128)}), f32[32,1,128]{2,1,0:T(1,128)S(1)}, u32[]{:S(2)}, u32[]{:S(2)}) async-start(f32[32,1,128]{2,1,0:T(1,128)} %broadcast_in_dim.17), calls=%async_computation | async-start | bytes 32768 | tf_op jit(solution)/shard_map/all_to_all | solution.py:754
  162.9 2.0 %arrange_back.1 = (bf16[1044,512]{1,0:T(8,128)(2,1)}, bf16[1044,512]{1,0:T(8,128)(2,1)}) custom-call(f32[8,128]{1,0:T(8,128)S(1)} %get-tuple-element.114.begin, bf16[1056,512]{1,0:T(8,128)(2,1)S(1)} %get-tuple-element.175.first, bf16[1056,512]{1,0:T(8,128)(2,1)S(1)} %get-tuple-element.176.second), custom_call_target="tpu_custom_call" | custom-call | tf_op jit(solution)/shard_map/arrange_back/pallas_call | solution.py:214
  164.9 5.1 %all-to-all-done = f32[32,1,128]{2,1,0:T(1,128)S(1)} async-done(((f32[32,1,128]{2,1,0:T(1,128)}), f32[32,1,128]{2,1,0:T(1,128)S(1)}, u32[]{:S(2)}, u32[]{:S(2)}) %all-to-all-start) | async-done | bytes 16416 | tf_op jit(solution)/shard_map/all_to_all | solution.py:754
  (104 shorter events, 25.9 us)
Async XLA Ops:
  2.3 8.8 %collective-permute-start.2 = (bf16[16,1664]{1,0:T(8,128)(2,1)S(1)}, bf16[16,1664]{1,0:T(8,128)(2,1)S(1)}, u32[]{:S(2)}, u32[]{:S(2)}) collective-permute-start(bf16[16,1664]{1,0:T(8,128)(2,1)S(1)} %fusion.1.refs_0_), channel_id=1, source_target_pairs={{0,3},{1,0},{2,1},{3,2},{4,28},{5,29},{6,30},{7,31},{8,11},{9,8},{... | collective-permute-start | bytes 159752 | tf_op jit(solution)/shard_map/ppermute | solution.py:66
  7.5 5.0 %collective-permute-start.1 = (bf16[16,1664]{1,0:T(8,128)(2,1)S(1)}, bf16[16,1664]{1,0:T(8,128)(2,1)S(1)}, u32[]{:S(2)}, u32[]{:S(2)}) collective-permute-start(bf16[16,1664]{1,0:T(8,128)(2,1)S(1)} %fusion.1.refs_0_), channel_id=1, source_target_pairs={{0,2},{1,3},{2,0},{3,1},{4,20},{5,21},{6,22},{7,23},{8,10},{9,11},... | collective-permute-start | bytes 159752 | tf_op jit(solution)/shard_map/ppermute | solution.py:66
  7.5 5.9 %collective-permute-start = (bf16[16,1664]{1,0:T(8,128)(2,1)S(1)}, bf16[16,1664]{1,0:T(8,128)(2,1)S(1)}, u32[]{:S(2)}, u32[]{:S(2)}) collective-permute-start(bf16[16,1664]{1,0:T(8,128)(2,1)S(1)} %fusion.1.refs_0_), channel_id=1, source_target_pairs={{0,1},{1,2},{2,3},{3,0},{4,12},{5,13},{6,14},{7,15},{8,9},{9,10},{... | collective-permute-start | bytes 159752 | tf_op jit(solution)/shard_map/ppermute | solution.py:66
  13.4 9.6 %collective-permute-start.12 = (bf16[16,4608]{1,0:T(8,128)(2,1)S(1)}, bf16[16,4608]{1,0:T(8,128)(2,1)S(1)}, u32[]{:S(2)}, u32[]{:S(2)}) collective-permute-start(bf16[16,4608]{1,0:T(8,128)(2,1)S(1)} %slice_dynamic-update-slice_fusion.refs_0_), channel_id=1, source_target_pairs={{0,3},{1,0},{2,1},{3,2},{4,28},{5,29},{6,30},{7,31},{8,11},{9,8},{... | collective-permute-start | bytes 442376 | tf_op jit(solution)/shard_map/ppermute | solution.py:66
  18.4 15.1 %collective-permute-start.5 = (bf16[64,1664]{1,0:T(8,128)(2,1)S(1)}, bf16[64,1664]{1,0:T(8,128)(2,1)S(1)}, u32[]{:S(2)}, u32[]{:S(2)}) collective-permute-start(bf16[64,1664]{1,0:T(8,128)(2,1)S(1)} %column.2.refs_0_), channel_id=1, source_target_pairs={{0,24},{1,25},{2,26},{3,27},{4,7},{5,4},{6,5},{7,6},{8,16},{9,17},... | collective-permute-start | bytes 638984 | tf_op jit(solution)/shard_map/ppermute | solution.py:66
  20.9 12.6 %collective-permute-start.4 = (bf16[64,1664]{1,0:T(8,128)(2,1)S(1)}, bf16[64,1664]{1,0:T(8,128)(2,1)S(1)}, u32[]{:S(2)}, u32[]{:S(2)}) collective-permute-start(bf16[64,1664]{1,0:T(8,128)(2,1)S(1)} %column.2.refs_0_), channel_id=1, source_target_pairs={{0,16},{1,17},{2,18},{3,19},{4,6},{5,7},{6,4},{7,5},{8,24},{9,25},... | collective-permute-start | bytes 638984 | tf_op jit(solution)/shard_map/ppermute | solution.py:66
  21.4 12.1 %collective-permute-start.3 = (bf16[64,1664]{1,0:T(8,128)(2,1)S(1)}, bf16[64,1664]{1,0:T(8,128)(2,1)S(1)}, u32[]{:S(2)}, u32[]{:S(2)}) collective-permute-start(bf16[64,1664]{1,0:T(8,128)(2,1)S(1)} %column.2.refs_0_), channel_id=1, source_target_pairs={{0,8},{1,9},{2,10},{3,11},{4,5},{5,6},{6,7},{7,4},{8,0},{9,1},{10,... | collective-permute-start | bytes 638984 | tf_op jit(solution)/shard_map/ppermute | solution.py:66
  22.0 11.5 %collective-permute-start.11 = (bf16[16,4608]{1,0:T(8,128)(2,1)S(1)}, bf16[16,4608]{1,0:T(8,128)(2,1)S(1)}, u32[]{:S(2)}, u32[]{:S(2)}) collective-permute-start(bf16[16,4608]{1,0:T(8,128)(2,1)S(1)} %slice_dynamic-update-slice_fusion.refs_0_), channel_id=1, source_target_pairs={{0,2},{1,3},{2,0},{3,1},{4,20},{5,21},{6,22},{7,23},{8,10},{9,11},... | collective-permute-start | bytes 442376 | tf_op jit(solution)/shard_map/ppermute | solution.py:66
  23.0 10.5 %collective-permute-start.10 = (bf16[16,4608]{1,0:T(8,128)(2,1)S(1)}, bf16[16,4608]{1,0:T(8,128)(2,1)S(1)}, u32[]{:S(2)}, u32[]{:S(2)}) collective-permute-start(bf16[16,4608]{1,0:T(8,128)(2,1)S(1)} %slice_dynamic-update-slice_fusion.refs_0_), channel_id=1, source_target_pairs={{0,1},{1,2},{2,3},{3,0},{4,12},{5,13},{6,14},{7,15},{8,9},{9,10},{... | collective-permute-start | bytes 442376 | tf_op jit(solution)/shard_map/ppermute | solution.py:66
  33.8 27.8 %collective-permute-start.15 = (bf16[64,4608]{1,0:T(8,128)(2,1)S(1)}, bf16[64,4608]{1,0:T(8,128)(2,1)S(1)}, u32[]{:S(2)}, u32[]{:S(2)}) collective-permute-start(bf16[64,4608]{1,0:T(8,128)(2,1)S(1)} %column.3.refs_0_), channel_id=1, source_target_pairs={{0,24},{1,25},{2,26},{3,27},{4,7},{5,4},{6,5},{7,6},{8,16},{9,17},... | collective-permute-start | bytes 1769480 | tf_op jit(solution)/shard_map/ppermute | solution.py:66
  35.1 26.4 %collective-permute-start.14 = (bf16[64,4608]{1,0:T(8,128)(2,1)S(1)}, bf16[64,4608]{1,0:T(8,128)(2,1)S(1)}, u32[]{:S(2)}, u32[]{:S(2)}) collective-permute-start(bf16[64,4608]{1,0:T(8,128)(2,1)S(1)} %column.3.refs_0_), channel_id=1, source_target_pairs={{0,16},{1,17},{2,18},{3,19},{4,6},{5,7},{6,4},{7,5},{8,24},{9,25},... | collective-permute-start | bytes 1769480 | tf_op jit(solution)/shard_map/ppermute | solution.py:66
  36.0 25.5 %collective-permute-start.13 = (bf16[64,4608]{1,0:T(8,128)(2,1)S(1)}, bf16[64,4608]{1,0:T(8,128)(2,1)S(1)}, u32[]{:S(2)}, u32[]{:S(2)}) collective-permute-start(bf16[64,4608]{1,0:T(8,128)(2,1)S(1)} %column.3.refs_0_), channel_id=1, source_target_pairs={{0,8},{1,9},{2,10},{3,11},{4,5},{5,6},{6,7},{7,4},{8,0},{9,1},{10,... | collective-permute-start | bytes 1769480 | tf_op jit(solution)/shard_map/ppermute | solution.py:66
  37.3 1.8 %collective-permute-start.9 = (bf16[64,1664]{1,0:T(8,128)(2,1)S(1)}, bf16[64,1664]{1,0:T(8,128)(2,1)S(1)}, u32[]{:S(2)}, u32[]{:S(2)}) collective-permute-start(bf16[64,1664]{1,0:T(8,128)(2,1)S(1)} %collective-permute-done.5.refs_3_), channel_id=1, source_target_pairs={{0,4},{1,5},{2,6},{3,7},{4,0},{5,1},{6,2},{7,3},{8,12},{9,13},{10,... | collective-permute-start | bytes 638984 | tf_op jit(solution)/shard_map/ppermute | solution.py:69
  61.5 2.1 %collective-permute-start.16 = (bf16[64,4608]{1,0:T(8,128)(2,1)S(1)}, bf16[64,4608]{1,0:T(8,128)(2,1)S(1)}, u32[]{:S(2)}, u32[]{:S(2)}) collective-permute-start(bf16[64,4608]{1,0:T(8,128)(2,1)S(1)} %column.3.refs_0_), channel_id=1, source_target_pairs={{0,4},{1,5},{2,6},{3,7},{4,0},{5,1},{6,2},{7,3},{8,12},{9,13},{10,... | collective-permute-start | bytes 1769480 | tf_op jit(solution)/shard_map/ppermute | solution.py:69
  62.0 2.5 %collective-permute-start.17 = (bf16[64,4608]{1,0:T(8,128)(2,1)S(1)}, bf16[64,4608]{1,0:T(8,128)(2,1)S(1)}, u32[]{:S(2)}, u32[]{:S(2)}) collective-permute-start(bf16[64,4608]{1,0:T(8,128)(2,1)S(1)} %collective-permute-done.13.refs_1_), channel_id=1, source_target_pairs={{0,4},{1,5},{2,6},{3,7},{4,0},{5,1},{6,2},{7,3},{8,12},{9,13},{10,... | collective-permute-start | bytes 1769480 | tf_op jit(solution)/shard_map/ppermute | solution.py:69
  62.1 3.2 %collective-permute-start.18 = (bf16[64,4608]{1,0:T(8,128)(2,1)S(1)}, bf16[64,4608]{1,0:T(8,128)(2,1)S(1)}, u32[]{:S(2)}, u32[]{:S(2)}) collective-permute-start(bf16[64,4608]{1,0:T(8,128)(2,1)S(1)} %collective-permute-done.14.refs_2_), channel_id=1, source_target_pairs={{0,4},{1,5},{2,6},{3,7},{4,0},{5,1},{6,2},{7,3},{8,12},{9,13},{10,... | collective-permute-start | bytes 1769480 | tf_op jit(solution)/shard_map/ppermute | solution.py:69
  62.5 3.7 %collective-permute-start.19 = (bf16[64,4608]{1,0:T(8,128)(2,1)S(1)}, bf16[64,4608]{1,0:T(8,128)(2,1)S(1)}, u32[]{:S(2)}, u32[]{:S(2)}) collective-permute-start(bf16[64,4608]{1,0:T(8,128)(2,1)S(1)} %collective-permute-done.15.refs_3_), channel_id=1, source_target_pairs={{0,4},{1,5},{2,6},{3,7},{4,0},{5,1},{6,2},{7,3},{8,12},{9,13},{10,... | collective-permute-start | bytes 1769480 | tf_op jit(solution)/shard_map/ppermute | solution.py:69
  91.8 4.6 %collective-permute-start.20 = (bf16[4,64,4608]{2,1,0:T(8,128)(2,1)S(1)}, bf16[4,64,4608]{2,1,0:T(8,128)(2,1)S(1)}, u32[]{:S(2)}, u32[]{:S(2)}) collective-permute-start(bf16[4,64,4608]{2,1,0:T(8,128)(2,1)S(1)} %get-tuple-element.152), channel_id=1, source_target_pairs={{0,4},{1,5},{2,6},{3,7},{4,0},{5,1},{6,2},{7,3},{8,12},{9,13},{10,... | collective-permute-start | bytes 7077896 | tf_op jit(solution)/shard_map/ppermute | solution.py:69
  97.6 25.6 %collective-permute-start.21 = (bf16[64,4608]{1,0:T(8,128)(2,1)S(1)}, bf16[64,4608]{1,0:T(8,128)(2,1)S(1)}, u32[]{:S(2)}, u32[]{:S(2)}) collective-permute-start(bf16[64,4608]{1,0:T(8,128)(2,1)S(1)} %get-tuple-element.153), channel_id=1, source_target_pairs={{0,8},{1,9},{2,10},{3,11},{4,5},{5,6},{6,7},{7,4},{8,0},{9,1},{10,... | collective-permute-start | bytes 1769480 | tf_op jit(solution)/shard_map/ppermute | solution.py:66
  98.4 24.8 %collective-permute-start.22 = (bf16[64,4608]{1,0:T(8,128)(2,1)S(1)}, bf16[64,4608]{1,0:T(8,128)(2,1)S(1)}, u32[]{:S(2)}, u32[]{:S(2)}) collective-permute-start(bf16[64,4608]{1,0:T(8,128)(2,1)S(1)} %get-tuple-element.154), channel_id=1, source_target_pairs={{0,16},{1,17},{2,18},{3,19},{4,6},{5,7},{6,4},{7,5},{8,24},{9,25},... | collective-permute-start | bytes 1769480 | tf_op jit(solution)/shard_map/ppermute | solution.py:66
  99.4 23.7 %collective-permute-start.23 = (bf16[64,4608]{1,0:T(8,128)(2,1)S(1)}, bf16[64,4608]{1,0:T(8,128)(2,1)S(1)}, u32[]{:S(2)}, u32[]{:S(2)}) collective-permute-start(bf16[64,4608]{1,0:T(8,128)(2,1)S(1)} %get-tuple-element.155), channel_id=1, source_target_pairs={{0,24},{1,25},{2,26},{3,27},{4,7},{5,4},{6,5},{7,6},{8,16},{9,17},... | collective-permute-start | bytes 1769480 | tf_op jit(solution)/shard_map/ppermute | solution.py:66
  127.9 2.8 %collective-permute-start.24 = (bf16[4,64,1664]{2,1,0:T(8,128)(2,1)S(1)}, bf16[4,64,1664]{2,1,0:T(8,128)(2,1)S(1)}, u32[]{:S(2)}, u32[]{:S(2)}) collective-permute-start(bf16[4,64,1664]{2,1,0:T(8,128)(2,1)S(1)} %get-tuple-element.171), channel_id=1, source_target_pairs={{0,4},{1,5},{2,6},{3,7},{4,0},{5,1},{6,2},{7,3},{8,12},{9,13},{10,... | collective-permute-start | bytes 2555912 | tf_op jit(solution)/shard_map/ppermute | solution.py:69
  130.9 8.6 %collective-permute-start.25 = (bf16[64,1664]{1,0:T(8,128)(2,1)S(1)}, bf16[64,1664]{1,0:T(8,128)(2,1)S(1)}, u32[]{:S(2)}, u32[]{:S(2)}) collective-permute-start(bf16[64,1664]{1,0:T(8,128)(2,1)S(1)} %get-tuple-element.172), channel_id=1, source_target_pairs={{0,8},{1,9},{2,10},{3,11},{4,5},{5,6},{6,7},{7,4},{8,0},{9,1},{10,... | collective-permute-start | bytes 638984 | tf_op jit(solution)/shard_map/ppermute | solution.py:66
  132.2 9.4 %collective-permute-start.26 = (bf16[64,1664]{1,0:T(8,128)(2,1)S(1)}, bf16[64,1664]{1,0:T(8,128)(2,1)S(1)}, u32[]{:S(2)}, u32[]{:S(2)}) collective-permute-start(bf16[64,1664]{1,0:T(8,128)(2,1)S(1)} %get-tuple-element.173), channel_id=1, source_target_pairs={{0,16},{1,17},{2,18},{3,19},{4,6},{5,7},{6,4},{7,5},{8,24},{9,25},... | collective-permute-start | bytes 638984 | tf_op jit(solution)/shard_map/ppermute | solution.py:66
  132.7 8.9 %collective-permute-start.27 = (bf16[64,1664]{1,0:T(8,128)(2,1)S(1)}, bf16[64,1664]{1,0:T(8,128)(2,1)S(1)}, u32[]{:S(2)}, u32[]{:S(2)}) collective-permute-start(bf16[64,1664]{1,0:T(8,128)(2,1)S(1)} %get-tuple-element.174), channel_id=1, source_target_pairs={{0,24},{1,25},{2,26},{3,27},{4,7},{5,4},{6,5},{7,6},{8,16},{9,17},... | collective-permute-start | bytes 638984 | tf_op jit(solution)/shard_map/ppermute | solution.py:66
  134.4 13.8 %collective-permute-start.31 = (bf16[16,4608]{1,0:T(8,128)(2,1)S(1)}, bf16[16,4608]{1,0:T(8,128)(2,1)S(1)}, u32[]{:S(2)}, u32[]{:S(2)}) collective-permute-start(bf16[16,4608]{1,0:T(8,128)(2,1)S(1)} %get-tuple-element.165), channel_id=1, source_target_pairs={{0,1},{1,2},{2,3},{3,0},{4,12},{5,13},{6,14},{7,15},{8,9},{9,10},{... | collective-permute-start | bytes 442376 | tf_op jit(solution)/shard_map/ppermute | solution.py:66
  137.9 10.4 %collective-permute-start.32 = (bf16[16,4608]{1,0:T(8,128)(2,1)S(1)}, bf16[16,4608]{1,0:T(8,128)(2,1)S(1)}, u32[]{:S(2)}, u32[]{:S(2)}) collective-permute-start(bf16[16,4608]{1,0:T(8,128)(2,1)S(1)} %get-tuple-element.166), channel_id=1, source_target_pairs={{0,2},{1,3},{2,0},{3,1},{4,20},{5,21},{6,22},{7,23},{8,10},{9,11},... | collective-permute-start | bytes 442376 | tf_op jit(solution)/shard_map/ppermute | solution.py:66
  139.5 8.8 %collective-permute-start.33 = (bf16[16,4608]{1,0:T(8,128)(2,1)S(1)}, bf16[16,4608]{1,0:T(8,128)(2,1)S(1)}, u32[]{:S(2)}, u32[]{:S(2)}) collective-permute-start(bf16[16,4608]{1,0:T(8,128)(2,1)S(1)} %get-tuple-element.167), channel_id=1, source_target_pairs={{0,3},{1,0},{2,1},{3,2},{4,28},{5,29},{6,30},{7,31},{8,11},{9,8},{... | collective-permute-start | bytes 442376 | tf_op jit(solution)/shard_map/ppermute | solution.py:66
  141.8 8.1 %collective-permute-start.28 = (bf16[16,1664]{1,0:T(8,128)(2,1)S(1)}, bf16[16,1664]{1,0:T(8,128)(2,1)S(1)}, u32[]{:S(2)}, u32[]{:S(2)}) collective-permute-start(bf16[16,1664]{1,0:T(8,128)(2,1)S(1)} %get-tuple-element.181), channel_id=1, source_target_pairs={{0,1},{1,2},{2,3},{3,0},{4,12},{5,13},{6,14},{7,15},{8,9},{9,10},{... | collective-permute-start | bytes 159752 | tf_op jit(solution)/shard_map/ppermute | solution.py:66
  145.3 7.9 %collective-permute-start.29 = (bf16[16,1664]{1,0:T(8,128)(2,1)S(1)}, bf16[16,1664]{1,0:T(8,128)(2,1)S(1)}, u32[]{:S(2)}, u32[]{:S(2)}) collective-permute-start(bf16[16,1664]{1,0:T(8,128)(2,1)S(1)} %get-tuple-element.182), channel_id=1, source_target_pairs={{0,2},{1,3},{2,0},{3,1},{4,20},{5,21},{6,22},{7,23},{8,10},{9,11},... | collective-permute-start | bytes 159752 | tf_op jit(solution)/shard_map/ppermute | solution.py:66
  148.2 4.9 %collective-permute-start.30 = (bf16[16,1664]{1,0:T(8,128)(2,1)S(1)}, bf16[16,1664]{1,0:T(8,128)(2,1)S(1)}, u32[]{:S(2)}, u32[]{:S(2)}) collective-permute-start(bf16[16,1664]{1,0:T(8,128)(2,1)S(1)} %get-tuple-element.183), channel_id=1, source_target_pairs={{0,3},{1,0},{2,1},{3,2},{4,28},{5,29},{6,30},{7,31},{8,11},{9,8},{... | collective-permute-start | bytes 159752 | tf_op jit(solution)/shard_map/ppermute | solution.py:66
  154.6 15.4 %all-to-all-start = ((f32[32,1,128]{2,1,0:T(1,128)}), f32[32,1,128]{2,1,0:T(1,128)S(1)}, u32[]{:S(2)}, u32[]{:S(2)}) async-start(f32[32,1,128]{2,1,0:T(1,128)} %broadcast_in_dim.17), calls=%async_computation | async-start | bytes 32768 | tf_op jit(solution)/shard_map/all_to_all | solution.py:754
  (21 other events, 236.2 us)

commit v2 on v1

--- a/solution.py
+++ b/solution.py
@@ -24,6 +24,7 @@
 TILE = 256
 THIN = 32
 CHUNK = 352
+DEEP_CHUNK = 528
 VMEM = pltpu.MemorySpace.VMEM
 AXES = ("dp", "rep")
 
@@ -43,11 +44,11 @@
 
 
 class Layout:
-    def __init__(self, mesh):
+    def __init__(self, mesh, mixed):
         self.dp = mesh.shape["dp"]
         self.rep = mesh.shape["rep"]
         self.plane = self.dp // 2
-        self.mixed = self.plane == self.rep
+        self.mixed = mixed and self.plane == self.rep
 
     def pairs(self, move):
         pairs = []
@@ -192,34 +193,38 @@
     )(inputs, cotangent, segments)
 
 
-def arrange_back_kernel(begin, first, second, first_out, second_out, room):
-    rows = first_out.shape[0]
-    half = (first.shape[0] - THIN) // 2
+def finish_kernel(begin, middle, active, contract, grad_in, outputs, grad_out, room):
+    rows = outputs.shape[0]
+    half = (middle.shape[0] - THIN) // 2
     memory = rows - 2 * half
-    row = lax.broadcasted_iota(jnp.int32, (half, LANES), 0).astype(jnp.float32)
-    early = row < begin[:1]
-    for source, target in ((first, first_out), (second, second_out)):
-        for at in range(0, first.shape[1], LANES):
-            columns = slice(at, at + LANES)
-            left = source[:half, columns].astype(jnp.float32)
-            right = source[half + THIN :, columns].astype(jnp.float32)
-            room[:THIN] = source[half : half + THIN, columns].astype(jnp.float32)
-            room[memory : memory + half] = jnp.where(early, right, left)
-            room[memory + half : rows] = jnp.where(early, left, right)
-            target[:, columns] = room[:rows].astype(target.dtype)
-
-
-def arrange_back(begin, first, second, rows):
-    width = first.shape[1]
-    return pl.pallas_call(
-        arrange_back_kernel,
-        out_shape=[jax.ShapeDtypeStruct((rows, width), first.dtype)] * 2,
-        in_specs=[pl.BlockSpec(memory_space=VMEM)] * 3,
+    wide = room.shape[1]
+    row = lax.broadcasted_iota(jnp.int32, (half, wide), 0).astype(jnp.float32)
+    early = row < begin[:1, :1]
+
+    def place(value, target, columns):
+        left, right = value[:half], value[half + THIN :]
+        room[:THIN] = value[half : half + THIN]
+        room[memory : memory + half] = jnp.where(early, right, left)
+        room[memory + half : rows] = jnp.where(early, left, right)
+        target[:, columns] = room[:rows].astype(target.dtype)
+
+    for at in range(0, middle.shape[1], wide):
+        columns = slice(at, at + wide)
+        place(middle[:, columns] + dot(active[...], contract[:, columns], 1, 0), outputs, columns)
+        place(grad_in[:, columns].astype(jnp.float32), grad_out, columns)
+
+
+def finish(begin, middle, active, contract, grad_in, rows):
+    width = middle.shape[1]
+    return pl.pallas_call(
+        finish_kernel,
+        out_shape=[jax.ShapeDtypeStruct((rows, width), grad_in.dtype)] * 2,
+        in_specs=[pl.BlockSpec(memory_space=VMEM)] * 5,
         out_specs=[pl.BlockSpec(memory_space=VMEM)] * 2,
-        scratch_shapes=[pltpu.VMEM((first.shape[0], LANES), jnp.float32)],
-        compiler_params=params(8),
-        name="arrange_back",
-    )(begin, first, second)
+        scratch_shapes=[pltpu.VMEM((middle.shape[0], 256), jnp.float32)],
+        compiler_params=params(10),
+        name="finish",
+    )(begin, middle, active, contract, grad_in)
 
 
 def attend_kernel(lay, count, x, labels, *refs):
@@ -370,51 +375,108 @@
 def feed_kernel(lay, count, deep_count, x, mixed, dy, gains, *refs):
     pieces = refs[:count]
     deep_pieces = refs[count : count + deep_count]
-    outputs, dox, middle_grad, keep2, send2, norm_grads, *deep_out = refs[count + deep_count : -8]
-    wide, contract, active, hidden_grad, second, middle_low, block, deep_block = refs[-8:]
+    outs = refs[count + deep_count : -5]
+    middle, middle_grad, middle_low, active, contract, out_weight, keep2, send2, norm_grads, *deep_out = outs
+    wide, hidden_grad, second, block, deep_block = refs[-5:]
     rows, width = x.shape
     hidden = contract.shape[0]
-    wide_part = slice(0, width + hidden)
-    assemble(lay, pieces, wide, wide_part)
+    assemble(lay, pieces, wide, slice(0, width + hidden))
     if deep_count:
         assemble(lay, deep_pieces, contract, slice(None))
     else:
         assemble_deep(lay, pieces, contract, width + hidden)
+    out_weight[...] = wide[:, :width]
     gain, bias = gains[2:3], gains[3:4]
     zero = jnp.zeros((1, width), jnp.float32)
 
     def one_chunk(i, carry):
         gain_sum, bias_sum = carry
-        span = pl.ds(pl.multiple_of(i * CHUNK, CHUNK), CHUNK)
-        middle = x[span].astype(jnp.float32) + dot(mixed[span], wide[:, :width], 1, 0)
-        normed, scale = normalize(middle)
+        span = pl.ds(pl.multiple_of(i * DEEP_CHUNK, DEEP_CHUNK), DEEP_CHUNK)
+        start = x[span].astype(jnp.float32) + dot(mixed[span], wide[:, :width], 1, 0)
+        middle[span] = start
+        normed, scale = normalize(start)
         low = (normed * gain + bias).astype(jnp.bfloat16)
         second[span] = low
-        result = middle
-        back = jnp.zeros_like(middle)
         for start in range(0, hidden, 512):
             part = slice(start, start + 512)
-            from_expand = wide[:, width + start : width + start + 512]
-            up = dot(low, from_expand, 1, 0)
+            up = dot(low, wide[:, width + start : width + start + 512], 1, 0)
             square = up * up
             bend = jnp.tanh(0.7978845608028654 * up * (1.0 + 0.044715 * square))
             half = 0.5 * (1.0 + bend)
-            act = (up * half).astype(jnp.bfloat16)
-            active[span, part] = act
+            active[span, part] = (up * half).astype(jnp.bfloat16)
             slope = half + 0.5 * up * (1.0 - bend * bend) * (0.7978845608028654 * (1.0 + 3 * 0.044715 * square))
-            down = (dot(dy[span], contract[part], 1, 1) * slope).astype(jnp.bfloat16)
-            hidden_grad[span, part] = down
-            result = result + dot(act, contract[part], 1, 0)
-            back = back + dot(down, from_expand, 1, 1)
-        outputs[span] = result.astype(jnp.bfloat16)
+            hidden_grad[span, part] = (dot(dy[span], contract[part], 1, 1) * slope).astype(jnp.bfloat16)
+        back = dot(hidden_grad[span], wide[:, width:], 1, 1)
         gain_sum = gain_sum + jnp.sum(back * normed, axis=0, keepdims=True)
         bias_sum = bias_sum + jnp.sum(back, axis=0, keepdims=True)
         grad = dy[span].astype(jnp.float32) + norm_back(back, normed, scale, gain)
         middle_grad[span] = grad
-        grad_low = grad.astype(jnp.bfloat16)
-        middle_low[span] = grad_low
-        mixed_grad = dot(grad_low, wide[:, :width], 1, 1).astype(jnp.bfloat16).astype(jnp.float32)
-        lane = lax.broadcasted_iota(jnp.int32, (CHUNK, LANES), 1)
+        middle_low[span] = grad.astype(jnp.bfloat16)
+        return gain_sum, bias_sum
+
+    gain_sum, bias_sum = lax.fori_loop(0, rows // DEEP_CHUNK, one_chunk, (zero, zero))
+    norm_grads[...] = jnp.concatenate([gain_sum, bias_sum, jnp.zeros((6, width), jnp.float32)], axis=0)
+
+    def one_block(i, carry):
+        columns = pl.ds(pl.multiple_of(i * 512, 512), 512)
+        deep_block[columns] = dot(active[:, columns], dy[...], 0, 0)
+        block[...] = dot(second[...], hidden_grad[:, columns], 0, 0)
+        split_rows(lay, block, keep2, send2, pl.ds(pl.multiple_of(width + i * 512, 512), 512))
+        return carry
+
+    lax.fori_loop(0, hidden // 512, one_block, 0)
+    if deep_count:
+        split_rows(lay, deep_block, *deep_out, slice(0, width))
+    else:
+        split_deep(lay, deep_block, keep2, send2, width + hidden)
+    block[...] = dot(mixed[...], middle_low[...], 0, 0)
+    split_rows(lay, block, keep2, send2, slice(0, width))
+
+
+def feed(lay, x, mixed, dy, gains, pieces, deep_pieces):
+    rows, width = x.shape
+    plane = len(pieces) // 2
+    deep = pieces[0].shape[0]
+    columns = pieces[0].shape[1]
+    hidden = 4 * width
+    out_shape = [
+        jax.ShapeDtypeStruct((rows, width), jnp.float32),
+        jax.ShapeDtypeStruct((rows, width), jnp.float32),
+        jax.ShapeDtypeStruct((rows, width), jnp.bfloat16),
+        jax.ShapeDtypeStruct((rows, hidden), jnp.bfloat16),
+        jax.ShapeDtypeStruct((hidden, width), jnp.bfloat16),
+        jax.ShapeDtypeStruct((width, width), jnp.bfloat16),
+        jax.ShapeDtypeStruct((plane, deep, columns), jnp.bfloat16),
+        jax.ShapeDtypeStruct((plane, deep, columns), jnp.bfloat16),
+        jax.ShapeDtypeStruct((8, width), jnp.float32),
+    ]
+    if deep_pieces:
+        out_shape.append(jax.ShapeDtypeStruct((plane, 4 * deep, width), jnp.bfloat16))
+        out_shape.append(jax.ShapeDtypeStruct((plane, 4 * deep, width), jnp.bfloat16))
+    return pl.pallas_call(
+        partial(feed_kernel, lay, len(pieces), len(deep_pieces)),
+        out_shape=out_shape,
+        in_specs=[pl.BlockSpec(memory_space=VMEM)] * (4 + len(pieces) + len(deep_pieces)),
+        out_specs=[pl.BlockSpec(memory_space=VMEM)] * len(out_shape),
+        scratch_shapes=[
+            pltpu.VMEM((width, width + hidden), jnp.bfloat16),
+            pltpu.VMEM((rows, hidden), jnp.bfloat16),
+            pltpu.VMEM((rows, width), jnp.bfloat16),
+            pltpu.VMEM((width, 512), jnp.float32),
+            pltpu.VMEM((hidden, width), jnp.float32),
+        ],
+        compiler_params=params(26),
+        name="feed",
+    )(x, mixed, dy, gains, *pieces, *deep_pieces)
+
+
+def mixed_back_kernel(middle_low, mixed, out_weight, dox):
+    rows, width = mixed.shape
+
+    def one_chunk(i, carry):
+        span = pl.ds(pl.multiple_of(i * DEEP_CHUNK, DEEP_CHUNK), DEEP_CHUNK)
+        mixed_grad = dot(middle_low[span], out_weight[...], 1, 1).astype(jnp.bfloat16).astype(jnp.float32)
+        lane = lax.broadcasted_iota(jnp.int32, (DEEP_CHUNK, LANES), 1)
         left = lane < HALF
         feature = lane % HALF
         for pair in range(width // LANES):
@@ -430,62 +492,21 @@
                 extra = jnp.where(feature == 0, one, jnp.where(feature == 1, two, jnp.where(feature == 2, three, 0.0)))
                 head = (2 * pair + side) * LANES
                 dox[span, head : head + LANES] = jnp.where(mine, piece, extra).astype(jnp.bfloat16)
-        return gain_sum, bias_sum
-
-    gain_sum, bias_sum = lax.fori_loop(0, rows // CHUNK, one_chunk, (zero, zero))
-    norm_grads[...] = jnp.concatenate([gain_sum, bias_sum, jnp.zeros((6, width), jnp.float32)], axis=0)
-
-    def one_block(i, carry):
-        columns = pl.ds(pl.multiple_of(i * 512, 512), 512)
-        deep_block[columns] = dot(active[:, columns], dy[...], 0, 0)
-        block[...] = dot(second[...], hidden_grad[:, columns], 0, 0)
-        split_rows(lay, block, keep2, send2, pl.ds(pl.multiple_of(width + i * 512, 512), 512))
         return carry
 
-    lax.fori_loop(0, hidden // 512, one_block, 0)
-    if deep_count:
-        split_rows(lay, deep_block, *deep_out, slice(0, width))
-    else:
-        split_deep(lay, deep_block, keep2, send2, width + hidden)
-    block[...] = dot(mixed[...], middle_low[...], 0, 0)
-    split_rows(lay, block, keep2, send2, slice(0, width))
-
-
-def feed(lay, x, mixed, dy, gains, pieces, deep_pieces):
-    rows, width = x.shape
-    plane = len(pieces) // 2
-    deep = pieces[0].shape[0]
-    columns = pieces[0].shape[1]
-    hidden = 4 * width
-    out_shape = [
-        jax.ShapeDtypeStruct((rows, width), jnp.bfloat16),
-        jax.ShapeDtypeStruct((rows, 2 * width), jnp.bfloat16),
-        jax.ShapeDtypeStruct((rows, width), jnp.float32),
-        jax.ShapeDtypeStruct((plane, deep, columns), jnp.bfloat16),
-        jax.ShapeDtypeStruct((plane, deep, columns), jnp.bfloat16),
-        jax.ShapeDtypeStruct((8, width), jnp.float32),
-    ]
-    if deep_pieces:
-        out_shape.append(jax.ShapeDtypeStruct((plane, 4 * deep, width), jnp.bfloat16))
-        out_shape.append(jax.ShapeDtypeStruct((plane, 4 * deep, width), jnp.bfloat16))
-    return pl.pallas_call(
-        partial(feed_kernel, lay, len(pieces), len(deep_pieces)),
-        out_shape=out_shape,
-        in_specs=[pl.BlockSpec(memory_space=VMEM)] * (4 + len(pieces) + len(deep_pieces)),
-        out_specs=[pl.BlockSpec(memory_space=VMEM)] * len(out_shape),
-        scratch_shapes=[
-            pltpu.VMEM((width, width + hidden), jnp.bfloat16),
-            pltpu.VMEM((hidden, width), jnp.bfloat16),
-            pltpu.VMEM((rows, hidden), jnp.bfloat16),
-            pltpu.VMEM((rows, hidden), jnp.bfloat16),
-            pltpu.VMEM((rows, width), jnp.bfloat16),
-            pltpu.VMEM((rows, width), jnp.bfloat16),
-            pltpu.VMEM((width, 512), jnp.float32),
-            pltpu.VMEM((hidden, width), jnp.float32),
-        ],
-        compiler_params=params(30),
-        name="feed",
-    )(x, mixed, dy, gains, *pieces, *deep_pieces)
+    lax.fori_loop(0, rows // DEEP_CHUNK, one_chunk, 0)
+
+
+def mixed_back(middle_low, mixed, out_weight):
+    rows, width = mixed.shape
+    return pl.pallas_call(
+        mixed_back_kernel,
+        out_shape=jax.ShapeDtypeStruct((rows, 2 * width), jnp.bfloat16),
+        in_specs=[pl.BlockSpec(memory_space=VMEM)] * 3,
+        out_specs=pl.BlockSpec(memory_space=VMEM),
+        compiler_params=params(10),
+        name="mixed_back",
+    )(middle_low, mixed, out_weight)
 
 
 def project_back_kernel(lay, x, packed, gains, first_norms, second_norms, keep, send, first, block):
@@ -655,9 +676,9 @@
     return out
 
 
-def moments_kernel(pieces_of, first_index, reps, *refs):
+def moments_kernel(pieces_of, first_index, reps, more, *refs):
     n = len(pieces_of)
-    grads, arrays = refs[:reps], refs[reps:]
+    grads, others, arrays = refs[:reps], refs[reps : reps + more], refs[reps + more :]
     total = grads[0][...]
     for ref in grads[1:]:
         total = total + ref[...].astype(jnp.float32)
@@ -665,7 +686,7 @@
     momenta, variances, directions = arrays[3 * n : 4 * n], arrays[4 * n : 5 * n], arrays[5 * n : 6 * n]
     sums = arrays[6 * n]
     lane = lax.broadcasted_iota(jnp.int32, (1, LANES), 1)
-    row = jnp.zeros((1, LANES), jnp.float32)
+    row = others[0][0] if more else jnp.zeros((1, LANES), jnp.float32)
     for i, parts in enumerate(pieces_of):
         weight_sum = jnp.zeros((1, 1), jnp.float32)
         step_sum = jnp.zeros((1, 1), jnp.float32)
@@ -685,15 +706,15 @@
             step_sum = step_sum + full_sum(direction * direction)
         row = jnp.where(lane == first_index[i], weight_sum, row)
         row = jnp.where(lane == 5 + first_index[i], step_sum, row)
-    sums[...] = row
-
-
-def moments(pieces_of, first_index, grads, weights, firsts, seconds):
-    arrays = [*grads, *weights, *firsts, *seconds]
+    sums[...] = jnp.broadcast_to(row, sums.shape)
+
+
+def moments(pieces_of, first_index, grads, others, copies, weights, firsts, seconds):
+    arrays = [*grads, *others, *weights, *firsts, *seconds]
     shapes = [jax.ShapeDtypeStruct(weight.shape, jnp.float32) for weight in weights]
     outs = pl.pallas_call(
-        partial(moments_kernel, pieces_of, first_index, len(grads)),
-        out_shape=shapes * 3 + [jax.ShapeDtypeStruct((1, LANES), jnp.float32)],
+        partial(moments_kernel, pieces_of, first_index, len(grads), len(others)),
+        out_shape=shapes * 3 + [jax.ShapeDtypeStruct((copies, 1, LANES), jnp.float32)],
         in_specs=[pl.BlockSpec(memory_space=VMEM)] * len(arrays),
         out_specs=[pl.BlockSpec(memory_space=VMEM)] * (3 * len(weights) + 1),
         compiler_params=params(8),
@@ -705,7 +726,7 @@
 
 def update_kernel(n, sums, *refs):
     weights, directions, updated, table = refs[:n], refs[n : 2 * n], refs[2 * n : 3 * n], refs[3 * n]
-    norms = jnp.sqrt(jnp.sum(sums[...], axis=0, keepdims=True))
+    norms = jnp.sqrt(jnp.sum(sums[...], axis=0))
     row = lax.broadcasted_iota(jnp.int32, table.shape, 0)
     lane = lax.broadcasted_iota(jnp.int32, table.shape, 1)
     out = jnp.zeros(table.shape, jnp.float32)
@@ -724,13 +745,13 @@
     outs = pl.pallas_call(
         partial(update_kernel, n),
         out_shape=[jax.ShapeDtypeStruct(weight.shape, jnp.float32) for weight in weights]
-        + [jax.ShapeDtypeStruct((8, LANES), jnp.float32)],
+        + [jax.ShapeDtypeStruct((3, n), jnp.float32)],
         in_specs=[pl.BlockSpec(memory_space=VMEM)] * (1 + 2 * n),
         out_specs=[pl.BlockSpec(memory_space=VMEM)] * (n + 1),
         compiler_params=params(6),
         name="update",
     )(sums, *weights, *directions)
-    return outs[:n], outs[n][:3, :n]
+    return outs[:n], outs[n]
 
 
 def over(lay, value, first):
@@ -775,40 +796,44 @@
     square_contract,
     square_norms,
 ):
+    plain, twin = lay
+    lay = plain
     masters = (attend_in, attend_out, expand, contract, layer_norms)
     width = attend_in.shape[1]
     depth = attend_out.shape[1]
     hidden = expand.shape[1]
     own = attend_in.shape[0]
     count = lay.dp * lay.rep
-    plain = own % 16 == 0
+    whole_tiles = own % 16 == 0
     norm_rows = jnp.pad(layer_norms.astype(jnp.bfloat16).T, ((0, 0), (0, LANES - 4)))
     shard1 = jnp.concatenate([attend_in.astype(jnp.bfloat16), norm_rows], axis=1)
-    column1 = over(lay, shard1, True)
+    column1 = over(plain, shard1, True)
     rows = inputs.shape[1]
     attend_out_, expand_, contract_ = after([attend_out, expand, contract], [shard1])
     deep = [contract_[j * own : (j + 1) * own] for j in range(4)]
     shard2 = jnp.concatenate([part.astype(jnp.bfloat16) for part in (attend_out_, expand_, *deep)], axis=1)
     (shard2,) = after([shard2], column1[1:])
-    column2 = over(lay, shard2, True)
-    (segments_,) = after([segments], [shard1])
+    column2 = over(twin, shard2, True)
+    blocks1 = over(plain, column_of(plain, column1), False)
+    (segments_,) = after([segments], blocks1[:1])
     x, dy, labels, begin = arrange(inputs[0], cotangent[0], segments_)
-    blocks1 = over(lay, column_of(lay, after(column1, [x])), False)
-    blocks2 = over(lay, column_of(lay, after(column2, blocks1)), False)
+    blocks2 = over(twin, column_of(twin, after(column2, [*blocks1, x])), False)
     pieces1 = over_core(lay, blocks1)
     *pieces1, x, labels = after([*pieces1, x, labels], blocks2[:1])
-    qx, kx, vx, mixed, gains = attend(lay, x, labels, pieces1)
-    pieces2 = over_core(lay, after(blocks2, [mixed]))
+    qx, kx, vx, mixed, gains = attend(plain, x, labels, pieces1)
+    near = lay.to_core(blocks2[0])
+    blocks2[1:] = after(blocks2[1:], [mixed])
+    pieces2 = [*blocks2, near, *[lay.to_core(block) for block in blocks2[1:]]]
     deep_pieces = []
-    if not plain:
+    if not whole_tiles:
         first = depth + hidden
         for piece in pieces2:
             part = piece[:, first:].reshape(lay.rep, own, 4, depth).transpose(0, 2, 1, 3)
             deep_pieces.append(part.reshape(-1, depth))
-    outputs, dox, middle_grad, keep2, send2, second_norms, *deep_out = feed(
-        lay, x, mixed, dy, gains, pieces2, deep_pieces
+    middle, middle_grad, middle_low, active, contract_all, out_weight, keep2, send2, second_norms, *deep_out = feed(
+        twin, x, mixed, dy, gains, pieces2, deep_pieces
     )
-    if not plain:
+    if not whole_tiles:
         keep2, send2 = [
             jnp.concatenate(
                 [
@@ -819,35 +844,38 @@
             )
             for wide, part in zip((keep2, send2), deep_out)
         ]
-    own2, *low2 = chip_sum(lay, keep2, lay.to_core(send2))
-    got2 = send_over(lay, low2, False)
+    chip2 = lay.to_core(send2)
+    dox = mixed_back(middle_low, mixed, out_weight)
+    keep2, chip2 = after([keep2, chip2], [dox])
+    own2, *low2 = chip_sum(twin, keep2, chip2)
+    got2 = send_over(twin, low2, False)
     (dox,) = after([dox], low2)
     packed = attend_back(qx, kx, vx, dox)
-    input_gradient, first_norms = input_back(lay, x, packed, gains, middle_grad, pieces1)
-    own2, *got2 = after([own2, *got2], [first_norms])
-    own2, *low2 = plane_sum(lay, own2, got2)
-    got2 = send_over(lay, low2, True)
-    (packed_,) = after([packed], low2)
-    keep1, send1 = project_back(lay, x, packed_, gains, first_norms, second_norms, own)
-    own1, *low1 = chip_sum(lay, keep1, lay.to_core(send1))
-    got1 = send_over(lay, low1, False)
-    outputs, input_gradient = after([outputs, input_gradient], low1)
-    outputs, input_gradient = arrange_back(begin, outputs, input_gradient, rows)
+    input_gradient, first_norms = input_back(plain, x, packed, gains, middle_grad, pieces1)
+    keep1, send1 = project_back(plain, x, packed, gains, first_norms, second_norms, own)
+    own2, *got2 = after([own2, *got2], [send1])
+    own2, *low2 = plane_sum(twin, own2, got2)
+    got2 = send_over(twin, low2, True)
+    (send1,) = after([send1], low2[:1])
+    own1, *low1 = chip_sum(plain, keep1, lay.to_core(send1))
+    got1 = send_over(plain, low1, False)
     spans = [[(0, own, (0, depth))], [(0, own, (depth, depth + hidden))]]
     spans.append([(j * own, own, (depth + hidden + j * depth, depth + hidden + (j + 1) * depth)) for j in range(4)])
     momenta2, variances2, directions2, sums2 = moments(
-        spans, (1, 2, 3), [own2, *got2], masters[1:4],
+        spans, (1, 2, 3), [own2, *got2], [], 1, masters[1:4],
         (moment_out, moment_expand, moment_contract), (square_out, square_expand, square_contract),
     )
-    own1, *low1 = plane_sum(lay, own1, got1)
-    got1 = send_over(lay, low1, True)
+    own1, *low1 = plane_sum(plain, own1, got1)
+    got1 = send_over(plain, low1, True)
     momenta1, variances1, directions1, sums1 = moments(
-        [[(0, own, (0, width))], [(0, 4, (width, width + 4, True))]], (0, 4), [own1, *got1], (attend_in, layer_norms),
+        [[(0, own, (0, width))], [(0, 4, (width, width + 4, True))]], (0, 4), [own1, *got1], [sums2], count, (attend_in, layer_norms),
         (moment_in, moment_norms), (square_in, square_norms),
     )
-    sums = exchange(lay, jnp.broadcast_to((sums1 + sums2)[None], (count, 1, LANES)))
+    sums = exchange(lay, sums1)
+    (middle,) = after([middle], [sums1])
+    outputs, input_gradient = finish(begin, middle, active, contract_all, input_gradient, rows)
     directions = (directions1[0], *directions2, directions1[1])
-    updated, trust_table = update(sums[:, 0], masters, directions)
+    updated, trust_table = update(sums, masters, directions)
     momenta = (momenta1[0], *momenta2, momenta1[1])
     variances = (variances1[0], *variances2, variances1[1])
     return (outputs[None], input_gradient[None], *updated, *momenta, *variances, trust_table)
@@ -875,7 +903,7 @@
         P(None, ("dp", "rep")),
     )
     return jax.shard_map(
-        partial(body, Layout(mesh)),
+        partial(body, (Layout(mesh, False), Layout(mesh, True))),
         mesh=mesh,
         in_specs=placed,
         out_specs=(

time: 172 us -> 167 us (0.971)
  local copies, waits for them, and re-layouts: 4.54 us -> 16.7 us
  starting transfers between devices: 48.4 us -> 39.1 us
  waiting for transfers between devices: 32.3 us -> 24.2 us
    unnamed x39 -> x77, local copies, waits for them, and re-layouts: 3.24 us -> 16.6 us
    ppermute x24, starting transfers between devices: 37 us -> 30.9 us  [over(): return lax.ppermute(value, AXES, self.pairs(move))]
    pallas_call x1, Pallas kernels: 25.6 us -> 20.5 us  [feed(): pl.pallas_call(partial(feed_kernel, lay, len(pieces), len(deep_pieces)),...]
    all_to_all x1, waiting for transfers between devices: 5.06 us -> 0.01 us  [exchange(): return lax.all_to_all(value, AXES, 0, 0)]
    pallas_call x1 -> x2, Pallas kernels: 2.03 us -> 7.03 us  [the longest x1 4.33 us: finish(): pl.pallas_call(finish_kernel, out_shape=[jax.ShapeDtypeStruct((rows, widt...]
    ppermute x10, waiting for transfers between devices: 12.1 us -> 8.43 us  [to_core(): return lax.ppermute(value, AXES, self.pairs(lambda p, c, z: (p, 1 - c, z)))]
    all_to_all x1, starting transfers between devices: 8.27 us -> 4.84 us  [exchange(): return lax.all_to_all(value, AXES, 0, 0)]
  transfers between devices with their start and end apart: 35 -> 35, of which waited for: 16 -> 16; matrix products, arithmetic and copies ran while one was open for 2% -> 2% of each run, Pallas kernels for 28% -> 34%
where the time goes in v2:
time: 167 us; the launch traced here: 166 us
  Pallas kernels  81 us (49%)
  starting transfers between devices  39.1 us (23%)
  waiting for transfers between devices  24.2 us (14%)
  local copies, waits for them, and re-layouts  16.7 us (10%)
  other arithmetic  4.18 us (3%)
    ppermute x24, starting transfers between devices, over(): return lax.ppermute(value, AXES, self.pairs(move))  30.9 us
    pallas_call x1, Pallas kernels, attend(): pl.pallas_call(partial(attend_kernel, lay, len(pieces)), out_shape=(wide,...  21.1 us
    pallas_call x1, Pallas kernels, feed(): pl.pallas_call(partial(feed_kernel, lay, len(pieces), len(deep_pieces)),...  20.5 us
    pallas_call x1, Pallas kernels, attend_back(): pl.pallas_call(attend_back_kernel, out_shape=jax.ShapeDtypeStruct((rows,...  18.8 us
    unnamed x77, local copies, waits for them, and re-layouts  16.6 us
    ppermute x24, waiting for transfers between devices, over(): return lax.ppermute(value, AXES, self.pairs(move))  15.7 us
    ppermute x10, waiting for transfers between devices, to_core(): return lax.ppermute(value, AXES, self.pairs(lambda p, c, z: (p, 1 - c, z)))  8.43 us
    all_to_all x1, starting transfers between devices, exchange(): return lax.all_to_all(value, AXES, 0, 0)  4.84 us
  transfers between devices with their start and end apart: 35, of which 16 were waited for; matrix products, arithmetic and copies ran while one was open for 2% of the time, Pallas kernels for 34%

profile of v2, /device:TPU:0, one launch (start us, length us, event | category | flops | bytes accessed | tf_op | source)
XLA Modules:
  0.0 166.3 jit_solution(18188155145647755219)
XLA Ops:
  2.3 5.1 %collective-permute-start.2 = (bf16[16,1664]{1,0:T(8,128)(2,1)S(1)}, bf16[16,1664]{1,0:T(8,128)(2,1)S(1)}, u32[]{:S(2)}, u32[]{:S(2)}) collective-permute-start(bf16[16,1664]{1,0:T(8,128)(2,1)S(1)} %fusion.1.refs_0_), channel_id=1, source_target_pairs={{0,3},{1,0},{2,1},{3,2},{4,7},{5,4},{6,5},{7,6},{8,11},{9,8},{10,9... | collective-permute-start | bytes 159752 | tf_op jit(solution)/shard_map/ppermute | solution.py:67
  11.1 1.4 collective-permute-done.1.refs_2_
  13.4 1.5 collective-permute-start.12
  15.0 2.5 %collective-permute-start.5 = (bf16[64,1664]{1,0:T(8,128)(2,1)S(1)}, bf16[64,1664]{1,0:T(8,128)(2,1)S(1)}, u32[]{:S(2)}, u32[]{:S(2)}) collective-permute-start(bf16[64,1664]{1,0:T(8,128)(2,1)S(1)} %column.2.refs_0_), channel_id=1, source_target_pairs={{0,24},{1,25},{2,26},{3,27},{4,28},{5,29},{6,30},{7,31},{8,16},{9,... | collective-permute-start | bytes 638984 | tf_op jit(solution)/shard_map/ppermute | solution.py:67
  18.8 1.7 %collective-permute-start.10 = (bf16[16,4608]{1,0:T(8,128)(2,1)S(1)}, bf16[16,4608]{1,0:T(8,128)(2,1)S(1)}, u32[]{:S(2)}, u32[]{:S(2)}) collective-permute-start(bf16[16,4608]{1,0:T(8,128)(2,1)S(1)} %slice_dynamic-update-slice_fusion.refs_0_), channel_id=1, source_target_pairs={{0,1},{1,2},{2,3},{3,0},{4,12},{5,13},{6,14},{7,15},{8,9},{9,10},{... | collective-permute-start | bytes 442376 | tf_op jit(solution)/shard_map/ppermute | solution.py:67
  20.5 1.2 copy-done.6
  21.7 1.2 copy-done.7
  24.7 3.0 %collective-permute-done.11.refs_2_ = bf16[16,4608]{1,0:T(8,128)(2,1)S(1)} collective-permute-done((bf16[16,4608]{1,0:T(8,128)(2,1)S(1)}, bf16[16,4608]{1,0:T(8,128)(2,1)S(1)}, u32[]{:S(2)}, u32[]{:S(2)}) %collective-permute-start.11) | collective-permute-done | bytes 147488 | tf_op jit(solution)/shard_map/ppermute | solution.py:67
  28.0 2.5 %collective-permute-start.15 = (bf16[64,4608]{1,0:T(8,128)(2,1)S(1)}, bf16[64,4608]{1,0:T(8,128)(2,1)S(1)}, u32[]{:S(2)}, u32[]{:S(2)}) collective-permute-start(bf16[64,4608]{1,0:T(8,128)(2,1)S(1)} %column.3.refs_0_), channel_id=1, source_target_pairs={{0,24},{1,25},{2,26},{3,27},{4,7},{5,4},{6,5},{7,6},{8,16},{9,17},... | collective-permute-start | bytes 1769480 | tf_op jit(solution)/shard_map/ppermute | solution.py:67
  34.7 21.1 %attend.1 = (bf16[1056,1024]{1,0:T(8,128)(2,1)S(1)}, bf16[1056,1024]{1,0:T(8,128)(2,1)S(1)}, bf16[1056,1024]{1,0:T(8,128)(2,1)S(1)}, bf16[1056,512]{1,0:T(8,128)(2,1)S(1)}, f32[8,512]{1,0:T(8,128)S(1)}) custom-call(bf16[1056,512]{1,0:T(8,128)(2,1)S(1)} %get-tuple-element.124.x, s32[1056,128]{1,0:T(8,128)S(1)} %get-tuple-element.125.labels, ...), custom_call_target="tpu_custom_call" | custom-call | tf_op jit(solution)/shard_map/attend/pallas_call | solution.py:301
  59.8 20.5 %feed.1 = (f32[1056,512]{1,0:T(8,128)S(1)}, f32[1056,512]{1,0:T(8,128)S(1)}, bf16[1056,512]{1,0:T(8,128)(2,1)S(1)}, bf16[1056,2048]{1,0:T(8,128)(2,1)S(1)}, bf16...) custom-call(bf16[1056,512]{1,0:T(8,128)(2,1)S(1)} %get-tuple-element, ...), custom_call_target="tpu_custom_call" | custom-call | tf_op jit(solution)/shard_map/feed/pallas_call | solution.py:456
  80.3 1.3 copy-done.2
  82.0 2.7 %mixed_back.1.dox = bf16[1056,1024]{1,0:T(8,128)(2,1)S(1)} custom-call(bf16[1056,512]{1,0:T(8,128)(2,1)S(1)} %get-tuple-element.144.middle_low, bf16[1056,512]{1,0:T(8,128)(2,1)S(1)} %get-tuple-element.134.mixed, bf16[512,512]{1,0:T(8,128)(2,1)S(1)} %get-tuple-element.145.out_weight), custom_call_target="tpu_custom_call" | custom-call | tf_op jit(solution)/shard_map/mixed_back/pallas_call | solution.py:502
  84.8 1.5 collective-permute-done.20.got
  87.4 1.5 collective-permute-start.21
  88.9 1.4 collective-permute-start.22
  90.9 18.8 %attend_back.1.packed = bf16[1056,1536]{1,0:T(8,128)(2,1)S(1)} custom-call(bf16[1056,1024]{1,0:T(8,128)(2,1)S(1)} %get-tuple-element.141.qx, bf16[1056,1024]{1,0:T(8,128)(2,1)S(1)} %get-tuple-element.142.kx, bf16[1056,1024]{1,0:T(8,128)(2,1)S(1)} %get-tuple-element.143.vx, bf16[1056,1024]{1,0:T(8,128)(2,1)S(1)} %mixed_back.1.dox), custom_call_target="tpu_custom_call" | custom-call | tf_op jit(solution)/shard_map/attend_back/pallas_call | solution.py:355
  109.7 3.2 %input_back.1 = (bf16[1056,512]{1,0:T(8,128)(2,1)S(1)}, f32[8,512]{1,0:T(8,128)S(1)}) custom-call(bf16[1056,512]{1,0:T(8,128)(2,1)S(1)} %get-tuple-element.124.x, bf16[1056,1536]{1,0:T(8,128)(2,1)S(1)} %attend_back.1.packed, f32[8,512]{1,0:T(8,128)S(1)} %get-tuple-element.136.gains, f32[1056,512]{1,0:T(8,128)S(1)} %get-tuple-element.154.middle_grad, ...), custom_call_target="tpu_custom_call" | custom-call | tf_op jit(solution)/shard_map/input_back/pallas_call | solution.py:574
  112.9 3.9 %project_back.1 = (bf16[4,64,1664]{2,1,0:T(8,128)(2,1)S(1)}, bf16[4,64,1664]{2,1,0:T(8,128)(2,1)S(1)}) custom-call(bf16[1056,512]{1,0:T(8,128)(2,1)S(1)} %get-tuple-element.124.x, bf16[1056,1536]{1,0:T(8,128)(2,1)S(1)} %attend_back.1.packed, f32[8,512]{1,0:T(8,128)S(1)} %get-tuple-element.136.gains, f32[8,512]{1,0:T(8,128)S(1)} %get-tuple-element.155.first_norms, ...), custom_call_target="tpu_custom_call" | custom-call | tf_op jit(solution)/shard_map/project_back/pallas_call | solution.py:540
  118.5 2.0 %collective-permute-done.24.got = bf16[4,64,1664]{2,1,0:T(8,128)(2,1)S(1)} collective-permute-done((bf16[4,64,1664]{2,1,0:T(8,128)(2,1)S(1)}, bf16[4,64,1664]{2,1,0:T(8,128)(2,1)S(1)}, u32[]{:S(2)}, u32[]{:S(2)}) %collective-permute-start.24) | collective-permute-done | bytes 852000 | tf_op jit(solution)/shard_map/ppermute | solution.py:70
  120.8 1.5 collective-permute-start.25
  122.4 1.2 collective-permute-start.26
  124.4 1.3 collective-permute-start.32
  125.7 1.3 collective-permute-start.33
  127.0 2.0 %collective-permute-done.25.refs_0_ = bf16[64,1664]{1,0:T(8,128)(2,1)S(1)} collective-permute-done((bf16[64,1664]{1,0:T(8,128)(2,1)S(1)}, bf16[64,1664]{1,0:T(8,128)(2,1)S(1)}, u32[]{:S(2)}, u32[]{:S(2)}) %collective-permute-start.25) | collective-permute-done | bytes 213024 | tf_op jit(solution)/shard_map/ppermute | solution.py:67
  129.2 7.4 %collective-permute-done.26.refs_1_ = bf16[64,1664]{1,0:T(8,128)(2,1)S(1)} collective-permute-done((bf16[64,1664]{1,0:T(8,128)(2,1)S(1)}, bf16[64,1664]{1,0:T(8,128)(2,1)S(1)}, u32[]{:S(2)}, u32[]{:S(2)}) %collective-permute-start.26) | collective-permute-done | bytes 213024 | tf_op jit(solution)/shard_map/ppermute | solution.py:67
  137.1 1.8 %collective-permute-start.29 = (bf16[16,1664]{1,0:T(8,128)(2,1)S(1)}, bf16[16,1664]{1,0:T(8,128)(2,1)S(1)}, u32[]{:S(2)}, u32[]{:S(2)}) collective-permute-start(bf16[16,1664]{1,0:T(8,128)(2,1)S(1)} %get-tuple-element.172), channel_id=1, source_target_pairs={{0,2},{1,3},{2,0},{3,1},{4,6},{5,7},{6,4},{7,5},{8,10},{9,11},{10,... | collective-permute-start | bytes 159752 | tf_op jit(solution)/shard_map/ppermute | solution.py:67
  138.9 2.1 %collective-permute-start.30 = (bf16[16,1664]{1,0:T(8,128)(2,1)S(1)}, bf16[16,1664]{1,0:T(8,128)(2,1)S(1)}, u32[]{:S(2)}, u32[]{:S(2)}) collective-permute-start(bf16[16,1664]{1,0:T(8,128)(2,1)S(1)} %get-tuple-element.173), channel_id=1, source_target_pairs={{0,3},{1,0},{2,1},{3,2},{4,7},{5,4},{6,5},{7,6},{8,11},{9,8},{10,9... | collective-permute-start | bytes 159752 | tf_op jit(solution)/shard_map/ppermute | solution.py:67
  146.0 4.8 %all-to-all-start = ((f32[32,1,128]{2,1,0:T(1,128)}), f32[32,1,128]{2,1,0:T(1,128)S(1)}, u32[]{:S(2)}, u32[]{:S(2)}) async-start(f32[32,1,128]{2,1,0:T(1,128)} %copy-done.29), calls=%async_computation | async-start | bytes 32768 | tf_op jit(solution)/shard_map/all_to_all | solution.py:775
  150.8 2.2 %copy-done.1 = bf16[1056,2048]{1,0:T(8,128)(2,1)S(1)} copy-done((bf16[1056,2048]{1,0:T(8,128)(2,1)S(1)}, bf16[1056,2048]{1,0:T(8,128)(2,1)}, u32[]{:S(2)}) %copy-start.1) | copy-done | bytes 4325400
  153.0 1.6 copy-done.3
  155.3 4.3 %finish.1 = (bf16[1044,512]{1,0:T(8,128)(2,1)}, bf16[1044,512]{1,0:T(8,128)(2,1)}) custom-call(f32[8,128]{1,0:T(8,128)S(1)} %copy-done.32, f32[1056,512]{1,0:T(8,128)S(1)} %get-tuple-element.179.middle, bf16[1056,2048]{1,0:T(8,128)(2,1)S(1)} %copy-done.1, bf16[2048,512]{1,0:T(8,128)(2,1)S(1)} %copy-done.3, bf16[1056,512]{1,0:T(8,128)(2,1)S(1)} %get-tuple-element.182.grad_in), custom_call_target="tpu_custom_call" | custom-call | tf_op jit(solution)/shard_map/finish/pallas_call | solution.py:219
  (140 shorter events, 35.4 us)
Async XLA Ops:
  2.3 8.8 %collective-permute-start.2 = (bf16[16,1664]{1,0:T(8,128)(2,1)S(1)}, bf16[16,1664]{1,0:T(8,128)(2,1)S(1)}, u32[]{:S(2)}, u32[]{:S(2)}) collective-permute-start(bf16[16,1664]{1,0:T(8,128)(2,1)S(1)} %fusion.1.refs_0_), channel_id=1, source_target_pairs={{0,3},{1,0},{2,1},{3,2},{4,7},{5,4},{6,5},{7,6},{8,11},{9,8},{10,9... | collective-permute-start | bytes 159752 | tf_op jit(solution)/shard_map/ppermute | solution.py:67
  7.5 5.1 %collective-permute-start.1 = (bf16[16,1664]{1,0:T(8,128)(2,1)S(1)}, bf16[16,1664]{1,0:T(8,128)(2,1)S(1)}, u32[]{:S(2)}, u32[]{:S(2)}) collective-permute-start(bf16[16,1664]{1,0:T(8,128)(2,1)S(1)} %fusion.1.refs_0_), channel_id=1, source_target_pairs={{0,2},{1,3},{2,0},{3,1},{4,6},{5,7},{6,4},{7,5},{8,10},{9,11},{10,... | collective-permute-start | bytes 159752 | tf_op jit(solution)/shard_map/ppermute | solution.py:67
  7.5 5.9 %collective-permute-start = (bf16[16,1664]{1,0:T(8,128)(2,1)S(1)}, bf16[16,1664]{1,0:T(8,128)(2,1)S(1)}, u32[]{:S(2)}, u32[]{:S(2)}) collective-permute-start(bf16[16,1664]{1,0:T(8,128)(2,1)S(1)} %fusion.1.refs_0_), channel_id=1, source_target_pairs={{0,1},{1,2},{2,3},{3,0},{4,5},{5,6},{6,7},{7,4},{8,9},{9,10},{10,1... | collective-permute-start | bytes 159752 | tf_op jit(solution)/shard_map/ppermute | solution.py:67
  13.4 5.4 %collective-permute-start.12 = (bf16[16,4608]{1,0:T(8,128)(2,1)S(1)}, bf16[16,4608]{1,0:T(8,128)(2,1)S(1)}, u32[]{:S(2)}, u32[]{:S(2)}) collective-permute-start(bf16[16,4608]{1,0:T(8,128)(2,1)S(1)} %slice_dynamic-update-slice_fusion.refs_0_), channel_id=1, source_target_pairs={{0,3},{1,0},{2,1},{3,2},{4,28},{5,29},{6,30},{7,31},{8,11},{9,8},{... | collective-permute-start | bytes 442376 | tf_op jit(solution)/shard_map/ppermute | solution.py:67
  15.0 12.7 %collective-permute-start.5 = (bf16[64,1664]{1,0:T(8,128)(2,1)S(1)}, bf16[64,1664]{1,0:T(8,128)(2,1)S(1)}, u32[]{:S(2)}, u32[]{:S(2)}) collective-permute-start(bf16[64,1664]{1,0:T(8,128)(2,1)S(1)} %column.2.refs_0_), channel_id=1, source_target_pairs={{0,24},{1,25},{2,26},{3,27},{4,28},{5,29},{6,30},{7,31},{8,16},{9,... | collective-permute-start | bytes 638984 | tf_op jit(solution)/shard_map/ppermute | solution.py:67
  17.5 10.2 %collective-permute-start.4 = (bf16[64,1664]{1,0:T(8,128)(2,1)S(1)}, bf16[64,1664]{1,0:T(8,128)(2,1)S(1)}, u32[]{:S(2)}, u32[]{:S(2)}) collective-permute-start(bf16[64,1664]{1,0:T(8,128)(2,1)S(1)} %column.2.refs_0_), channel_id=1, source_target_pairs={{0,16},{1,17},{2,18},{3,19},{4,20},{5,21},{6,22},{7,23},{8,24},{9,... | collective-permute-start | bytes 638984 | tf_op jit(solution)/shard_map/ppermute | solution.py:67
  18.0 9.7 %collective-permute-start.3 = (bf16[64,1664]{1,0:T(8,128)(2,1)S(1)}, bf16[64,1664]{1,0:T(8,128)(2,1)S(1)}, u32[]{:S(2)}, u32[]{:S(2)}) collective-permute-start(bf16[64,1664]{1,0:T(8,128)(2,1)S(1)} %column.2.refs_0_), channel_id=1, source_target_pairs={{0,8},{1,9},{2,10},{3,11},{4,12},{5,13},{6,14},{7,15},{8,0},{9,1},... | collective-permute-start | bytes 638984 | tf_op jit(solution)/shard_map/ppermute | solution.py:67
  18.6 9.1 %collective-permute-start.11 = (bf16[16,4608]{1,0:T(8,128)(2,1)S(1)}, bf16[16,4608]{1,0:T(8,128)(2,1)S(1)}, u32[]{:S(2)}, u32[]{:S(2)}) collective-permute-start(bf16[16,4608]{1,0:T(8,128)(2,1)S(1)} %slice_dynamic-update-slice_fusion.refs_0_), channel_id=1, source_target_pairs={{0,2},{1,3},{2,0},{3,1},{4,20},{5,21},{6,22},{7,23},{8,10},{9,11},... | collective-permute-start | bytes 442376 | tf_op jit(solution)/shard_map/ppermute | solution.py:67
  18.8 8.9 %collective-permute-start.10 = (bf16[16,4608]{1,0:T(8,128)(2,1)S(1)}, bf16[16,4608]{1,0:T(8,128)(2,1)S(1)}, u32[]{:S(2)}, u32[]{:S(2)}) collective-permute-start(bf16[16,4608]{1,0:T(8,128)(2,1)S(1)} %slice_dynamic-update-slice_fusion.refs_0_), channel_id=1, source_target_pairs={{0,1},{1,2},{2,3},{3,0},{4,12},{5,13},{6,14},{7,15},{8,9},{9,10},{... | collective-permute-start | bytes 442376 | tf_op jit(solution)/shard_map/ppermute | solution.py:67
  28.0 27.9 %collective-permute-start.15 = (bf16[64,4608]{1,0:T(8,128)(2,1)S(1)}, bf16[64,4608]{1,0:T(8,128)(2,1)S(1)}, u32[]{:S(2)}, u32[]{:S(2)}) collective-permute-start(bf16[64,4608]{1,0:T(8,128)(2,1)S(1)} %column.3.refs_0_), channel_id=1, source_target_pairs={{0,24},{1,25},{2,26},{3,27},{4,7},{5,4},{6,5},{7,6},{8,16},{9,17},... | collective-permute-start | bytes 1769480 | tf_op jit(solution)/shard_map/ppermute | solution.py:67
  30.5 25.4 %collective-permute-start.14 = (bf16[64,4608]{1,0:T(8,128)(2,1)S(1)}, bf16[64,4608]{1,0:T(8,128)(2,1)S(1)}, u32[]{:S(2)}, u32[]{:S(2)}) collective-permute-start(bf16[64,4608]{1,0:T(8,128)(2,1)S(1)} %column.3.refs_0_), channel_id=1, source_target_pairs={{0,16},{1,17},{2,18},{3,19},{4,6},{5,7},{6,4},{7,5},{8,24},{9,25},... | collective-permute-start | bytes 1769480 | tf_op jit(solution)/shard_map/ppermute | solution.py:67
  31.0 24.9 %collective-permute-start.13 = (bf16[64,4608]{1,0:T(8,128)(2,1)S(1)}, bf16[64,4608]{1,0:T(8,128)(2,1)S(1)}, u32[]{:S(2)}, u32[]{:S(2)}) collective-permute-start(bf16[64,4608]{1,0:T(8,128)(2,1)S(1)} %column.3.refs_0_), channel_id=1, source_target_pairs={{0,8},{1,9},{2,10},{3,11},{4,5},{5,6},{6,7},{7,4},{8,0},{9,1},{10,... | collective-permute-start | bytes 1769480 | tf_op jit(solution)/shard_map/ppermute | solution.py:67
  31.7 1.6 collective-permute-start.9
  34.4 22.5 %collective-permute-start.16 = (bf16[64,4608]{1,0:T(8,128)(2,1)S(1)}, bf16[64,4608]{1,0:T(8,128)(2,1)S(1)}, u32[]{:S(2)}, u32[]{:S(2)}) collective-permute-start(bf16[64,4608]{1,0:T(8,128)(2,1)S(1)} %column.3.refs_0_), channel_id=1, source_target_pairs={{0,4},{1,5},{2,6},{3,7},{4,0},{5,1},{6,2},{7,3},{8,12},{9,13},{10,... | collective-permute-start | bytes 1769480 | tf_op jit(solution)/shard_map/ppermute | solution.py:70
  55.9 2.2 %collective-permute-start.17 = (bf16[64,4608]{1,0:T(8,128)(2,1)S(1)}, bf16[64,4608]{1,0:T(8,128)(2,1)S(1)}, u32[]{:S(2)}, u32[]{:S(2)}) collective-permute-start(bf16[64,4608]{1,0:T(8,128)(2,1)S(1)} %collective-permute-done.13.refs_1_), channel_id=1, source_target_pairs={{0,4},{1,5},{2,6},{3,7},{4,0},{5,1},{6,2},{7,3},{8,12},{9,13},{10,... | collective-permute-start | bytes 1769480 | tf_op jit(solution)/shard_map/ppermute | solution.py:70
  56.5 2.5 %collective-permute-start.18 = (bf16[64,4608]{1,0:T(8,128)(2,1)S(1)}, bf16[64,4608]{1,0:T(8,128)(2,1)S(1)}, u32[]{:S(2)}, u32[]{:S(2)}) collective-permute-start(bf16[64,4608]{1,0:T(8,128)(2,1)S(1)} %collective-permute-done.14.refs_2_), channel_id=1, source_target_pairs={{0,4},{1,5},{2,6},{3,7},{4,0},{5,1},{6,2},{7,3},{8,12},{9,13},{10,... | collective-permute-start | bytes 1769480 | tf_op jit(solution)/shard_map/ppermute | solution.py:70
  56.5 3.3 %collective-permute-start.19 = (bf16[64,4608]{1,0:T(8,128)(2,1)S(1)}, bf16[64,4608]{1,0:T(8,128)(2,1)S(1)}, u32[]{:S(2)}, u32[]{:S(2)}) collective-permute-start(bf16[64,4608]{1,0:T(8,128)(2,1)S(1)} %collective-permute-done.15.refs_3_), channel_id=1, source_target_pairs={{0,4},{1,5},{2,6},{3,7},{4,0},{5,1},{6,2},{7,3},{8,12},{9,13},{10,... | collective-permute-start | bytes 1769480 | tf_op jit(solution)/shard_map/ppermute | solution.py:70
  81.7 4.5 %collective-permute-start.20 = (bf16[4,64,4608]{2,1,0:T(8,128)(2,1)S(1)}, bf16[4,64,4608]{2,1,0:T(8,128)(2,1)S(1)}, u32[]{:S(2)}, u32[]{:S(2)}) collective-permute-start(bf16[4,64,4608]{2,1,0:T(8,128)(2,1)S(1)} %get-tuple-element.147), channel_id=1, source_target_pairs={{0,4},{1,5},{2,6},{3,7},{4,0},{5,1},{6,2},{7,3},{8,12},{9,13},{10,... | collective-permute-start | bytes 7077896 | tf_op jit(solution)/shard_map/ppermute | solution.py:70
  87.4 29.5 %collective-permute-start.21 = (bf16[64,4608]{1,0:T(8,128)(2,1)S(1)}, bf16[64,4608]{1,0:T(8,128)(2,1)S(1)}, u32[]{:S(2)}, u32[]{:S(2)}) collective-permute-start(bf16[64,4608]{1,0:T(8,128)(2,1)S(1)} %get-tuple-element.150), channel_id=1, source_target_pairs={{0,8},{1,9},{2,10},{3,11},{4,5},{5,6},{6,7},{7,4},{8,0},{9,1},{10,... | collective-permute-start | bytes 1769480 | tf_op jit(solution)/shard_map/ppermute | solution.py:67
  88.9 27.9 %collective-permute-start.22 = (bf16[64,4608]{1,0:T(8,128)(2,1)S(1)}, bf16[64,4608]{1,0:T(8,128)(2,1)S(1)}, u32[]{:S(2)}, u32[]{:S(2)}) collective-permute-start(bf16[64,4608]{1,0:T(8,128)(2,1)S(1)} %get-tuple-element.151), channel_id=1, source_target_pairs={{0,16},{1,17},{2,18},{3,19},{4,6},{5,7},{6,4},{7,5},{8,24},{9,25},... | collective-permute-start | bytes 1769480 | tf_op jit(solution)/shard_map/ppermute | solution.py:67
  90.3 26.5 %collective-permute-start.23 = (bf16[64,4608]{1,0:T(8,128)(2,1)S(1)}, bf16[64,4608]{1,0:T(8,128)(2,1)S(1)}, u32[]{:S(2)}, u32[]{:S(2)}) collective-permute-start(bf16[64,4608]{1,0:T(8,128)(2,1)S(1)} %get-tuple-element.152), channel_id=1, source_target_pairs={{0,24},{1,25},{2,26},{3,27},{4,7},{5,4},{6,5},{7,6},{8,16},{9,17},... | collective-permute-start | bytes 1769480 | tf_op jit(solution)/shard_map/ppermute | solution.py:67
  117.7 2.8 %collective-permute-start.24 = (bf16[4,64,1664]{2,1,0:T(8,128)(2,1)S(1)}, bf16[4,64,1664]{2,1,0:T(8,128)(2,1)S(1)}, u32[]{:S(2)}, u32[]{:S(2)}) collective-permute-start(bf16[4,64,1664]{2,1,0:T(8,128)(2,1)S(1)} %get-tuple-element.165), channel_id=1, source_target_pairs={{0,4},{1,5},{2,6},{3,7},{4,0},{5,1},{6,2},{7,3},{8,12},{9,13},{10,... | collective-permute-start | bytes 2555912 | tf_op jit(solution)/shard_map/ppermute | solution.py:70
  120.8 8.2 %collective-permute-start.25 = (bf16[64,1664]{1,0:T(8,128)(2,1)S(1)}, bf16[64,1664]{1,0:T(8,128)(2,1)S(1)}, u32[]{:S(2)}, u32[]{:S(2)}) collective-permute-start(bf16[64,1664]{1,0:T(8,128)(2,1)S(1)} %get-tuple-element.167), channel_id=1, source_target_pairs={{0,8},{1,9},{2,10},{3,11},{4,12},{5,13},{6,14},{7,15},{8,0},{9,1},... | collective-permute-start | bytes 638984 | tf_op jit(solution)/shard_map/ppermute | solution.py:67
  122.4 14.3 %collective-permute-start.26 = (bf16[64,1664]{1,0:T(8,128)(2,1)S(1)}, bf16[64,1664]{1,0:T(8,128)(2,1)S(1)}, u32[]{:S(2)}, u32[]{:S(2)}) collective-permute-start(bf16[64,1664]{1,0:T(8,128)(2,1)S(1)} %get-tuple-element.168), channel_id=1, source_target_pairs={{0,16},{1,17},{2,18},{3,19},{4,20},{5,21},{6,22},{7,23},{8,24},{9,... | collective-permute-start | bytes 638984 | tf_op jit(solution)/shard_map/ppermute | solution.py:67
  123.6 13.0 %collective-permute-start.27 = (bf16[64,1664]{1,0:T(8,128)(2,1)S(1)}, bf16[64,1664]{1,0:T(8,128)(2,1)S(1)}, u32[]{:S(2)}, u32[]{:S(2)}) collective-permute-start(bf16[64,1664]{1,0:T(8,128)(2,1)S(1)} %get-tuple-element.169), channel_id=1, source_target_pairs={{0,24},{1,25},{2,26},{3,27},{4,28},{5,29},{6,30},{7,31},{8,16},{9,... | collective-permute-start | bytes 638984 | tf_op jit(solution)/shard_map/ppermute | solution.py:67
  124.4 14.5 %collective-permute-start.32 = (bf16[16,4608]{1,0:T(8,128)(2,1)S(1)}, bf16[16,4608]{1,0:T(8,128)(2,1)S(1)}, u32[]{:S(2)}, u32[]{:S(2)}) collective-permute-start(bf16[16,4608]{1,0:T(8,128)(2,1)S(1)} %get-tuple-element.175), channel_id=1, source_target_pairs={{0,2},{1,3},{2,0},{3,1},{4,20},{5,21},{6,22},{7,23},{8,10},{9,11},... | collective-permute-start | bytes 442376 | tf_op jit(solution)/shard_map/ppermute | solution.py:67
  125.7 15.4 %collective-permute-start.33 = (bf16[16,4608]{1,0:T(8,128)(2,1)S(1)}, bf16[16,4608]{1,0:T(8,128)(2,1)S(1)}, u32[]{:S(2)}, u32[]{:S(2)}) collective-permute-start(bf16[16,4608]{1,0:T(8,128)(2,1)S(1)} %get-tuple-element.176), channel_id=1, source_target_pairs={{0,3},{1,0},{2,1},{3,2},{4,28},{5,29},{6,30},{7,31},{8,11},{9,8},{... | collective-permute-start | bytes 442376 | tf_op jit(solution)/shard_map/ppermute | solution.py:67
  129.0 12.1 %collective-permute-start.31 = (bf16[16,4608]{1,0:T(8,128)(2,1)S(1)}, bf16[16,4608]{1,0:T(8,128)(2,1)S(1)}, u32[]{:S(2)}, u32[]{:S(2)}) collective-permute-start(bf16[16,4608]{1,0:T(8,128)(2,1)S(1)} %get-tuple-element.164), channel_id=1, source_target_pairs={{0,1},{1,2},{2,3},{3,0},{4,12},{5,13},{6,14},{7,15},{8,9},{9,10},{... | collective-permute-start | bytes 442376 | tf_op jit(solution)/shard_map/ppermute | solution.py:67
  136.8 6.0 %collective-permute-start.28 = (bf16[16,1664]{1,0:T(8,128)(2,1)S(1)}, bf16[16,1664]{1,0:T(8,128)(2,1)S(1)}, u32[]{:S(2)}, u32[]{:S(2)}) collective-permute-start(bf16[16,1664]{1,0:T(8,128)(2,1)S(1)} %get-tuple-element.171), channel_id=1, source_target_pairs={{0,1},{1,2},{2,3},{3,0},{4,5},{5,6},{6,7},{7,4},{8,9},{9,10},{10,1... | collective-permute-start | bytes 159752 | tf_op jit(solution)/shard_map/ppermute | solution.py:67
  137.1 5.6 %collective-permute-start.29 = (bf16[16,1664]{1,0:T(8,128)(2,1)S(1)}, bf16[16,1664]{1,0:T(8,128)(2,1)S(1)}, u32[]{:S(2)}, u32[]{:S(2)}) collective-permute-start(bf16[16,1664]{1,0:T(8,128)(2,1)S(1)} %get-tuple-element.172), channel_id=1, source_target_pairs={{0,2},{1,3},{2,0},{3,1},{4,6},{5,7},{6,4},{7,5},{8,10},{9,11},{10,... | collective-permute-start | bytes 159752 | tf_op jit(solution)/shard_map/ppermute | solution.py:67
  138.9 4.4 %collective-permute-start.30 = (bf16[16,1664]{1,0:T(8,128)(2,1)S(1)}, bf16[16,1664]{1,0:T(8,128)(2,1)S(1)}, u32[]{:S(2)}, u32[]{:S(2)}) collective-permute-start(bf16[16,1664]{1,0:T(8,128)(2,1)S(1)} %get-tuple-element.173), channel_id=1, source_target_pairs={{0,3},{1,0},{2,1},{3,2},{4,7},{5,4},{6,5},{7,6},{8,11},{9,8},{10,9... | collective-permute-start | bytes 159752 | tf_op jit(solution)/shard_map/ppermute | solution.py:67
  146.0 13.7 %all-to-all-start = ((f32[32,1,128]{2,1,0:T(1,128)}), f32[32,1,128]{2,1,0:T(1,128)S(1)}, u32[]{:S(2)}, u32[]{:S(2)}) async-start(f32[32,1,128]{2,1,0:T(1,128)} %copy-done.29), calls=%async_computation | async-start | bytes 32768 | tf_op jit(solution)/shard_map/all_to_all | solution.py:775
  (40 other events, 391.7 us)

commit v3 on v2

--- a/solution.py
+++ b/solution.py
@@ -859,6 +859,9 @@
     (send1,) = after([send1], low2[:1])
     own1, *low1 = chip_sum(plain, keep1, lay.to_core(send1))
     got1 = send_over(plain, low1, False)
+    (middle,) = after([middle], low1)
+    outputs, input_gradient = finish(begin, middle, active, contract_all, input_gradient, rows)
+    own1, *got1 = after([own1, *got1], [outputs])
     spans = [[(0, own, (0, depth))], [(0, own, (depth, depth + hidden))]]
     spans.append([(j * own, own, (depth + hidden + j * depth, depth + hidden + (j + 1) * depth)) for j in range(4)])
     momenta2, variances2, directions2, sums2 = moments(
@@ -872,8 +875,6 @@
         (moment_in, moment_norms), (square_in, square_norms),
     )
     sums = exchange(lay, sums1)
-    (middle,) = after([middle], [sums1])
-    outputs, input_gradient = finish(begin, middle, active, contract_all, input_gradient, rows)
     directions = (directions1[0], *directions2, directions1[1])
     updated, trust_table = update(sums, masters, directions)
     momenta = (momenta1[0], *momenta2, momenta1[1])

time: 167 us -> 156 us (0.934)
  local copies, waits for them, and re-layouts: 16.7 us -> 3.34 us
  blocking collectives: 0 us -> 11.8 us
  starting transfers between devices: 39.1 us -> 34.3 us
  waiting for transfers between devices: 24.2 us -> 19.7 us
    unnamed x77 -> x39, local copies, waits for them, and re-layouts: 16.6 us -> 3.23 us
    all_to_all x0 -> x1, blocking collectives: none -> 11.8 us  [exchange(): return lax.all_to_all(value, AXES, 0, 0)]
    all_to_all x1 -> x0, starting transfers between devices: 4.84 us -> none  [exchange(): return lax.all_to_all(value, AXES, 0, 0)]
    ppermute x24, waiting for transfers between devices: 15.7 us -> 11.3 us  [over(): return lax.ppermute(value, AXES, self.pairs(move))]
  transfers between devices with their start and end apart: 35 -> 34, of which waited for: 16 -> 16; matrix products, arithmetic and copies ran while one was open for 2% -> 2% of each run, Pallas kernels for 34% -> 36%
where the time goes in v3:
time: 156 us; the launch traced here: 155 us
  Pallas kernels  81 us (52%)
  starting transfers between devices  34.3 us (22%)
  waiting for transfers between devices  19.7 us (13%)
  blocking collectives  11.8 us (8%)
  other arithmetic  4.18 us (3%)
  local copies, waits for them, and re-layouts  3.34 us (2%)
    ppermute x24, starting transfers between devices, over(): return lax.ppermute(value, AXES, self.pairs(move))  30.9 us
    pallas_call x1, Pallas kernels, attend(): pl.pallas_call(partial(attend_kernel, lay, len(pieces)), out_shape=(wide,...  21.1 us
    pallas_call x1, Pallas kernels, feed(): pl.pallas_call(partial(feed_kernel, lay, len(pieces), len(deep_pieces)),...  20.6 us
    pallas_call x1, Pallas kernels, attend_back(): pl.pallas_call(attend_back_kernel, out_shape=jax.ShapeDtypeStruct((rows,...  18.8 us
    all_to_all x1, blocking collectives, exchange(): return lax.all_to_all(value, AXES, 0, 0)  11.8 us
    ppermute x24, waiting for transfers between devices, over(): return lax.ppermute(value, AXES, self.pairs(move))  11.3 us
    ppermute x10, waiting for transfers between devices, to_core(): return lax.ppermute(value, AXES, self.pairs(lambda p, c, z: (p, 1 - c, z)))  8.44 us
    pallas_call x1, Pallas kernels, finish(): pl.pallas_call(finish_kernel, out_shape=[jax.ShapeDtypeStruct((rows, widt...  4.34 us
  transfers between devices with their start and end apart: 34, of which 16 were waited for; matrix products, arithmetic and copies ran while one was open for 2% of the time, Pallas kernels for 36%

profile of v3, /device:TPU:0, one launch (start us, length us, event | category | flops | bytes accessed | tf_op | source)
XLA Modules:
  0.0 155.4 jit_solution(11956605692924562720)
XLA Ops:
  2.3 5.1 %collective-permute-start.2 = (bf16[16,1664]{1,0:T(8,128)(2,1)S(1)}, bf16[16,1664]{1,0:T(8,128)(2,1)S(1)}, u32[]{:S(2)}, u32[]{:S(2)}) collective-permute-start(bf16[16,1664]{1,0:T(8,128)(2,1)S(1)} %fusion.1.refs_0_), channel_id=1, source_target_pairs={{0,3},{1,0},{2,1},{3,2},{4,7},{5,4},{6,5},{7,6},{8,11},{9,8},{10,9... | collective-permute-start | bytes 159752 | tf_op jit(solution)/shard_map/ppermute | solution.py:67
  11.1 1.4 collective-permute-done.1.refs_2_
  13.4 1.5 collective-permute-start.12
  15.0 2.5 %collective-permute-start.5 = (bf16[64,1664]{1,0:T(8,128)(2,1)S(1)}, bf16[64,1664]{1,0:T(8,128)(2,1)S(1)}, u32[]{:S(2)}, u32[]{:S(2)}) collective-permute-start(bf16[64,1664]{1,0:T(8,128)(2,1)S(1)} %column.2.refs_0_), channel_id=1, source_target_pairs={{0,24},{1,25},{2,26},{3,27},{4,28},{5,29},{6,30},{7,31},{8,16},{9,... | collective-permute-start | bytes 638984 | tf_op jit(solution)/shard_map/ppermute | solution.py:67
  18.8 1.7 %collective-permute-start.10 = (bf16[16,4608]{1,0:T(8,128)(2,1)S(1)}, bf16[16,4608]{1,0:T(8,128)(2,1)S(1)}, u32[]{:S(2)}, u32[]{:S(2)}) collective-permute-start(bf16[16,4608]{1,0:T(8,128)(2,1)S(1)} %slice_dynamic-update-slice_fusion.refs_0_), channel_id=1, source_target_pairs={{0,1},{1,2},{2,3},{3,0},{4,12},{5,13},{6,14},{7,15},{8,9},{9,10},{... | collective-permute-start | bytes 442376 | tf_op jit(solution)/shard_map/ppermute | solution.py:67
  20.4 1.2 copy-done.2
  21.7 1.2 copy-done.3
  23.6 1.1 arrange.1
  24.7 3.0 %collective-permute-done.11.refs_2_ = bf16[16,4608]{1,0:T(8,128)(2,1)S(1)} collective-permute-done((bf16[16,4608]{1,0:T(8,128)(2,1)S(1)}, bf16[16,4608]{1,0:T(8,128)(2,1)S(1)}, u32[]{:S(2)}, u32[]{:S(2)}) %collective-permute-start.11) | collective-permute-done | bytes 147488 | tf_op jit(solution)/shard_map/ppermute | solution.py:67
  28.0 2.5 %collective-permute-start.15 = (bf16[64,4608]{1,0:T(8,128)(2,1)S(1)}, bf16[64,4608]{1,0:T(8,128)(2,1)S(1)}, u32[]{:S(2)}, u32[]{:S(2)}) collective-permute-start(bf16[64,4608]{1,0:T(8,128)(2,1)S(1)} %column.3.refs_0_), channel_id=1, source_target_pairs={{0,24},{1,25},{2,26},{3,27},{4,7},{5,4},{6,5},{7,6},{8,16},{9,17},... | collective-permute-start | bytes 1769480 | tf_op jit(solution)/shard_map/ppermute | solution.py:67
  34.7 21.1 %attend.1 = (bf16[1056,1024]{1,0:T(8,128)(2,1)S(1)}, bf16[1056,1024]{1,0:T(8,128)(2,1)S(1)}, bf16[1056,1024]{1,0:T(8,128)(2,1)S(1)}, bf16[1056,512]{1,0:T(8,128)(2,1)S(1)}, f32[8,512]{1,0:T(8,128)S(1)}) custom-call(bf16[1056,512]{1,0:T(8,128)(2,1)S(1)} %get-tuple-element.128.x, s32[1056,128]{1,0:T(8,128)S(1)} %get-tuple-element.129.labels, ...), custom_call_target="tpu_custom_call" | custom-call | tf_op jit(solution)/shard_map/attend/pallas_call | solution.py:301
  57.0 1.1 collective-permute-done.17.refs_5_
  59.8 20.6 %feed.1 = (f32[1056,512]{1,0:T(8,128)S(1)}, f32[1056,512]{1,0:T(8,128)S(1)}, bf16[1056,512]{1,0:T(8,128)(2,1)S(1)}, bf16[1056,2048]{1,0:T(8,128)(2,1)S(1)}, bf16...) custom-call(bf16[1056,512]{1,0:T(8,128)(2,1)S(1)} %get-tuple-element, ...), custom_call_target="tpu_custom_call" | custom-call | tf_op jit(solution)/shard_map/feed/pallas_call | solution.py:456
  80.8 2.7 %mixed_back.1.dox = bf16[1056,1024]{1,0:T(8,128)(2,1)S(1)} custom-call(bf16[1056,512]{1,0:T(8,128)(2,1)S(1)} %get-tuple-element.148.middle_low, bf16[1056,512]{1,0:T(8,128)(2,1)S(1)} %get-tuple-element.138.mixed, bf16[512,512]{1,0:T(8,128)(2,1)S(1)} %get-tuple-element.149.out_weight), custom_call_target="tpu_custom_call" | custom-call | tf_op jit(solution)/shard_map/mixed_back/pallas_call | solution.py:502
  83.5 1.5 collective-permute-done.20.got
  84.9 1.1 chip_sum.2
  86.1 1.5 collective-permute-start.21
  87.6 1.4 collective-permute-start.22
  89.6 18.8 %attend_back.1.packed = bf16[1056,1536]{1,0:T(8,128)(2,1)S(1)} custom-call(bf16[1056,1024]{1,0:T(8,128)(2,1)S(1)} %get-tuple-element.145.qx, bf16[1056,1024]{1,0:T(8,128)(2,1)S(1)} %get-tuple-element.146.kx, bf16[1056,1024]{1,0:T(8,128)(2,1)S(1)} %get-tuple-element.147.vx, bf16[1056,1024]{1,0:T(8,128)(2,1)S(1)} %mixed_back.1.dox), custom_call_target="tpu_custom_call" | custom-call | tf_op jit(solution)/shard_map/attend_back/pallas_call | solution.py:355
  108.5 3.2 %input_back.1 = (bf16[1056,512]{1,0:T(8,128)(2,1)S(1)}, f32[8,512]{1,0:T(8,128)S(1)}) custom-call(bf16[1056,512]{1,0:T(8,128)(2,1)S(1)} %get-tuple-element.128.x, bf16[1056,1536]{1,0:T(8,128)(2,1)S(1)} %attend_back.1.packed, f32[8,512]{1,0:T(8,128)S(1)} %get-tuple-element.140.gains, f32[1056,512]{1,0:T(8,128)S(1)} %get-tuple-element.158.middle_grad, ...), custom_call_target="tpu_custom_call" | custom-call | tf_op jit(solution)/shard_map/input_back/pallas_call | solution.py:574
  111.6 3.9 %project_back.1 = (bf16[4,64,1664]{2,1,0:T(8,128)(2,1)S(1)}, bf16[4,64,1664]{2,1,0:T(8,128)(2,1)S(1)}) custom-call(bf16[1056,512]{1,0:T(8,128)(2,1)S(1)} %get-tuple-element.128.x, bf16[1056,1536]{1,0:T(8,128)(2,1)S(1)} %attend_back.1.packed, f32[8,512]{1,0:T(8,128)S(1)} %get-tuple-element.140.gains, f32[8,512]{1,0:T(8,128)S(1)} %get-tuple-element.159.first_norms, ...), custom_call_target="tpu_custom_call" | custom-call | tf_op jit(solution)/shard_map/project_back/pallas_call | solution.py:540
  117.2 2.0 %collective-permute-done.24.got = bf16[4,64,1664]{2,1,0:T(8,128)(2,1)S(1)} collective-permute-done((bf16[4,64,1664]{2,1,0:T(8,128)(2,1)S(1)}, bf16[4,64,1664]{2,1,0:T(8,128)(2,1)S(1)}, u32[]{:S(2)}, u32[]{:S(2)}) %collective-permute-start.24) | collective-permute-done | bytes 852000 | tf_op jit(solution)/shard_map/ppermute | solution.py:70
  119.4 1.5 collective-permute-start.25
  120.9 1.2 collective-permute-start.26
  122.9 1.3 collective-permute-start.32
  124.2 1.3 collective-permute-start.33
  125.6 2.0 %collective-permute-done.25.refs_0_ = bf16[64,1664]{1,0:T(8,128)(2,1)S(1)} collective-permute-done((bf16[64,1664]{1,0:T(8,128)(2,1)S(1)}, bf16[64,1664]{1,0:T(8,128)(2,1)S(1)}, u32[]{:S(2)}, u32[]{:S(2)}) %collective-permute-start.25) | collective-permute-done | bytes 213024 | tf_op jit(solution)/shard_map/ppermute | solution.py:67
  127.9 4.3 %finish.1 = (bf16[1044,512]{1,0:T(8,128)(2,1)}, bf16[1044,512]{1,0:T(8,128)(2,1)}) custom-call(f32[8,128]{1,0:T(8,128)S(1)} %get-tuple-element.117.begin, f32[1056,512]{1,0:T(8,128)S(1)} %get-tuple-element.173.middle, bf16[1056,2048]{1,0:T(8,128)(2,1)S(1)} %get-tuple-element.174.active, bf16[2048,512]{1,0:T(8,128)(2,1)S(1)} %get-tuple-element.175.contract, ...), custom_call_target="tpu_custom_call" | custom-call | tf_op jit(solution)/shard_map/finish/pallas_call | solution.py:219
  132.2 2.9 %collective-permute-done.26.refs_1_ = bf16[64,1664]{1,0:T(8,128)(2,1)S(1)} collective-permute-done((bf16[64,1664]{1,0:T(8,128)(2,1)S(1)}, bf16[64,1664]{1,0:T(8,128)(2,1)S(1)}, u32[]{:S(2)}, u32[]{:S(2)}) %collective-permute-start.26) | collective-permute-done | bytes 213024 | tf_op jit(solution)/shard_map/ppermute | solution.py:67
  135.7 1.8 %collective-permute-start.29 = (bf16[16,1664]{1,0:T(8,128)(2,1)S(1)}, bf16[16,1664]{1,0:T(8,128)(2,1)S(1)}, u32[]{:S(2)}, u32[]{:S(2)}) collective-permute-start(bf16[16,1664]{1,0:T(8,128)(2,1)S(1)} %get-tuple-element.186), channel_id=1, source_target_pairs={{0,2},{1,3},{2,0},{3,1},{4,6},{5,7},{6,4},{7,5},{8,10},{9,11},{10,... | collective-permute-start | bytes 159752 | tf_op jit(solution)/shard_map/ppermute | solution.py:67
  137.5 2.1 %collective-permute-start.30 = (bf16[16,1664]{1,0:T(8,128)(2,1)S(1)}, bf16[16,1664]{1,0:T(8,128)(2,1)S(1)}, u32[]{:S(2)}, u32[]{:S(2)}) collective-permute-start(bf16[16,1664]{1,0:T(8,128)(2,1)S(1)} %get-tuple-element.187), channel_id=1, source_target_pairs={{0,3},{1,0},{2,1},{3,2},{4,7},{5,4},{6,5},{7,6},{8,11},{9,8},{10,9... | collective-permute-start | bytes 159752 | tf_op jit(solution)/shard_map/ppermute | solution.py:67
  142.7 11.8 %all_to_all.5.sums = f32[32,1,128]{2,1,0:T(1,128)S(1)} all-to-all(f32[32,1,128]{2,1,0:T(1,128)S(1)} %get-tuple-element.192), channel_id=1, replica_groups=mesh['dp'=8,'rep'=4] {'dp','rep'}, dimensions={0} | all-to-all | bytes 32768 | tf_op jit(solution)/shard_map/all_to_all | solution.py:775
  (101 shorter events, 23.8 us)
Async XLA Ops:
  2.3 8.8 %collective-permute-start.2 = (bf16[16,1664]{1,0:T(8,128)(2,1)S(1)}, bf16[16,1664]{1,0:T(8,128)(2,1)S(1)}, u32[]{:S(2)}, u32[]{:S(2)}) collective-permute-start(bf16[16,1664]{1,0:T(8,128)(2,1)S(1)} %fusion.1.refs_0_), channel_id=1, source_target_pairs={{0,3},{1,0},{2,1},{3,2},{4,7},{5,4},{6,5},{7,6},{8,11},{9,8},{10,9... | collective-permute-start | bytes 159752 | tf_op jit(solution)/shard_map/ppermute | solution.py:67
  7.5 5.1 %collective-permute-start.1 = (bf16[16,1664]{1,0:T(8,128)(2,1)S(1)}, bf16[16,1664]{1,0:T(8,128)(2,1)S(1)}, u32[]{:S(2)}, u32[]{:S(2)}) collective-permute-start(bf16[16,1664]{1,0:T(8,128)(2,1)S(1)} %fusion.1.refs_0_), channel_id=1, source_target_pairs={{0,2},{1,3},{2,0},{3,1},{4,6},{5,7},{6,4},{7,5},{8,10},{9,11},{10,... | collective-permute-start | bytes 159752 | tf_op jit(solution)/shard_map/ppermute | solution.py:67
  7.5 5.9 %collective-permute-start = (bf16[16,1664]{1,0:T(8,128)(2,1)S(1)}, bf16[16,1664]{1,0:T(8,128)(2,1)S(1)}, u32[]{:S(2)}, u32[]{:S(2)}) collective-permute-start(bf16[16,1664]{1,0:T(8,128)(2,1)S(1)} %fusion.1.refs_0_), channel_id=1, source_target_pairs={{0,1},{1,2},{2,3},{3,0},{4,5},{5,6},{6,7},{7,4},{8,9},{9,10},{10,1... | collective-permute-start | bytes 159752 | tf_op jit(solution)/shard_map/ppermute | solution.py:67
  13.4 5.4 %collective-permute-start.12 = (bf16[16,4608]{1,0:T(8,128)(2,1)S(1)}, bf16[16,4608]{1,0:T(8,128)(2,1)S(1)}, u32[]{:S(2)}, u32[]{:S(2)}) collective-permute-start(bf16[16,4608]{1,0:T(8,128)(2,1)S(1)} %slice_dynamic-update-slice_fusion.refs_0_), channel_id=1, source_target_pairs={{0,3},{1,0},{2,1},{3,2},{4,28},{5,29},{6,30},{7,31},{8,11},{9,8},{... | collective-permute-start | bytes 442376 | tf_op jit(solution)/shard_map/ppermute | solution.py:67
  15.0 12.7 %collective-permute-start.5 = (bf16[64,1664]{1,0:T(8,128)(2,1)S(1)}, bf16[64,1664]{1,0:T(8,128)(2,1)S(1)}, u32[]{:S(2)}, u32[]{:S(2)}) collective-permute-start(bf16[64,1664]{1,0:T(8,128)(2,1)S(1)} %column.2.refs_0_), channel_id=1, source_target_pairs={{0,24},{1,25},{2,26},{3,27},{4,28},{5,29},{6,30},{7,31},{8,16},{9,... | collective-permute-start | bytes 638984 | tf_op jit(solution)/shard_map/ppermute | solution.py:67
  17.5 10.2 %collective-permute-start.4 = (bf16[64,1664]{1,0:T(8,128)(2,1)S(1)}, bf16[64,1664]{1,0:T(8,128)(2,1)S(1)}, u32[]{:S(2)}, u32[]{:S(2)}) collective-permute-start(bf16[64,1664]{1,0:T(8,128)(2,1)S(1)} %column.2.refs_0_), channel_id=1, source_target_pairs={{0,16},{1,17},{2,18},{3,19},{4,20},{5,21},{6,22},{7,23},{8,24},{9,... | collective-permute-start | bytes 638984 | tf_op jit(solution)/shard_map/ppermute | solution.py:67
  18.0 9.7 %collective-permute-start.3 = (bf16[64,1664]{1,0:T(8,128)(2,1)S(1)}, bf16[64,1664]{1,0:T(8,128)(2,1)S(1)}, u32[]{:S(2)}, u32[]{:S(2)}) collective-permute-start(bf16[64,1664]{1,0:T(8,128)(2,1)S(1)} %column.2.refs_0_), channel_id=1, source_target_pairs={{0,8},{1,9},{2,10},{3,11},{4,12},{5,13},{6,14},{7,15},{8,0},{9,1},... | collective-permute-start | bytes 638984 | tf_op jit(solution)/shard_map/ppermute | solution.py:67
  18.6 9.1 %collective-permute-start.11 = (bf16[16,4608]{1,0:T(8,128)(2,1)S(1)}, bf16[16,4608]{1,0:T(8,128)(2,1)S(1)}, u32[]{:S(2)}, u32[]{:S(2)}) collective-permute-start(bf16[16,4608]{1,0:T(8,128)(2,1)S(1)} %slice_dynamic-update-slice_fusion.refs_0_), channel_id=1, source_target_pairs={{0,2},{1,3},{2,0},{3,1},{4,20},{5,21},{6,22},{7,23},{8,10},{9,11},... | collective-permute-start | bytes 442376 | tf_op jit(solution)/shard_map/ppermute | solution.py:67
  18.8 8.9 %collective-permute-start.10 = (bf16[16,4608]{1,0:T(8,128)(2,1)S(1)}, bf16[16,4608]{1,0:T(8,128)(2,1)S(1)}, u32[]{:S(2)}, u32[]{:S(2)}) collective-permute-start(bf16[16,4608]{1,0:T(8,128)(2,1)S(1)} %slice_dynamic-update-slice_fusion.refs_0_), channel_id=1, source_target_pairs={{0,1},{1,2},{2,3},{3,0},{4,12},{5,13},{6,14},{7,15},{8,9},{9,10},{... | collective-permute-start | bytes 442376 | tf_op jit(solution)/shard_map/ppermute | solution.py:67
  28.0 27.9 %collective-permute-start.15 = (bf16[64,4608]{1,0:T(8,128)(2,1)S(1)}, bf16[64,4608]{1,0:T(8,128)(2,1)S(1)}, u32[]{:S(2)}, u32[]{:S(2)}) collective-permute-start(bf16[64,4608]{1,0:T(8,128)(2,1)S(1)} %column.3.refs_0_), channel_id=1, source_target_pairs={{0,24},{1,25},{2,26},{3,27},{4,7},{5,4},{6,5},{7,6},{8,16},{9,17},... | collective-permute-start | bytes 1769480 | tf_op jit(solution)/shard_map/ppermute | solution.py:67
  30.5 25.4 %collective-permute-start.14 = (bf16[64,4608]{1,0:T(8,128)(2,1)S(1)}, bf16[64,4608]{1,0:T(8,128)(2,1)S(1)}, u32[]{:S(2)}, u32[]{:S(2)}) collective-permute-start(bf16[64,4608]{1,0:T(8,128)(2,1)S(1)} %column.3.refs_0_), channel_id=1, source_target_pairs={{0,16},{1,17},{2,18},{3,19},{4,6},{5,7},{6,4},{7,5},{8,24},{9,25},... | collective-permute-start | bytes 1769480 | tf_op jit(solution)/shard_map/ppermute | solution.py:67
  31.0 24.9 %collective-permute-start.13 = (bf16[64,4608]{1,0:T(8,128)(2,1)S(1)}, bf16[64,4608]{1,0:T(8,128)(2,1)S(1)}, u32[]{:S(2)}, u32[]{:S(2)}) collective-permute-start(bf16[64,4608]{1,0:T(8,128)(2,1)S(1)} %column.3.refs_0_), channel_id=1, source_target_pairs={{0,8},{1,9},{2,10},{3,11},{4,5},{5,6},{6,7},{7,4},{8,0},{9,1},{10,... | collective-permute-start | bytes 1769480 | tf_op jit(solution)/shard_map/ppermute | solution.py:67
  31.5 1.5 collective-permute-start.6
  31.7 1.6 %collective-permute-start.9 = (bf16[64,1664]{1,0:T(8,128)(2,1)S(1)}, bf16[64,1664]{1,0:T(8,128)(2,1)S(1)}, u32[]{:S(2)}, u32[]{:S(2)}) collective-permute-start(bf16[64,1664]{1,0:T(8,128)(2,1)S(1)} %collective-permute-done.5.refs_3_), channel_id=1, source_target_pairs={{0,4},{1,5},{2,6},{3,7},{4,0},{5,1},{6,2},{7,3},{8,12},{9,13},{10,... | collective-permute-start | bytes 638984 | tf_op jit(solution)/shard_map/ppermute | solution.py:70
  34.4 22.5 %collective-permute-start.16 = (bf16[64,4608]{1,0:T(8,128)(2,1)S(1)}, bf16[64,4608]{1,0:T(8,128)(2,1)S(1)}, u32[]{:S(2)}, u32[]{:S(2)}) collective-permute-start(bf16[64,4608]{1,0:T(8,128)(2,1)S(1)} %column.3.refs_0_), channel_id=1, source_target_pairs={{0,4},{1,5},{2,6},{3,7},{4,0},{5,1},{6,2},{7,3},{8,12},{9,13},{10,... | collective-permute-start | bytes 1769480 | tf_op jit(solution)/shard_map/ppermute | solution.py:70
  55.9 2.2 %collective-permute-start.17 = (bf16[64,4608]{1,0:T(8,128)(2,1)S(1)}, bf16[64,4608]{1,0:T(8,128)(2,1)S(1)}, u32[]{:S(2)}, u32[]{:S(2)}) collective-permute-start(bf16[64,4608]{1,0:T(8,128)(2,1)S(1)} %collective-permute-done.13.refs_1_), channel_id=1, source_target_pairs={{0,4},{1,5},{2,6},{3,7},{4,0},{5,1},{6,2},{7,3},{8,12},{9,13},{10,... | collective-permute-start | bytes 1769480 | tf_op jit(solution)/shard_map/ppermute | solution.py:70
  56.5 2.5 %collective-permute-start.18 = (bf16[64,4608]{1,0:T(8,128)(2,1)S(1)}, bf16[64,4608]{1,0:T(8,128)(2,1)S(1)}, u32[]{:S(2)}, u32[]{:S(2)}) collective-permute-start(bf16[64,4608]{1,0:T(8,128)(2,1)S(1)} %collective-permute-done.14.refs_2_), channel_id=1, source_target_pairs={{0,4},{1,5},{2,6},{3,7},{4,0},{5,1},{6,2},{7,3},{8,12},{9,13},{10,... | collective-permute-start | bytes 1769480 | tf_op jit(solution)/shard_map/ppermute | solution.py:70
  56.5 3.3 %collective-permute-start.19 = (bf16[64,4608]{1,0:T(8,128)(2,1)S(1)}, bf16[64,4608]{1,0:T(8,128)(2,1)S(1)}, u32[]{:S(2)}, u32[]{:S(2)}) collective-permute-start(bf16[64,4608]{1,0:T(8,128)(2,1)S(1)} %collective-permute-done.15.refs_3_), channel_id=1, source_target_pairs={{0,4},{1,5},{2,6},{3,7},{4,0},{5,1},{6,2},{7,3},{8,12},{9,13},{10,... | collective-permute-start | bytes 1769480 | tf_op jit(solution)/shard_map/ppermute | solution.py:70
  80.3 4.6 %collective-permute-start.20 = (bf16[4,64,4608]{2,1,0:T(8,128)(2,1)S(1)}, bf16[4,64,4608]{2,1,0:T(8,128)(2,1)S(1)}, u32[]{:S(2)}, u32[]{:S(2)}) collective-permute-start(bf16[4,64,4608]{2,1,0:T(8,128)(2,1)S(1)} %get-tuple-element.151), channel_id=1, source_target_pairs={{0,4},{1,5},{2,6},{3,7},{4,0},{5,1},{6,2},{7,3},{8,12},{9,13},{10,... | collective-permute-start | bytes 7077896 | tf_op jit(solution)/shard_map/ppermute | solution.py:70
  86.1 29.5 %collective-permute-start.21 = (bf16[64,4608]{1,0:T(8,128)(2,1)S(1)}, bf16[64,4608]{1,0:T(8,128)(2,1)S(1)}, u32[]{:S(2)}, u32[]{:S(2)}) collective-permute-start(bf16[64,4608]{1,0:T(8,128)(2,1)S(1)} %get-tuple-element.154), channel_id=1, source_target_pairs={{0,8},{1,9},{2,10},{3,11},{4,5},{5,6},{6,7},{7,4},{8,0},{9,1},{10,... | collective-permute-start | bytes 1769480 | tf_op jit(solution)/shard_map/ppermute | solution.py:67
  87.6 27.9 %collective-permute-start.22 = (bf16[64,4608]{1,0:T(8,128)(2,1)S(1)}, bf16[64,4608]{1,0:T(8,128)(2,1)S(1)}, u32[]{:S(2)}, u32[]{:S(2)}) collective-permute-start(bf16[64,4608]{1,0:T(8,128)(2,1)S(1)} %get-tuple-element.155), channel_id=1, source_target_pairs={{0,16},{1,17},{2,18},{3,19},{4,6},{5,7},{6,4},{7,5},{8,24},{9,25},... | collective-permute-start | bytes 1769480 | tf_op jit(solution)/shard_map/ppermute | solution.py:67
  89.1 26.5 %collective-permute-start.23 = (bf16[64,4608]{1,0:T(8,128)(2,1)S(1)}, bf16[64,4608]{1,0:T(8,128)(2,1)S(1)}, u32[]{:S(2)}, u32[]{:S(2)}) collective-permute-start(bf16[64,4608]{1,0:T(8,128)(2,1)S(1)} %get-tuple-element.156), channel_id=1, source_target_pairs={{0,24},{1,25},{2,26},{3,27},{4,7},{5,4},{6,5},{7,6},{8,16},{9,17},... | collective-permute-start | bytes 1769480 | tf_op jit(solution)/shard_map/ppermute | solution.py:67
  116.3 2.8 %collective-permute-start.24 = (bf16[4,64,1664]{2,1,0:T(8,128)(2,1)S(1)}, bf16[4,64,1664]{2,1,0:T(8,128)(2,1)S(1)}, u32[]{:S(2)}, u32[]{:S(2)}) collective-permute-start(bf16[4,64,1664]{2,1,0:T(8,128)(2,1)S(1)} %get-tuple-element.169), channel_id=1, source_target_pairs={{0,4},{1,5},{2,6},{3,7},{4,0},{5,1},{6,2},{7,3},{8,12},{9,13},{10,... | collective-permute-start | bytes 2555912 | tf_op jit(solution)/shard_map/ppermute | solution.py:70
  119.4 8.2 %collective-permute-start.25 = (bf16[64,1664]{1,0:T(8,128)(2,1)S(1)}, bf16[64,1664]{1,0:T(8,128)(2,1)S(1)}, u32[]{:S(2)}, u32[]{:S(2)}) collective-permute-start(bf16[64,1664]{1,0:T(8,128)(2,1)S(1)} %get-tuple-element.170), channel_id=1, source_target_pairs={{0,8},{1,9},{2,10},{3,11},{4,12},{5,13},{6,14},{7,15},{8,0},{9,1},... | collective-permute-start | bytes 638984 | tf_op jit(solution)/shard_map/ppermute | solution.py:67
  120.9 14.3 %collective-permute-start.26 = (bf16[64,1664]{1,0:T(8,128)(2,1)S(1)}, bf16[64,1664]{1,0:T(8,128)(2,1)S(1)}, u32[]{:S(2)}, u32[]{:S(2)}) collective-permute-start(bf16[64,1664]{1,0:T(8,128)(2,1)S(1)} %get-tuple-element.171), channel_id=1, source_target_pairs={{0,16},{1,17},{2,18},{3,19},{4,20},{5,21},{6,22},{7,23},{8,24},{9,... | collective-permute-start | bytes 638984 | tf_op jit(solution)/shard_map/ppermute | solution.py:67
  122.1 13.0 %collective-permute-start.27 = (bf16[64,1664]{1,0:T(8,128)(2,1)S(1)}, bf16[64,1664]{1,0:T(8,128)(2,1)S(1)}, u32[]{:S(2)}, u32[]{:S(2)}) collective-permute-start(bf16[64,1664]{1,0:T(8,128)(2,1)S(1)} %get-tuple-element.172), channel_id=1, source_target_pairs={{0,24},{1,25},{2,26},{3,27},{4,28},{5,29},{6,30},{7,31},{8,16},{9,... | collective-permute-start | bytes 638984 | tf_op jit(solution)/shard_map/ppermute | solution.py:67
  122.9 14.5 %collective-permute-start.32 = (bf16[16,4608]{1,0:T(8,128)(2,1)S(1)}, bf16[16,4608]{1,0:T(8,128)(2,1)S(1)}, u32[]{:S(2)}, u32[]{:S(2)}) collective-permute-start(bf16[16,4608]{1,0:T(8,128)(2,1)S(1)} %get-tuple-element.189), channel_id=1, source_target_pairs={{0,2},{1,3},{2,0},{3,1},{4,20},{5,21},{6,22},{7,23},{8,10},{9,11},... | collective-permute-start | bytes 442376 | tf_op jit(solution)/shard_map/ppermute | solution.py:67
  124.2 15.4 %collective-permute-start.33 = (bf16[16,4608]{1,0:T(8,128)(2,1)S(1)}, bf16[16,4608]{1,0:T(8,128)(2,1)S(1)}, u32[]{:S(2)}, u32[]{:S(2)}) collective-permute-start(bf16[16,4608]{1,0:T(8,128)(2,1)S(1)} %get-tuple-element.190), channel_id=1, source_target_pairs={{0,3},{1,0},{2,1},{3,2},{4,28},{5,29},{6,30},{7,31},{8,11},{9,8},{... | collective-permute-start | bytes 442376 | tf_op jit(solution)/shard_map/ppermute | solution.py:67
  127.5 12.1 %collective-permute-start.31 = (bf16[16,4608]{1,0:T(8,128)(2,1)S(1)}, bf16[16,4608]{1,0:T(8,128)(2,1)S(1)}, u32[]{:S(2)}, u32[]{:S(2)}) collective-permute-start(bf16[16,4608]{1,0:T(8,128)(2,1)S(1)} %get-tuple-element.168), channel_id=1, source_target_pairs={{0,1},{1,2},{2,3},{3,0},{4,12},{5,13},{6,14},{7,15},{8,9},{9,10},{... | collective-permute-start | bytes 442376 | tf_op jit(solution)/shard_map/ppermute | solution.py:67
  135.3 6.0 %collective-permute-start.28 = (bf16[16,1664]{1,0:T(8,128)(2,1)S(1)}, bf16[16,1664]{1,0:T(8,128)(2,1)S(1)}, u32[]{:S(2)}, u32[]{:S(2)}) collective-permute-start(bf16[16,1664]{1,0:T(8,128)(2,1)S(1)} %get-tuple-element.185), channel_id=1, source_target_pairs={{0,1},{1,2},{2,3},{3,0},{4,5},{5,6},{6,7},{7,4},{8,9},{9,10},{10,1... | collective-permute-start | bytes 159752 | tf_op jit(solution)/shard_map/ppermute | solution.py:67
  135.7 5.6 %collective-permute-start.29 = (bf16[16,1664]{1,0:T(8,128)(2,1)S(1)}, bf16[16,1664]{1,0:T(8,128)(2,1)S(1)}, u32[]{:S(2)}, u32[]{:S(2)}) collective-permute-start(bf16[16,1664]{1,0:T(8,128)(2,1)S(1)} %get-tuple-element.186), channel_id=1, source_target_pairs={{0,2},{1,3},{2,0},{3,1},{4,6},{5,7},{6,4},{7,5},{8,10},{9,11},{10,... | collective-permute-start | bytes 159752 | tf_op jit(solution)/shard_map/ppermute | solution.py:67
  137.5 4.4 %collective-permute-start.30 = (bf16[16,1664]{1,0:T(8,128)(2,1)S(1)}, bf16[16,1664]{1,0:T(8,128)(2,1)S(1)}, u32[]{:S(2)}, u32[]{:S(2)}) collective-permute-start(bf16[16,1664]{1,0:T(8,128)(2,1)S(1)} %get-tuple-element.187), channel_id=1, source_target_pairs={{0,3},{1,0},{2,1},{3,2},{4,7},{5,4},{6,5},{7,6},{8,11},{9,8},{10,9... | collective-permute-start | bytes 159752 | tf_op jit(solution)/shard_map/ppermute | solution.py:67
  (20 other events, 170.4 us)

commit v4 on v3

--- a/solution.py
+++ b/solution.py
@@ -25,6 +25,8 @@
 THIN = 32
 CHUNK = 352
 DEEP_CHUNK = 528
+GELU_ONE = 0.7978845608028654
+GELU_CUBE = 0.044715 * GELU_ONE
 VMEM = pltpu.MemorySpace.VMEM
 AXES = ("dp", "rep")
 
@@ -401,10 +403,9 @@
             part = slice(start, start + 512)
             up = dot(low, wide[:, width + start : width + start + 512], 1, 0)
             square = up * up
-            bend = jnp.tanh(0.7978845608028654 * up * (1.0 + 0.044715 * square))
-            half = 0.5 * (1.0 + bend)
+            half = 0.5 + 0.5 * jnp.tanh(up * (GELU_ONE + GELU_CUBE * square))
             active[span, part] = (up * half).astype(jnp.bfloat16)
-            slope = half + 0.5 * up * (1.0 - bend * bend) * (0.7978845608028654 * (1.0 + 3 * 0.044715 * square))
+            slope = half * (1.0 + (1.0 - half) * (up * (2.0 * GELU_ONE + 6.0 * GELU_CUBE * square)))
             hidden_grad[span, part] = (dot(dy[span], contract[part], 1, 1) * slope).astype(jnp.bfloat16)
         back = dot(hidden_grad[span], wide[:, width:], 1, 1)
         gain_sum = gain_sum + jnp.sum(back * normed, axis=0, keepdims=True)
@@ -580,6 +581,30 @@
         compiler_params=params(10),
         name="input_back",
     )(x, packed, gains, middle_grad, *pieces)
+
+
+def pack_kernel(weight, norms, out):
+    rows, width = weight.shape
+    out[:, :width] = weight[...].astype(out.dtype)
+    same = lax.broadcasted_iota(jnp.int32, (rows, rows), 0) == lax.broadcasted_iota(jnp.int32, (rows, rows), 1)
+    lane = lax.broadcasted_iota(jnp.int32, (rows, LANES), 1)
+    tile = jnp.zeros((rows, LANES), jnp.float32)
+    for j in range(norms.shape[0]):
+        column = jnp.sum(jnp.where(same, norms[j : j + 1, :], 0.0), axis=1, keepdims=True)
+        tile = jnp.where(lane == j, column, tile)
+    out[:, width:] = tile.astype(out.dtype)
+
+
+def pack(weight, norms):
+    rows, width = weight.shape
+    return pl.pallas_call(
+        pack_kernel,
+        out_shape=jax.ShapeDtypeStruct((rows, width + LANES), jnp.bfloat16),
+        in_specs=[pl.BlockSpec(memory_space=VMEM)] * 2,
+        out_specs=pl.BlockSpec(memory_space=VMEM),
+        compiler_params=params(4),
+        name="pack",
+    )(weight, norms)
 
 
 def column_kernel(lay, *refs):
@@ -805,8 +830,7 @@
     own = attend_in.shape[0]
     count = lay.dp * lay.rep
     whole_tiles = own % 16 == 0
-    norm_rows = jnp.pad(layer_norms.astype(jnp.bfloat16).T, ((0, 0), (0, LANES - 4)))
-    shard1 = jnp.concatenate([attend_in.astype(jnp.bfloat16), norm_rows], axis=1)
+    shard1 = pack(attend_in, layer_norms)
     column1 = over(plain, shard1, True)
     rows = inputs.shape[1]
     attend_out_, expand_, contract_ = after([attend_out, expand, contract], [shard1])
@@ -853,10 +877,9 @@
     packed = attend_back(qx, kx, vx, dox)
     input_gradient, first_norms = input_back(plain, x, packed, gains, middle_grad, pieces1)
     keep1, send1 = project_back(plain, x, packed, gains, first_norms, second_norms, own)
-    own2, *got2 = after([own2, *got2], [send1])
+    own2, send1, *got2 = after([own2, send1, *got2], [])
     own2, *low2 = plane_sum(twin, own2, got2)
     got2 = send_over(twin, low2, True)
-    (send1,) = after([send1], low2[:1])
     own1, *low1 = chip_sum(plain, keep1, lay.to_core(send1))
     got1 = send_over(plain, low1, False)
     (middle,) = after([middle], low1)

time: 156 us -> 154 us (0.987)
  waiting for transfers between devices: 19.7 us -> 17.2 us
  other arithmetic: 4.18 us -> 2.59 us
    ppermute x24, waiting for transfers between devices: 11.3 us -> 8.71 us  [over(): return lax.ppermute(value, AXES, self.pairs(move))]
    convert_element_type x2 -> x0, other arithmetic: 1.59 us -> none  [the longest x1 0.9 us: body(): attend_in.astype(jnp.bfloat16)]
    unnamed x39 -> x43, local copies, waits for them, and re-layouts: 3.23 us -> 4.8 us
  transfers between devices with their start and end apart: 34 -> 34, of which waited for: 16 -> 16; matrix products, arithmetic and copies ran while one was open for 2% -> 2% of each run, Pallas kernels for 36% -> 37%
where the time goes in v4:
time: 154 us; the launch traced here: 153 us
  Pallas kernels  79.8 us (52%)
  starting transfers between devices  35 us (23%)
  waiting for transfers between devices  17.2 us (11%)
  blocking collectives  12.9 us (8%)
  local copies, waits for them, and re-layouts  4.81 us (3%)
  other arithmetic  2.59 us (2%)
    ppermute x24, starting transfers between devices, over(): return lax.ppermute(value, AXES, self.pairs(move))  31.6 us
    pallas_call x1, Pallas kernels, attend(): pl.pallas_call(partial(attend_kernel, lay, len(pieces)), out_shape=(wide,...  21.1 us
    pallas_call x1, Pallas kernels, feed(): pl.pallas_call(partial(feed_kernel, lay, len(pieces), len(deep_pieces)),...  19.3 us
    pallas_call x1, Pallas kernels, attend_back(): pl.pallas_call(attend_back_kernel, out_shape=jax.ShapeDtypeStruct((rows,...  18.8 us
    all_to_all x1, blocking collectives, exchange(): return lax.all_to_all(value, AXES, 0, 0)  12.9 us
    ppermute x24, waiting for transfers between devices, over(): return lax.ppermute(value, AXES, self.pairs(move))  8.71 us
    ppermute x10, waiting for transfers between devices, to_core(): return lax.ppermute(value, AXES, self.pairs(lambda p, c, z: (p, 1 - c, z)))  8.45 us
    unnamed x43, local copies, waits for them, and re-layouts  4.8 us
  transfers between devices with their start and end apart: 34, of which 16 were waited for; matrix products, arithmetic and copies ran while one was open for 2% of the time, Pallas kernels for 37%

profile of v4, /device:TPU:0, one launch (start us, length us, event | category | flops | bytes accessed | tf_op | source)
XLA Modules:
  0.0 153.3 jit_solution(2727263352771656934)
XLA Ops:
  2.3 5.0 %collective-permute-start.2 = (bf16[16,1664]{1,0:T(8,128)(2,1)S(1)}, bf16[16,1664]{1,0:T(8,128)(2,1)S(1)}, u32[]{:S(2)}, u32[]{:S(2)}) collective-permute-start(bf16[16,1664]{1,0:T(8,128)(2,1)S(1)} %pack.1.refs_0_), channel_id=1, source_target_pairs={{0,3},{1,0},{2,1},{3,2},{4,7},{5,4},{6,5},{7,6},{8,11},{9,8},{10,9... | collective-permute-start | bytes 159752 | tf_op jit(solution)/shard_map/ppermute | solution.py:69
  11.0 1.4 collective-permute-done.1.refs_2_
  13.3 1.5 %collective-permute-start.12 = (bf16[16,4608]{1,0:T(8,128)(2,1)S(1)}, bf16[16,4608]{1,0:T(8,128)(2,1)S(1)}, u32[]{:S(2)}, u32[]{:S(2)}) collective-permute-start(bf16[16,4608]{1,0:T(8,128)(2,1)S(1)} %slice_dynamic-update-slice_fusion.refs_0_), channel_id=1, source_target_pairs={{0,3},{1,0},{2,1},{3,2},{4,28},{5,29},{6,30},{7,31},{8,11},{9,8},{... | collective-permute-start | bytes 442376 | tf_op jit(solution)/shard_map/ppermute | solution.py:69
  14.9 2.5 %collective-permute-start.5 = (bf16[64,1664]{1,0:T(8,128)(2,1)S(1)}, bf16[64,1664]{1,0:T(8,128)(2,1)S(1)}, u32[]{:S(2)}, u32[]{:S(2)}) collective-permute-start(bf16[64,1664]{1,0:T(8,128)(2,1)S(1)} %column.2.refs_0_), channel_id=1, source_target_pairs={{0,24},{1,25},{2,26},{3,27},{4,28},{5,29},{6,30},{7,31},{8,16},{9,... | collective-permute-start | bytes 638984 | tf_op jit(solution)/shard_map/ppermute | solution.py:69
  18.7 1.7 %collective-permute-start.10 = (bf16[16,4608]{1,0:T(8,128)(2,1)S(1)}, bf16[16,4608]{1,0:T(8,128)(2,1)S(1)}, u32[]{:S(2)}, u32[]{:S(2)}) collective-permute-start(bf16[16,4608]{1,0:T(8,128)(2,1)S(1)} %slice_dynamic-update-slice_fusion.refs_0_), channel_id=1, source_target_pairs={{0,1},{1,2},{2,3},{3,0},{4,12},{5,13},{6,14},{7,15},{8,9},{9,10},{... | collective-permute-start | bytes 442376 | tf_op jit(solution)/shard_map/ppermute | solution.py:69
  20.4 1.2 copy-done.2
  21.6 1.2 copy-done.3
  23.5 1.1 arrange.1
  24.6 3.0 %collective-permute-done.11.refs_2_ = bf16[16,4608]{1,0:T(8,128)(2,1)S(1)} collective-permute-done((bf16[16,4608]{1,0:T(8,128)(2,1)S(1)}, bf16[16,4608]{1,0:T(8,128)(2,1)S(1)}, u32[]{:S(2)}, u32[]{:S(2)}) %collective-permute-start.11) | collective-permute-done | bytes 147488 | tf_op jit(solution)/shard_map/ppermute | solution.py:69
  27.9 2.5 %collective-permute-start.15 = (bf16[64,4608]{1,0:T(8,128)(2,1)S(1)}, bf16[64,4608]{1,0:T(8,128)(2,1)S(1)}, u32[]{:S(2)}, u32[]{:S(2)}) collective-permute-start(bf16[64,4608]{1,0:T(8,128)(2,1)S(1)} %column.3.refs_0_), channel_id=1, source_target_pairs={{0,24},{1,25},{2,26},{3,27},{4,7},{5,4},{6,5},{7,6},{8,16},{9,17},... | collective-permute-start | bytes 1769480 | tf_op jit(solution)/shard_map/ppermute | solution.py:69
  34.7 21.1 %attend.1 = (bf16[1056,1024]{1,0:T(8,128)(2,1)S(1)}, bf16[1056,1024]{1,0:T(8,128)(2,1)S(1)}, bf16[1056,1024]{1,0:T(8,128)(2,1)S(1)}, bf16[1056,512]{1,0:T(8,128)(2,1)S(1)}, f32[8,512]{1,0:T(8,128)S(1)}) custom-call(bf16[1056,512]{1,0:T(8,128)(2,1)S(1)} %get-tuple-element.128.x, s32[1056,128]{1,0:T(8,128)S(1)} %get-tuple-element.129.labels, ...), custom_call_target="tpu_custom_call" | custom-call | tf_op jit(solution)/shard_map/attend/pallas_call | solution.py:303
  56.9 1.1 collective-permute-done.17.refs_5_
  59.7 19.3 %feed.1 = (f32[1056,512]{1,0:T(8,128)S(1)}, f32[1056,512]{1,0:T(8,128)S(1)}, bf16[1056,512]{1,0:T(8,128)(2,1)S(1)}, bf16[1056,2048]{1,0:T(8,128)(2,1)S(1)}, bf16...) custom-call(bf16[1056,512]{1,0:T(8,128)(2,1)S(1)} %get-tuple-element, ...), custom_call_target="tpu_custom_call" | custom-call | tf_op jit(solution)/shard_map/feed/pallas_call | solution.py:457
  79.4 2.7 %mixed_back.1.dox = bf16[1056,1024]{1,0:T(8,128)(2,1)S(1)} custom-call(bf16[1056,512]{1,0:T(8,128)(2,1)S(1)} %get-tuple-element.148.middle_low, bf16[1056,512]{1,0:T(8,128)(2,1)S(1)} %get-tuple-element.138.mixed, bf16[512,512]{1,0:T(8,128)(2,1)S(1)} %get-tuple-element.149.out_weight), custom_call_target="tpu_custom_call" | custom-call | tf_op jit(solution)/shard_map/mixed_back/pallas_call | solution.py:503
  82.1 1.5 collective-permute-done.20.got
  83.6 1.1 chip_sum.2
  84.7 1.5 %collective-permute-start.21 = (bf16[64,4608]{1,0:T(8,128)(2,1)S(1)}, bf16[64,4608]{1,0:T(8,128)(2,1)S(1)}, u32[]{:S(2)}, u32[]{:S(2)}) collective-permute-start(bf16[64,4608]{1,0:T(8,128)(2,1)S(1)} %get-tuple-element.154), channel_id=1, source_target_pairs={{0,8},{1,9},{2,10},{3,11},{4,5},{5,6},{6,7},{7,4},{8,0},{9,1},{10,... | collective-permute-start | bytes 1769480 | tf_op jit(solution)/shard_map/ppermute | solution.py:69
  86.3 1.4 collective-permute-start.22
  88.3 18.8 %attend_back.1.packed = bf16[1056,1536]{1,0:T(8,128)(2,1)S(1)} custom-call(bf16[1056,1024]{1,0:T(8,128)(2,1)S(1)} %get-tuple-element.145.qx, bf16[1056,1024]{1,0:T(8,128)(2,1)S(1)} %get-tuple-element.146.kx, bf16[1056,1024]{1,0:T(8,128)(2,1)S(1)} %get-tuple-element.147.vx, bf16[1056,1024]{1,0:T(8,128)(2,1)S(1)} %mixed_back.1.dox), custom_call_target="tpu_custom_call" | custom-call | tf_op jit(solution)/shard_map/attend_back/pallas_call | solution.py:357
  107.1 3.2 %input_back.1 = (bf16[1056,512]{1,0:T(8,128)(2,1)S(1)}, f32[8,512]{1,0:T(8,128)S(1)}) custom-call(bf16[1056,512]{1,0:T(8,128)(2,1)S(1)} %get-tuple-element.128.x, bf16[1056,1536]{1,0:T(8,128)(2,1)S(1)} %attend_back.1.packed, f32[8,512]{1,0:T(8,128)S(1)} %get-tuple-element.140.gains, f32[1056,512]{1,0:T(8,128)S(1)} %get-tuple-element.158.middle_grad, ...), custom_call_target="tpu_custom_call" | custom-call | tf_op jit(solution)/shard_map/input_back/pallas_call | solution.py:575
  110.3 3.9 %project_back.1 = (bf16[4,64,1664]{2,1,0:T(8,128)(2,1)S(1)}, bf16[4,64,1664]{2,1,0:T(8,128)(2,1)S(1)}) custom-call(bf16[1056,512]{1,0:T(8,128)(2,1)S(1)} %get-tuple-element.128.x, bf16[1056,1536]{1,0:T(8,128)(2,1)S(1)} %attend_back.1.packed, f32[8,512]{1,0:T(8,128)S(1)} %get-tuple-element.140.gains, f32[8,512]{1,0:T(8,128)S(1)} %get-tuple-element.159.first_norms, ...), custom_call_target="tpu_custom_call" | custom-call | tf_op jit(solution)/shard_map/project_back/pallas_call | solution.py:541
  115.0 2.0 %collective-permute-done.24.got = bf16[4,64,1664]{2,1,0:T(8,128)(2,1)S(1)} collective-permute-done((bf16[4,64,1664]{2,1,0:T(8,128)(2,1)S(1)}, bf16[4,64,1664]{2,1,0:T(8,128)(2,1)S(1)}, u32[]{:S(2)}, u32[]{:S(2)}) %collective-permute-start.24) | collective-permute-done | bytes 852000 | tf_op jit(solution)/shard_map/ppermute | solution.py:72
  117.2 1.5 %collective-permute-start.25 = (bf16[64,1664]{1,0:T(8,128)(2,1)S(1)}, bf16[64,1664]{1,0:T(8,128)(2,1)S(1)}, u32[]{:S(2)}, u32[]{:S(2)}) collective-permute-start(bf16[64,1664]{1,0:T(8,128)(2,1)S(1)} %get-tuple-element.165), channel_id=1, source_target_pairs={{0,8},{1,9},{2,10},{3,11},{4,12},{5,13},{6,14},{7,15},{8,0},{9,1},... | collective-permute-start | bytes 638984 | tf_op jit(solution)/shard_map/ppermute | solution.py:69
  118.8 1.2 collective-permute-start.26
  121.9 1.8 %collective-permute-start.32 = (bf16[16,4608]{1,0:T(8,128)(2,1)S(1)}, bf16[16,4608]{1,0:T(8,128)(2,1)S(1)}, u32[]{:S(2)}, u32[]{:S(2)}) collective-permute-start(bf16[16,4608]{1,0:T(8,128)(2,1)S(1)} %get-tuple-element.189), channel_id=1, source_target_pairs={{0,2},{1,3},{2,0},{3,1},{4,20},{5,21},{6,22},{7,23},{8,10},{9,11},... | collective-permute-start | bytes 442376 | tf_op jit(solution)/shard_map/ppermute | solution.py:69
  123.7 1.7 %collective-permute-done.25.refs_0_ = bf16[64,1664]{1,0:T(8,128)(2,1)S(1)} collective-permute-done((bf16[64,1664]{1,0:T(8,128)(2,1)S(1)}, bf16[64,1664]{1,0:T(8,128)(2,1)S(1)}, u32[]{:S(2)}, u32[]{:S(2)}) %collective-permute-start.25) | collective-permute-done | bytes 213024 | tf_op jit(solution)/shard_map/ppermute | solution.py:69
  125.4 1.5 collective-permute-start.33
  127.0 4.3 %finish.1 = (bf16[1044,512]{1,0:T(8,128)(2,1)}, bf16[1044,512]{1,0:T(8,128)(2,1)}) custom-call(f32[8,128]{1,0:T(8,128)S(1)} %get-tuple-element.117.begin, f32[1056,512]{1,0:T(8,128)S(1)} %get-tuple-element.168.middle, bf16[1056,2048]{1,0:T(8,128)(2,1)S(1)} %get-tuple-element.169.active, bf16[2048,512]{1,0:T(8,128)(2,1)S(1)} %get-tuple-element.170.contract, ...), custom_call_target="tpu_custom_call" | custom-call | tf_op jit(solution)/shard_map/finish/pallas_call | solution.py:221
  132.1 2.1 %collective-permute-start.29 = (bf16[16,1664]{1,0:T(8,128)(2,1)S(1)}, bf16[16,1664]{1,0:T(8,128)(2,1)S(1)}, u32[]{:S(2)}, u32[]{:S(2)}) collective-permute-start(bf16[16,1664]{1,0:T(8,128)(2,1)S(1)} %get-tuple-element.181), channel_id=1, source_target_pairs={{0,2},{1,3},{2,0},{3,1},{4,6},{5,7},{6,4},{7,5},{8,10},{9,11},{10,... | collective-permute-start | bytes 159752 | tf_op jit(solution)/shard_map/ppermute | solution.py:69
  134.2 1.8 %collective-permute-start.30 = (bf16[16,1664]{1,0:T(8,128)(2,1)S(1)}, bf16[16,1664]{1,0:T(8,128)(2,1)S(1)}, u32[]{:S(2)}, u32[]{:S(2)}) collective-permute-start(bf16[16,1664]{1,0:T(8,128)(2,1)S(1)} %get-tuple-element.182), channel_id=1, source_target_pairs={{0,3},{1,0},{2,1},{3,2},{4,7},{5,4},{6,5},{7,6},{8,11},{9,8},{10,9... | collective-permute-start | bytes 159752 | tf_op jit(solution)/shard_map/ppermute | solution.py:69
  136.0 1.1 moments.2
  139.4 12.9 %all_to_all.5.sums = f32[32,1,128]{2,1,0:T(1,128)S(1)} all-to-all(f32[32,1,128]{2,1,0:T(1,128)S(1)} %get-tuple-element.192), channel_id=1, replica_groups=mesh['dp'=8,'rep'=4] {'dp','rep'}, dimensions={0} | all-to-all | bytes 32768 | tf_op jit(solution)/shard_map/all_to_all | solution.py:800
  (102 shorter events, 23.4 us)
Async XLA Ops:
  2.3 8.7 %collective-permute-start.2 = (bf16[16,1664]{1,0:T(8,128)(2,1)S(1)}, bf16[16,1664]{1,0:T(8,128)(2,1)S(1)}, u32[]{:S(2)}, u32[]{:S(2)}) collective-permute-start(bf16[16,1664]{1,0:T(8,128)(2,1)S(1)} %pack.1.refs_0_), channel_id=1, source_target_pairs={{0,3},{1,0},{2,1},{3,2},{4,7},{5,4},{6,5},{7,6},{8,11},{9,8},{10,9... | collective-permute-start | bytes 159752 | tf_op jit(solution)/shard_map/ppermute | solution.py:69
  7.4 5.1 %collective-permute-start.1 = (bf16[16,1664]{1,0:T(8,128)(2,1)S(1)}, bf16[16,1664]{1,0:T(8,128)(2,1)S(1)}, u32[]{:S(2)}, u32[]{:S(2)}) collective-permute-start(bf16[16,1664]{1,0:T(8,128)(2,1)S(1)} %pack.1.refs_0_), channel_id=1, source_target_pairs={{0,2},{1,3},{2,0},{3,1},{4,6},{5,7},{6,4},{7,5},{8,10},{9,11},{10,... | collective-permute-start | bytes 159752 | tf_op jit(solution)/shard_map/ppermute | solution.py:69
  7.4 5.9 %collective-permute-start = (bf16[16,1664]{1,0:T(8,128)(2,1)S(1)}, bf16[16,1664]{1,0:T(8,128)(2,1)S(1)}, u32[]{:S(2)}, u32[]{:S(2)}) collective-permute-start(bf16[16,1664]{1,0:T(8,128)(2,1)S(1)} %pack.1.refs_0_), channel_id=1, source_target_pairs={{0,1},{1,2},{2,3},{3,0},{4,5},{5,6},{6,7},{7,4},{8,9},{9,10},{10,1... | collective-permute-start | bytes 159752 | tf_op jit(solution)/shard_map/ppermute | solution.py:69
  13.3 5.4 %collective-permute-start.12 = (bf16[16,4608]{1,0:T(8,128)(2,1)S(1)}, bf16[16,4608]{1,0:T(8,128)(2,1)S(1)}, u32[]{:S(2)}, u32[]{:S(2)}) collective-permute-start(bf16[16,4608]{1,0:T(8,128)(2,1)S(1)} %slice_dynamic-update-slice_fusion.refs_0_), channel_id=1, source_target_pairs={{0,3},{1,0},{2,1},{3,2},{4,28},{5,29},{6,30},{7,31},{8,11},{9,8},{... | collective-permute-start | bytes 442376 | tf_op jit(solution)/shard_map/ppermute | solution.py:69
  14.9 12.7 %collective-permute-start.5 = (bf16[64,1664]{1,0:T(8,128)(2,1)S(1)}, bf16[64,1664]{1,0:T(8,128)(2,1)S(1)}, u32[]{:S(2)}, u32[]{:S(2)}) collective-permute-start(bf16[64,1664]{1,0:T(8,128)(2,1)S(1)} %column.2.refs_0_), channel_id=1, source_target_pairs={{0,24},{1,25},{2,26},{3,27},{4,28},{5,29},{6,30},{7,31},{8,16},{9,... | collective-permute-start | bytes 638984 | tf_op jit(solution)/shard_map/ppermute | solution.py:69
  17.5 10.2 %collective-permute-start.4 = (bf16[64,1664]{1,0:T(8,128)(2,1)S(1)}, bf16[64,1664]{1,0:T(8,128)(2,1)S(1)}, u32[]{:S(2)}, u32[]{:S(2)}) collective-permute-start(bf16[64,1664]{1,0:T(8,128)(2,1)S(1)} %column.2.refs_0_), channel_id=1, source_target_pairs={{0,16},{1,17},{2,18},{3,19},{4,20},{5,21},{6,22},{7,23},{8,24},{9,... | collective-permute-start | bytes 638984 | tf_op jit(solution)/shard_map/ppermute | solution.py:69
  18.0 9.7 %collective-permute-start.3 = (bf16[64,1664]{1,0:T(8,128)(2,1)S(1)}, bf16[64,1664]{1,0:T(8,128)(2,1)S(1)}, u32[]{:S(2)}, u32[]{:S(2)}) collective-permute-start(bf16[64,1664]{1,0:T(8,128)(2,1)S(1)} %column.2.refs_0_), channel_id=1, source_target_pairs={{0,8},{1,9},{2,10},{3,11},{4,12},{5,13},{6,14},{7,15},{8,0},{9,1},... | collective-permute-start | bytes 638984 | tf_op jit(solution)/shard_map/ppermute | solution.py:69
  18.5 9.1 %collective-permute-start.11 = (bf16[16,4608]{1,0:T(8,128)(2,1)S(1)}, bf16[16,4608]{1,0:T(8,128)(2,1)S(1)}, u32[]{:S(2)}, u32[]{:S(2)}) collective-permute-start(bf16[16,4608]{1,0:T(8,128)(2,1)S(1)} %slice_dynamic-update-slice_fusion.refs_0_), channel_id=1, source_target_pairs={{0,2},{1,3},{2,0},{3,1},{4,20},{5,21},{6,22},{7,23},{8,10},{9,11},... | collective-permute-start | bytes 442376 | tf_op jit(solution)/shard_map/ppermute | solution.py:69
  18.7 8.9 %collective-permute-start.10 = (bf16[16,4608]{1,0:T(8,128)(2,1)S(1)}, bf16[16,4608]{1,0:T(8,128)(2,1)S(1)}, u32[]{:S(2)}, u32[]{:S(2)}) collective-permute-start(bf16[16,4608]{1,0:T(8,128)(2,1)S(1)} %slice_dynamic-update-slice_fusion.refs_0_), channel_id=1, source_target_pairs={{0,1},{1,2},{2,3},{3,0},{4,12},{5,13},{6,14},{7,15},{8,9},{9,10},{... | collective-permute-start | bytes 442376 | tf_op jit(solution)/shard_map/ppermute | solution.py:69
  27.9 27.9 %collective-permute-start.15 = (bf16[64,4608]{1,0:T(8,128)(2,1)S(1)}, bf16[64,4608]{1,0:T(8,128)(2,1)S(1)}, u32[]{:S(2)}, u32[]{:S(2)}) collective-permute-start(bf16[64,4608]{1,0:T(8,128)(2,1)S(1)} %column.3.refs_0_), channel_id=1, source_target_pairs={{0,24},{1,25},{2,26},{3,27},{4,7},{5,4},{6,5},{7,6},{8,16},{9,17},... | collective-permute-start | bytes 1769480 | tf_op jit(solution)/shard_map/ppermute | solution.py:69
  30.4 25.4 %collective-permute-start.14 = (bf16[64,4608]{1,0:T(8,128)(2,1)S(1)}, bf16[64,4608]{1,0:T(8,128)(2,1)S(1)}, u32[]{:S(2)}, u32[]{:S(2)}) collective-permute-start(bf16[64,4608]{1,0:T(8,128)(2,1)S(1)} %column.3.refs_0_), channel_id=1, source_target_pairs={{0,16},{1,17},{2,18},{3,19},{4,6},{5,7},{6,4},{7,5},{8,24},{9,25},... | collective-permute-start | bytes 1769480 | tf_op jit(solution)/shard_map/ppermute | solution.py:69
  30.9 24.9 %collective-permute-start.13 = (bf16[64,4608]{1,0:T(8,128)(2,1)S(1)}, bf16[64,4608]{1,0:T(8,128)(2,1)S(1)}, u32[]{:S(2)}, u32[]{:S(2)}) collective-permute-start(bf16[64,4608]{1,0:T(8,128)(2,1)S(1)} %column.3.refs_0_), channel_id=1, source_target_pairs={{0,8},{1,9},{2,10},{3,11},{4,5},{5,6},{6,7},{7,4},{8,0},{9,1},{10,... | collective-permute-start | bytes 1769480 | tf_op jit(solution)/shard_map/ppermute | solution.py:69
  31.4 1.5 collective-permute-start.6
  31.6 1.6 %collective-permute-start.9 = (bf16[64,1664]{1,0:T(8,128)(2,1)S(1)}, bf16[64,1664]{1,0:T(8,128)(2,1)S(1)}, u32[]{:S(2)}, u32[]{:S(2)}) collective-permute-start(bf16[64,1664]{1,0:T(8,128)(2,1)S(1)} %collective-permute-done.5.refs_3_), channel_id=1, source_target_pairs={{0,4},{1,5},{2,6},{3,7},{4,0},{5,1},{6,2},{7,3},{8,12},{9,13},{10,... | collective-permute-start | bytes 638984 | tf_op jit(solution)/shard_map/ppermute | solution.py:72
  34.4 22.5 %collective-permute-start.16 = (bf16[64,4608]{1,0:T(8,128)(2,1)S(1)}, bf16[64,4608]{1,0:T(8,128)(2,1)S(1)}, u32[]{:S(2)}, u32[]{:S(2)}) collective-permute-start(bf16[64,4608]{1,0:T(8,128)(2,1)S(1)} %column.3.refs_0_), channel_id=1, source_target_pairs={{0,4},{1,5},{2,6},{3,7},{4,0},{5,1},{6,2},{7,3},{8,12},{9,13},{10,... | collective-permute-start | bytes 1769480 | tf_op jit(solution)/shard_map/ppermute | solution.py:72
  55.8 2.2 %collective-permute-start.17 = (bf16[64,4608]{1,0:T(8,128)(2,1)S(1)}, bf16[64,4608]{1,0:T(8,128)(2,1)S(1)}, u32[]{:S(2)}, u32[]{:S(2)}) collective-permute-start(bf16[64,4608]{1,0:T(8,128)(2,1)S(1)} %collective-permute-done.13.refs_1_), channel_id=1, source_target_pairs={{0,4},{1,5},{2,6},{3,7},{4,0},{5,1},{6,2},{7,3},{8,12},{9,13},{10,... | collective-permute-start | bytes 1769480 | tf_op jit(solution)/shard_map/ppermute | solution.py:72
  56.4 2.5 %collective-permute-start.18 = (bf16[64,4608]{1,0:T(8,128)(2,1)S(1)}, bf16[64,4608]{1,0:T(8,128)(2,1)S(1)}, u32[]{:S(2)}, u32[]{:S(2)}) collective-permute-start(bf16[64,4608]{1,0:T(8,128)(2,1)S(1)} %collective-permute-done.14.refs_2_), channel_id=1, source_target_pairs={{0,4},{1,5},{2,6},{3,7},{4,0},{5,1},{6,2},{7,3},{8,12},{9,13},{10,... | collective-permute-start | bytes 1769480 | tf_op jit(solution)/shard_map/ppermute | solution.py:72
  56.4 3.3 %collective-permute-start.19 = (bf16[64,4608]{1,0:T(8,128)(2,1)S(1)}, bf16[64,4608]{1,0:T(8,128)(2,1)S(1)}, u32[]{:S(2)}, u32[]{:S(2)}) collective-permute-start(bf16[64,4608]{1,0:T(8,128)(2,1)S(1)} %collective-permute-done.15.refs_3_), channel_id=1, source_target_pairs={{0,4},{1,5},{2,6},{3,7},{4,0},{5,1},{6,2},{7,3},{8,12},{9,13},{10,... | collective-permute-start | bytes 1769480 | tf_op jit(solution)/shard_map/ppermute | solution.py:72
  79.0 4.6 %collective-permute-start.20 = (bf16[4,64,4608]{2,1,0:T(8,128)(2,1)S(1)}, bf16[4,64,4608]{2,1,0:T(8,128)(2,1)S(1)}, u32[]{:S(2)}, u32[]{:S(2)}) collective-permute-start(bf16[4,64,4608]{2,1,0:T(8,128)(2,1)S(1)} %get-tuple-element.151), channel_id=1, source_target_pairs={{0,4},{1,5},{2,6},{3,7},{4,0},{5,1},{6,2},{7,3},{8,12},{9,13},{10,... | collective-permute-start | bytes 7077896 | tf_op jit(solution)/shard_map/ppermute | solution.py:72
  84.7 29.5 %collective-permute-start.21 = (bf16[64,4608]{1,0:T(8,128)(2,1)S(1)}, bf16[64,4608]{1,0:T(8,128)(2,1)S(1)}, u32[]{:S(2)}, u32[]{:S(2)}) collective-permute-start(bf16[64,4608]{1,0:T(8,128)(2,1)S(1)} %get-tuple-element.154), channel_id=1, source_target_pairs={{0,8},{1,9},{2,10},{3,11},{4,5},{5,6},{6,7},{7,4},{8,0},{9,1},{10,... | collective-permute-start | bytes 1769480 | tf_op jit(solution)/shard_map/ppermute | solution.py:69
  86.3 27.9 %collective-permute-start.22 = (bf16[64,4608]{1,0:T(8,128)(2,1)S(1)}, bf16[64,4608]{1,0:T(8,128)(2,1)S(1)}, u32[]{:S(2)}, u32[]{:S(2)}) collective-permute-start(bf16[64,4608]{1,0:T(8,128)(2,1)S(1)} %get-tuple-element.155), channel_id=1, source_target_pairs={{0,16},{1,17},{2,18},{3,19},{4,6},{5,7},{6,4},{7,5},{8,24},{9,25},... | collective-permute-start | bytes 1769480 | tf_op jit(solution)/shard_map/ppermute | solution.py:69
  87.7 26.5 %collective-permute-start.23 = (bf16[64,4608]{1,0:T(8,128)(2,1)S(1)}, bf16[64,4608]{1,0:T(8,128)(2,1)S(1)}, u32[]{:S(2)}, u32[]{:S(2)}) collective-permute-start(bf16[64,4608]{1,0:T(8,128)(2,1)S(1)} %get-tuple-element.156), channel_id=1, source_target_pairs={{0,24},{1,25},{2,26},{3,27},{4,7},{5,4},{6,5},{7,6},{8,16},{9,17},... | collective-permute-start | bytes 1769480 | tf_op jit(solution)/shard_map/ppermute | solution.py:69
  114.2 2.8 %collective-permute-start.24 = (bf16[4,64,1664]{2,1,0:T(8,128)(2,1)S(1)}, bf16[4,64,1664]{2,1,0:T(8,128)(2,1)S(1)}, u32[]{:S(2)}, u32[]{:S(2)}) collective-permute-start(bf16[4,64,1664]{2,1,0:T(8,128)(2,1)S(1)} %get-tuple-element.164), channel_id=1, source_target_pairs={{0,4},{1,5},{2,6},{3,7},{4,0},{5,1},{6,2},{7,3},{8,12},{9,13},{10,... | collective-permute-start | bytes 2555912 | tf_op jit(solution)/shard_map/ppermute | solution.py:72
  117.2 8.2 %collective-permute-start.25 = (bf16[64,1664]{1,0:T(8,128)(2,1)S(1)}, bf16[64,1664]{1,0:T(8,128)(2,1)S(1)}, u32[]{:S(2)}, u32[]{:S(2)}) collective-permute-start(bf16[64,1664]{1,0:T(8,128)(2,1)S(1)} %get-tuple-element.165), channel_id=1, source_target_pairs={{0,8},{1,9},{2,10},{3,11},{4,12},{5,13},{6,14},{7,15},{8,0},{9,1},... | collective-permute-start | bytes 638984 | tf_op jit(solution)/shard_map/ppermute | solution.py:69
  118.8 12.7 %collective-permute-start.26 = (bf16[64,1664]{1,0:T(8,128)(2,1)S(1)}, bf16[64,1664]{1,0:T(8,128)(2,1)S(1)}, u32[]{:S(2)}, u32[]{:S(2)}) collective-permute-start(bf16[64,1664]{1,0:T(8,128)(2,1)S(1)} %get-tuple-element.166), channel_id=1, source_target_pairs={{0,16},{1,17},{2,18},{3,19},{4,20},{5,21},{6,22},{7,23},{8,24},{9,... | collective-permute-start | bytes 638984 | tf_op jit(solution)/shard_map/ppermute | solution.py:69
  120.0 11.5 %collective-permute-start.27 = (bf16[64,1664]{1,0:T(8,128)(2,1)S(1)}, bf16[64,1664]{1,0:T(8,128)(2,1)S(1)}, u32[]{:S(2)}, u32[]{:S(2)}) collective-permute-start(bf16[64,1664]{1,0:T(8,128)(2,1)S(1)} %get-tuple-element.167), channel_id=1, source_target_pairs={{0,24},{1,25},{2,26},{3,27},{4,28},{5,29},{6,30},{7,31},{8,16},{9,... | collective-permute-start | bytes 638984 | tf_op jit(solution)/shard_map/ppermute | solution.py:69
  121.6 12.6 %collective-permute-start.31 = (bf16[16,4608]{1,0:T(8,128)(2,1)S(1)}, bf16[16,4608]{1,0:T(8,128)(2,1)S(1)}, u32[]{:S(2)}, u32[]{:S(2)}) collective-permute-start(bf16[16,4608]{1,0:T(8,128)(2,1)S(1)} %get-tuple-element.188), channel_id=1, source_target_pairs={{0,1},{1,2},{2,3},{3,0},{4,12},{5,13},{6,14},{7,15},{8,9},{9,10},{... | collective-permute-start | bytes 442376 | tf_op jit(solution)/shard_map/ppermute | solution.py:69
  121.9 14.0 %collective-permute-start.32 = (bf16[16,4608]{1,0:T(8,128)(2,1)S(1)}, bf16[16,4608]{1,0:T(8,128)(2,1)S(1)}, u32[]{:S(2)}, u32[]{:S(2)}) collective-permute-start(bf16[16,4608]{1,0:T(8,128)(2,1)S(1)} %get-tuple-element.189), channel_id=1, source_target_pairs={{0,2},{1,3},{2,0},{3,1},{4,20},{5,21},{6,22},{7,23},{8,10},{9,11},... | collective-permute-start | bytes 442376 | tf_op jit(solution)/shard_map/ppermute | solution.py:69
  125.4 10.5 %collective-permute-start.33 = (bf16[16,4608]{1,0:T(8,128)(2,1)S(1)}, bf16[16,4608]{1,0:T(8,128)(2,1)S(1)}, u32[]{:S(2)}, u32[]{:S(2)}) collective-permute-start(bf16[16,4608]{1,0:T(8,128)(2,1)S(1)} %get-tuple-element.190), channel_id=1, source_target_pairs={{0,3},{1,0},{2,1},{3,2},{4,28},{5,29},{6,30},{7,31},{8,11},{9,8},{... | collective-permute-start | bytes 442376 | tf_op jit(solution)/shard_map/ppermute | solution.py:69
  131.6 6.1 %collective-permute-start.28 = (bf16[16,1664]{1,0:T(8,128)(2,1)S(1)}, bf16[16,1664]{1,0:T(8,128)(2,1)S(1)}, u32[]{:S(2)}, u32[]{:S(2)}) collective-permute-start(bf16[16,1664]{1,0:T(8,128)(2,1)S(1)} %get-tuple-element.180), channel_id=1, source_target_pairs={{0,1},{1,2},{2,3},{3,0},{4,5},{5,6},{6,7},{7,4},{8,9},{9,10},{10,1... | collective-permute-start | bytes 159752 | tf_op jit(solution)/shard_map/ppermute | solution.py:69
  132.1 6.5 %collective-permute-start.29 = (bf16[16,1664]{1,0:T(8,128)(2,1)S(1)}, bf16[16,1664]{1,0:T(8,128)(2,1)S(1)}, u32[]{:S(2)}, u32[]{:S(2)}) collective-permute-start(bf16[16,1664]{1,0:T(8,128)(2,1)S(1)} %get-tuple-element.181), channel_id=1, source_target_pairs={{0,2},{1,3},{2,0},{3,1},{4,6},{5,7},{6,4},{7,5},{8,10},{9,11},{10,... | collective-permute-start | bytes 159752 | tf_op jit(solution)/shard_map/ppermute | solution.py:69
  134.2 4.5 %collective-permute-start.30 = (bf16[16,1664]{1,0:T(8,128)(2,1)S(1)}, bf16[16,1664]{1,0:T(8,128)(2,1)S(1)}, u32[]{:S(2)}, u32[]{:S(2)}) collective-permute-start(bf16[16,1664]{1,0:T(8,128)(2,1)S(1)} %get-tuple-element.182), channel_id=1, source_target_pairs={{0,3},{1,0},{2,1},{3,2},{4,7},{5,4},{6,5},{7,6},{8,11},{9,8},{10,9... | collective-permute-start | bytes 159752 | tf_op jit(solution)/shard_map/ppermute | solution.py:69
  (22 other events, 132.9 us)

commit v5 on v4

--- a/solution.py
+++ b/solution.py
@@ -405,7 +405,7 @@
             square = up * up
             half = 0.5 + 0.5 * jnp.tanh(up * (GELU_ONE + GELU_CUBE * square))
             active[span, part] = (up * half).astype(jnp.bfloat16)
-            slope = half * (1.0 + (1.0 - half) * (up * (2.0 * GELU_ONE + 6.0 * GELU_CUBE * square)))
+            slope = half + (half * (1.0 - half) * up) * (2.0 * GELU_ONE + 6.0 * GELU_CUBE * square)
             hidden_grad[span, part] = (dot(dy[span], contract[part], 1, 1) * slope).astype(jnp.bfloat16)
         back = dot(hidden_grad[span], wide[:, width:], 1, 1)
         gain_sum = gain_sum + jnp.sum(back * normed, axis=0, keepdims=True)
@@ -583,16 +583,24 @@
     )(x, packed, gains, middle_grad, *pieces)
 
 
-def pack_kernel(weight, norms, out):
-    rows, width = weight.shape
-    out[:, :width] = weight[...].astype(out.dtype)
+def pack_kernel(weight, norms, out, weight_here, norms_here, done):
+    copies = [
+        pltpu.make_async_copy(norms, norms_here, done.at[0]),
+        pltpu.make_async_copy(weight, weight_here, done.at[1]),
+    ]
+    for copy in copies:
+        copy.start()
+    rows, width = weight_here.shape
     same = lax.broadcasted_iota(jnp.int32, (rows, rows), 0) == lax.broadcasted_iota(jnp.int32, (rows, rows), 1)
     lane = lax.broadcasted_iota(jnp.int32, (rows, LANES), 1)
     tile = jnp.zeros((rows, LANES), jnp.float32)
-    for j in range(norms.shape[0]):
-        column = jnp.sum(jnp.where(same, norms[j : j + 1, :], 0.0), axis=1, keepdims=True)
+    copies[0].wait()
+    for j in range(norms_here.shape[0]):
+        column = jnp.sum(jnp.where(same, norms_here[j : j + 1, :], 0.0), axis=1, keepdims=True)
         tile = jnp.where(lane == j, column, tile)
     out[:, width:] = tile.astype(out.dtype)
+    copies[1].wait()
+    out[:, :width] = weight_here[...].astype(out.dtype)
 
 
 def pack(weight, norms):
@@ -600,8 +608,13 @@
     return pl.pallas_call(
         pack_kernel,
         out_shape=jax.ShapeDtypeStruct((rows, width + LANES), jnp.bfloat16),
-        in_specs=[pl.BlockSpec(memory_space=VMEM)] * 2,
+        in_specs=[pl.BlockSpec(memory_space=pltpu.MemorySpace.HBM)] * 2,
         out_specs=pl.BlockSpec(memory_space=VMEM),
+        scratch_shapes=[
+            pltpu.VMEM(weight.shape, weight.dtype),
+            pltpu.VMEM(norms.shape, norms.dtype),
+            pltpu.SemaphoreType.DMA((2,)),
+        ],
         compiler_params=params(4),
         name="pack",
     )(weight, norms)
@@ -639,17 +652,13 @@
 
 def chip_sum(lay, keep, got):
     plane, rows, cols = keep.shape
-    block = cols if cols < 2048 else 1536
-    part = pl.BlockSpec((rows, block), lambda i: (0, i))
-    whole = pl.BlockSpec((plane, rows, block), lambda i: (0, 0, i))
     return pl.pallas_call(
         partial(chip_sum_kernel, lay),
-        grid=(cols // block,),
         out_shape=[jax.ShapeDtypeStruct((rows, cols), jnp.float32)]
         + [jax.ShapeDtypeStruct((rows, cols), jnp.bfloat16)] * (plane - 1),
-        in_specs=[whole, whole],
-        out_specs=[part] * plane,
-        compiler_params=params(12),
+        in_specs=[pl.BlockSpec(memory_space=VMEM)] * 2,
+        out_specs=[pl.BlockSpec(memory_space=VMEM)] * plane,
+        compiler_params=params(14),
         name="chip_sum",
     )(keep, got)
 
@@ -671,16 +680,12 @@
 def plane_sum(lay, own, got):
     rows, cols = own.shape
     reps = lay.rep
-    block = cols if cols < 2048 else 1536
-    part = pl.BlockSpec((rows, block), lambda i: (0, i))
-    small = pl.BlockSpec((rows // reps, block), lambda i: (0, i))
     return pl.pallas_call(
         partial(plane_sum_kernel, lay),
-        grid=(cols // block,),
         out_shape=[jax.ShapeDtypeStruct((rows // reps, cols), jnp.float32)]
         + [jax.ShapeDtypeStruct((rows // reps, cols), jnp.bfloat16)] * (reps - 1),
-        in_specs=[part] * (1 + len(got)),
-        out_specs=[small] * reps,
+        in_specs=[pl.BlockSpec(memory_space=VMEM)] * (1 + len(got)),
+        out_specs=[pl.BlockSpec(memory_space=VMEM)] * reps,
         compiler_params=params(10),
         name="plane_sum",
     )(own, *got)

time: 154 us -> 154 us (level)
  no operation moved by 1% of the time
where the time goes in v5:
time: 154 us; the launch traced here: 153 us
  Pallas kernels  79.2 us (51%)
  starting transfers between devices  34.9 us (23%)
  waiting for transfers between devices  17.8 us (12%)
  blocking collectives  12.9 us (8%)
  local copies, waits for them, and re-layouts  4.81 us (3%)
  other arithmetic  2.59 us (2%)
    ppermute x24, starting transfers between devices, over(): return lax.ppermute(value, AXES, self.pairs(move))  31.4 us
    pallas_call x1, Pallas kernels, attend(): pl.pallas_call(partial(attend_kernel, lay, len(pieces)), out_shape=(wide,...  21 us
    pallas_call x1, Pallas kernels, feed(): pl.pallas_call(partial(feed_kernel, lay, len(pieces), len(deep_pieces)),...  19.7 us
    pallas_call x1, Pallas kernels, attend_back(): pl.pallas_call(attend_back_kernel, out_shape=jax.ShapeDtypeStruct((rows,...  18.8 us
    all_to_all x1, blocking collectives, exchange(): return lax.all_to_all(value, AXES, 0, 0)  12.9 us
    ppermute x24, waiting for transfers between devices, over(): return lax.ppermute(value, AXES, self.pairs(move))  9.33 us
    ppermute x10, waiting for transfers between devices, to_core(): return lax.ppermute(value, AXES, self.pairs(lambda p, c, z: (p, 1 - c, z)))  8.44 us
    unnamed x43, local copies, waits for them, and re-layouts  4.8 us
  transfers between devices with their start and end apart: 34, of which 16 were waited for; matrix products, arithmetic and copies ran while one was open for 2% of the time, Pallas kernels for 37%

profile of v5, /device:TPU:0, one launch (start us, length us, event | category | flops | bytes accessed | tf_op | source)
XLA Modules:
  0.0 153.3 jit_solution(13712837035807701076)
XLA Ops:
  2.5 5.1 %collective-permute-start.2 = (bf16[16,1664]{1,0:T(8,128)(2,1)S(1)}, bf16[16,1664]{1,0:T(8,128)(2,1)S(1)}, u32[]{:S(2)}, u32[]{:S(2)}) collective-permute-start(bf16[16,1664]{1,0:T(8,128)(2,1)S(1)} %pack.1.refs_0_), channel_id=1, source_target_pairs={{0,3},{1,0},{2,1},{3,2},{4,7},{5,4},{6,5},{7,6},{8,11},{9,8},{10,9... | collective-permute-start | bytes 159752 | tf_op jit(solution)/shard_map/ppermute | solution.py:69
  7.6 1.0 collective-permute-start
  11.2 1.4 collective-permute-done.1.refs_2_
  13.5 1.5 %collective-permute-start.12 = (bf16[16,4608]{1,0:T(8,128)(2,1)S(1)}, bf16[16,4608]{1,0:T(8,128)(2,1)S(1)}, u32[]{:S(2)}, u32[]{:S(2)}) collective-permute-start(bf16[16,4608]{1,0:T(8,128)(2,1)S(1)} %slice_dynamic-update-slice_fusion.refs_0_), channel_id=1, source_target_pairs={{0,3},{1,0},{2,1},{3,2},{4,28},{5,29},{6,30},{7,31},{8,11},{9,8},{... | collective-permute-start | bytes 442376 | tf_op jit(solution)/shard_map/ppermute | solution.py:69
  15.1 2.5 %collective-permute-start.5 = (bf16[64,1664]{1,0:T(8,128)(2,1)S(1)}, bf16[64,1664]{1,0:T(8,128)(2,1)S(1)}, u32[]{:S(2)}, u32[]{:S(2)}) collective-permute-start(bf16[64,1664]{1,0:T(8,128)(2,1)S(1)} %column.2.refs_0_), channel_id=1, source_target_pairs={{0,24},{1,25},{2,26},{3,27},{4,28},{5,29},{6,30},{7,31},{8,16},{9,... | collective-permute-start | bytes 638984 | tf_op jit(solution)/shard_map/ppermute | solution.py:69
  18.9 1.7 %collective-permute-start.10 = (bf16[16,4608]{1,0:T(8,128)(2,1)S(1)}, bf16[16,4608]{1,0:T(8,128)(2,1)S(1)}, u32[]{:S(2)}, u32[]{:S(2)}) collective-permute-start(bf16[16,4608]{1,0:T(8,128)(2,1)S(1)} %slice_dynamic-update-slice_fusion.refs_0_), channel_id=1, source_target_pairs={{0,1},{1,2},{2,3},{3,0},{4,12},{5,13},{6,14},{7,15},{8,9},{9,10},{... | collective-permute-start | bytes 442376 | tf_op jit(solution)/shard_map/ppermute | solution.py:69
  20.6 1.2 copy-done.2
  21.8 1.2 copy-done.3
  23.7 1.1 arrange.1
  24.8 3.0 %collective-permute-done.11.refs_2_ = bf16[16,4608]{1,0:T(8,128)(2,1)S(1)} collective-permute-done((bf16[16,4608]{1,0:T(8,128)(2,1)S(1)}, bf16[16,4608]{1,0:T(8,128)(2,1)S(1)}, u32[]{:S(2)}, u32[]{:S(2)}) %collective-permute-start.11) | collective-permute-done | bytes 147488 | tf_op jit(solution)/shard_map/ppermute | solution.py:69
  28.1 2.5 %collective-permute-start.15 = (bf16[64,4608]{1,0:T(8,128)(2,1)S(1)}, bf16[64,4608]{1,0:T(8,128)(2,1)S(1)}, u32[]{:S(2)}, u32[]{:S(2)}) collective-permute-start(bf16[64,4608]{1,0:T(8,128)(2,1)S(1)} %column.3.refs_0_), channel_id=1, source_target_pairs={{0,24},{1,25},{2,26},{3,27},{4,7},{5,4},{6,5},{7,6},{8,16},{9,17},... | collective-permute-start | bytes 1769480 | tf_op jit(solution)/shard_map/ppermute | solution.py:69
  34.9 21.0 %attend.1 = (bf16[1056,1024]{1,0:T(8,128)(2,1)S(1)}, bf16[1056,1024]{1,0:T(8,128)(2,1)S(1)}, bf16[1056,1024]{1,0:T(8,128)(2,1)S(1)}, bf16[1056,512]{1,0:T(8,128)(2,1)S(1)}, f32[8,512]{1,0:T(8,128)S(1)}) custom-call(bf16[1056,512]{1,0:T(8,128)(2,1)S(1)} %get-tuple-element.128.x, s32[1056,128]{1,0:T(8,128)S(1)} %get-tuple-element.129.labels, ...), custom_call_target="tpu_custom_call" | custom-call | tf_op jit(solution)/shard_map/attend/pallas_call | solution.py:303
  57.1 1.1 collective-permute-done.17.refs_5_
  59.9 19.7 %feed.1 = (f32[1056,512]{1,0:T(8,128)S(1)}, f32[1056,512]{1,0:T(8,128)S(1)}, bf16[1056,512]{1,0:T(8,128)(2,1)S(1)}, bf16[1056,2048]{1,0:T(8,128)(2,1)S(1)}, bf16...) custom-call(bf16[1056,512]{1,0:T(8,128)(2,1)S(1)} %get-tuple-element, ...), custom_call_target="tpu_custom_call" | custom-call | tf_op jit(solution)/shard_map/feed/pallas_call | solution.py:457
  80.0 2.7 %mixed_back.1.dox = bf16[1056,1024]{1,0:T(8,128)(2,1)S(1)} custom-call(bf16[1056,512]{1,0:T(8,128)(2,1)S(1)} %get-tuple-element.148.middle_low, bf16[1056,512]{1,0:T(8,128)(2,1)S(1)} %get-tuple-element.138.mixed, bf16[512,512]{1,0:T(8,128)(2,1)S(1)} %get-tuple-element.149.out_weight), custom_call_target="tpu_custom_call" | custom-call | tf_op jit(solution)/shard_map/mixed_back/pallas_call | solution.py:503
  82.7 1.5 collective-permute-done.20.got
  84.7 1.5 %collective-permute-start.21 = (bf16[64,4608]{1,0:T(8,128)(2,1)S(1)}, bf16[64,4608]{1,0:T(8,128)(2,1)S(1)}, u32[]{:S(2)}, u32[]{:S(2)}) collective-permute-start(bf16[64,4608]{1,0:T(8,128)(2,1)S(1)} %get-tuple-element.154), channel_id=1, source_target_pairs={{0,8},{1,9},{2,10},{3,11},{4,5},{5,6},{6,7},{7,4},{8,0},{9,1},{10,... | collective-permute-start | bytes 1769480 | tf_op jit(solution)/shard_map/ppermute | solution.py:69
  86.2 1.4 collective-permute-start.22
  88.2 18.8 %attend_back.1.packed = bf16[1056,1536]{1,0:T(8,128)(2,1)S(1)} custom-call(bf16[1056,1024]{1,0:T(8,128)(2,1)S(1)} %get-tuple-element.145.qx, bf16[1056,1024]{1,0:T(8,128)(2,1)S(1)} %get-tuple-element.146.kx, bf16[1056,1024]{1,0:T(8,128)(2,1)S(1)} %get-tuple-element.147.vx, bf16[1056,1024]{1,0:T(8,128)(2,1)S(1)} %mixed_back.1.dox), custom_call_target="tpu_custom_call" | custom-call | tf_op jit(solution)/shard_map/attend_back/pallas_call | solution.py:357
  107.1 3.2 %input_back.1 = (bf16[1056,512]{1,0:T(8,128)(2,1)S(1)}, f32[8,512]{1,0:T(8,128)S(1)}) custom-call(bf16[1056,512]{1,0:T(8,128)(2,1)S(1)} %get-tuple-element.128.x, bf16[1056,1536]{1,0:T(8,128)(2,1)S(1)} %attend_back.1.packed, f32[8,512]{1,0:T(8,128)S(1)} %get-tuple-element.140.gains, f32[1056,512]{1,0:T(8,128)S(1)} %get-tuple-element.158.middle_grad, ...), custom_call_target="tpu_custom_call" | custom-call | tf_op jit(solution)/shard_map/input_back/pallas_call | solution.py:575
  110.2 3.9 %project_back.1 = (bf16[4,64,1664]{2,1,0:T(8,128)(2,1)S(1)}, bf16[4,64,1664]{2,1,0:T(8,128)(2,1)S(1)}) custom-call(bf16[1056,512]{1,0:T(8,128)(2,1)S(1)} %get-tuple-element.128.x, bf16[1056,1536]{1,0:T(8,128)(2,1)S(1)} %attend_back.1.packed, f32[8,512]{1,0:T(8,128)S(1)} %get-tuple-element.140.gains, f32[8,512]{1,0:T(8,128)S(1)} %get-tuple-element.159.first_norms, ...), custom_call_target="tpu_custom_call" | custom-call | tf_op jit(solution)/shard_map/project_back/pallas_call | solution.py:541
  115.0 2.0 %collective-permute-done.24.got = bf16[4,64,1664]{2,1,0:T(8,128)(2,1)S(1)} collective-permute-done((bf16[4,64,1664]{2,1,0:T(8,128)(2,1)S(1)}, bf16[4,64,1664]{2,1,0:T(8,128)(2,1)S(1)}, u32[]{:S(2)}, u32[]{:S(2)}) %collective-permute-start.24) | collective-permute-done | bytes 852000 | tf_op jit(solution)/shard_map/ppermute | solution.py:72
  117.2 1.5 %collective-permute-start.25 = (bf16[64,1664]{1,0:T(8,128)(2,1)S(1)}, bf16[64,1664]{1,0:T(8,128)(2,1)S(1)}, u32[]{:S(2)}, u32[]{:S(2)}) collective-permute-start(bf16[64,1664]{1,0:T(8,128)(2,1)S(1)} %get-tuple-element.165), channel_id=1, source_target_pairs={{0,8},{1,9},{2,10},{3,11},{4,12},{5,13},{6,14},{7,15},{8,0},{9,1},... | collective-permute-start | bytes 638984 | tf_op jit(solution)/shard_map/ppermute | solution.py:69
  118.7 1.2 collective-permute-start.26
  121.4 1.8 %collective-permute-start.32 = (bf16[16,4608]{1,0:T(8,128)(2,1)S(1)}, bf16[16,4608]{1,0:T(8,128)(2,1)S(1)}, u32[]{:S(2)}, u32[]{:S(2)}) collective-permute-start(bf16[16,4608]{1,0:T(8,128)(2,1)S(1)} %get-tuple-element.189), channel_id=1, source_target_pairs={{0,2},{1,3},{2,0},{3,1},{4,20},{5,21},{6,22},{7,23},{8,10},{9,11},... | collective-permute-start | bytes 442376 | tf_op jit(solution)/shard_map/ppermute | solution.py:69
  123.2 2.2 %collective-permute-done.25.refs_0_ = bf16[64,1664]{1,0:T(8,128)(2,1)S(1)} collective-permute-done((bf16[64,1664]{1,0:T(8,128)(2,1)S(1)}, bf16[64,1664]{1,0:T(8,128)(2,1)S(1)}, u32[]{:S(2)}, u32[]{:S(2)}) %collective-permute-start.25) | collective-permute-done | bytes 213024 | tf_op jit(solution)/shard_map/ppermute | solution.py:69
  125.4 1.4 collective-permute-start.33
  126.8 4.3 %finish.1 = (bf16[1044,512]{1,0:T(8,128)(2,1)}, bf16[1044,512]{1,0:T(8,128)(2,1)}) custom-call(f32[8,128]{1,0:T(8,128)S(1)} %get-tuple-element.117.begin, f32[1056,512]{1,0:T(8,128)S(1)} %get-tuple-element.168.middle, bf16[1056,2048]{1,0:T(8,128)(2,1)S(1)} %get-tuple-element.169.active, bf16[2048,512]{1,0:T(8,128)(2,1)S(1)} %get-tuple-element.170.contract, ...), custom_call_target="tpu_custom_call" | custom-call | tf_op jit(solution)/shard_map/finish/pallas_call | solution.py:221
  132.1 1.9 %collective-permute-start.29 = (bf16[16,1664]{1,0:T(8,128)(2,1)S(1)}, bf16[16,1664]{1,0:T(8,128)(2,1)S(1)}, u32[]{:S(2)}, u32[]{:S(2)}) collective-permute-start(bf16[16,1664]{1,0:T(8,128)(2,1)S(1)} %get-tuple-element.181), channel_id=1, source_target_pairs={{0,2},{1,3},{2,0},{3,1},{4,6},{5,7},{6,4},{7,5},{8,10},{9,11},{10,... | collective-permute-start | bytes 159752 | tf_op jit(solution)/shard_map/ppermute | solution.py:69
  134.0 1.9 %collective-permute-start.30 = (bf16[16,1664]{1,0:T(8,128)(2,1)S(1)}, bf16[16,1664]{1,0:T(8,128)(2,1)S(1)}, u32[]{:S(2)}, u32[]{:S(2)}) collective-permute-start(bf16[16,1664]{1,0:T(8,128)(2,1)S(1)} %get-tuple-element.182), channel_id=1, source_target_pairs={{0,3},{1,0},{2,1},{3,2},{4,7},{5,4},{6,5},{7,6},{8,11},{9,8},{10,9... | collective-permute-start | bytes 159752 | tf_op jit(solution)/shard_map/ppermute | solution.py:69
  136.0 1.1 moments.2
  139.4 12.9 %all_to_all.5.sums = f32[32,1,128]{2,1,0:T(1,128)S(1)} all-to-all(f32[32,1,128]{2,1,0:T(1,128)S(1)} %get-tuple-element.192), channel_id=1, replica_groups=mesh['dp'=8,'rep'=4] {'dp','rep'}, dimensions={0} | all-to-all | bytes 32768 | tf_op jit(solution)/shard_map/all_to_all | solution.py:805
  (102 shorter events, 22.9 us)
Async XLA Ops:
  2.5 8.8 %collective-permute-start.2 = (bf16[16,1664]{1,0:T(8,128)(2,1)S(1)}, bf16[16,1664]{1,0:T(8,128)(2,1)S(1)}, u32[]{:S(2)}, u32[]{:S(2)}) collective-permute-start(bf16[16,1664]{1,0:T(8,128)(2,1)S(1)} %pack.1.refs_0_), channel_id=1, source_target_pairs={{0,3},{1,0},{2,1},{3,2},{4,7},{5,4},{6,5},{7,6},{8,11},{9,8},{10,9... | collective-permute-start | bytes 159752 | tf_op jit(solution)/shard_map/ppermute | solution.py:69
  7.6 5.1 %collective-permute-start.1 = (bf16[16,1664]{1,0:T(8,128)(2,1)S(1)}, bf16[16,1664]{1,0:T(8,128)(2,1)S(1)}, u32[]{:S(2)}, u32[]{:S(2)}) collective-permute-start(bf16[16,1664]{1,0:T(8,128)(2,1)S(1)} %pack.1.refs_0_), channel_id=1, source_target_pairs={{0,2},{1,3},{2,0},{3,1},{4,6},{5,7},{6,4},{7,5},{8,10},{9,11},{10,... | collective-permute-start | bytes 159752 | tf_op jit(solution)/shard_map/ppermute | solution.py:69
  7.6 5.9 %collective-permute-start = (bf16[16,1664]{1,0:T(8,128)(2,1)S(1)}, bf16[16,1664]{1,0:T(8,128)(2,1)S(1)}, u32[]{:S(2)}, u32[]{:S(2)}) collective-permute-start(bf16[16,1664]{1,0:T(8,128)(2,1)S(1)} %pack.1.refs_0_), channel_id=1, source_target_pairs={{0,1},{1,2},{2,3},{3,0},{4,5},{5,6},{6,7},{7,4},{8,9},{9,10},{10,1... | collective-permute-start | bytes 159752 | tf_op jit(solution)/shard_map/ppermute | solution.py:69
  13.5 5.4 %collective-permute-start.12 = (bf16[16,4608]{1,0:T(8,128)(2,1)S(1)}, bf16[16,4608]{1,0:T(8,128)(2,1)S(1)}, u32[]{:S(2)}, u32[]{:S(2)}) collective-permute-start(bf16[16,4608]{1,0:T(8,128)(2,1)S(1)} %slice_dynamic-update-slice_fusion.refs_0_), channel_id=1, source_target_pairs={{0,3},{1,0},{2,1},{3,2},{4,28},{5,29},{6,30},{7,31},{8,11},{9,8},{... | collective-permute-start | bytes 442376 | tf_op jit(solution)/shard_map/ppermute | solution.py:69
  15.1 12.7 %collective-permute-start.5 = (bf16[64,1664]{1,0:T(8,128)(2,1)S(1)}, bf16[64,1664]{1,0:T(8,128)(2,1)S(1)}, u32[]{:S(2)}, u32[]{:S(2)}) collective-permute-start(bf16[64,1664]{1,0:T(8,128)(2,1)S(1)} %column.2.refs_0_), channel_id=1, source_target_pairs={{0,24},{1,25},{2,26},{3,27},{4,28},{5,29},{6,30},{7,31},{8,16},{9,... | collective-permute-start | bytes 638984 | tf_op jit(solution)/shard_map/ppermute | solution.py:69
  17.6 10.2 %collective-permute-start.4 = (bf16[64,1664]{1,0:T(8,128)(2,1)S(1)}, bf16[64,1664]{1,0:T(8,128)(2,1)S(1)}, u32[]{:S(2)}, u32[]{:S(2)}) collective-permute-start(bf16[64,1664]{1,0:T(8,128)(2,1)S(1)} %column.2.refs_0_), channel_id=1, source_target_pairs={{0,16},{1,17},{2,18},{3,19},{4,20},{5,21},{6,22},{7,23},{8,24},{9,... | collective-permute-start | bytes 638984 | tf_op jit(solution)/shard_map/ppermute | solution.py:69
  18.2 9.7 %collective-permute-start.3 = (bf16[64,1664]{1,0:T(8,128)(2,1)S(1)}, bf16[64,1664]{1,0:T(8,128)(2,1)S(1)}, u32[]{:S(2)}, u32[]{:S(2)}) collective-permute-start(bf16[64,1664]{1,0:T(8,128)(2,1)S(1)} %column.2.refs_0_), channel_id=1, source_target_pairs={{0,8},{1,9},{2,10},{3,11},{4,12},{5,13},{6,14},{7,15},{8,0},{9,1},... | collective-permute-start | bytes 638984 | tf_op jit(solution)/shard_map/ppermute | solution.py:69
  18.7 9.1 %collective-permute-start.11 = (bf16[16,4608]{1,0:T(8,128)(2,1)S(1)}, bf16[16,4608]{1,0:T(8,128)(2,1)S(1)}, u32[]{:S(2)}, u32[]{:S(2)}) collective-permute-start(bf16[16,4608]{1,0:T(8,128)(2,1)S(1)} %slice_dynamic-update-slice_fusion.refs_0_), channel_id=1, source_target_pairs={{0,2},{1,3},{2,0},{3,1},{4,20},{5,21},{6,22},{7,23},{8,10},{9,11},... | collective-permute-start | bytes 442376 | tf_op jit(solution)/shard_map/ppermute | solution.py:69
  18.9 8.9 %collective-permute-start.10 = (bf16[16,4608]{1,0:T(8,128)(2,1)S(1)}, bf16[16,4608]{1,0:T(8,128)(2,1)S(1)}, u32[]{:S(2)}, u32[]{:S(2)}) collective-permute-start(bf16[16,4608]{1,0:T(8,128)(2,1)S(1)} %slice_dynamic-update-slice_fusion.refs_0_), channel_id=1, source_target_pairs={{0,1},{1,2},{2,3},{3,0},{4,12},{5,13},{6,14},{7,15},{8,9},{9,10},{... | collective-permute-start | bytes 442376 | tf_op jit(solution)/shard_map/ppermute | solution.py:69
  28.1 27.7 %collective-permute-start.15 = (bf16[64,4608]{1,0:T(8,128)(2,1)S(1)}, bf16[64,4608]{1,0:T(8,128)(2,1)S(1)}, u32[]{:S(2)}, u32[]{:S(2)}) collective-permute-start(bf16[64,4608]{1,0:T(8,128)(2,1)S(1)} %column.3.refs_0_), channel_id=1, source_target_pairs={{0,24},{1,25},{2,26},{3,27},{4,7},{5,4},{6,5},{7,6},{8,16},{9,17},... | collective-permute-start | bytes 1769480 | tf_op jit(solution)/shard_map/ppermute | solution.py:69
  30.6 25.3 %collective-permute-start.14 = (bf16[64,4608]{1,0:T(8,128)(2,1)S(1)}, bf16[64,4608]{1,0:T(8,128)(2,1)S(1)}, u32[]{:S(2)}, u32[]{:S(2)}) collective-permute-start(bf16[64,4608]{1,0:T(8,128)(2,1)S(1)} %column.3.refs_0_), channel_id=1, source_target_pairs={{0,16},{1,17},{2,18},{3,19},{4,6},{5,7},{6,4},{7,5},{8,24},{9,25},... | collective-permute-start | bytes 1769480 | tf_op jit(solution)/shard_map/ppermute | solution.py:69
  31.1 24.8 %collective-permute-start.13 = (bf16[64,4608]{1,0:T(8,128)(2,1)S(1)}, bf16[64,4608]{1,0:T(8,128)(2,1)S(1)}, u32[]{:S(2)}, u32[]{:S(2)}) collective-permute-start(bf16[64,4608]{1,0:T(8,128)(2,1)S(1)} %column.3.refs_0_), channel_id=1, source_target_pairs={{0,8},{1,9},{2,10},{3,11},{4,5},{5,6},{6,7},{7,4},{8,0},{9,1},{10,... | collective-permute-start | bytes 1769480 | tf_op jit(solution)/shard_map/ppermute | solution.py:69
  31.6 1.5 collective-permute-start.6
  31.8 1.6 %collective-permute-start.9 = (bf16[64,1664]{1,0:T(8,128)(2,1)S(1)}, bf16[64,1664]{1,0:T(8,128)(2,1)S(1)}, u32[]{:S(2)}, u32[]{:S(2)}) collective-permute-start(bf16[64,1664]{1,0:T(8,128)(2,1)S(1)} %collective-permute-done.5.refs_3_), channel_id=1, source_target_pairs={{0,4},{1,5},{2,6},{3,7},{4,0},{5,1},{6,2},{7,3},{8,12},{9,13},{10,... | collective-permute-start | bytes 638984 | tf_op jit(solution)/shard_map/ppermute | solution.py:72
  34.5 22.5 %collective-permute-start.16 = (bf16[64,4608]{1,0:T(8,128)(2,1)S(1)}, bf16[64,4608]{1,0:T(8,128)(2,1)S(1)}, u32[]{:S(2)}, u32[]{:S(2)}) collective-permute-start(bf16[64,4608]{1,0:T(8,128)(2,1)S(1)} %column.3.refs_0_), channel_id=1, source_target_pairs={{0,4},{1,5},{2,6},{3,7},{4,0},{5,1},{6,2},{7,3},{8,12},{9,13},{10,... | collective-permute-start | bytes 1769480 | tf_op jit(solution)/shard_map/ppermute | solution.py:72
  55.8 2.3 %collective-permute-start.17 = (bf16[64,4608]{1,0:T(8,128)(2,1)S(1)}, bf16[64,4608]{1,0:T(8,128)(2,1)S(1)}, u32[]{:S(2)}, u32[]{:S(2)}) collective-permute-start(bf16[64,4608]{1,0:T(8,128)(2,1)S(1)} %collective-permute-done.13.refs_1_), channel_id=1, source_target_pairs={{0,4},{1,5},{2,6},{3,7},{4,0},{5,1},{6,2},{7,3},{8,12},{9,13},{10,... | collective-permute-start | bytes 1769480 | tf_op jit(solution)/shard_map/ppermute | solution.py:72
  56.6 2.5 %collective-permute-start.18 = (bf16[64,4608]{1,0:T(8,128)(2,1)S(1)}, bf16[64,4608]{1,0:T(8,128)(2,1)S(1)}, u32[]{:S(2)}, u32[]{:S(2)}) collective-permute-start(bf16[64,4608]{1,0:T(8,128)(2,1)S(1)} %collective-permute-done.14.refs_2_), channel_id=1, source_target_pairs={{0,4},{1,5},{2,6},{3,7},{4,0},{5,1},{6,2},{7,3},{8,12},{9,13},{10,... | collective-permute-start | bytes 1769480 | tf_op jit(solution)/shard_map/ppermute | solution.py:72
  56.6 3.3 %collective-permute-start.19 = (bf16[64,4608]{1,0:T(8,128)(2,1)S(1)}, bf16[64,4608]{1,0:T(8,128)(2,1)S(1)}, u32[]{:S(2)}, u32[]{:S(2)}) collective-permute-start(bf16[64,4608]{1,0:T(8,128)(2,1)S(1)} %collective-permute-done.15.refs_3_), channel_id=1, source_target_pairs={{0,4},{1,5},{2,6},{3,7},{4,0},{5,1},{6,2},{7,3},{8,12},{9,13},{10,... | collective-permute-start | bytes 1769480 | tf_op jit(solution)/shard_map/ppermute | solution.py:72
  79.6 4.6 %collective-permute-start.20 = (bf16[4,64,4608]{2,1,0:T(8,128)(2,1)S(1)}, bf16[4,64,4608]{2,1,0:T(8,128)(2,1)S(1)}, u32[]{:S(2)}, u32[]{:S(2)}) collective-permute-start(bf16[4,64,4608]{2,1,0:T(8,128)(2,1)S(1)} %get-tuple-element.151), channel_id=1, source_target_pairs={{0,4},{1,5},{2,6},{3,7},{4,0},{5,1},{6,2},{7,3},{8,12},{9,13},{10,... | collective-permute-start | bytes 7077896 | tf_op jit(solution)/shard_map/ppermute | solution.py:72
  84.7 29.5 %collective-permute-start.21 = (bf16[64,4608]{1,0:T(8,128)(2,1)S(1)}, bf16[64,4608]{1,0:T(8,128)(2,1)S(1)}, u32[]{:S(2)}, u32[]{:S(2)}) collective-permute-start(bf16[64,4608]{1,0:T(8,128)(2,1)S(1)} %get-tuple-element.154), channel_id=1, source_target_pairs={{0,8},{1,9},{2,10},{3,11},{4,5},{5,6},{6,7},{7,4},{8,0},{9,1},{10,... | collective-permute-start | bytes 1769480 | tf_op jit(solution)/shard_map/ppermute | solution.py:69
  86.2 27.9 %collective-permute-start.22 = (bf16[64,4608]{1,0:T(8,128)(2,1)S(1)}, bf16[64,4608]{1,0:T(8,128)(2,1)S(1)}, u32[]{:S(2)}, u32[]{:S(2)}) collective-permute-start(bf16[64,4608]{1,0:T(8,128)(2,1)S(1)} %get-tuple-element.155), channel_id=1, source_target_pairs={{0,16},{1,17},{2,18},{3,19},{4,6},{5,7},{6,4},{7,5},{8,24},{9,25},... | collective-permute-start | bytes 1769480 | tf_op jit(solution)/shard_map/ppermute | solution.py:69
  87.7 26.5 %collective-permute-start.23 = (bf16[64,4608]{1,0:T(8,128)(2,1)S(1)}, bf16[64,4608]{1,0:T(8,128)(2,1)S(1)}, u32[]{:S(2)}, u32[]{:S(2)}) collective-permute-start(bf16[64,4608]{1,0:T(8,128)(2,1)S(1)} %get-tuple-element.156), channel_id=1, source_target_pairs={{0,24},{1,25},{2,26},{3,27},{4,7},{5,4},{6,5},{7,6},{8,16},{9,17},... | collective-permute-start | bytes 1769480 | tf_op jit(solution)/shard_map/ppermute | solution.py:69
  114.2 2.8 %collective-permute-start.24 = (bf16[4,64,1664]{2,1,0:T(8,128)(2,1)S(1)}, bf16[4,64,1664]{2,1,0:T(8,128)(2,1)S(1)}, u32[]{:S(2)}, u32[]{:S(2)}) collective-permute-start(bf16[4,64,1664]{2,1,0:T(8,128)(2,1)S(1)} %get-tuple-element.164), channel_id=1, source_target_pairs={{0,4},{1,5},{2,6},{3,7},{4,0},{5,1},{6,2},{7,3},{8,12},{9,13},{10,... | collective-permute-start | bytes 2555912 | tf_op jit(solution)/shard_map/ppermute | solution.py:72
  117.2 8.2 %collective-permute-start.25 = (bf16[64,1664]{1,0:T(8,128)(2,1)S(1)}, bf16[64,1664]{1,0:T(8,128)(2,1)S(1)}, u32[]{:S(2)}, u32[]{:S(2)}) collective-permute-start(bf16[64,1664]{1,0:T(8,128)(2,1)S(1)} %get-tuple-element.165), channel_id=1, source_target_pairs={{0,8},{1,9},{2,10},{3,11},{4,12},{5,13},{6,14},{7,15},{8,0},{9,1},... | collective-permute-start | bytes 638984 | tf_op jit(solution)/shard_map/ppermute | solution.py:69
  118.7 12.7 %collective-permute-start.26 = (bf16[64,1664]{1,0:T(8,128)(2,1)S(1)}, bf16[64,1664]{1,0:T(8,128)(2,1)S(1)}, u32[]{:S(2)}, u32[]{:S(2)}) collective-permute-start(bf16[64,1664]{1,0:T(8,128)(2,1)S(1)} %get-tuple-element.166), channel_id=1, source_target_pairs={{0,16},{1,17},{2,18},{3,19},{4,20},{5,21},{6,22},{7,23},{8,24},{9,... | collective-permute-start | bytes 638984 | tf_op jit(solution)/shard_map/ppermute | solution.py:69
  120.0 11.5 %collective-permute-start.27 = (bf16[64,1664]{1,0:T(8,128)(2,1)S(1)}, bf16[64,1664]{1,0:T(8,128)(2,1)S(1)}, u32[]{:S(2)}, u32[]{:S(2)}) collective-permute-start(bf16[64,1664]{1,0:T(8,128)(2,1)S(1)} %get-tuple-element.167), channel_id=1, source_target_pairs={{0,24},{1,25},{2,26},{3,27},{4,28},{5,29},{6,30},{7,31},{8,16},{9,... | collective-permute-start | bytes 638984 | tf_op jit(solution)/shard_map/ppermute | solution.py:69
  121.2 12.8 %collective-permute-start.31 = (bf16[16,4608]{1,0:T(8,128)(2,1)S(1)}, bf16[16,4608]{1,0:T(8,128)(2,1)S(1)}, u32[]{:S(2)}, u32[]{:S(2)}) collective-permute-start(bf16[16,4608]{1,0:T(8,128)(2,1)S(1)} %get-tuple-element.188), channel_id=1, source_target_pairs={{0,1},{1,2},{2,3},{3,0},{4,12},{5,13},{6,14},{7,15},{8,9},{9,10},{... | collective-permute-start | bytes 442376 | tf_op jit(solution)/shard_map/ppermute | solution.py:69
  121.4 14.5 %collective-permute-start.32 = (bf16[16,4608]{1,0:T(8,128)(2,1)S(1)}, bf16[16,4608]{1,0:T(8,128)(2,1)S(1)}, u32[]{:S(2)}, u32[]{:S(2)}) collective-permute-start(bf16[16,4608]{1,0:T(8,128)(2,1)S(1)} %get-tuple-element.189), channel_id=1, source_target_pairs={{0,2},{1,3},{2,0},{3,1},{4,20},{5,21},{6,22},{7,23},{8,10},{9,11},... | collective-permute-start | bytes 442376 | tf_op jit(solution)/shard_map/ppermute | solution.py:69
  125.4 10.5 %collective-permute-start.33 = (bf16[16,4608]{1,0:T(8,128)(2,1)S(1)}, bf16[16,4608]{1,0:T(8,128)(2,1)S(1)}, u32[]{:S(2)}, u32[]{:S(2)}) collective-permute-start(bf16[16,4608]{1,0:T(8,128)(2,1)S(1)} %get-tuple-element.190), channel_id=1, source_target_pairs={{0,3},{1,0},{2,1},{3,2},{4,28},{5,29},{6,30},{7,31},{8,11},{9,8},{... | collective-permute-start | bytes 442376 | tf_op jit(solution)/shard_map/ppermute | solution.py:69
  131.6 6.1 %collective-permute-start.28 = (bf16[16,1664]{1,0:T(8,128)(2,1)S(1)}, bf16[16,1664]{1,0:T(8,128)(2,1)S(1)}, u32[]{:S(2)}, u32[]{:S(2)}) collective-permute-start(bf16[16,1664]{1,0:T(8,128)(2,1)S(1)} %get-tuple-element.180), channel_id=1, source_target_pairs={{0,1},{1,2},{2,3},{3,0},{4,5},{5,6},{6,7},{7,4},{8,9},{9,10},{10,1... | collective-permute-start | bytes 159752 | tf_op jit(solution)/shard_map/ppermute | solution.py:69
  132.1 6.5 %collective-permute-start.29 = (bf16[16,1664]{1,0:T(8,128)(2,1)S(1)}, bf16[16,1664]{1,0:T(8,128)(2,1)S(1)}, u32[]{:S(2)}, u32[]{:S(2)}) collective-permute-start(bf16[16,1664]{1,0:T(8,128)(2,1)S(1)} %get-tuple-element.181), channel_id=1, source_target_pairs={{0,2},{1,3},{2,0},{3,1},{4,6},{5,7},{6,4},{7,5},{8,10},{9,11},{10,... | collective-permute-start | bytes 159752 | tf_op jit(solution)/shard_map/ppermute | solution.py:69
  134.0 4.6 %collective-permute-start.30 = (bf16[16,1664]{1,0:T(8,128)(2,1)S(1)}, bf16[16,1664]{1,0:T(8,128)(2,1)S(1)}, u32[]{:S(2)}, u32[]{:S(2)}) collective-permute-start(bf16[16,1664]{1,0:T(8,128)(2,1)S(1)} %get-tuple-element.182), channel_id=1, source_target_pairs={{0,3},{1,0},{2,1},{3,2},{4,7},{5,4},{6,5},{7,6},{8,11},{9,8},{10,9... | collective-permute-start | bytes 159752 | tf_op jit(solution)/shard_map/ppermute | solution.py:69
  (22 other events, 134.8 us)

commit v6 on v5

--- a/solution.py
+++ b/solution.py
@@ -404,8 +404,9 @@
             up = dot(low, wide[:, width + start : width + start + 512], 1, 0)
             square = up * up
             half = 0.5 + 0.5 * jnp.tanh(up * (GELU_ONE + GELU_CUBE * square))
-            active[span, part] = (up * half).astype(jnp.bfloat16)
-            slope = half + (half * (1.0 - half) * up) * (2.0 * GELU_ONE + 6.0 * GELU_CUBE * square)
+            act = up * half
+            active[span, part] = act.astype(jnp.bfloat16)
+            slope = half + act * ((1.0 - half) * (2.0 * GELU_ONE + 6.0 * GELU_CUBE * square))
             hidden_grad[span, part] = (dot(dy[span], contract[part], 1, 1) * slope).astype(jnp.bfloat16)
         back = dot(hidden_grad[span], wide[:, width:], 1, 1)
         gain_sum = gain_sum + jnp.sum(back * normed, axis=0, keepdims=True)
@@ -615,7 +616,7 @@
             pltpu.VMEM(norms.shape, norms.dtype),
             pltpu.SemaphoreType.DMA((2,)),
         ],
-        compiler_params=params(4),
+        compiler_params=params(60),
         name="pack",
     )(weight, norms)
 

time: 154 us -> 153 us (level)
    unnamed x43 -> x41, local copies, waits for them, and re-layouts: 4.8 us -> 4.04 us
  transfers between devices with their start and end apart: 34 -> 34, of which waited for: 16 -> 15; matrix products, arithmetic and copies ran while one was open for 2% -> 2% of each run, Pallas kernels for 37% -> 37%
where the time goes in v6:
time: 153 us
  Pallas kernels  79.7 us (52%)
  starting transfers between devices  35 us (23%)
  waiting for transfers between devices  17.5 us (11%)
  blocking collectives  13 us (8%)
  local copies, waits for them, and re-layouts  4.05 us (3%)
  other arithmetic  2.59 us (2%)
    ppermute x24, starting transfers between devices, over(): return lax.ppermute(value, AXES, self.pairs(move))  32.1 us
    pallas_call x1, Pallas kernels, attend(): pl.pallas_call(partial(attend_kernel, lay, len(pieces)), out_shape=(wide,...  21.1 us
    pallas_call x1, Pallas kernels, attend_back(): pl.pallas_call(attend_back_kernel, out_shape=jax.ShapeDtypeStruct((rows,...  18.8 us
    pallas_call x1, Pallas kernels, feed(): pl.pallas_call(partial(feed_kernel, lay, len(pieces), len(deep_pieces)),...  18.6 us
    all_to_all x1, blocking collectives, exchange(): return lax.all_to_all(value, AXES, 0, 0)  13 us
    ppermute x24, waiting for transfers between devices, over(): return lax.ppermute(value, AXES, self.pairs(move))  8.95 us
    ppermute x10, waiting for transfers between devices, to_core(): return lax.ppermute(value, AXES, self.pairs(lambda p, c, z: (p, 1 - c, z)))  8.51 us
    pallas_call x1, Pallas kernels, finish(): pl.pallas_call(finish_kernel, out_shape=[jax.ShapeDtypeStruct((rows, widt...  4.33 us
  transfers between devices with their start and end apart: 34, of which 15 were waited for; matrix products, arithmetic and copies ran while one was open for 2% of the time, Pallas kernels for 37%

profile of v6, /device:TPU:0, one launch (start us, length us, event | category | flops | bytes accessed | tf_op | source)
XLA Modules:
  0.0 152.8 jit_solution(4137473221164991835)
XLA Ops:
  0.7 1.6 %pack.1.refs_0_ = bf16[16,1664]{1,0:T(8,128)(2,1)} custom-call(f32[16,1536]{1,0:T(8,128)} %refs_0_.1, f32[4,16]{1,0:T(4,128)} %refs_4_.3), custom_call_target="tpu_custom_call" | custom-call | tf_op jit(solution)/shard_map/pack/pallas_call | solution.py:609
  2.2 5.1 %collective-permute-start.2 = (bf16[16,1664]{1,0:T(8,128)(2,1)}, bf16[16,1664]{1,0:T(8,128)(2,1)S(1)}, u32[]{:S(2)}, u32[]{:S(2)}) collective-permute-start(bf16[16,1664]{1,0:T(8,128)(2,1)} %pack.1.refs_0_), channel_id=1, source_target_pairs={{0,3},{1,0},{2,1},{3,2},{4,7},{5,4},{6,5},{7,6},{8,11},{9,8},{10,9... | collective-permute-start | bytes 159752 | tf_op jit(solution)/shard_map/ppermute | solution.py:69
  11.0 1.6 %collective-permute-done.1.refs_2_ = bf16[16,1664]{1,0:T(8,128)(2,1)S(1)} collective-permute-done((bf16[16,1664]{1,0:T(8,128)(2,1)}, bf16[16,1664]{1,0:T(8,128)(2,1)S(1)}, u32[]{:S(2)}, u32[]{:S(2)}) %collective-permute-start.1) | collective-permute-done | bytes 53280 | tf_op jit(solution)/shard_map/ppermute | solution.py:69
  13.5 1.5 %collective-permute-start.12 = (bf16[16,4608]{1,0:T(8,128)(2,1)S(1)}, bf16[16,4608]{1,0:T(8,128)(2,1)S(1)}, u32[]{:S(2)}, u32[]{:S(2)}) collective-permute-start(bf16[16,4608]{1,0:T(8,128)(2,1)S(1)} %slice_dynamic-update-slice_fusion.refs_0_), channel_id=1, source_target_pairs={{0,3},{1,0},{2,1},{3,2},{4,28},{5,29},{6,30},{7,31},{8,11},{9,8},{... | collective-permute-start | bytes 442376 | tf_op jit(solution)/shard_map/ppermute | solution.py:69
  15.9 2.5 %collective-permute-start.5 = (bf16[64,1664]{1,0:T(8,128)(2,1)S(1)}, bf16[64,1664]{1,0:T(8,128)(2,1)S(1)}, u32[]{:S(2)}, u32[]{:S(2)}) collective-permute-start(bf16[64,1664]{1,0:T(8,128)(2,1)S(1)} %column.2.refs_0_), channel_id=1, source_target_pairs={{0,24},{1,25},{2,26},{3,27},{4,28},{5,29},{6,30},{7,31},{8,16},{9,... | collective-permute-start | bytes 638984 | tf_op jit(solution)/shard_map/ppermute | solution.py:69
  19.5 1.9 %collective-permute-start.10 = (bf16[16,4608]{1,0:T(8,128)(2,1)S(1)}, bf16[16,4608]{1,0:T(8,128)(2,1)S(1)}, u32[]{:S(2)}, u32[]{:S(2)}) collective-permute-start(bf16[16,4608]{1,0:T(8,128)(2,1)S(1)} %slice_dynamic-update-slice_fusion.refs_0_), channel_id=1, source_target_pairs={{0,1},{1,2},{2,3},{3,0},{4,12},{5,13},{6,14},{7,15},{8,9},{9,10},{... | collective-permute-start | bytes 442376 | tf_op jit(solution)/shard_map/ppermute | solution.py:69
  21.3 1.2 copy-done.2
  22.6 1.2 copy-done.3
  24.5 1.1 arrange.1
  25.6 3.0 %collective-permute-done.11.refs_2_ = bf16[16,4608]{1,0:T(8,128)(2,1)S(1)} collective-permute-done((bf16[16,4608]{1,0:T(8,128)(2,1)S(1)}, bf16[16,4608]{1,0:T(8,128)(2,1)S(1)}, u32[]{:S(2)}, u32[]{:S(2)}) %collective-permute-start.11) | collective-permute-done | bytes 147488 | tf_op jit(solution)/shard_map/ppermute | solution.py:69
  28.9 2.5 %collective-permute-start.15 = (bf16[64,4608]{1,0:T(8,128)(2,1)S(1)}, bf16[64,4608]{1,0:T(8,128)(2,1)S(1)}, u32[]{:S(2)}, u32[]{:S(2)}) collective-permute-start(bf16[64,4608]{1,0:T(8,128)(2,1)S(1)} %column.3.refs_0_), channel_id=1, source_target_pairs={{0,24},{1,25},{2,26},{3,27},{4,7},{5,4},{6,5},{7,6},{8,16},{9,17},... | collective-permute-start | bytes 1769480 | tf_op jit(solution)/shard_map/ppermute | solution.py:69
  35.6 21.1 %attend.1 = (bf16[1056,1024]{1,0:T(8,128)(2,1)S(1)}, bf16[1056,1024]{1,0:T(8,128)(2,1)S(1)}, bf16[1056,1024]{1,0:T(8,128)(2,1)S(1)}, bf16[1056,512]{1,0:T(8,128)(2,1)S(1)}, f32[8,512]{1,0:T(8,128)S(1)}) custom-call(bf16[1056,512]{1,0:T(8,128)(2,1)S(1)} %get-tuple-element.128.x, s32[1056,128]{1,0:T(8,128)S(1)} %get-tuple-element.129.labels, ...), custom_call_target="tpu_custom_call" | custom-call | tf_op jit(solution)/shard_map/attend/pallas_call | solution.py:303
  57.7 1.1 collective-permute-done.17.refs_5_
  60.5 18.6 %feed.1 = (f32[1056,512]{1,0:T(8,128)S(1)}, f32[1056,512]{1,0:T(8,128)S(1)}, bf16[1056,512]{1,0:T(8,128)(2,1)S(1)}, bf16[1056,2048]{1,0:T(8,128)(2,1)S(1)}, bf16...) custom-call(bf16[1056,512]{1,0:T(8,128)(2,1)S(1)} %get-tuple-element, ...), custom_call_target="tpu_custom_call" | custom-call | tf_op jit(solution)/shard_map/feed/pallas_call | solution.py:458
  79.6 2.7 %mixed_back.1.dox = bf16[1056,1024]{1,0:T(8,128)(2,1)S(1)} custom-call(bf16[1056,512]{1,0:T(8,128)(2,1)S(1)} %get-tuple-element.148.middle_low, bf16[1056,512]{1,0:T(8,128)(2,1)S(1)} %get-tuple-element.138.mixed, bf16[512,512]{1,0:T(8,128)(2,1)S(1)} %get-tuple-element.149.out_weight), custom_call_target="tpu_custom_call" | custom-call | tf_op jit(solution)/shard_map/mixed_back/pallas_call | solution.py:504
  82.3 1.5 collective-permute-done.20.got
  84.3 1.5 collective-permute-start.21
  85.8 1.5 collective-permute-start.22
  87.9 18.8 %attend_back.1.packed = bf16[1056,1536]{1,0:T(8,128)(2,1)S(1)} custom-call(bf16[1056,1024]{1,0:T(8,128)(2,1)S(1)} %get-tuple-element.145.qx, bf16[1056,1024]{1,0:T(8,128)(2,1)S(1)} %get-tuple-element.146.kx, bf16[1056,1024]{1,0:T(8,128)(2,1)S(1)} %get-tuple-element.147.vx, bf16[1056,1024]{1,0:T(8,128)(2,1)S(1)} %mixed_back.1.dox), custom_call_target="tpu_custom_call" | custom-call | tf_op jit(solution)/shard_map/attend_back/pallas_call | solution.py:357
  106.7 3.2 %input_back.1 = (bf16[1056,512]{1,0:T(8,128)(2,1)S(1)}, f32[8,512]{1,0:T(8,128)S(1)}) custom-call(bf16[1056,512]{1,0:T(8,128)(2,1)S(1)} %get-tuple-element.128.x, bf16[1056,1536]{1,0:T(8,128)(2,1)S(1)} %attend_back.1.packed, f32[8,512]{1,0:T(8,128)S(1)} %get-tuple-element.140.gains, f32[1056,512]{1,0:T(8,128)S(1)} %get-tuple-element.158.middle_grad, ...), custom_call_target="tpu_custom_call" | custom-call | tf_op jit(solution)/shard_map/input_back/pallas_call | solution.py:576
  109.9 3.9 %project_back.1 = (bf16[4,64,1664]{2,1,0:T(8,128)(2,1)S(1)}, bf16[4,64,1664]{2,1,0:T(8,128)(2,1)S(1)}) custom-call(bf16[1056,512]{1,0:T(8,128)(2,1)S(1)} %get-tuple-element.128.x, bf16[1056,1536]{1,0:T(8,128)(2,1)S(1)} %attend_back.1.packed, f32[8,512]{1,0:T(8,128)S(1)} %get-tuple-element.140.gains, f32[8,512]{1,0:T(8,128)S(1)} %get-tuple-element.159.first_norms, ...), custom_call_target="tpu_custom_call" | custom-call | tf_op jit(solution)/shard_map/project_back/pallas_call | solution.py:542
  114.3 2.0 %collective-permute-done.24.got = bf16[4,64,1664]{2,1,0:T(8,128)(2,1)S(1)} collective-permute-done((bf16[4,64,1664]{2,1,0:T(8,128)(2,1)S(1)}, bf16[4,64,1664]{2,1,0:T(8,128)(2,1)S(1)}, u32[]{:S(2)}, u32[]{:S(2)}) %collective-permute-start.24) | collective-permute-done | bytes 852000 | tf_op jit(solution)/shard_map/ppermute | solution.py:72
  116.5 1.4 collective-permute-start.25
  118.0 1.5 collective-permute-start.26
  120.9 2.0 %collective-permute-start.32 = (bf16[16,4608]{1,0:T(8,128)(2,1)S(1)}, bf16[16,4608]{1,0:T(8,128)(2,1)S(1)}, u32[]{:S(2)}, u32[]{:S(2)}) collective-permute-start(bf16[16,4608]{1,0:T(8,128)(2,1)S(1)} %get-tuple-element.189), channel_id=1, source_target_pairs={{0,2},{1,3},{2,0},{3,1},{4,20},{5,21},{6,22},{7,23},{8,10},{9,11},... | collective-permute-start | bytes 442376 | tf_op jit(solution)/shard_map/ppermute | solution.py:69
  122.9 1.8 %collective-permute-done.25.refs_0_ = bf16[64,1664]{1,0:T(8,128)(2,1)S(1)} collective-permute-done((bf16[64,1664]{1,0:T(8,128)(2,1)S(1)}, bf16[64,1664]{1,0:T(8,128)(2,1)S(1)}, u32[]{:S(2)}, u32[]{:S(2)}) %collective-permute-start.25) | collective-permute-done | bytes 213024 | tf_op jit(solution)/shard_map/ppermute | solution.py:69
  124.7 1.8 %collective-permute-start.33 = (bf16[16,4608]{1,0:T(8,128)(2,1)S(1)}, bf16[16,4608]{1,0:T(8,128)(2,1)S(1)}, u32[]{:S(2)}, u32[]{:S(2)}) collective-permute-start(bf16[16,4608]{1,0:T(8,128)(2,1)S(1)} %get-tuple-element.190), channel_id=1, source_target_pairs={{0,3},{1,0},{2,1},{3,2},{4,28},{5,29},{6,30},{7,31},{8,11},{9,8},{... | collective-permute-start | bytes 442376 | tf_op jit(solution)/shard_map/ppermute | solution.py:69
  126.6 4.3 %finish.1 = (bf16[1044,512]{1,0:T(8,128)(2,1)}, bf16[1044,512]{1,0:T(8,128)(2,1)}) custom-call(f32[8,128]{1,0:T(8,128)S(1)} %get-tuple-element.117.begin, f32[1056,512]{1,0:T(8,128)S(1)} %get-tuple-element.168.middle, bf16[1056,2048]{1,0:T(8,128)(2,1)S(1)} %get-tuple-element.169.active, bf16[2048,512]{1,0:T(8,128)(2,1)S(1)} %get-tuple-element.170.contract, ...), custom_call_target="tpu_custom_call" | custom-call | tf_op jit(solution)/shard_map/finish/pallas_call | solution.py:221
  131.4 1.8 %collective-permute-start.29 = (bf16[16,1664]{1,0:T(8,128)(2,1)S(1)}, bf16[16,1664]{1,0:T(8,128)(2,1)S(1)}, u32[]{:S(2)}, u32[]{:S(2)}) collective-permute-start(bf16[16,1664]{1,0:T(8,128)(2,1)S(1)} %get-tuple-element.181), channel_id=1, source_target_pairs={{0,2},{1,3},{2,0},{3,1},{4,6},{5,7},{6,4},{7,5},{8,10},{9,11},{10,... | collective-permute-start | bytes 159752 | tf_op jit(solution)/shard_map/ppermute | solution.py:69
  133.2 2.1 %collective-permute-start.30 = (bf16[16,1664]{1,0:T(8,128)(2,1)S(1)}, bf16[16,1664]{1,0:T(8,128)(2,1)S(1)}, u32[]{:S(2)}, u32[]{:S(2)}) collective-permute-start(bf16[16,1664]{1,0:T(8,128)(2,1)S(1)} %get-tuple-element.182), channel_id=1, source_target_pairs={{0,3},{1,0},{2,1},{3,2},{4,7},{5,4},{6,5},{7,6},{8,11},{9,8},{10,9... | collective-permute-start | bytes 159752 | tf_op jit(solution)/shard_map/ppermute | solution.py:69
  135.3 1.1 moments.2
  138.9 13.0 %all_to_all.5.sums = f32[32,1,128]{2,1,0:T(1,128)S(1)} all-to-all(f32[32,1,128]{2,1,0:T(1,128)S(1)} %get-tuple-element.192), channel_id=1, replica_groups=mesh['dp'=8,'rep'=4] {'dp','rep'}, dimensions={0} | all-to-all | bytes 32768 | tf_op jit(solution)/shard_map/all_to_all | solution.py:806
  (100 shorter events, 21.8 us)
Async XLA Ops:
  2.2 8.8 %collective-permute-start.2 = (bf16[16,1664]{1,0:T(8,128)(2,1)}, bf16[16,1664]{1,0:T(8,128)(2,1)S(1)}, u32[]{:S(2)}, u32[]{:S(2)}) collective-permute-start(bf16[16,1664]{1,0:T(8,128)(2,1)} %pack.1.refs_0_), channel_id=1, source_target_pairs={{0,3},{1,0},{2,1},{3,2},{4,7},{5,4},{6,5},{7,6},{8,11},{9,8},{10,9... | collective-permute-start | bytes 159752 | tf_op jit(solution)/shard_map/ppermute | solution.py:69
  7.3 5.3 %collective-permute-start.1 = (bf16[16,1664]{1,0:T(8,128)(2,1)}, bf16[16,1664]{1,0:T(8,128)(2,1)S(1)}, u32[]{:S(2)}, u32[]{:S(2)}) collective-permute-start(bf16[16,1664]{1,0:T(8,128)(2,1)} %pack.1.refs_0_), channel_id=1, source_target_pairs={{0,2},{1,3},{2,0},{3,1},{4,6},{5,7},{6,4},{7,5},{8,10},{9,11},{10,... | collective-permute-start | bytes 159752 | tf_op jit(solution)/shard_map/ppermute | solution.py:69
  7.3 6.1 %collective-permute-start = (bf16[16,1664]{1,0:T(8,128)(2,1)}, bf16[16,1664]{1,0:T(8,128)(2,1)S(1)}, u32[]{:S(2)}, u32[]{:S(2)}) collective-permute-start(bf16[16,1664]{1,0:T(8,128)(2,1)} %pack.1.refs_0_), channel_id=1, source_target_pairs={{0,1},{1,2},{2,3},{3,0},{4,5},{5,6},{6,7},{7,4},{8,9},{9,10},{10,1... | collective-permute-start | bytes 159752 | tf_op jit(solution)/shard_map/ppermute | solution.py:69
  13.5 6.0 %collective-permute-start.12 = (bf16[16,4608]{1,0:T(8,128)(2,1)S(1)}, bf16[16,4608]{1,0:T(8,128)(2,1)S(1)}, u32[]{:S(2)}, u32[]{:S(2)}) collective-permute-start(bf16[16,4608]{1,0:T(8,128)(2,1)S(1)} %slice_dynamic-update-slice_fusion.refs_0_), channel_id=1, source_target_pairs={{0,3},{1,0},{2,1},{3,2},{4,28},{5,29},{6,30},{7,31},{8,11},{9,8},{... | collective-permute-start | bytes 442376 | tf_op jit(solution)/shard_map/ppermute | solution.py:69
  15.9 12.7 %collective-permute-start.5 = (bf16[64,1664]{1,0:T(8,128)(2,1)S(1)}, bf16[64,1664]{1,0:T(8,128)(2,1)S(1)}, u32[]{:S(2)}, u32[]{:S(2)}) collective-permute-start(bf16[64,1664]{1,0:T(8,128)(2,1)S(1)} %column.2.refs_0_), channel_id=1, source_target_pairs={{0,24},{1,25},{2,26},{3,27},{4,28},{5,29},{6,30},{7,31},{8,16},{9,... | collective-permute-start | bytes 638984 | tf_op jit(solution)/shard_map/ppermute | solution.py:69
  18.4 10.2 %collective-permute-start.4 = (bf16[64,1664]{1,0:T(8,128)(2,1)S(1)}, bf16[64,1664]{1,0:T(8,128)(2,1)S(1)}, u32[]{:S(2)}, u32[]{:S(2)}) collective-permute-start(bf16[64,1664]{1,0:T(8,128)(2,1)S(1)} %column.2.refs_0_), channel_id=1, source_target_pairs={{0,16},{1,17},{2,18},{3,19},{4,20},{5,21},{6,22},{7,23},{8,24},{9,... | collective-permute-start | bytes 638984 | tf_op jit(solution)/shard_map/ppermute | solution.py:69
  18.9 9.7 %collective-permute-start.3 = (bf16[64,1664]{1,0:T(8,128)(2,1)S(1)}, bf16[64,1664]{1,0:T(8,128)(2,1)S(1)}, u32[]{:S(2)}, u32[]{:S(2)}) collective-permute-start(bf16[64,1664]{1,0:T(8,128)(2,1)S(1)} %column.2.refs_0_), channel_id=1, source_target_pairs={{0,8},{1,9},{2,10},{3,11},{4,12},{5,13},{6,14},{7,15},{8,0},{9,1},... | collective-permute-start | bytes 638984 | tf_op jit(solution)/shard_map/ppermute | solution.py:69
  19.5 9.1 %collective-permute-start.11 = (bf16[16,4608]{1,0:T(8,128)(2,1)S(1)}, bf16[16,4608]{1,0:T(8,128)(2,1)S(1)}, u32[]{:S(2)}, u32[]{:S(2)}) collective-permute-start(bf16[16,4608]{1,0:T(8,128)(2,1)S(1)} %slice_dynamic-update-slice_fusion.refs_0_), channel_id=1, source_target_pairs={{0,2},{1,3},{2,0},{3,1},{4,20},{5,21},{6,22},{7,23},{8,10},{9,11},... | collective-permute-start | bytes 442376 | tf_op jit(solution)/shard_map/ppermute | solution.py:69
  19.5 9.1 %collective-permute-start.10 = (bf16[16,4608]{1,0:T(8,128)(2,1)S(1)}, bf16[16,4608]{1,0:T(8,128)(2,1)S(1)}, u32[]{:S(2)}, u32[]{:S(2)}) collective-permute-start(bf16[16,4608]{1,0:T(8,128)(2,1)S(1)} %slice_dynamic-update-slice_fusion.refs_0_), channel_id=1, source_target_pairs={{0,1},{1,2},{2,3},{3,0},{4,12},{5,13},{6,14},{7,15},{8,9},{9,10},{... | collective-permute-start | bytes 442376 | tf_op jit(solution)/shard_map/ppermute | solution.py:69
  28.9 27.9 %collective-permute-start.15 = (bf16[64,4608]{1,0:T(8,128)(2,1)S(1)}, bf16[64,4608]{1,0:T(8,128)(2,1)S(1)}, u32[]{:S(2)}, u32[]{:S(2)}) collective-permute-start(bf16[64,4608]{1,0:T(8,128)(2,1)S(1)} %column.3.refs_0_), channel_id=1, source_target_pairs={{0,24},{1,25},{2,26},{3,27},{4,7},{5,4},{6,5},{7,6},{8,16},{9,17},... | collective-permute-start | bytes 1769480 | tf_op jit(solution)/shard_map/ppermute | solution.py:69
  31.4 25.4 %collective-permute-start.14 = (bf16[64,4608]{1,0:T(8,128)(2,1)S(1)}, bf16[64,4608]{1,0:T(8,128)(2,1)S(1)}, u32[]{:S(2)}, u32[]{:S(2)}) collective-permute-start(bf16[64,4608]{1,0:T(8,128)(2,1)S(1)} %column.3.refs_0_), channel_id=1, source_target_pairs={{0,16},{1,17},{2,18},{3,19},{4,6},{5,7},{6,4},{7,5},{8,24},{9,25},... | collective-permute-start | bytes 1769480 | tf_op jit(solution)/shard_map/ppermute | solution.py:69
  31.9 24.9 %collective-permute-start.13 = (bf16[64,4608]{1,0:T(8,128)(2,1)S(1)}, bf16[64,4608]{1,0:T(8,128)(2,1)S(1)}, u32[]{:S(2)}, u32[]{:S(2)}) collective-permute-start(bf16[64,4608]{1,0:T(8,128)(2,1)S(1)} %column.3.refs_0_), channel_id=1, source_target_pairs={{0,8},{1,9},{2,10},{3,11},{4,5},{5,6},{6,7},{7,4},{8,0},{9,1},{10,... | collective-permute-start | bytes 1769480 | tf_op jit(solution)/shard_map/ppermute | solution.py:69
  32.4 1.5 collective-permute-start.6
  32.5 1.7 %collective-permute-start.9 = (bf16[64,1664]{1,0:T(8,128)(2,1)S(1)}, bf16[64,1664]{1,0:T(8,128)(2,1)S(1)}, u32[]{:S(2)}, u32[]{:S(2)}) collective-permute-start(bf16[64,1664]{1,0:T(8,128)(2,1)S(1)} %collective-permute-done.5.refs_3_), channel_id=1, source_target_pairs={{0,4},{1,5},{2,6},{3,7},{4,0},{5,1},{6,2},{7,3},{8,12},{9,13},{10,... | collective-permute-start | bytes 638984 | tf_op jit(solution)/shard_map/ppermute | solution.py:72
  35.3 22.4 %collective-permute-start.16 = (bf16[64,4608]{1,0:T(8,128)(2,1)S(1)}, bf16[64,4608]{1,0:T(8,128)(2,1)S(1)}, u32[]{:S(2)}, u32[]{:S(2)}) collective-permute-start(bf16[64,4608]{1,0:T(8,128)(2,1)S(1)} %column.3.refs_0_), channel_id=1, source_target_pairs={{0,4},{1,5},{2,6},{3,7},{4,0},{5,1},{6,2},{7,3},{8,12},{9,13},{10,... | collective-permute-start | bytes 1769480 | tf_op jit(solution)/shard_map/ppermute | solution.py:72
  56.8 2.1 %collective-permute-start.17 = (bf16[64,4608]{1,0:T(8,128)(2,1)S(1)}, bf16[64,4608]{1,0:T(8,128)(2,1)S(1)}, u32[]{:S(2)}, u32[]{:S(2)}) collective-permute-start(bf16[64,4608]{1,0:T(8,128)(2,1)S(1)} %collective-permute-done.13.refs_1_), channel_id=1, source_target_pairs={{0,4},{1,5},{2,6},{3,7},{4,0},{5,1},{6,2},{7,3},{8,12},{9,13},{10,... | collective-permute-start | bytes 1769480 | tf_op jit(solution)/shard_map/ppermute | solution.py:72
  57.2 2.5 %collective-permute-start.18 = (bf16[64,4608]{1,0:T(8,128)(2,1)S(1)}, bf16[64,4608]{1,0:T(8,128)(2,1)S(1)}, u32[]{:S(2)}, u32[]{:S(2)}) collective-permute-start(bf16[64,4608]{1,0:T(8,128)(2,1)S(1)} %collective-permute-done.14.refs_2_), channel_id=1, source_target_pairs={{0,4},{1,5},{2,6},{3,7},{4,0},{5,1},{6,2},{7,3},{8,12},{9,13},{10,... | collective-permute-start | bytes 1769480 | tf_op jit(solution)/shard_map/ppermute | solution.py:72
  57.3 3.2 %collective-permute-start.19 = (bf16[64,4608]{1,0:T(8,128)(2,1)S(1)}, bf16[64,4608]{1,0:T(8,128)(2,1)S(1)}, u32[]{:S(2)}, u32[]{:S(2)}) collective-permute-start(bf16[64,4608]{1,0:T(8,128)(2,1)S(1)} %collective-permute-done.15.refs_3_), channel_id=1, source_target_pairs={{0,4},{1,5},{2,6},{3,7},{4,0},{5,1},{6,2},{7,3},{8,12},{9,13},{10,... | collective-permute-start | bytes 1769480 | tf_op jit(solution)/shard_map/ppermute | solution.py:72
  79.2 4.6 %collective-permute-start.20 = (bf16[4,64,4608]{2,1,0:T(8,128)(2,1)S(1)}, bf16[4,64,4608]{2,1,0:T(8,128)(2,1)S(1)}, u32[]{:S(2)}, u32[]{:S(2)}) collective-permute-start(bf16[4,64,4608]{2,1,0:T(8,128)(2,1)S(1)} %get-tuple-element.151), channel_id=1, source_target_pairs={{0,4},{1,5},{2,6},{3,7},{4,0},{5,1},{6,2},{7,3},{8,12},{9,13},{10,... | collective-permute-start | bytes 7077896 | tf_op jit(solution)/shard_map/ppermute | solution.py:72
  84.3 29.5 %collective-permute-start.21 = (bf16[64,4608]{1,0:T(8,128)(2,1)S(1)}, bf16[64,4608]{1,0:T(8,128)(2,1)S(1)}, u32[]{:S(2)}, u32[]{:S(2)}) collective-permute-start(bf16[64,4608]{1,0:T(8,128)(2,1)S(1)} %get-tuple-element.154), channel_id=1, source_target_pairs={{0,8},{1,9},{2,10},{3,11},{4,5},{5,6},{6,7},{7,4},{8,0},{9,1},{10,... | collective-permute-start | bytes 1769480 | tf_op jit(solution)/shard_map/ppermute | solution.py:69
  85.8 28.0 %collective-permute-start.22 = (bf16[64,4608]{1,0:T(8,128)(2,1)S(1)}, bf16[64,4608]{1,0:T(8,128)(2,1)S(1)}, u32[]{:S(2)}, u32[]{:S(2)}) collective-permute-start(bf16[64,4608]{1,0:T(8,128)(2,1)S(1)} %get-tuple-element.155), channel_id=1, source_target_pairs={{0,16},{1,17},{2,18},{3,19},{4,6},{5,7},{6,4},{7,5},{8,24},{9,25},... | collective-permute-start | bytes 1769480 | tf_op jit(solution)/shard_map/ppermute | solution.py:69
  87.4 26.5 %collective-permute-start.23 = (bf16[64,4608]{1,0:T(8,128)(2,1)S(1)}, bf16[64,4608]{1,0:T(8,128)(2,1)S(1)}, u32[]{:S(2)}, u32[]{:S(2)}) collective-permute-start(bf16[64,4608]{1,0:T(8,128)(2,1)S(1)} %get-tuple-element.156), channel_id=1, source_target_pairs={{0,24},{1,25},{2,26},{3,27},{4,7},{5,4},{6,5},{7,6},{8,16},{9,17},... | collective-permute-start | bytes 1769480 | tf_op jit(solution)/shard_map/ppermute | solution.py:69
  113.8 2.5 %collective-permute-start.24 = (bf16[4,64,1664]{2,1,0:T(8,128)(2,1)S(1)}, bf16[4,64,1664]{2,1,0:T(8,128)(2,1)S(1)}, u32[]{:S(2)}, u32[]{:S(2)}) collective-permute-start(bf16[4,64,1664]{2,1,0:T(8,128)(2,1)S(1)} %get-tuple-element.164), channel_id=1, source_target_pairs={{0,4},{1,5},{2,6},{3,7},{4,0},{5,1},{6,2},{7,3},{8,12},{9,13},{10,... | collective-permute-start | bytes 2555912 | tf_op jit(solution)/shard_map/ppermute | solution.py:72
  116.5 8.2 %collective-permute-start.25 = (bf16[64,1664]{1,0:T(8,128)(2,1)S(1)}, bf16[64,1664]{1,0:T(8,128)(2,1)S(1)}, u32[]{:S(2)}, u32[]{:S(2)}) collective-permute-start(bf16[64,1664]{1,0:T(8,128)(2,1)S(1)} %get-tuple-element.165), channel_id=1, source_target_pairs={{0,8},{1,9},{2,10},{3,11},{4,12},{5,13},{6,14},{7,15},{8,0},{9,1},... | collective-permute-start | bytes 638984 | tf_op jit(solution)/shard_map/ppermute | solution.py:69
  118.0 13.0 %collective-permute-start.26 = (bf16[64,1664]{1,0:T(8,128)(2,1)S(1)}, bf16[64,1664]{1,0:T(8,128)(2,1)S(1)}, u32[]{:S(2)}, u32[]{:S(2)}) collective-permute-start(bf16[64,1664]{1,0:T(8,128)(2,1)S(1)} %get-tuple-element.166), channel_id=1, source_target_pairs={{0,16},{1,17},{2,18},{3,19},{4,20},{5,21},{6,22},{7,23},{8,24},{9,... | collective-permute-start | bytes 638984 | tf_op jit(solution)/shard_map/ppermute | solution.py:69
  119.5 11.5 %collective-permute-start.27 = (bf16[64,1664]{1,0:T(8,128)(2,1)S(1)}, bf16[64,1664]{1,0:T(8,128)(2,1)S(1)}, u32[]{:S(2)}, u32[]{:S(2)}) collective-permute-start(bf16[64,1664]{1,0:T(8,128)(2,1)S(1)} %get-tuple-element.167), channel_id=1, source_target_pairs={{0,24},{1,25},{2,26},{3,27},{4,28},{5,29},{6,30},{7,31},{8,16},{9,... | collective-permute-start | bytes 638984 | tf_op jit(solution)/shard_map/ppermute | solution.py:69
  120.5 12.7 %collective-permute-start.31 = (bf16[16,4608]{1,0:T(8,128)(2,1)S(1)}, bf16[16,4608]{1,0:T(8,128)(2,1)S(1)}, u32[]{:S(2)}, u32[]{:S(2)}) collective-permute-start(bf16[16,4608]{1,0:T(8,128)(2,1)S(1)} %get-tuple-element.188), channel_id=1, source_target_pairs={{0,1},{1,2},{2,3},{3,0},{4,12},{5,13},{6,14},{7,15},{8,9},{9,10},{... | collective-permute-start | bytes 442376 | tf_op jit(solution)/shard_map/ppermute | solution.py:69
  120.9 14.3 %collective-permute-start.32 = (bf16[16,4608]{1,0:T(8,128)(2,1)S(1)}, bf16[16,4608]{1,0:T(8,128)(2,1)S(1)}, u32[]{:S(2)}, u32[]{:S(2)}) collective-permute-start(bf16[16,4608]{1,0:T(8,128)(2,1)S(1)} %get-tuple-element.189), channel_id=1, source_target_pairs={{0,2},{1,3},{2,0},{3,1},{4,20},{5,21},{6,22},{7,23},{8,10},{9,11},... | collective-permute-start | bytes 442376 | tf_op jit(solution)/shard_map/ppermute | solution.py:69
  124.7 10.6 %collective-permute-start.33 = (bf16[16,4608]{1,0:T(8,128)(2,1)S(1)}, bf16[16,4608]{1,0:T(8,128)(2,1)S(1)}, u32[]{:S(2)}, u32[]{:S(2)}) collective-permute-start(bf16[16,4608]{1,0:T(8,128)(2,1)S(1)} %get-tuple-element.190), channel_id=1, source_target_pairs={{0,3},{1,0},{2,1},{3,2},{4,28},{5,29},{6,30},{7,31},{8,11},{9,8},{... | collective-permute-start | bytes 442376 | tf_op jit(solution)/shard_map/ppermute | solution.py:69
  131.1 6.1 %collective-permute-start.28 = (bf16[16,1664]{1,0:T(8,128)(2,1)S(1)}, bf16[16,1664]{1,0:T(8,128)(2,1)S(1)}, u32[]{:S(2)}, u32[]{:S(2)}) collective-permute-start(bf16[16,1664]{1,0:T(8,128)(2,1)S(1)} %get-tuple-element.180), channel_id=1, source_target_pairs={{0,1},{1,2},{2,3},{3,0},{4,5},{5,6},{6,7},{7,4},{8,9},{9,10},{10,1... | collective-permute-start | bytes 159752 | tf_op jit(solution)/shard_map/ppermute | solution.py:69
  131.4 6.7 %collective-permute-start.29 = (bf16[16,1664]{1,0:T(8,128)(2,1)S(1)}, bf16[16,1664]{1,0:T(8,128)(2,1)S(1)}, u32[]{:S(2)}, u32[]{:S(2)}) collective-permute-start(bf16[16,1664]{1,0:T(8,128)(2,1)S(1)} %get-tuple-element.181), channel_id=1, source_target_pairs={{0,2},{1,3},{2,0},{3,1},{4,6},{5,7},{6,4},{7,5},{8,10},{9,11},{10,... | collective-permute-start | bytes 159752 | tf_op jit(solution)/shard_map/ppermute | solution.py:69
  133.2 4.9 %collective-permute-start.30 = (bf16[16,1664]{1,0:T(8,128)(2,1)S(1)}, bf16[16,1664]{1,0:T(8,128)(2,1)S(1)}, u32[]{:S(2)}, u32[]{:S(2)}) collective-permute-start(bf16[16,1664]{1,0:T(8,128)(2,1)S(1)} %get-tuple-element.182), channel_id=1, source_target_pairs={{0,3},{1,0},{2,1},{3,2},{4,7},{5,4},{6,5},{7,6},{8,11},{9,8},{10,9... | collective-permute-start | bytes 159752 | tf_op jit(solution)/shard_map/ppermute | solution.py:69
  (21 other events, 129.0 us)

commit v7 on v6

--- a/solution.py
+++ b/solution.py
@@ -584,41 +584,52 @@
     )(x, packed, gains, middle_grad, *pieces)
 
 
-def pack_kernel(weight, norms, out, weight_here, norms_here, done):
-    copies = [
-        pltpu.make_async_copy(norms, norms_here, done.at[0]),
-        pltpu.make_async_copy(weight, weight_here, done.at[1]),
-    ]
+def pack_kernel(*refs):
+    count = 5
+    sources, (first, second), here, done = refs[:count], refs[count : count + 2], refs[count + 2 : -1], refs[-1]
+    copies = [pltpu.make_async_copy(source, local, done.at[i]) for i, (source, local) in enumerate(zip(sources, here))]
     for copy in copies:
         copy.start()
-    rows, width = weight_here.shape
+    norms, weight, out_weight, expand, contract = here
+    rows, width = weight.shape
+    depth, hidden = out_weight.shape[1], expand.shape[1]
     same = lax.broadcasted_iota(jnp.int32, (rows, rows), 0) == lax.broadcasted_iota(jnp.int32, (rows, rows), 1)
     lane = lax.broadcasted_iota(jnp.int32, (rows, LANES), 1)
     tile = jnp.zeros((rows, LANES), jnp.float32)
     copies[0].wait()
-    for j in range(norms_here.shape[0]):
-        column = jnp.sum(jnp.where(same, norms_here[j : j + 1, :], 0.0), axis=1, keepdims=True)
+    for j in range(norms.shape[0]):
+        column = jnp.sum(jnp.where(same, norms[j : j + 1, :], 0.0), axis=1, keepdims=True)
         tile = jnp.where(lane == j, column, tile)
-    out[:, width:] = tile.astype(out.dtype)
+    first[:, width:] = tile.astype(first.dtype)
     copies[1].wait()
-    out[:, :width] = weight_here[...].astype(out.dtype)
-
-
-def pack(weight, norms):
+    first[:, :width] = weight[...].astype(first.dtype)
+    copies[2].wait()
+    second[:, :depth] = out_weight[...].astype(second.dtype)
+    copies[3].wait()
+    second[:, depth : depth + hidden] = expand[...].astype(second.dtype)
+    copies[4].wait()
+    for j in range(4):
+        at = depth + hidden + j * depth
+        second[:, at : at + depth] = contract[j * rows : (j + 1) * rows].astype(second.dtype)
+
+
+def pack(norms, weight, out_weight, expand, contract):
     rows, width = weight.shape
+    sources = (norms, weight, out_weight, expand, contract)
+    rest = out_weight.shape[1] + expand.shape[1] + 4 * contract.shape[1]
     return pl.pallas_call(
         pack_kernel,
-        out_shape=jax.ShapeDtypeStruct((rows, width + LANES), jnp.bfloat16),
-        in_specs=[pl.BlockSpec(memory_space=pltpu.MemorySpace.HBM)] * 2,
-        out_specs=pl.BlockSpec(memory_space=VMEM),
-        scratch_shapes=[
-            pltpu.VMEM(weight.shape, weight.dtype),
-            pltpu.VMEM(norms.shape, norms.dtype),
-            pltpu.SemaphoreType.DMA((2,)),
-        ],
+        out_shape=(
+            jax.ShapeDtypeStruct((rows, width + LANES), jnp.bfloat16),
+            jax.ShapeDtypeStruct((rows, rest), jnp.bfloat16),
+        ),
+        in_specs=[pl.BlockSpec(memory_space=pltpu.MemorySpace.HBM)] * len(sources),
+        out_specs=[pl.BlockSpec(memory_space=VMEM)] * 2,
+        scratch_shapes=[pltpu.VMEM(source.shape, source.dtype) for source in sources]
+        + [pltpu.SemaphoreType.DMA((len(sources),))],
         compiler_params=params(60),
         name="pack",
-    )(weight, norms)
+    )(*sources)
 
 
 def column_kernel(lay, *refs):
@@ -836,12 +847,9 @@
     own = attend_in.shape[0]
     count = lay.dp * lay.rep
     whole_tiles = own % 16 == 0
-    shard1 = pack(attend_in, layer_norms)
+    shard1, shard2 = pack(layer_norms, attend_in, attend_out, expand, contract)
     column1 = over(plain, shard1, True)
     rows = inputs.shape[1]
-    attend_out_, expand_, contract_ = after([attend_out, expand, contract], [shard1])
-    deep = [contract_[j * own : (j + 1) * own] for j in range(4)]
-    shard2 = jnp.concatenate([part.astype(jnp.bfloat16) for part in (attend_out_, expand_, *deep)], axis=1)
     (shard2,) = after([shard2], column1[1:])
     column2 = over(twin, shard2, True)
     blocks1 = over(plain, column_of(plain, column1), False)

time: 153 us -> 154 us (level)
  waiting for transfers between devices: 17.5 us -> 21.1 us
  other arithmetic: 2.59 us -> 0 us
    ppermute x24, waiting for transfers between devices: 8.95 us -> 12.1 us  [over(): return lax.ppermute(value, AXES, self.pairs(move))]
    unnamed x2 -> x0, other arithmetic: 1.68 us -> none
    unnamed x41 -> x40, local copies, waits for them, and re-layouts: 4.04 us -> 4.04 us
  transfers between devices with their start and end apart: 34 -> 34, of which waited for: 15 -> 17; matrix products, arithmetic and copies ran while one was open for 2% -> 0% of each run, Pallas kernels for 37% -> 37%
where the time goes in v7:
time: 154 us; the launch traced here: 153 us
  Pallas kernels  79.9 us (52%)
  starting transfers between devices  34.2 us (22%)
  waiting for transfers between devices  21.1 us (14%)
  blocking collectives  13 us (8%)
  local copies, waits for them, and re-layouts  4.04 us (3%)
    ppermute x24, starting transfers between devices, over(): return lax.ppermute(value, AXES, self.pairs(move))  31.9 us
    pallas_call x1, Pallas kernels, attend(): pl.pallas_call(partial(attend_kernel, lay, len(pieces)), out_shape=(wide,...  21.1 us
    pallas_call x1, Pallas kernels, attend_back(): pl.pallas_call(attend_back_kernel, out_shape=jax.ShapeDtypeStruct((rows,...  18.8 us
    pallas_call x1, Pallas kernels, feed(): pl.pallas_call(partial(feed_kernel, lay, len(pieces), len(deep_pieces)),...  18.7 us
    all_to_all x1, blocking collectives, exchange(): return lax.all_to_all(value, AXES, 0, 0)  13 us
    ppermute x24, waiting for transfers between devices, over(): return lax.ppermute(value, AXES, self.pairs(move))  12.1 us
    ppermute x10, waiting for transfers between devices, to_core(): return lax.ppermute(value, AXES, self.pairs(lambda p, c, z: (p, 1 - c, z)))  8.99 us
    pallas_call x1, Pallas kernels, finish(): pl.pallas_call(finish_kernel, out_shape=[jax.ShapeDtypeStruct((rows, widt...  4.33 us
  transfers between devices with their start and end apart: 34, of which 17 were waited for; matrix products, arithmetic and copies ran while one was open for 0% of the time, Pallas kernels for 37%

profile of v7, /device:TPU:0, one launch (start us, length us, event | category | flops | bytes accessed | tf_op | source)
XLA Modules:
  0.0 153.3 jit_solution(1278796096470693299)
XLA Ops:
  0.7 1.8 %pack.1 = (bf16[16,1664]{1,0:T(8,128)(2,1)}, bf16[16,4608]{1,0:T(8,128)(2,1)}) custom-call(f32[4,16]{1,0:T(4,128)} %refs_4_.5, f32[16,1536]{1,0:T(8,128)} %refs_0_.3, f32[16,512]{1,0:T(8,128)} %refs_1_.3, f32[16,2048]{1,0:T(8,128)} %refs_2_.3, f32[64,512]{1,0:T(8,128)} %refs_3_.3), custom_call_target="tpu_custom_call" | custom-call | tf_op jit(solution)/shard_map/pack/pallas_call | solution.py:620
  2.5 5.1 %collective-permute-start.2 = (bf16[16,1664]{1,0:T(8,128)(2,1)}, bf16[16,1664]{1,0:T(8,128)(2,1)S(1)}, u32[]{:S(2)}, u32[]{:S(2)}) collective-permute-start(bf16[16,1664]{1,0:T(8,128)(2,1)} %get-tuple-element.115.refs_0_), channel_id=1, source_target_pairs={{0,3},{1,0},{2,1},{3,2},{4,7},{5,4},{6,5},{7,6},{8,11},{9,8},{10,9... | collective-permute-start | bytes 159752 | tf_op jit(solution)/shard_map/ppermute | solution.py:69
  8.6 1.5 collective-permute-done.2.refs_3_
  10.1 2.8 %collective-permute-done.1.refs_2_ = bf16[16,1664]{1,0:T(8,128)(2,1)S(1)} collective-permute-done((bf16[16,1664]{1,0:T(8,128)(2,1)}, bf16[16,1664]{1,0:T(8,128)(2,1)S(1)}, u32[]{:S(2)}, u32[]{:S(2)}) %collective-permute-start.1) | collective-permute-done | bytes 53280 | tf_op jit(solution)/shard_map/ppermute | solution.py:69
  13.7 1.5 %collective-permute-start.12 = (bf16[16,4608]{1,0:T(8,128)(2,1)}, bf16[16,4608]{1,0:T(8,128)(2,1)S(1)}, u32[]{:S(2)}, u32[]{:S(2)}) collective-permute-start(bf16[16,4608]{1,0:T(8,128)(2,1)} %get-tuple-element.122.refs_0_), channel_id=1, source_target_pairs={{0,3},{1,0},{2,1},{3,2},{4,28},{5,29},{6,30},{7,31},{8,11},{9,8},{... | collective-permute-start | bytes 442376 | tf_op jit(solution)/shard_map/ppermute | solution.py:69
  16.1 2.5 %collective-permute-start.5 = (bf16[64,1664]{1,0:T(8,128)(2,1)S(1)}, bf16[64,1664]{1,0:T(8,128)(2,1)S(1)}, u32[]{:S(2)}, u32[]{:S(2)}) collective-permute-start(bf16[64,1664]{1,0:T(8,128)(2,1)S(1)} %column.2.refs_0_), channel_id=1, source_target_pairs={{0,24},{1,25},{2,26},{3,27},{4,28},{5,29},{6,30},{7,31},{8,16},{9,... | collective-permute-start | bytes 638984 | tf_op jit(solution)/shard_map/ppermute | solution.py:69
  19.7 1.9 %collective-permute-start.10 = (bf16[16,4608]{1,0:T(8,128)(2,1)}, bf16[16,4608]{1,0:T(8,128)(2,1)S(1)}, u32[]{:S(2)}, u32[]{:S(2)}) collective-permute-start(bf16[16,4608]{1,0:T(8,128)(2,1)} %get-tuple-element.122.refs_0_), channel_id=1, source_target_pairs={{0,1},{1,2},{2,3},{3,0},{4,12},{5,13},{6,14},{7,15},{8,9},{9,10},{... | collective-permute-start | bytes 442376 | tf_op jit(solution)/shard_map/ppermute | solution.py:69
  21.6 1.2 copy-done.2
  22.8 1.2 copy-done.3
  24.7 1.1 arrange.1
  25.8 3.2 %collective-permute-done.11.refs_2_ = bf16[16,4608]{1,0:T(8,128)(2,1)S(1)} collective-permute-done((bf16[16,4608]{1,0:T(8,128)(2,1)}, bf16[16,4608]{1,0:T(8,128)(2,1)S(1)}, u32[]{:S(2)}, u32[]{:S(2)}) %collective-permute-start.11) | collective-permute-done | bytes 147488 | tf_op jit(solution)/shard_map/ppermute | solution.py:69
  29.3 2.5 %collective-permute-start.15 = (bf16[64,4608]{1,0:T(8,128)(2,1)S(1)}, bf16[64,4608]{1,0:T(8,128)(2,1)S(1)}, u32[]{:S(2)}, u32[]{:S(2)}) collective-permute-start(bf16[64,4608]{1,0:T(8,128)(2,1)S(1)} %column.3.refs_0_), channel_id=1, source_target_pairs={{0,24},{1,25},{2,26},{3,27},{4,7},{5,4},{6,5},{7,6},{8,16},{9,17},... | collective-permute-start | bytes 1769480 | tf_op jit(solution)/shard_map/ppermute | solution.py:69
  36.1 21.1 %attend.1 = (bf16[1056,1024]{1,0:T(8,128)(2,1)S(1)}, bf16[1056,1024]{1,0:T(8,128)(2,1)S(1)}, bf16[1056,1024]{1,0:T(8,128)(2,1)S(1)}, bf16[1056,512]{1,0:T(8,128)(2,1)S(1)}, f32[8,512]{1,0:T(8,128)S(1)}) custom-call(bf16[1056,512]{1,0:T(8,128)(2,1)S(1)} %get-tuple-element.126.x, s32[1056,128]{1,0:T(8,128)S(1)} %get-tuple-element.127.labels, ...), custom_call_target="tpu_custom_call" | custom-call | tf_op jit(solution)/shard_map/attend/pallas_call | solution.py:303
  58.0 1.3 collective-permute-done.17.refs_5_
  61.0 18.7 %feed.1 = (f32[1056,512]{1,0:T(8,128)S(1)}, f32[1056,512]{1,0:T(8,128)S(1)}, bf16[1056,512]{1,0:T(8,128)(2,1)S(1)}, bf16[1056,2048]{1,0:T(8,128)(2,1)S(1)}, bf16...) custom-call(bf16[1056,512]{1,0:T(8,128)(2,1)S(1)} %get-tuple-element, ...), custom_call_target="tpu_custom_call" | custom-call | tf_op jit(solution)/shard_map/feed/pallas_call | solution.py:458
  79.9 2.7 %mixed_back.1.dox = bf16[1056,1024]{1,0:T(8,128)(2,1)S(1)} custom-call(bf16[1056,512]{1,0:T(8,128)(2,1)S(1)} %get-tuple-element.146.middle_low, bf16[1056,512]{1,0:T(8,128)(2,1)S(1)} %get-tuple-element.136.mixed, bf16[512,512]{1,0:T(8,128)(2,1)S(1)} %get-tuple-element.147.out_weight), custom_call_target="tpu_custom_call" | custom-call | tf_op jit(solution)/shard_map/mixed_back/pallas_call | solution.py:504
  82.6 1.6 %collective-permute-done.20.got = bf16[4,64,4608]{2,1,0:T(8,128)(2,1)S(1)} collective-permute-done((bf16[4,64,4608]{2,1,0:T(8,128)(2,1)S(1)}, bf16[4,64,4608]{2,1,0:T(8,128)(2,1)S(1)}, u32[]{:S(2)}, u32[]{:S(2)}) %collective-permute-start.20) | collective-permute-done | bytes 2359328 | tf_op jit(solution)/shard_map/ppermute | solution.py:72
  84.7 1.5 %collective-permute-start.21 = (bf16[64,4608]{1,0:T(8,128)(2,1)S(1)}, bf16[64,4608]{1,0:T(8,128)(2,1)S(1)}, u32[]{:S(2)}, u32[]{:S(2)}) collective-permute-start(bf16[64,4608]{1,0:T(8,128)(2,1)S(1)} %get-tuple-element.152), channel_id=1, source_target_pairs={{0,8},{1,9},{2,10},{3,11},{4,5},{5,6},{6,7},{7,4},{8,0},{9,1},{10,... | collective-permute-start | bytes 1769480 | tf_op jit(solution)/shard_map/ppermute | solution.py:69
  86.3 1.5 collective-permute-start.22
  88.3 18.8 %attend_back.1.packed = bf16[1056,1536]{1,0:T(8,128)(2,1)S(1)} custom-call(bf16[1056,1024]{1,0:T(8,128)(2,1)S(1)} %get-tuple-element.143.qx, bf16[1056,1024]{1,0:T(8,128)(2,1)S(1)} %get-tuple-element.144.kx, bf16[1056,1024]{1,0:T(8,128)(2,1)S(1)} %get-tuple-element.145.vx, bf16[1056,1024]{1,0:T(8,128)(2,1)S(1)} %mixed_back.1.dox), custom_call_target="tpu_custom_call" | custom-call | tf_op jit(solution)/shard_map/attend_back/pallas_call | solution.py:357
  107.1 3.2 %input_back.1 = (bf16[1056,512]{1,0:T(8,128)(2,1)S(1)}, f32[8,512]{1,0:T(8,128)S(1)}) custom-call(bf16[1056,512]{1,0:T(8,128)(2,1)S(1)} %get-tuple-element.126.x, bf16[1056,1536]{1,0:T(8,128)(2,1)S(1)} %attend_back.1.packed, f32[8,512]{1,0:T(8,128)S(1)} %get-tuple-element.138.gains, f32[1056,512]{1,0:T(8,128)S(1)} %get-tuple-element.156.middle_grad, ...), custom_call_target="tpu_custom_call" | custom-call | tf_op jit(solution)/shard_map/input_back/pallas_call | solution.py:576
  110.3 3.9 %project_back.1 = (bf16[4,64,1664]{2,1,0:T(8,128)(2,1)S(1)}, bf16[4,64,1664]{2,1,0:T(8,128)(2,1)S(1)}) custom-call(bf16[1056,512]{1,0:T(8,128)(2,1)S(1)} %get-tuple-element.126.x, bf16[1056,1536]{1,0:T(8,128)(2,1)S(1)} %attend_back.1.packed, f32[8,512]{1,0:T(8,128)S(1)} %get-tuple-element.138.gains, f32[8,512]{1,0:T(8,128)S(1)} %get-tuple-element.157.first_norms, ...), custom_call_target="tpu_custom_call" | custom-call | tf_op jit(solution)/shard_map/project_back/pallas_call | solution.py:542
  114.5 2.2 %collective-permute-done.24.got = bf16[4,64,1664]{2,1,0:T(8,128)(2,1)S(1)} collective-permute-done((bf16[4,64,1664]{2,1,0:T(8,128)(2,1)S(1)}, bf16[4,64,1664]{2,1,0:T(8,128)(2,1)S(1)}, u32[]{:S(2)}, u32[]{:S(2)}) %collective-permute-start.24) | collective-permute-done | bytes 852000 | tf_op jit(solution)/shard_map/ppermute | solution.py:72
  116.9 1.6 %collective-permute-start.25 = (bf16[64,1664]{1,0:T(8,128)(2,1)S(1)}, bf16[64,1664]{1,0:T(8,128)(2,1)S(1)}, u32[]{:S(2)}, u32[]{:S(2)}) collective-permute-start(bf16[64,1664]{1,0:T(8,128)(2,1)S(1)} %get-tuple-element.163), channel_id=1, source_target_pairs={{0,8},{1,9},{2,10},{3,11},{4,12},{5,13},{6,14},{7,15},{8,0},{9,1},... | collective-permute-start | bytes 638984 | tf_op jit(solution)/shard_map/ppermute | solution.py:69
  118.4 1.5 collective-permute-start.26
  121.2 1.8 %collective-permute-start.32 = (bf16[16,4608]{1,0:T(8,128)(2,1)S(1)}, bf16[16,4608]{1,0:T(8,128)(2,1)S(1)}, u32[]{:S(2)}, u32[]{:S(2)}) collective-permute-start(bf16[16,4608]{1,0:T(8,128)(2,1)S(1)} %get-tuple-element.187), channel_id=1, source_target_pairs={{0,2},{1,3},{2,0},{3,1},{4,20},{5,21},{6,22},{7,23},{8,10},{9,11},... | collective-permute-start | bytes 442376 | tf_op jit(solution)/shard_map/ppermute | solution.py:69
  123.0 2.0 %collective-permute-done.25.refs_0_ = bf16[64,1664]{1,0:T(8,128)(2,1)S(1)} collective-permute-done((bf16[64,1664]{1,0:T(8,128)(2,1)S(1)}, bf16[64,1664]{1,0:T(8,128)(2,1)S(1)}, u32[]{:S(2)}, u32[]{:S(2)}) %collective-permute-start.25) | collective-permute-done | bytes 213024 | tf_op jit(solution)/shard_map/ppermute | solution.py:69
  125.0 1.6 %collective-permute-start.33 = (bf16[16,4608]{1,0:T(8,128)(2,1)S(1)}, bf16[16,4608]{1,0:T(8,128)(2,1)S(1)}, u32[]{:S(2)}, u32[]{:S(2)}) collective-permute-start(bf16[16,4608]{1,0:T(8,128)(2,1)S(1)} %get-tuple-element.188), channel_id=1, source_target_pairs={{0,3},{1,0},{2,1},{3,2},{4,28},{5,29},{6,30},{7,31},{8,11},{9,8},{... | collective-permute-start | bytes 442376 | tf_op jit(solution)/shard_map/ppermute | solution.py:69
  126.7 4.3 %finish.1 = (bf16[1044,512]{1,0:T(8,128)(2,1)}, bf16[1044,512]{1,0:T(8,128)(2,1)}) custom-call(f32[8,128]{1,0:T(8,128)S(1)} %get-tuple-element.117.begin, f32[1056,512]{1,0:T(8,128)S(1)} %get-tuple-element.166.middle, bf16[1056,2048]{1,0:T(8,128)(2,1)S(1)} %get-tuple-element.167.active, bf16[2048,512]{1,0:T(8,128)(2,1)S(1)} %get-tuple-element.168.contract, ...), custom_call_target="tpu_custom_call" | custom-call | tf_op jit(solution)/shard_map/finish/pallas_call | solution.py:221
  132.1 1.4 collective-permute-start.29
  133.4 2.8 %collective-permute-start.30 = (bf16[16,1664]{1,0:T(8,128)(2,1)S(1)}, bf16[16,1664]{1,0:T(8,128)(2,1)S(1)}, u32[]{:S(2)}, u32[]{:S(2)}) collective-permute-start(bf16[16,1664]{1,0:T(8,128)(2,1)S(1)} %get-tuple-element.180), channel_id=1, source_target_pairs={{0,3},{1,0},{2,1},{3,2},{4,7},{5,4},{6,5},{7,6},{8,11},{9,8},{10,9... | collective-permute-start | bytes 159752 | tf_op jit(solution)/shard_map/ppermute | solution.py:69
  139.3 13.0 %all_to_all.5.sums = f32[32,1,128]{2,1,0:T(1,128)S(1)} all-to-all(f32[32,1,128]{2,1,0:T(1,128)S(1)} %get-tuple-element.190), channel_id=1, replica_groups=mesh['dp'=8,'rep'=4] {'dp','rep'}, dimensions={0} | all-to-all | bytes 32768 | tf_op jit(solution)/shard_map/all_to_all | solution.py:817
  (95 shorter events, 19.5 us)
Async XLA Ops:
  2.5 7.6 %collective-permute-start.2 = (bf16[16,1664]{1,0:T(8,128)(2,1)}, bf16[16,1664]{1,0:T(8,128)(2,1)S(1)}, u32[]{:S(2)}, u32[]{:S(2)}) collective-permute-start(bf16[16,1664]{1,0:T(8,128)(2,1)} %get-tuple-element.115.refs_0_), channel_id=1, source_target_pairs={{0,3},{1,0},{2,1},{3,2},{4,7},{5,4},{6,5},{7,6},{8,11},{9,8},{10,9... | collective-permute-start | bytes 159752 | tf_op jit(solution)/shard_map/ppermute | solution.py:69
  7.6 5.3 %collective-permute-start.1 = (bf16[16,1664]{1,0:T(8,128)(2,1)}, bf16[16,1664]{1,0:T(8,128)(2,1)S(1)}, u32[]{:S(2)}, u32[]{:S(2)}) collective-permute-start(bf16[16,1664]{1,0:T(8,128)(2,1)} %get-tuple-element.115.refs_0_), channel_id=1, source_target_pairs={{0,2},{1,3},{2,0},{3,1},{4,6},{5,7},{6,4},{7,5},{8,10},{9,11},{10,... | collective-permute-start | bytes 159752 | tf_op jit(solution)/shard_map/ppermute | solution.py:69
  7.6 6.1 %collective-permute-start = (bf16[16,1664]{1,0:T(8,128)(2,1)}, bf16[16,1664]{1,0:T(8,128)(2,1)S(1)}, u32[]{:S(2)}, u32[]{:S(2)}) collective-permute-start(bf16[16,1664]{1,0:T(8,128)(2,1)} %get-tuple-element.115.refs_0_), channel_id=1, source_target_pairs={{0,1},{1,2},{2,3},{3,0},{4,5},{5,6},{6,7},{7,4},{8,9},{9,10},{10,1... | collective-permute-start | bytes 159752 | tf_op jit(solution)/shard_map/ppermute | solution.py:69
  13.7 6.0 %collective-permute-start.12 = (bf16[16,4608]{1,0:T(8,128)(2,1)}, bf16[16,4608]{1,0:T(8,128)(2,1)S(1)}, u32[]{:S(2)}, u32[]{:S(2)}) collective-permute-start(bf16[16,4608]{1,0:T(8,128)(2,1)} %get-tuple-element.122.refs_0_), channel_id=1, source_target_pairs={{0,3},{1,0},{2,1},{3,2},{4,28},{5,29},{6,30},{7,31},{8,11},{9,8},{... | collective-permute-start | bytes 442376 | tf_op jit(solution)/shard_map/ppermute | solution.py:69
  16.1 12.9 %collective-permute-start.5 = (bf16[64,1664]{1,0:T(8,128)(2,1)S(1)}, bf16[64,1664]{1,0:T(8,128)(2,1)S(1)}, u32[]{:S(2)}, u32[]{:S(2)}) collective-permute-start(bf16[64,1664]{1,0:T(8,128)(2,1)S(1)} %column.2.refs_0_), channel_id=1, source_target_pairs={{0,24},{1,25},{2,26},{3,27},{4,28},{5,29},{6,30},{7,31},{8,16},{9,... | collective-permute-start | bytes 638984 | tf_op jit(solution)/shard_map/ppermute | solution.py:69
  18.7 10.4 %collective-permute-start.4 = (bf16[64,1664]{1,0:T(8,128)(2,1)S(1)}, bf16[64,1664]{1,0:T(8,128)(2,1)S(1)}, u32[]{:S(2)}, u32[]{:S(2)}) collective-permute-start(bf16[64,1664]{1,0:T(8,128)(2,1)S(1)} %column.2.refs_0_), channel_id=1, source_target_pairs={{0,16},{1,17},{2,18},{3,19},{4,20},{5,21},{6,22},{7,23},{8,24},{9,... | collective-permute-start | bytes 638984 | tf_op jit(solution)/shard_map/ppermute | solution.py:69
  19.2 9.9 %collective-permute-start.3 = (bf16[64,1664]{1,0:T(8,128)(2,1)S(1)}, bf16[64,1664]{1,0:T(8,128)(2,1)S(1)}, u32[]{:S(2)}, u32[]{:S(2)}) collective-permute-start(bf16[64,1664]{1,0:T(8,128)(2,1)S(1)} %column.2.refs_0_), channel_id=1, source_target_pairs={{0,8},{1,9},{2,10},{3,11},{4,12},{5,13},{6,14},{7,15},{8,0},{9,1},... | collective-permute-start | bytes 638984 | tf_op jit(solution)/shard_map/ppermute | solution.py:69
  19.7 9.3 %collective-permute-start.11 = (bf16[16,4608]{1,0:T(8,128)(2,1)}, bf16[16,4608]{1,0:T(8,128)(2,1)S(1)}, u32[]{:S(2)}, u32[]{:S(2)}) collective-permute-start(bf16[16,4608]{1,0:T(8,128)(2,1)} %get-tuple-element.122.refs_0_), channel_id=1, source_target_pairs={{0,2},{1,3},{2,0},{3,1},{4,20},{5,21},{6,22},{7,23},{8,10},{9,11},... | collective-permute-start | bytes 442376 | tf_op jit(solution)/shard_map/ppermute | solution.py:69
  19.7 9.3 %collective-permute-start.10 = (bf16[16,4608]{1,0:T(8,128)(2,1)}, bf16[16,4608]{1,0:T(8,128)(2,1)S(1)}, u32[]{:S(2)}, u32[]{:S(2)}) collective-permute-start(bf16[16,4608]{1,0:T(8,128)(2,1)} %get-tuple-element.122.refs_0_), channel_id=1, source_target_pairs={{0,1},{1,2},{2,3},{3,0},{4,12},{5,13},{6,14},{7,15},{8,9},{9,10},{... | collective-permute-start | bytes 442376 | tf_op jit(solution)/shard_map/ppermute | solution.py:69
  29.3 27.9 %collective-permute-start.15 = (bf16[64,4608]{1,0:T(8,128)(2,1)S(1)}, bf16[64,4608]{1,0:T(8,128)(2,1)S(1)}, u32[]{:S(2)}, u32[]{:S(2)}) collective-permute-start(bf16[64,4608]{1,0:T(8,128)(2,1)S(1)} %column.3.refs_0_), channel_id=1, source_target_pairs={{0,24},{1,25},{2,26},{3,27},{4,7},{5,4},{6,5},{7,6},{8,16},{9,17},... | collective-permute-start | bytes 1769480 | tf_op jit(solution)/shard_map/ppermute | solution.py:69
  31.8 25.4 %collective-permute-start.14 = (bf16[64,4608]{1,0:T(8,128)(2,1)S(1)}, bf16[64,4608]{1,0:T(8,128)(2,1)S(1)}, u32[]{:S(2)}, u32[]{:S(2)}) collective-permute-start(bf16[64,4608]{1,0:T(8,128)(2,1)S(1)} %column.3.refs_0_), channel_id=1, source_target_pairs={{0,16},{1,17},{2,18},{3,19},{4,6},{5,7},{6,4},{7,5},{8,24},{9,25},... | collective-permute-start | bytes 1769480 | tf_op jit(solution)/shard_map/ppermute | solution.py:69
  32.3 24.9 %collective-permute-start.13 = (bf16[64,4608]{1,0:T(8,128)(2,1)S(1)}, bf16[64,4608]{1,0:T(8,128)(2,1)S(1)}, u32[]{:S(2)}, u32[]{:S(2)}) collective-permute-start(bf16[64,4608]{1,0:T(8,128)(2,1)S(1)} %column.3.refs_0_), channel_id=1, source_target_pairs={{0,8},{1,9},{2,10},{3,11},{4,5},{5,6},{6,7},{7,4},{8,0},{9,1},{10,... | collective-permute-start | bytes 1769480 | tf_op jit(solution)/shard_map/ppermute | solution.py:69
  32.8 1.5 collective-permute-start.6
  32.8 1.8 %collective-permute-start.9 = (bf16[64,1664]{1,0:T(8,128)(2,1)S(1)}, bf16[64,1664]{1,0:T(8,128)(2,1)S(1)}, u32[]{:S(2)}, u32[]{:S(2)}) collective-permute-start(bf16[64,1664]{1,0:T(8,128)(2,1)S(1)} %collective-permute-done.5.refs_3_), channel_id=1, source_target_pairs={{0,4},{1,5},{2,6},{3,7},{4,0},{5,1},{6,2},{7,3},{8,12},{9,13},{10,... | collective-permute-start | bytes 638984 | tf_op jit(solution)/shard_map/ppermute | solution.py:72
  35.8 22.2 %collective-permute-start.16 = (bf16[64,4608]{1,0:T(8,128)(2,1)S(1)}, bf16[64,4608]{1,0:T(8,128)(2,1)S(1)}, u32[]{:S(2)}, u32[]{:S(2)}) collective-permute-start(bf16[64,4608]{1,0:T(8,128)(2,1)S(1)} %column.3.refs_0_), channel_id=1, source_target_pairs={{0,4},{1,5},{2,6},{3,7},{4,0},{5,1},{6,2},{7,3},{8,12},{9,13},{10,... | collective-permute-start | bytes 1769480 | tf_op jit(solution)/shard_map/ppermute | solution.py:72
  57.2 2.1 %collective-permute-start.17 = (bf16[64,4608]{1,0:T(8,128)(2,1)S(1)}, bf16[64,4608]{1,0:T(8,128)(2,1)S(1)}, u32[]{:S(2)}, u32[]{:S(2)}) collective-permute-start(bf16[64,4608]{1,0:T(8,128)(2,1)S(1)} %collective-permute-done.13.refs_1_), channel_id=1, source_target_pairs={{0,4},{1,5},{2,6},{3,7},{4,0},{5,1},{6,2},{7,3},{8,12},{9,13},{10,... | collective-permute-start | bytes 1769480 | tf_op jit(solution)/shard_map/ppermute | solution.py:72
  57.5 2.6 %collective-permute-start.18 = (bf16[64,4608]{1,0:T(8,128)(2,1)S(1)}, bf16[64,4608]{1,0:T(8,128)(2,1)S(1)}, u32[]{:S(2)}, u32[]{:S(2)}) collective-permute-start(bf16[64,4608]{1,0:T(8,128)(2,1)S(1)} %collective-permute-done.14.refs_2_), channel_id=1, source_target_pairs={{0,4},{1,5},{2,6},{3,7},{4,0},{5,1},{6,2},{7,3},{8,12},{9,13},{10,... | collective-permute-start | bytes 1769480 | tf_op jit(solution)/shard_map/ppermute | solution.py:72
  57.8 3.2 %collective-permute-start.19 = (bf16[64,4608]{1,0:T(8,128)(2,1)S(1)}, bf16[64,4608]{1,0:T(8,128)(2,1)S(1)}, u32[]{:S(2)}, u32[]{:S(2)}) collective-permute-start(bf16[64,4608]{1,0:T(8,128)(2,1)S(1)} %collective-permute-done.15.refs_3_), channel_id=1, source_target_pairs={{0,4},{1,5},{2,6},{3,7},{4,0},{5,1},{6,2},{7,3},{8,12},{9,13},{10,... | collective-permute-start | bytes 1769480 | tf_op jit(solution)/shard_map/ppermute | solution.py:72
  79.6 4.6 %collective-permute-start.20 = (bf16[4,64,4608]{2,1,0:T(8,128)(2,1)S(1)}, bf16[4,64,4608]{2,1,0:T(8,128)(2,1)S(1)}, u32[]{:S(2)}, u32[]{:S(2)}) collective-permute-start(bf16[4,64,4608]{2,1,0:T(8,128)(2,1)S(1)} %get-tuple-element.149), channel_id=1, source_target_pairs={{0,4},{1,5},{2,6},{3,7},{4,0},{5,1},{6,2},{7,3},{8,12},{9,13},{10,... | collective-permute-start | bytes 7077896 | tf_op jit(solution)/shard_map/ppermute | solution.py:72
  84.7 29.5 %collective-permute-start.21 = (bf16[64,4608]{1,0:T(8,128)(2,1)S(1)}, bf16[64,4608]{1,0:T(8,128)(2,1)S(1)}, u32[]{:S(2)}, u32[]{:S(2)}) collective-permute-start(bf16[64,4608]{1,0:T(8,128)(2,1)S(1)} %get-tuple-element.152), channel_id=1, source_target_pairs={{0,8},{1,9},{2,10},{3,11},{4,5},{5,6},{6,7},{7,4},{8,0},{9,1},{10,... | collective-permute-start | bytes 1769480 | tf_op jit(solution)/shard_map/ppermute | solution.py:69
  86.3 27.9 %collective-permute-start.22 = (bf16[64,4608]{1,0:T(8,128)(2,1)S(1)}, bf16[64,4608]{1,0:T(8,128)(2,1)S(1)}, u32[]{:S(2)}, u32[]{:S(2)}) collective-permute-start(bf16[64,4608]{1,0:T(8,128)(2,1)S(1)} %get-tuple-element.153), channel_id=1, source_target_pairs={{0,16},{1,17},{2,18},{3,19},{4,6},{5,7},{6,4},{7,5},{8,24},{9,25},... | collective-permute-start | bytes 1769480 | tf_op jit(solution)/shard_map/ppermute | solution.py:69
  87.8 26.4 %collective-permute-start.23 = (bf16[64,4608]{1,0:T(8,128)(2,1)S(1)}, bf16[64,4608]{1,0:T(8,128)(2,1)S(1)}, u32[]{:S(2)}, u32[]{:S(2)}) collective-permute-start(bf16[64,4608]{1,0:T(8,128)(2,1)S(1)} %get-tuple-element.154), channel_id=1, source_target_pairs={{0,24},{1,25},{2,26},{3,27},{4,7},{5,4},{6,5},{7,6},{8,16},{9,17},... | collective-permute-start | bytes 1769480 | tf_op jit(solution)/shard_map/ppermute | solution.py:69
  114.2 2.4 %collective-permute-start.24 = (bf16[4,64,1664]{2,1,0:T(8,128)(2,1)S(1)}, bf16[4,64,1664]{2,1,0:T(8,128)(2,1)S(1)}, u32[]{:S(2)}, u32[]{:S(2)}) collective-permute-start(bf16[4,64,1664]{2,1,0:T(8,128)(2,1)S(1)} %get-tuple-element.162), channel_id=1, source_target_pairs={{0,4},{1,5},{2,6},{3,7},{4,0},{5,1},{6,2},{7,3},{8,12},{9,13},{10,... | collective-permute-start | bytes 2555912 | tf_op jit(solution)/shard_map/ppermute | solution.py:72
  116.9 8.2 %collective-permute-start.25 = (bf16[64,1664]{1,0:T(8,128)(2,1)S(1)}, bf16[64,1664]{1,0:T(8,128)(2,1)S(1)}, u32[]{:S(2)}, u32[]{:S(2)}) collective-permute-start(bf16[64,1664]{1,0:T(8,128)(2,1)S(1)} %get-tuple-element.163), channel_id=1, source_target_pairs={{0,8},{1,9},{2,10},{3,11},{4,12},{5,13},{6,14},{7,15},{8,0},{9,1},... | collective-permute-start | bytes 638984 | tf_op jit(solution)/shard_map/ppermute | solution.py:69
  118.4 13.2 %collective-permute-start.26 = (bf16[64,1664]{1,0:T(8,128)(2,1)S(1)}, bf16[64,1664]{1,0:T(8,128)(2,1)S(1)}, u32[]{:S(2)}, u32[]{:S(2)}) collective-permute-start(bf16[64,1664]{1,0:T(8,128)(2,1)S(1)} %get-tuple-element.164), channel_id=1, source_target_pairs={{0,16},{1,17},{2,18},{3,19},{4,20},{5,21},{6,22},{7,23},{8,24},{9,... | collective-permute-start | bytes 638984 | tf_op jit(solution)/shard_map/ppermute | solution.py:69
  119.9 11.7 %collective-permute-start.27 = (bf16[64,1664]{1,0:T(8,128)(2,1)S(1)}, bf16[64,1664]{1,0:T(8,128)(2,1)S(1)}, u32[]{:S(2)}, u32[]{:S(2)}) collective-permute-start(bf16[64,1664]{1,0:T(8,128)(2,1)S(1)} %get-tuple-element.165), channel_id=1, source_target_pairs={{0,24},{1,25},{2,26},{3,27},{4,28},{5,29},{6,30},{7,31},{8,16},{9,... | collective-permute-start | bytes 638984 | tf_op jit(solution)/shard_map/ppermute | solution.py:69
  120.8 12.6 %collective-permute-start.31 = (bf16[16,4608]{1,0:T(8,128)(2,1)S(1)}, bf16[16,4608]{1,0:T(8,128)(2,1)S(1)}, u32[]{:S(2)}, u32[]{:S(2)}) collective-permute-start(bf16[16,4608]{1,0:T(8,128)(2,1)S(1)} %get-tuple-element.186), channel_id=1, source_target_pairs={{0,1},{1,2},{2,3},{3,0},{4,12},{5,13},{6,14},{7,15},{8,9},{9,10},{... | collective-permute-start | bytes 442376 | tf_op jit(solution)/shard_map/ppermute | solution.py:69
  121.2 15.0 %collective-permute-start.32 = (bf16[16,4608]{1,0:T(8,128)(2,1)S(1)}, bf16[16,4608]{1,0:T(8,128)(2,1)S(1)}, u32[]{:S(2)}, u32[]{:S(2)}) collective-permute-start(bf16[16,4608]{1,0:T(8,128)(2,1)S(1)} %get-tuple-element.187), channel_id=1, source_target_pairs={{0,2},{1,3},{2,0},{3,1},{4,20},{5,21},{6,22},{7,23},{8,10},{9,11},... | collective-permute-start | bytes 442376 | tf_op jit(solution)/shard_map/ppermute | solution.py:69
  125.0 11.2 %collective-permute-start.33 = (bf16[16,4608]{1,0:T(8,128)(2,1)S(1)}, bf16[16,4608]{1,0:T(8,128)(2,1)S(1)}, u32[]{:S(2)}, u32[]{:S(2)}) collective-permute-start(bf16[16,4608]{1,0:T(8,128)(2,1)S(1)} %get-tuple-element.188), channel_id=1, source_target_pairs={{0,3},{1,0},{2,1},{3,2},{4,28},{5,29},{6,30},{7,31},{8,11},{9,8},{... | collective-permute-start | bytes 442376 | tf_op jit(solution)/shard_map/ppermute | solution.py:69
  131.8 6.1 %collective-permute-start.28 = (bf16[16,1664]{1,0:T(8,128)(2,1)S(1)}, bf16[16,1664]{1,0:T(8,128)(2,1)S(1)}, u32[]{:S(2)}, u32[]{:S(2)}) collective-permute-start(bf16[16,1664]{1,0:T(8,128)(2,1)S(1)} %get-tuple-element.178), channel_id=1, source_target_pairs={{0,1},{1,2},{2,3},{3,0},{4,5},{5,6},{6,7},{7,4},{8,9},{9,10},{10,1... | collective-permute-start | bytes 159752 | tf_op jit(solution)/shard_map/ppermute | solution.py:69
  132.1 6.4 %collective-permute-start.29 = (bf16[16,1664]{1,0:T(8,128)(2,1)S(1)}, bf16[16,1664]{1,0:T(8,128)(2,1)S(1)}, u32[]{:S(2)}, u32[]{:S(2)}) collective-permute-start(bf16[16,1664]{1,0:T(8,128)(2,1)S(1)} %get-tuple-element.179), channel_id=1, source_target_pairs={{0,2},{1,3},{2,0},{3,1},{4,6},{5,7},{6,4},{7,5},{8,10},{9,11},{10,... | collective-permute-start | bytes 159752 | tf_op jit(solution)/shard_map/ppermute | solution.py:69
  133.4 5.1 %collective-permute-start.30 = (bf16[16,1664]{1,0:T(8,128)(2,1)S(1)}, bf16[16,1664]{1,0:T(8,128)(2,1)S(1)}, u32[]{:S(2)}, u32[]{:S(2)}) collective-permute-start(bf16[16,1664]{1,0:T(8,128)(2,1)S(1)} %get-tuple-element.180), channel_id=1, source_target_pairs={{0,3},{1,0},{2,1},{3,2},{4,7},{5,4},{6,5},{7,6},{8,11},{9,8},{10,9... | collective-permute-start | bytes 159752 | tf_op jit(solution)/shard_map/ppermute | solution.py:69
  (22 other events, 165.2 us)

commit v8 on v4

--- a/solution.py
+++ b/solution.py
@@ -404,8 +404,9 @@
             up = dot(low, wide[:, width + start : width + start + 512], 1, 0)
             square = up * up
             half = 0.5 + 0.5 * jnp.tanh(up * (GELU_ONE + GELU_CUBE * square))
-            active[span, part] = (up * half).astype(jnp.bfloat16)
-            slope = half * (1.0 + (1.0 - half) * (up * (2.0 * GELU_ONE + 6.0 * GELU_CUBE * square)))
+            act = up * half
+            active[span, part] = act.astype(jnp.bfloat16)
+            slope = half + act * ((1.0 - half) * (2.0 * GELU_ONE + 6.0 * GELU_CUBE * square))
             hidden_grad[span, part] = (dot(dy[span], contract[part], 1, 1) * slope).astype(jnp.bfloat16)
         back = dot(hidden_grad[span], wide[:, width:], 1, 1)
         gain_sum = gain_sum + jnp.sum(back * normed, axis=0, keepdims=True)
@@ -639,17 +640,13 @@
 
 def chip_sum(lay, keep, got):
     plane, rows, cols = keep.shape
-    block = cols if cols < 2048 else 1536
-    part = pl.BlockSpec((rows, block), lambda i: (0, i))
-    whole = pl.BlockSpec((plane, rows, block), lambda i: (0, 0, i))
     return pl.pallas_call(
         partial(chip_sum_kernel, lay),
-        grid=(cols // block,),
         out_shape=[jax.ShapeDtypeStruct((rows, cols), jnp.float32)]
         + [jax.ShapeDtypeStruct((rows, cols), jnp.bfloat16)] * (plane - 1),
-        in_specs=[whole, whole],
-        out_specs=[part] * plane,
-        compiler_params=params(12),
+        in_specs=[pl.BlockSpec(memory_space=VMEM)] * 2,
+        out_specs=[pl.BlockSpec(memory_space=VMEM)] * plane,
+        compiler_params=params(14),
         name="chip_sum",
     )(keep, got)
 
@@ -671,16 +668,12 @@
 def plane_sum(lay, own, got):
     rows, cols = own.shape
     reps = lay.rep
-    block = cols if cols < 2048 else 1536
-    part = pl.BlockSpec((rows, block), lambda i: (0, i))
-    small = pl.BlockSpec((rows // reps, block), lambda i: (0, i))
     return pl.pallas_call(
         partial(plane_sum_kernel, lay),
-        grid=(cols // block,),
         out_shape=[jax.ShapeDtypeStruct((rows // reps, cols), jnp.float32)]
         + [jax.ShapeDtypeStruct((rows // reps, cols), jnp.bfloat16)] * (reps - 1),
-        in_specs=[part] * (1 + len(got)),
-        out_specs=[small] * reps,
+        in_specs=[pl.BlockSpec(memory_space=VMEM)] * (1 + len(got)),
+        out_specs=[pl.BlockSpec(memory_space=VMEM)] * reps,
         compiler_params=params(10),
         name="plane_sum",
     )(own, *got)

time: 154 us -> 152 us (0.987)
  Pallas kernels: 79.8 us -> 78.2 us
where the time goes in v8:
time: 152 us
  Pallas kernels  78.2 us (51%)
  starting transfers between devices  35 us (23%)
  waiting for transfers between devices  17.5 us (12%)
  blocking collectives  12.9 us (8%)
  local copies, waits for them, and re-layouts  4.81 us (3%)
  other arithmetic  2.59 us (2%)
    ppermute x24, starting transfers between devices, over(): return lax.ppermute(value, AXES, self.pairs(move))  31.6 us
    pallas_call x1, Pallas kernels, attend(): pl.pallas_call(partial(attend_kernel, lay, len(pieces)), out_shape=(wide,...  21.1 us
    pallas_call x1, Pallas kernels, attend_back(): pl.pallas_call(attend_back_kernel, out_shape=jax.ShapeDtypeStruct((rows,...  18.8 us
    pallas_call x1, Pallas kernels, feed(): pl.pallas_call(partial(feed_kernel, lay, len(pieces), len(deep_pieces)),...  18.7 us
    all_to_all x1, blocking collectives, exchange(): return lax.all_to_all(value, AXES, 0, 0)  12.9 us
    ppermute x24, waiting for transfers between devices, over(): return lax.ppermute(value, AXES, self.pairs(move))  9.05 us
    ppermute x10, waiting for transfers between devices, to_core(): return lax.ppermute(value, AXES, self.pairs(lambda p, c, z: (p, 1 - c, z)))  8.44 us
    unnamed x43, local copies, waits for them, and re-layouts  4.8 us
  transfers between devices with their start and end apart: 34, of which 16 were waited for; matrix products, arithmetic and copies ran while one was open for 2% of the time, Pallas kernels for 37%

profile of v8, /device:TPU:0, one launch (start us, length us, event | category | flops | bytes accessed | tf_op | source)
XLA Modules:
  0.0 152.1 jit_solution(1093802033819867283)
XLA Ops:
  2.3 5.0 %collective-permute-start.2 = (bf16[16,1664]{1,0:T(8,128)(2,1)S(1)}, bf16[16,1664]{1,0:T(8,128)(2,1)S(1)}, u32[]{:S(2)}, u32[]{:S(2)}) collective-permute-start(bf16[16,1664]{1,0:T(8,128)(2,1)S(1)} %pack.1.refs_0_), channel_id=1, source_target_pairs={{0,3},{1,0},{2,1},{3,2},{4,7},{5,4},{6,5},{7,6},{8,11},{9,8},{10,9... | collective-permute-start | bytes 159752 | tf_op jit(solution)/shard_map/ppermute | solution.py:69
  7.4 1.0 collective-permute-start
  11.0 1.4 collective-permute-done.1.refs_2_
  13.3 1.5 %collective-permute-start.12 = (bf16[16,4608]{1,0:T(8,128)(2,1)S(1)}, bf16[16,4608]{1,0:T(8,128)(2,1)S(1)}, u32[]{:S(2)}, u32[]{:S(2)}) collective-permute-start(bf16[16,4608]{1,0:T(8,128)(2,1)S(1)} %slice_dynamic-update-slice_fusion.refs_0_), channel_id=1, source_target_pairs={{0,3},{1,0},{2,1},{3,2},{4,28},{5,29},{6,30},{7,31},{8,11},{9,8},{... | collective-permute-start | bytes 442376 | tf_op jit(solution)/shard_map/ppermute | solution.py:69
  14.9 2.5 %collective-permute-start.5 = (bf16[64,1664]{1,0:T(8,128)(2,1)S(1)}, bf16[64,1664]{1,0:T(8,128)(2,1)S(1)}, u32[]{:S(2)}, u32[]{:S(2)}) collective-permute-start(bf16[64,1664]{1,0:T(8,128)(2,1)S(1)} %column.2.refs_0_), channel_id=1, source_target_pairs={{0,24},{1,25},{2,26},{3,27},{4,28},{5,29},{6,30},{7,31},{8,16},{9,... | collective-permute-start | bytes 638984 | tf_op jit(solution)/shard_map/ppermute | solution.py:69
  18.7 1.7 %collective-permute-start.10 = (bf16[16,4608]{1,0:T(8,128)(2,1)S(1)}, bf16[16,4608]{1,0:T(8,128)(2,1)S(1)}, u32[]{:S(2)}, u32[]{:S(2)}) collective-permute-start(bf16[16,4608]{1,0:T(8,128)(2,1)S(1)} %slice_dynamic-update-slice_fusion.refs_0_), channel_id=1, source_target_pairs={{0,1},{1,2},{2,3},{3,0},{4,12},{5,13},{6,14},{7,15},{8,9},{9,10},{... | collective-permute-start | bytes 442376 | tf_op jit(solution)/shard_map/ppermute | solution.py:69
  20.4 1.2 copy-done.2
  21.6 1.2 copy-done.3
  23.5 1.1 arrange.1
  24.6 3.0 %collective-permute-done.11.refs_2_ = bf16[16,4608]{1,0:T(8,128)(2,1)S(1)} collective-permute-done((bf16[16,4608]{1,0:T(8,128)(2,1)S(1)}, bf16[16,4608]{1,0:T(8,128)(2,1)S(1)}, u32[]{:S(2)}, u32[]{:S(2)}) %collective-permute-start.11) | collective-permute-done | bytes 147488 | tf_op jit(solution)/shard_map/ppermute | solution.py:69
  27.9 2.5 %collective-permute-start.15 = (bf16[64,4608]{1,0:T(8,128)(2,1)S(1)}, bf16[64,4608]{1,0:T(8,128)(2,1)S(1)}, u32[]{:S(2)}, u32[]{:S(2)}) collective-permute-start(bf16[64,4608]{1,0:T(8,128)(2,1)S(1)} %column.3.refs_0_), channel_id=1, source_target_pairs={{0,24},{1,25},{2,26},{3,27},{4,7},{5,4},{6,5},{7,6},{8,16},{9,17},... | collective-permute-start | bytes 1769480 | tf_op jit(solution)/shard_map/ppermute | solution.py:69
  34.7 21.1 %attend.1 = (bf16[1056,1024]{1,0:T(8,128)(2,1)S(1)}, bf16[1056,1024]{1,0:T(8,128)(2,1)S(1)}, bf16[1056,1024]{1,0:T(8,128)(2,1)S(1)}, bf16[1056,512]{1,0:T(8,128)(2,1)S(1)}, f32[8,512]{1,0:T(8,128)S(1)}) custom-call(bf16[1056,512]{1,0:T(8,128)(2,1)S(1)} %get-tuple-element.128.x, s32[1056,128]{1,0:T(8,128)S(1)} %get-tuple-element.129.labels, ...), custom_call_target="tpu_custom_call" | custom-call | tf_op jit(solution)/shard_map/attend/pallas_call | solution.py:303
  56.9 1.1 collective-permute-done.17.refs_5_
  59.7 18.7 %feed.1 = (f32[1056,512]{1,0:T(8,128)S(1)}, f32[1056,512]{1,0:T(8,128)S(1)}, bf16[1056,512]{1,0:T(8,128)(2,1)S(1)}, bf16[1056,2048]{1,0:T(8,128)(2,1)S(1)}, bf16...) custom-call(bf16[1056,512]{1,0:T(8,128)(2,1)S(1)} %get-tuple-element, ...), custom_call_target="tpu_custom_call" | custom-call | tf_op jit(solution)/shard_map/feed/pallas_call | solution.py:458
  78.8 2.7 %mixed_back.1.dox = bf16[1056,1024]{1,0:T(8,128)(2,1)S(1)} custom-call(bf16[1056,512]{1,0:T(8,128)(2,1)S(1)} %get-tuple-element.148.middle_low, bf16[1056,512]{1,0:T(8,128)(2,1)S(1)} %get-tuple-element.138.mixed, bf16[512,512]{1,0:T(8,128)(2,1)S(1)} %get-tuple-element.149.out_weight), custom_call_target="tpu_custom_call" | custom-call | tf_op jit(solution)/shard_map/mixed_back/pallas_call | solution.py:504
  81.5 1.5 collective-permute-done.20.got
  83.5 1.5 %collective-permute-start.21 = (bf16[64,4608]{1,0:T(8,128)(2,1)S(1)}, bf16[64,4608]{1,0:T(8,128)(2,1)S(1)}, u32[]{:S(2)}, u32[]{:S(2)}) collective-permute-start(bf16[64,4608]{1,0:T(8,128)(2,1)S(1)} %get-tuple-element.154), channel_id=1, source_target_pairs={{0,8},{1,9},{2,10},{3,11},{4,5},{5,6},{6,7},{7,4},{8,0},{9,1},{10,... | collective-permute-start | bytes 1769480 | tf_op jit(solution)/shard_map/ppermute | solution.py:69
  85.0 1.4 collective-permute-start.22
  87.0 18.8 %attend_back.1.packed = bf16[1056,1536]{1,0:T(8,128)(2,1)S(1)} custom-call(bf16[1056,1024]{1,0:T(8,128)(2,1)S(1)} %get-tuple-element.145.qx, bf16[1056,1024]{1,0:T(8,128)(2,1)S(1)} %get-tuple-element.146.kx, bf16[1056,1024]{1,0:T(8,128)(2,1)S(1)} %get-tuple-element.147.vx, bf16[1056,1024]{1,0:T(8,128)(2,1)S(1)} %mixed_back.1.dox), custom_call_target="tpu_custom_call" | custom-call | tf_op jit(solution)/shard_map/attend_back/pallas_call | solution.py:357
  105.9 3.2 %input_back.1 = (bf16[1056,512]{1,0:T(8,128)(2,1)S(1)}, f32[8,512]{1,0:T(8,128)S(1)}) custom-call(bf16[1056,512]{1,0:T(8,128)(2,1)S(1)} %get-tuple-element.128.x, bf16[1056,1536]{1,0:T(8,128)(2,1)S(1)} %attend_back.1.packed, f32[8,512]{1,0:T(8,128)S(1)} %get-tuple-element.140.gains, f32[1056,512]{1,0:T(8,128)S(1)} %get-tuple-element.158.middle_grad, ...), custom_call_target="tpu_custom_call" | custom-call | tf_op jit(solution)/shard_map/input_back/pallas_call | solution.py:576
  109.0 3.9 %project_back.1 = (bf16[4,64,1664]{2,1,0:T(8,128)(2,1)S(1)}, bf16[4,64,1664]{2,1,0:T(8,128)(2,1)S(1)}) custom-call(bf16[1056,512]{1,0:T(8,128)(2,1)S(1)} %get-tuple-element.128.x, bf16[1056,1536]{1,0:T(8,128)(2,1)S(1)} %attend_back.1.packed, f32[8,512]{1,0:T(8,128)S(1)} %get-tuple-element.140.gains, f32[8,512]{1,0:T(8,128)S(1)} %get-tuple-element.159.first_norms, ...), custom_call_target="tpu_custom_call" | custom-call | tf_op jit(solution)/shard_map/project_back/pallas_call | solution.py:542
  113.8 2.0 %collective-permute-done.24.got = bf16[4,64,1664]{2,1,0:T(8,128)(2,1)S(1)} collective-permute-done((bf16[4,64,1664]{2,1,0:T(8,128)(2,1)S(1)}, bf16[4,64,1664]{2,1,0:T(8,128)(2,1)S(1)}, u32[]{:S(2)}, u32[]{:S(2)}) %collective-permute-start.24) | collective-permute-done | bytes 852000 | tf_op jit(solution)/shard_map/ppermute | solution.py:72
  116.0 1.5 %collective-permute-start.25 = (bf16[64,1664]{1,0:T(8,128)(2,1)S(1)}, bf16[64,1664]{1,0:T(8,128)(2,1)S(1)}, u32[]{:S(2)}, u32[]{:S(2)}) collective-permute-start(bf16[64,1664]{1,0:T(8,128)(2,1)S(1)} %get-tuple-element.165), channel_id=1, source_target_pairs={{0,8},{1,9},{2,10},{3,11},{4,12},{5,13},{6,14},{7,15},{8,0},{9,1},... | collective-permute-start | bytes 638984 | tf_op jit(solution)/shard_map/ppermute | solution.py:69
  117.5 1.2 collective-permute-start.26
  120.3 1.8 %collective-permute-start.32 = (bf16[16,4608]{1,0:T(8,128)(2,1)S(1)}, bf16[16,4608]{1,0:T(8,128)(2,1)S(1)}, u32[]{:S(2)}, u32[]{:S(2)}) collective-permute-start(bf16[16,4608]{1,0:T(8,128)(2,1)S(1)} %get-tuple-element.189), channel_id=1, source_target_pairs={{0,2},{1,3},{2,0},{3,1},{4,20},{5,21},{6,22},{7,23},{8,10},{9,11},... | collective-permute-start | bytes 442376 | tf_op jit(solution)/shard_map/ppermute | solution.py:69
  122.1 2.1 %collective-permute-done.25.refs_0_ = bf16[64,1664]{1,0:T(8,128)(2,1)S(1)} collective-permute-done((bf16[64,1664]{1,0:T(8,128)(2,1)S(1)}, bf16[64,1664]{1,0:T(8,128)(2,1)S(1)}, u32[]{:S(2)}, u32[]{:S(2)}) %collective-permute-start.25) | collective-permute-done | bytes 213024 | tf_op jit(solution)/shard_map/ppermute | solution.py:69
  124.1 1.5 collective-permute-start.33
  125.7 4.3 %finish.1 = (bf16[1044,512]{1,0:T(8,128)(2,1)}, bf16[1044,512]{1,0:T(8,128)(2,1)}) custom-call(f32[8,128]{1,0:T(8,128)S(1)} %get-tuple-element.117.begin, f32[1056,512]{1,0:T(8,128)S(1)} %get-tuple-element.168.middle, bf16[1056,2048]{1,0:T(8,128)(2,1)S(1)} %get-tuple-element.169.active, bf16[2048,512]{1,0:T(8,128)(2,1)S(1)} %get-tuple-element.170.contract, ...), custom_call_target="tpu_custom_call" | custom-call | tf_op jit(solution)/shard_map/finish/pallas_call | solution.py:221
  130.8 2.1 %collective-permute-start.29 = (bf16[16,1664]{1,0:T(8,128)(2,1)S(1)}, bf16[16,1664]{1,0:T(8,128)(2,1)S(1)}, u32[]{:S(2)}, u32[]{:S(2)}) collective-permute-start(bf16[16,1664]{1,0:T(8,128)(2,1)S(1)} %get-tuple-element.181), channel_id=1, source_target_pairs={{0,2},{1,3},{2,0},{3,1},{4,6},{5,7},{6,4},{7,5},{8,10},{9,11},{10,... | collective-permute-start | bytes 159752 | tf_op jit(solution)/shard_map/ppermute | solution.py:69
  132.9 1.7 %collective-permute-start.30 = (bf16[16,1664]{1,0:T(8,128)(2,1)S(1)}, bf16[16,1664]{1,0:T(8,128)(2,1)S(1)}, u32[]{:S(2)}, u32[]{:S(2)}) collective-permute-start(bf16[16,1664]{1,0:T(8,128)(2,1)S(1)} %get-tuple-element.182), channel_id=1, source_target_pairs={{0,3},{1,0},{2,1},{3,2},{4,7},{5,4},{6,5},{7,6},{8,11},{9,8},{10,9... | collective-permute-start | bytes 159752 | tf_op jit(solution)/shard_map/ppermute | solution.py:69
  134.7 1.1 moments.2
  138.2 12.9 %all_to_all.5.sums = f32[32,1,128]{2,1,0:T(1,128)S(1)} all-to-all(f32[32,1,128]{2,1,0:T(1,128)S(1)} %get-tuple-element.192), channel_id=1, replica_groups=mesh['dp'=8,'rep'=4] {'dp','rep'}, dimensions={0} | all-to-all | bytes 32768 | tf_op jit(solution)/shard_map/all_to_all | solution.py:793
  (102 shorter events, 22.6 us)
Async XLA Ops:
  2.3 8.7 %collective-permute-start.2 = (bf16[16,1664]{1,0:T(8,128)(2,1)S(1)}, bf16[16,1664]{1,0:T(8,128)(2,1)S(1)}, u32[]{:S(2)}, u32[]{:S(2)}) collective-permute-start(bf16[16,1664]{1,0:T(8,128)(2,1)S(1)} %pack.1.refs_0_), channel_id=1, source_target_pairs={{0,3},{1,0},{2,1},{3,2},{4,7},{5,4},{6,5},{7,6},{8,11},{9,8},{10,9... | collective-permute-start | bytes 159752 | tf_op jit(solution)/shard_map/ppermute | solution.py:69
  7.4 5.1 %collective-permute-start.1 = (bf16[16,1664]{1,0:T(8,128)(2,1)S(1)}, bf16[16,1664]{1,0:T(8,128)(2,1)S(1)}, u32[]{:S(2)}, u32[]{:S(2)}) collective-permute-start(bf16[16,1664]{1,0:T(8,128)(2,1)S(1)} %pack.1.refs_0_), channel_id=1, source_target_pairs={{0,2},{1,3},{2,0},{3,1},{4,6},{5,7},{6,4},{7,5},{8,10},{9,11},{10,... | collective-permute-start | bytes 159752 | tf_op jit(solution)/shard_map/ppermute | solution.py:69
  7.4 5.9 %collective-permute-start = (bf16[16,1664]{1,0:T(8,128)(2,1)S(1)}, bf16[16,1664]{1,0:T(8,128)(2,1)S(1)}, u32[]{:S(2)}, u32[]{:S(2)}) collective-permute-start(bf16[16,1664]{1,0:T(8,128)(2,1)S(1)} %pack.1.refs_0_), channel_id=1, source_target_pairs={{0,1},{1,2},{2,3},{3,0},{4,5},{5,6},{6,7},{7,4},{8,9},{9,10},{10,1... | collective-permute-start | bytes 159752 | tf_op jit(solution)/shard_map/ppermute | solution.py:69
  13.3 5.4 %collective-permute-start.12 = (bf16[16,4608]{1,0:T(8,128)(2,1)S(1)}, bf16[16,4608]{1,0:T(8,128)(2,1)S(1)}, u32[]{:S(2)}, u32[]{:S(2)}) collective-permute-start(bf16[16,4608]{1,0:T(8,128)(2,1)S(1)} %slice_dynamic-update-slice_fusion.refs_0_), channel_id=1, source_target_pairs={{0,3},{1,0},{2,1},{3,2},{4,28},{5,29},{6,30},{7,31},{8,11},{9,8},{... | collective-permute-start | bytes 442376 | tf_op jit(solution)/shard_map/ppermute | solution.py:69
  14.9 12.7 %collective-permute-start.5 = (bf16[64,1664]{1,0:T(8,128)(2,1)S(1)}, bf16[64,1664]{1,0:T(8,128)(2,1)S(1)}, u32[]{:S(2)}, u32[]{:S(2)}) collective-permute-start(bf16[64,1664]{1,0:T(8,128)(2,1)S(1)} %column.2.refs_0_), channel_id=1, source_target_pairs={{0,24},{1,25},{2,26},{3,27},{4,28},{5,29},{6,30},{7,31},{8,16},{9,... | collective-permute-start | bytes 638984 | tf_op jit(solution)/shard_map/ppermute | solution.py:69
  17.5 10.2 %collective-permute-start.4 = (bf16[64,1664]{1,0:T(8,128)(2,1)S(1)}, bf16[64,1664]{1,0:T(8,128)(2,1)S(1)}, u32[]{:S(2)}, u32[]{:S(2)}) collective-permute-start(bf16[64,1664]{1,0:T(8,128)(2,1)S(1)} %column.2.refs_0_), channel_id=1, source_target_pairs={{0,16},{1,17},{2,18},{3,19},{4,20},{5,21},{6,22},{7,23},{8,24},{9,... | collective-permute-start | bytes 638984 | tf_op jit(solution)/shard_map/ppermute | solution.py:69
  18.0 9.7 %collective-permute-start.3 = (bf16[64,1664]{1,0:T(8,128)(2,1)S(1)}, bf16[64,1664]{1,0:T(8,128)(2,1)S(1)}, u32[]{:S(2)}, u32[]{:S(2)}) collective-permute-start(bf16[64,1664]{1,0:T(8,128)(2,1)S(1)} %column.2.refs_0_), channel_id=1, source_target_pairs={{0,8},{1,9},{2,10},{3,11},{4,12},{5,13},{6,14},{7,15},{8,0},{9,1},... | collective-permute-start | bytes 638984 | tf_op jit(solution)/shard_map/ppermute | solution.py:69
  18.5 9.1 %collective-permute-start.11 = (bf16[16,4608]{1,0:T(8,128)(2,1)S(1)}, bf16[16,4608]{1,0:T(8,128)(2,1)S(1)}, u32[]{:S(2)}, u32[]{:S(2)}) collective-permute-start(bf16[16,4608]{1,0:T(8,128)(2,1)S(1)} %slice_dynamic-update-slice_fusion.refs_0_), channel_id=1, source_target_pairs={{0,2},{1,3},{2,0},{3,1},{4,20},{5,21},{6,22},{7,23},{8,10},{9,11},... | collective-permute-start | bytes 442376 | tf_op jit(solution)/shard_map/ppermute | solution.py:69
  18.7 8.9 %collective-permute-start.10 = (bf16[16,4608]{1,0:T(8,128)(2,1)S(1)}, bf16[16,4608]{1,0:T(8,128)(2,1)S(1)}, u32[]{:S(2)}, u32[]{:S(2)}) collective-permute-start(bf16[16,4608]{1,0:T(8,128)(2,1)S(1)} %slice_dynamic-update-slice_fusion.refs_0_), channel_id=1, source_target_pairs={{0,1},{1,2},{2,3},{3,0},{4,12},{5,13},{6,14},{7,15},{8,9},{9,10},{... | collective-permute-start | bytes 442376 | tf_op jit(solution)/shard_map/ppermute | solution.py:69
  27.9 27.9 %collective-permute-start.15 = (bf16[64,4608]{1,0:T(8,128)(2,1)S(1)}, bf16[64,4608]{1,0:T(8,128)(2,1)S(1)}, u32[]{:S(2)}, u32[]{:S(2)}) collective-permute-start(bf16[64,4608]{1,0:T(8,128)(2,1)S(1)} %column.3.refs_0_), channel_id=1, source_target_pairs={{0,24},{1,25},{2,26},{3,27},{4,7},{5,4},{6,5},{7,6},{8,16},{9,17},... | collective-permute-start | bytes 1769480 | tf_op jit(solution)/shard_map/ppermute | solution.py:69
  30.4 25.4 %collective-permute-start.14 = (bf16[64,4608]{1,0:T(8,128)(2,1)S(1)}, bf16[64,4608]{1,0:T(8,128)(2,1)S(1)}, u32[]{:S(2)}, u32[]{:S(2)}) collective-permute-start(bf16[64,4608]{1,0:T(8,128)(2,1)S(1)} %column.3.refs_0_), channel_id=1, source_target_pairs={{0,16},{1,17},{2,18},{3,19},{4,6},{5,7},{6,4},{7,5},{8,24},{9,25},... | collective-permute-start | bytes 1769480 | tf_op jit(solution)/shard_map/ppermute | solution.py:69
  30.9 24.9 %collective-permute-start.13 = (bf16[64,4608]{1,0:T(8,128)(2,1)S(1)}, bf16[64,4608]{1,0:T(8,128)(2,1)S(1)}, u32[]{:S(2)}, u32[]{:S(2)}) collective-permute-start(bf16[64,4608]{1,0:T(8,128)(2,1)S(1)} %column.3.refs_0_), channel_id=1, source_target_pairs={{0,8},{1,9},{2,10},{3,11},{4,5},{5,6},{6,7},{7,4},{8,0},{9,1},{10,... | collective-permute-start | bytes 1769480 | tf_op jit(solution)/shard_map/ppermute | solution.py:69
  31.4 1.5 collective-permute-start.6
  31.6 1.6 %collective-permute-start.9 = (bf16[64,1664]{1,0:T(8,128)(2,1)S(1)}, bf16[64,1664]{1,0:T(8,128)(2,1)S(1)}, u32[]{:S(2)}, u32[]{:S(2)}) collective-permute-start(bf16[64,1664]{1,0:T(8,128)(2,1)S(1)} %collective-permute-done.5.refs_3_), channel_id=1, source_target_pairs={{0,4},{1,5},{2,6},{3,7},{4,0},{5,1},{6,2},{7,3},{8,12},{9,13},{10,... | collective-permute-start | bytes 638984 | tf_op jit(solution)/shard_map/ppermute | solution.py:72
  34.4 22.5 %collective-permute-start.16 = (bf16[64,4608]{1,0:T(8,128)(2,1)S(1)}, bf16[64,4608]{1,0:T(8,128)(2,1)S(1)}, u32[]{:S(2)}, u32[]{:S(2)}) collective-permute-start(bf16[64,4608]{1,0:T(8,128)(2,1)S(1)} %column.3.refs_0_), channel_id=1, source_target_pairs={{0,4},{1,5},{2,6},{3,7},{4,0},{5,1},{6,2},{7,3},{8,12},{9,13},{10,... | collective-permute-start | bytes 1769480 | tf_op jit(solution)/shard_map/ppermute | solution.py:72
  55.8 2.2 %collective-permute-start.17 = (bf16[64,4608]{1,0:T(8,128)(2,1)S(1)}, bf16[64,4608]{1,0:T(8,128)(2,1)S(1)}, u32[]{:S(2)}, u32[]{:S(2)}) collective-permute-start(bf16[64,4608]{1,0:T(8,128)(2,1)S(1)} %collective-permute-done.13.refs_1_), channel_id=1, source_target_pairs={{0,4},{1,5},{2,6},{3,7},{4,0},{5,1},{6,2},{7,3},{8,12},{9,13},{10,... | collective-permute-start | bytes 1769480 | tf_op jit(solution)/shard_map/ppermute | solution.py:72
  56.4 2.5 %collective-permute-start.18 = (bf16[64,4608]{1,0:T(8,128)(2,1)S(1)}, bf16[64,4608]{1,0:T(8,128)(2,1)S(1)}, u32[]{:S(2)}, u32[]{:S(2)}) collective-permute-start(bf16[64,4608]{1,0:T(8,128)(2,1)S(1)} %collective-permute-done.14.refs_2_), channel_id=1, source_target_pairs={{0,4},{1,5},{2,6},{3,7},{4,0},{5,1},{6,2},{7,3},{8,12},{9,13},{10,... | collective-permute-start | bytes 1769480 | tf_op jit(solution)/shard_map/ppermute | solution.py:72
  56.4 3.3 %collective-permute-start.19 = (bf16[64,4608]{1,0:T(8,128)(2,1)S(1)}, bf16[64,4608]{1,0:T(8,128)(2,1)S(1)}, u32[]{:S(2)}, u32[]{:S(2)}) collective-permute-start(bf16[64,4608]{1,0:T(8,128)(2,1)S(1)} %collective-permute-done.15.refs_3_), channel_id=1, source_target_pairs={{0,4},{1,5},{2,6},{3,7},{4,0},{5,1},{6,2},{7,3},{8,12},{9,13},{10,... | collective-permute-start | bytes 1769480 | tf_op jit(solution)/shard_map/ppermute | solution.py:72
  78.4 4.6 %collective-permute-start.20 = (bf16[4,64,4608]{2,1,0:T(8,128)(2,1)S(1)}, bf16[4,64,4608]{2,1,0:T(8,128)(2,1)S(1)}, u32[]{:S(2)}, u32[]{:S(2)}) collective-permute-start(bf16[4,64,4608]{2,1,0:T(8,128)(2,1)S(1)} %get-tuple-element.151), channel_id=1, source_target_pairs={{0,4},{1,5},{2,6},{3,7},{4,0},{5,1},{6,2},{7,3},{8,12},{9,13},{10,... | collective-permute-start | bytes 7077896 | tf_op jit(solution)/shard_map/ppermute | solution.py:72
  83.5 29.5 %collective-permute-start.21 = (bf16[64,4608]{1,0:T(8,128)(2,1)S(1)}, bf16[64,4608]{1,0:T(8,128)(2,1)S(1)}, u32[]{:S(2)}, u32[]{:S(2)}) collective-permute-start(bf16[64,4608]{1,0:T(8,128)(2,1)S(1)} %get-tuple-element.154), channel_id=1, source_target_pairs={{0,8},{1,9},{2,10},{3,11},{4,5},{5,6},{6,7},{7,4},{8,0},{9,1},{10,... | collective-permute-start | bytes 1769480 | tf_op jit(solution)/shard_map/ppermute | solution.py:69
  85.0 27.9 %collective-permute-start.22 = (bf16[64,4608]{1,0:T(8,128)(2,1)S(1)}, bf16[64,4608]{1,0:T(8,128)(2,1)S(1)}, u32[]{:S(2)}, u32[]{:S(2)}) collective-permute-start(bf16[64,4608]{1,0:T(8,128)(2,1)S(1)} %get-tuple-element.155), channel_id=1, source_target_pairs={{0,16},{1,17},{2,18},{3,19},{4,6},{5,7},{6,4},{7,5},{8,24},{9,25},... | collective-permute-start | bytes 1769480 | tf_op jit(solution)/shard_map/ppermute | solution.py:69
  86.5 26.5 %collective-permute-start.23 = (bf16[64,4608]{1,0:T(8,128)(2,1)S(1)}, bf16[64,4608]{1,0:T(8,128)(2,1)S(1)}, u32[]{:S(2)}, u32[]{:S(2)}) collective-permute-start(bf16[64,4608]{1,0:T(8,128)(2,1)S(1)} %get-tuple-element.156), channel_id=1, source_target_pairs={{0,24},{1,25},{2,26},{3,27},{4,7},{5,4},{6,5},{7,6},{8,16},{9,17},... | collective-permute-start | bytes 1769480 | tf_op jit(solution)/shard_map/ppermute | solution.py:69
  113.0 2.8 %collective-permute-start.24 = (bf16[4,64,1664]{2,1,0:T(8,128)(2,1)S(1)}, bf16[4,64,1664]{2,1,0:T(8,128)(2,1)S(1)}, u32[]{:S(2)}, u32[]{:S(2)}) collective-permute-start(bf16[4,64,1664]{2,1,0:T(8,128)(2,1)S(1)} %get-tuple-element.164), channel_id=1, source_target_pairs={{0,4},{1,5},{2,6},{3,7},{4,0},{5,1},{6,2},{7,3},{8,12},{9,13},{10,... | collective-permute-start | bytes 2555912 | tf_op jit(solution)/shard_map/ppermute | solution.py:72
  116.0 8.2 %collective-permute-start.25 = (bf16[64,1664]{1,0:T(8,128)(2,1)S(1)}, bf16[64,1664]{1,0:T(8,128)(2,1)S(1)}, u32[]{:S(2)}, u32[]{:S(2)}) collective-permute-start(bf16[64,1664]{1,0:T(8,128)(2,1)S(1)} %get-tuple-element.165), channel_id=1, source_target_pairs={{0,8},{1,9},{2,10},{3,11},{4,12},{5,13},{6,14},{7,15},{8,0},{9,1},... | collective-permute-start | bytes 638984 | tf_op jit(solution)/shard_map/ppermute | solution.py:69
  117.5 12.7 %collective-permute-start.26 = (bf16[64,1664]{1,0:T(8,128)(2,1)S(1)}, bf16[64,1664]{1,0:T(8,128)(2,1)S(1)}, u32[]{:S(2)}, u32[]{:S(2)}) collective-permute-start(bf16[64,1664]{1,0:T(8,128)(2,1)S(1)} %get-tuple-element.166), channel_id=1, source_target_pairs={{0,16},{1,17},{2,18},{3,19},{4,20},{5,21},{6,22},{7,23},{8,24},{9,... | collective-permute-start | bytes 638984 | tf_op jit(solution)/shard_map/ppermute | solution.py:69
  118.8 11.4 %collective-permute-start.27 = (bf16[64,1664]{1,0:T(8,128)(2,1)S(1)}, bf16[64,1664]{1,0:T(8,128)(2,1)S(1)}, u32[]{:S(2)}, u32[]{:S(2)}) collective-permute-start(bf16[64,1664]{1,0:T(8,128)(2,1)S(1)} %get-tuple-element.167), channel_id=1, source_target_pairs={{0,24},{1,25},{2,26},{3,27},{4,28},{5,29},{6,30},{7,31},{8,16},{9,... | collective-permute-start | bytes 638984 | tf_op jit(solution)/shard_map/ppermute | solution.py:69
  120.0 12.9 %collective-permute-start.31 = (bf16[16,4608]{1,0:T(8,128)(2,1)S(1)}, bf16[16,4608]{1,0:T(8,128)(2,1)S(1)}, u32[]{:S(2)}, u32[]{:S(2)}) collective-permute-start(bf16[16,4608]{1,0:T(8,128)(2,1)S(1)} %get-tuple-element.188), channel_id=1, source_target_pairs={{0,1},{1,2},{2,3},{3,0},{4,12},{5,13},{6,14},{7,15},{8,9},{9,10},{... | collective-permute-start | bytes 442376 | tf_op jit(solution)/shard_map/ppermute | solution.py:69
  120.3 14.4 %collective-permute-start.32 = (bf16[16,4608]{1,0:T(8,128)(2,1)S(1)}, bf16[16,4608]{1,0:T(8,128)(2,1)S(1)}, u32[]{:S(2)}, u32[]{:S(2)}) collective-permute-start(bf16[16,4608]{1,0:T(8,128)(2,1)S(1)} %get-tuple-element.189), channel_id=1, source_target_pairs={{0,2},{1,3},{2,0},{3,1},{4,20},{5,21},{6,22},{7,23},{8,10},{9,11},... | collective-permute-start | bytes 442376 | tf_op jit(solution)/shard_map/ppermute | solution.py:69
  124.1 10.5 %collective-permute-start.33 = (bf16[16,4608]{1,0:T(8,128)(2,1)S(1)}, bf16[16,4608]{1,0:T(8,128)(2,1)S(1)}, u32[]{:S(2)}, u32[]{:S(2)}) collective-permute-start(bf16[16,4608]{1,0:T(8,128)(2,1)S(1)} %get-tuple-element.190), channel_id=1, source_target_pairs={{0,3},{1,0},{2,1},{3,2},{4,28},{5,29},{6,30},{7,31},{8,11},{9,8},{... | collective-permute-start | bytes 442376 | tf_op jit(solution)/shard_map/ppermute | solution.py:69
  130.3 6.1 %collective-permute-start.28 = (bf16[16,1664]{1,0:T(8,128)(2,1)S(1)}, bf16[16,1664]{1,0:T(8,128)(2,1)S(1)}, u32[]{:S(2)}, u32[]{:S(2)}) collective-permute-start(bf16[16,1664]{1,0:T(8,128)(2,1)S(1)} %get-tuple-element.180), channel_id=1, source_target_pairs={{0,1},{1,2},{2,3},{3,0},{4,5},{5,6},{6,7},{7,4},{8,9},{9,10},{10,1... | collective-permute-start | bytes 159752 | tf_op jit(solution)/shard_map/ppermute | solution.py:69
  130.8 6.5 %collective-permute-start.29 = (bf16[16,1664]{1,0:T(8,128)(2,1)S(1)}, bf16[16,1664]{1,0:T(8,128)(2,1)S(1)}, u32[]{:S(2)}, u32[]{:S(2)}) collective-permute-start(bf16[16,1664]{1,0:T(8,128)(2,1)S(1)} %get-tuple-element.181), channel_id=1, source_target_pairs={{0,2},{1,3},{2,0},{3,1},{4,6},{5,7},{6,4},{7,5},{8,10},{9,11},{10,... | collective-permute-start | bytes 159752 | tf_op jit(solution)/shard_map/ppermute | solution.py:69
  132.9 4.5 %collective-permute-start.30 = (bf16[16,1664]{1,0:T(8,128)(2,1)S(1)}, bf16[16,1664]{1,0:T(8,128)(2,1)S(1)}, u32[]{:S(2)}, u32[]{:S(2)}) collective-permute-start(bf16[16,1664]{1,0:T(8,128)(2,1)S(1)} %get-tuple-element.182), channel_id=1, source_target_pairs={{0,3},{1,0},{2,1},{3,2},{4,7},{5,4},{6,5},{7,6},{8,11},{9,8},{10,9... | collective-permute-start | bytes 159752 | tf_op jit(solution)/shard_map/ppermute | solution.py:69
  (22 other events, 132.9 us)

commit v9 on v8

--- a/solution.py
+++ b/solution.py
@@ -393,7 +393,7 @@
 
     def one_chunk(i, carry):
         gain_sum, bias_sum = carry
-        span = pl.ds(pl.multiple_of(i * DEEP_CHUNK, DEEP_CHUNK), DEEP_CHUNK)
+        span = pl.ds(i * DEEP_CHUNK, DEEP_CHUNK)
         start = x[span].astype(jnp.float32) + dot(mixed[span], wide[:, :width], 1, 0)
         middle[span] = start
         normed, scale = normalize(start)
@@ -416,7 +416,10 @@
         middle_low[span] = grad.astype(jnp.bfloat16)
         return gain_sum, bias_sum
 
-    gain_sum, bias_sum = lax.fori_loop(0, rows // DEEP_CHUNK, one_chunk, (zero, zero))
+    sums = (zero, zero)
+    for i in range(rows // DEEP_CHUNK):
+        sums = one_chunk(i, sums)
+    gain_sum, bias_sum = sums
     norm_grads[...] = jnp.concatenate([gain_sum, bias_sum, jnp.zeros((6, width), jnp.float32)], axis=0)
 
     def one_block(i, carry):

time: 152 us -> 152 us (level)
  no operation moved by 1% of the time
where the time goes in v9:
time: 152 us
  Pallas kernels  77.9 us (51%)
  starting transfers between devices  35 us (23%)
  waiting for transfers between devices  17.4 us (11%)
  blocking collectives  12.9 us (8%)
  local copies, waits for them, and re-layouts  4.81 us (3%)
  other arithmetic  2.59 us (2%)
    ppermute x24, starting transfers between devices, over(): return lax.ppermute(value, AXES, self.pairs(move))  31.6 us
    pallas_call x1, Pallas kernels, attend(): pl.pallas_call(partial(attend_kernel, lay, len(pieces)), out_shape=(wide,...  21.1 us
    pallas_call x1, Pallas kernels, attend_back(): pl.pallas_call(attend_back_kernel, out_shape=jax.ShapeDtypeStruct((rows,...  18.8 us
    pallas_call x1, Pallas kernels, feed(): pl.pallas_call(partial(feed_kernel, lay, len(pieces), len(deep_pieces)),...  18.3 us
    all_to_all x1, blocking collectives, exchange(): return lax.all_to_all(value, AXES, 0, 0)  12.9 us
    ppermute x24, waiting for transfers between devices, over(): return lax.ppermute(value, AXES, self.pairs(move))  9 us
    ppermute x10, waiting for transfers between devices, to_core(): return lax.ppermute(value, AXES, self.pairs(lambda p, c, z: (p, 1 - c, z)))  8.44 us
    unnamed x43, local copies, waits for them, and re-layouts  4.8 us
  transfers between devices with their start and end apart: 34, of which 16 were waited for; matrix products, arithmetic and copies ran while one was open for 2% of the time, Pallas kernels for 37%

profile of v9, /device:TPU:0, one launch (start us, length us, event | category | flops | bytes accessed | tf_op | source)
XLA Modules:
  0.0 151.8 jit_solution(8745499901800910699)
XLA Ops:
  2.3 5.0 %collective-permute-start.2 = (bf16[16,1664]{1,0:T(8,128)(2,1)S(1)}, bf16[16,1664]{1,0:T(8,128)(2,1)S(1)}, u32[]{:S(2)}, u32[]{:S(2)}) collective-permute-start(bf16[16,1664]{1,0:T(8,128)(2,1)S(1)} %pack.1.refs_0_), channel_id=1, source_target_pairs={{0,3},{1,0},{2,1},{3,2},{4,7},{5,4},{6,5},{7,6},{8,11},{9,8},{10,9... | collective-permute-start | bytes 159752 | tf_op jit(solution)/shard_map/ppermute | solution.py:69
  7.4 1.0 collective-permute-start
  11.0 1.4 collective-permute-done.1.refs_2_
  13.3 1.5 %collective-permute-start.12 = (bf16[16,4608]{1,0:T(8,128)(2,1)S(1)}, bf16[16,4608]{1,0:T(8,128)(2,1)S(1)}, u32[]{:S(2)}, u32[]{:S(2)}) collective-permute-start(bf16[16,4608]{1,0:T(8,128)(2,1)S(1)} %slice_dynamic-update-slice_fusion.refs_0_), channel_id=1, source_target_pairs={{0,3},{1,0},{2,1},{3,2},{4,28},{5,29},{6,30},{7,31},{8,11},{9,8},{... | collective-permute-start | bytes 442376 | tf_op jit(solution)/shard_map/ppermute | solution.py:69
  14.9 2.5 %collective-permute-start.5 = (bf16[64,1664]{1,0:T(8,128)(2,1)S(1)}, bf16[64,1664]{1,0:T(8,128)(2,1)S(1)}, u32[]{:S(2)}, u32[]{:S(2)}) collective-permute-start(bf16[64,1664]{1,0:T(8,128)(2,1)S(1)} %column.2.refs_0_), channel_id=1, source_target_pairs={{0,24},{1,25},{2,26},{3,27},{4,28},{5,29},{6,30},{7,31},{8,16},{9,... | collective-permute-start | bytes 638984 | tf_op jit(solution)/shard_map/ppermute | solution.py:69
  18.7 1.7 %collective-permute-start.10 = (bf16[16,4608]{1,0:T(8,128)(2,1)S(1)}, bf16[16,4608]{1,0:T(8,128)(2,1)S(1)}, u32[]{:S(2)}, u32[]{:S(2)}) collective-permute-start(bf16[16,4608]{1,0:T(8,128)(2,1)S(1)} %slice_dynamic-update-slice_fusion.refs_0_), channel_id=1, source_target_pairs={{0,1},{1,2},{2,3},{3,0},{4,12},{5,13},{6,14},{7,15},{8,9},{9,10},{... | collective-permute-start | bytes 442376 | tf_op jit(solution)/shard_map/ppermute | solution.py:69
  20.4 1.2 copy-done.2
  21.6 1.2 copy-done.3
  23.5 1.1 arrange.1
  24.6 3.0 %collective-permute-done.11.refs_2_ = bf16[16,4608]{1,0:T(8,128)(2,1)S(1)} collective-permute-done((bf16[16,4608]{1,0:T(8,128)(2,1)S(1)}, bf16[16,4608]{1,0:T(8,128)(2,1)S(1)}, u32[]{:S(2)}, u32[]{:S(2)}) %collective-permute-start.11) | collective-permute-done | bytes 147488 | tf_op jit(solution)/shard_map/ppermute | solution.py:69
  27.9 2.5 %collective-permute-start.15 = (bf16[64,4608]{1,0:T(8,128)(2,1)S(1)}, bf16[64,4608]{1,0:T(8,128)(2,1)S(1)}, u32[]{:S(2)}, u32[]{:S(2)}) collective-permute-start(bf16[64,4608]{1,0:T(8,128)(2,1)S(1)} %column.3.refs_0_), channel_id=1, source_target_pairs={{0,24},{1,25},{2,26},{3,27},{4,7},{5,4},{6,5},{7,6},{8,16},{9,17},... | collective-permute-start | bytes 1769480 | tf_op jit(solution)/shard_map/ppermute | solution.py:69
  34.7 21.1 %attend.1 = (bf16[1056,1024]{1,0:T(8,128)(2,1)S(1)}, bf16[1056,1024]{1,0:T(8,128)(2,1)S(1)}, bf16[1056,1024]{1,0:T(8,128)(2,1)S(1)}, bf16[1056,512]{1,0:T(8,128)(2,1)S(1)}, f32[8,512]{1,0:T(8,128)S(1)}) custom-call(bf16[1056,512]{1,0:T(8,128)(2,1)S(1)} %get-tuple-element.128.x, s32[1056,128]{1,0:T(8,128)S(1)} %get-tuple-element.129.labels, ...), custom_call_target="tpu_custom_call" | custom-call | tf_op jit(solution)/shard_map/attend/pallas_call | solution.py:303
  56.9 1.1 collective-permute-done.17.refs_5_
  59.7 18.3 %feed.1 = (f32[1056,512]{1,0:T(8,128)S(1)}, f32[1056,512]{1,0:T(8,128)S(1)}, bf16[1056,512]{1,0:T(8,128)(2,1)S(1)}, bf16[1056,2048]{1,0:T(8,128)(2,1)S(1)}, bf16...) custom-call(bf16[1056,512]{1,0:T(8,128)(2,1)S(1)} %get-tuple-element, ...), custom_call_target="tpu_custom_call" | custom-call | tf_op jit(solution)/shard_map/feed/pallas_call | solution.py:461
  78.5 2.7 %mixed_back.1.dox = bf16[1056,1024]{1,0:T(8,128)(2,1)S(1)} custom-call(bf16[1056,512]{1,0:T(8,128)(2,1)S(1)} %get-tuple-element.148.middle_low, bf16[1056,512]{1,0:T(8,128)(2,1)S(1)} %get-tuple-element.138.mixed, bf16[512,512]{1,0:T(8,128)(2,1)S(1)} %get-tuple-element.149.out_weight), custom_call_target="tpu_custom_call" | custom-call | tf_op jit(solution)/shard_map/mixed_back/pallas_call | solution.py:507
  81.2 1.5 collective-permute-done.20.got
  83.2 1.5 %collective-permute-start.21 = (bf16[64,4608]{1,0:T(8,128)(2,1)S(1)}, bf16[64,4608]{1,0:T(8,128)(2,1)S(1)}, u32[]{:S(2)}, u32[]{:S(2)}) collective-permute-start(bf16[64,4608]{1,0:T(8,128)(2,1)S(1)} %get-tuple-element.154), channel_id=1, source_target_pairs={{0,8},{1,9},{2,10},{3,11},{4,5},{5,6},{6,7},{7,4},{8,0},{9,1},{10,... | collective-permute-start | bytes 1769480 | tf_op jit(solution)/shard_map/ppermute | solution.py:69
  84.7 1.4 collective-permute-start.22
  86.7 18.8 %attend_back.1.packed = bf16[1056,1536]{1,0:T(8,128)(2,1)S(1)} custom-call(bf16[1056,1024]{1,0:T(8,128)(2,1)S(1)} %get-tuple-element.145.qx, bf16[1056,1024]{1,0:T(8,128)(2,1)S(1)} %get-tuple-element.146.kx, bf16[1056,1024]{1,0:T(8,128)(2,1)S(1)} %get-tuple-element.147.vx, bf16[1056,1024]{1,0:T(8,128)(2,1)S(1)} %mixed_back.1.dox), custom_call_target="tpu_custom_call" | custom-call | tf_op jit(solution)/shard_map/attend_back/pallas_call | solution.py:357
  105.5 3.2 %input_back.1 = (bf16[1056,512]{1,0:T(8,128)(2,1)S(1)}, f32[8,512]{1,0:T(8,128)S(1)}) custom-call(bf16[1056,512]{1,0:T(8,128)(2,1)S(1)} %get-tuple-element.128.x, bf16[1056,1536]{1,0:T(8,128)(2,1)S(1)} %attend_back.1.packed, f32[8,512]{1,0:T(8,128)S(1)} %get-tuple-element.140.gains, f32[1056,512]{1,0:T(8,128)S(1)} %get-tuple-element.158.middle_grad, ...), custom_call_target="tpu_custom_call" | custom-call | tf_op jit(solution)/shard_map/input_back/pallas_call | solution.py:579
  108.7 3.9 %project_back.1 = (bf16[4,64,1664]{2,1,0:T(8,128)(2,1)S(1)}, bf16[4,64,1664]{2,1,0:T(8,128)(2,1)S(1)}) custom-call(bf16[1056,512]{1,0:T(8,128)(2,1)S(1)} %get-tuple-element.128.x, bf16[1056,1536]{1,0:T(8,128)(2,1)S(1)} %attend_back.1.packed, f32[8,512]{1,0:T(8,128)S(1)} %get-tuple-element.140.gains, f32[8,512]{1,0:T(8,128)S(1)} %get-tuple-element.159.first_norms, ...), custom_call_target="tpu_custom_call" | custom-call | tf_op jit(solution)/shard_map/project_back/pallas_call | solution.py:545
  113.5 2.0 %collective-permute-done.24.got = bf16[4,64,1664]{2,1,0:T(8,128)(2,1)S(1)} collective-permute-done((bf16[4,64,1664]{2,1,0:T(8,128)(2,1)S(1)}, bf16[4,64,1664]{2,1,0:T(8,128)(2,1)S(1)}, u32[]{:S(2)}, u32[]{:S(2)}) %collective-permute-start.24) | collective-permute-done | bytes 852000 | tf_op jit(solution)/shard_map/ppermute | solution.py:72
  115.7 1.5 %collective-permute-start.25 = (bf16[64,1664]{1,0:T(8,128)(2,1)S(1)}, bf16[64,1664]{1,0:T(8,128)(2,1)S(1)}, u32[]{:S(2)}, u32[]{:S(2)}) collective-permute-start(bf16[64,1664]{1,0:T(8,128)(2,1)S(1)} %get-tuple-element.165), channel_id=1, source_target_pairs={{0,8},{1,9},{2,10},{3,11},{4,12},{5,13},{6,14},{7,15},{8,0},{9,1},... | collective-permute-start | bytes 638984 | tf_op jit(solution)/shard_map/ppermute | solution.py:69
  117.2 1.2 collective-permute-start.26
  120.0 1.8 %collective-permute-start.32 = (bf16[16,4608]{1,0:T(8,128)(2,1)S(1)}, bf16[16,4608]{1,0:T(8,128)(2,1)S(1)}, u32[]{:S(2)}, u32[]{:S(2)}) collective-permute-start(bf16[16,4608]{1,0:T(8,128)(2,1)S(1)} %get-tuple-element.189), channel_id=1, source_target_pairs={{0,2},{1,3},{2,0},{3,1},{4,20},{5,21},{6,22},{7,23},{8,10},{9,11},... | collective-permute-start | bytes 442376 | tf_op jit(solution)/shard_map/ppermute | solution.py:69
  121.8 2.0 %collective-permute-done.25.refs_0_ = bf16[64,1664]{1,0:T(8,128)(2,1)S(1)} collective-permute-done((bf16[64,1664]{1,0:T(8,128)(2,1)S(1)}, bf16[64,1664]{1,0:T(8,128)(2,1)S(1)}, u32[]{:S(2)}, u32[]{:S(2)}) %collective-permute-start.25) | collective-permute-done | bytes 213024 | tf_op jit(solution)/shard_map/ppermute | solution.py:69
  123.8 1.5 %collective-permute-start.33 = (bf16[16,4608]{1,0:T(8,128)(2,1)S(1)}, bf16[16,4608]{1,0:T(8,128)(2,1)S(1)}, u32[]{:S(2)}, u32[]{:S(2)}) collective-permute-start(bf16[16,4608]{1,0:T(8,128)(2,1)S(1)} %get-tuple-element.190), channel_id=1, source_target_pairs={{0,3},{1,0},{2,1},{3,2},{4,28},{5,29},{6,30},{7,31},{8,11},{9,8},{... | collective-permute-start | bytes 442376 | tf_op jit(solution)/shard_map/ppermute | solution.py:69
  125.4 4.3 %finish.1 = (bf16[1044,512]{1,0:T(8,128)(2,1)}, bf16[1044,512]{1,0:T(8,128)(2,1)}) custom-call(f32[8,128]{1,0:T(8,128)S(1)} %get-tuple-element.117.begin, f32[1056,512]{1,0:T(8,128)S(1)} %get-tuple-element.168.middle, bf16[1056,2048]{1,0:T(8,128)(2,1)S(1)} %get-tuple-element.169.active, bf16[2048,512]{1,0:T(8,128)(2,1)S(1)} %get-tuple-element.170.contract, ...), custom_call_target="tpu_custom_call" | custom-call | tf_op jit(solution)/shard_map/finish/pallas_call | solution.py:221
  130.5 2.1 %collective-permute-start.29 = (bf16[16,1664]{1,0:T(8,128)(2,1)S(1)}, bf16[16,1664]{1,0:T(8,128)(2,1)S(1)}, u32[]{:S(2)}, u32[]{:S(2)}) collective-permute-start(bf16[16,1664]{1,0:T(8,128)(2,1)S(1)} %get-tuple-element.181), channel_id=1, source_target_pairs={{0,2},{1,3},{2,0},{3,1},{4,6},{5,7},{6,4},{7,5},{8,10},{9,11},{10,... | collective-permute-start | bytes 159752 | tf_op jit(solution)/shard_map/ppermute | solution.py:69
  132.6 1.7 %collective-permute-start.30 = (bf16[16,1664]{1,0:T(8,128)(2,1)S(1)}, bf16[16,1664]{1,0:T(8,128)(2,1)S(1)}, u32[]{:S(2)}, u32[]{:S(2)}) collective-permute-start(bf16[16,1664]{1,0:T(8,128)(2,1)S(1)} %get-tuple-element.182), channel_id=1, source_target_pairs={{0,3},{1,0},{2,1},{3,2},{4,7},{5,4},{6,5},{7,6},{8,11},{9,8},{10,9... | collective-permute-start | bytes 159752 | tf_op jit(solution)/shard_map/ppermute | solution.py:69
  134.4 1.1 moments.2
  137.9 12.9 %all_to_all.5.sums = f32[32,1,128]{2,1,0:T(1,128)S(1)} all-to-all(f32[32,1,128]{2,1,0:T(1,128)S(1)} %get-tuple-element.192), channel_id=1, replica_groups=mesh['dp'=8,'rep'=4] {'dp','rep'}, dimensions={0} | all-to-all | bytes 32768 | tf_op jit(solution)/shard_map/all_to_all | solution.py:796
  (102 shorter events, 22.6 us)
Async XLA Ops:
  2.3 8.7 %collective-permute-start.2 = (bf16[16,1664]{1,0:T(8,128)(2,1)S(1)}, bf16[16,1664]{1,0:T(8,128)(2,1)S(1)}, u32[]{:S(2)}, u32[]{:S(2)}) collective-permute-start(bf16[16,1664]{1,0:T(8,128)(2,1)S(1)} %pack.1.refs_0_), channel_id=1, source_target_pairs={{0,3},{1,0},{2,1},{3,2},{4,7},{5,4},{6,5},{7,6},{8,11},{9,8},{10,9... | collective-permute-start | bytes 159752 | tf_op jit(solution)/shard_map/ppermute | solution.py:69
  7.4 5.1 %collective-permute-start.1 = (bf16[16,1664]{1,0:T(8,128)(2,1)S(1)}, bf16[16,1664]{1,0:T(8,128)(2,1)S(1)}, u32[]{:S(2)}, u32[]{:S(2)}) collective-permute-start(bf16[16,1664]{1,0:T(8,128)(2,1)S(1)} %pack.1.refs_0_), channel_id=1, source_target_pairs={{0,2},{1,3},{2,0},{3,1},{4,6},{5,7},{6,4},{7,5},{8,10},{9,11},{10,... | collective-permute-start | bytes 159752 | tf_op jit(solution)/shard_map/ppermute | solution.py:69
  7.4 5.9 %collective-permute-start = (bf16[16,1664]{1,0:T(8,128)(2,1)S(1)}, bf16[16,1664]{1,0:T(8,128)(2,1)S(1)}, u32[]{:S(2)}, u32[]{:S(2)}) collective-permute-start(bf16[16,1664]{1,0:T(8,128)(2,1)S(1)} %pack.1.refs_0_), channel_id=1, source_target_pairs={{0,1},{1,2},{2,3},{3,0},{4,5},{5,6},{6,7},{7,4},{8,9},{9,10},{10,1... | collective-permute-start | bytes 159752 | tf_op jit(solution)/shard_map/ppermute | solution.py:69
  13.3 5.4 %collective-permute-start.12 = (bf16[16,4608]{1,0:T(8,128)(2,1)S(1)}, bf16[16,4608]{1,0:T(8,128)(2,1)S(1)}, u32[]{:S(2)}, u32[]{:S(2)}) collective-permute-start(bf16[16,4608]{1,0:T(8,128)(2,1)S(1)} %slice_dynamic-update-slice_fusion.refs_0_), channel_id=1, source_target_pairs={{0,3},{1,0},{2,1},{3,2},{4,28},{5,29},{6,30},{7,31},{8,11},{9,8},{... | collective-permute-start | bytes 442376 | tf_op jit(solution)/shard_map/ppermute | solution.py:69
  14.9 12.7 %collective-permute-start.5 = (bf16[64,1664]{1,0:T(8,128)(2,1)S(1)}, bf16[64,1664]{1,0:T(8,128)(2,1)S(1)}, u32[]{:S(2)}, u32[]{:S(2)}) collective-permute-start(bf16[64,1664]{1,0:T(8,128)(2,1)S(1)} %column.2.refs_0_), channel_id=1, source_target_pairs={{0,24},{1,25},{2,26},{3,27},{4,28},{5,29},{6,30},{7,31},{8,16},{9,... | collective-permute-start | bytes 638984 | tf_op jit(solution)/shard_map/ppermute | solution.py:69
  17.5 10.2 %collective-permute-start.4 = (bf16[64,1664]{1,0:T(8,128)(2,1)S(1)}, bf16[64,1664]{1,0:T(8,128)(2,1)S(1)}, u32[]{:S(2)}, u32[]{:S(2)}) collective-permute-start(bf16[64,1664]{1,0:T(8,128)(2,1)S(1)} %column.2.refs_0_), channel_id=1, source_target_pairs={{0,16},{1,17},{2,18},{3,19},{4,20},{5,21},{6,22},{7,23},{8,24},{9,... | collective-permute-start | bytes 638984 | tf_op jit(solution)/shard_map/ppermute | solution.py:69
  18.0 9.7 %collective-permute-start.3 = (bf16[64,1664]{1,0:T(8,128)(2,1)S(1)}, bf16[64,1664]{1,0:T(8,128)(2,1)S(1)}, u32[]{:S(2)}, u32[]{:S(2)}) collective-permute-start(bf16[64,1664]{1,0:T(8,128)(2,1)S(1)} %column.2.refs_0_), channel_id=1, source_target_pairs={{0,8},{1,9},{2,10},{3,11},{4,12},{5,13},{6,14},{7,15},{8,0},{9,1},... | collective-permute-start | bytes 638984 | tf_op jit(solution)/shard_map/ppermute | solution.py:69
  18.5 9.1 %collective-permute-start.11 = (bf16[16,4608]{1,0:T(8,128)(2,1)S(1)}, bf16[16,4608]{1,0:T(8,128)(2,1)S(1)}, u32[]{:S(2)}, u32[]{:S(2)}) collective-permute-start(bf16[16,4608]{1,0:T(8,128)(2,1)S(1)} %slice_dynamic-update-slice_fusion.refs_0_), channel_id=1, source_target_pairs={{0,2},{1,3},{2,0},{3,1},{4,20},{5,21},{6,22},{7,23},{8,10},{9,11},... | collective-permute-start | bytes 442376 | tf_op jit(solution)/shard_map/ppermute | solution.py:69
  18.7 8.9 %collective-permute-start.10 = (bf16[16,4608]{1,0:T(8,128)(2,1)S(1)}, bf16[16,4608]{1,0:T(8,128)(2,1)S(1)}, u32[]{:S(2)}, u32[]{:S(2)}) collective-permute-start(bf16[16,4608]{1,0:T(8,128)(2,1)S(1)} %slice_dynamic-update-slice_fusion.refs_0_), channel_id=1, source_target_pairs={{0,1},{1,2},{2,3},{3,0},{4,12},{5,13},{6,14},{7,15},{8,9},{9,10},{... | collective-permute-start | bytes 442376 | tf_op jit(solution)/shard_map/ppermute | solution.py:69
  27.9 27.9 %collective-permute-start.15 = (bf16[64,4608]{1,0:T(8,128)(2,1)S(1)}, bf16[64,4608]{1,0:T(8,128)(2,1)S(1)}, u32[]{:S(2)}, u32[]{:S(2)}) collective-permute-start(bf16[64,4608]{1,0:T(8,128)(2,1)S(1)} %column.3.refs_0_), channel_id=1, source_target_pairs={{0,24},{1,25},{2,26},{3,27},{4,7},{5,4},{6,5},{7,6},{8,16},{9,17},... | collective-permute-start | bytes 1769480 | tf_op jit(solution)/shard_map/ppermute | solution.py:69
  30.4 25.4 %collective-permute-start.14 = (bf16[64,4608]{1,0:T(8,128)(2,1)S(1)}, bf16[64,4608]{1,0:T(8,128)(2,1)S(1)}, u32[]{:S(2)}, u32[]{:S(2)}) collective-permute-start(bf16[64,4608]{1,0:T(8,128)(2,1)S(1)} %column.3.refs_0_), channel_id=1, source_target_pairs={{0,16},{1,17},{2,18},{3,19},{4,6},{5,7},{6,4},{7,5},{8,24},{9,25},... | collective-permute-start | bytes 1769480 | tf_op jit(solution)/shard_map/ppermute | solution.py:69
  30.9 24.9 %collective-permute-start.13 = (bf16[64,4608]{1,0:T(8,128)(2,1)S(1)}, bf16[64,4608]{1,0:T(8,128)(2,1)S(1)}, u32[]{:S(2)}, u32[]{:S(2)}) collective-permute-start(bf16[64,4608]{1,0:T(8,128)(2,1)S(1)} %column.3.refs_0_), channel_id=1, source_target_pairs={{0,8},{1,9},{2,10},{3,11},{4,5},{5,6},{6,7},{7,4},{8,0},{9,1},{10,... | collective-permute-start | bytes 1769480 | tf_op jit(solution)/shard_map/ppermute | solution.py:69
  31.4 1.5 collective-permute-start.6
  31.6 1.6 %collective-permute-start.9 = (bf16[64,1664]{1,0:T(8,128)(2,1)S(1)}, bf16[64,1664]{1,0:T(8,128)(2,1)S(1)}, u32[]{:S(2)}, u32[]{:S(2)}) collective-permute-start(bf16[64,1664]{1,0:T(8,128)(2,1)S(1)} %collective-permute-done.5.refs_3_), channel_id=1, source_target_pairs={{0,4},{1,5},{2,6},{3,7},{4,0},{5,1},{6,2},{7,3},{8,12},{9,13},{10,... | collective-permute-start | bytes 638984 | tf_op jit(solution)/shard_map/ppermute | solution.py:72
  34.4 22.5 %collective-permute-start.16 = (bf16[64,4608]{1,0:T(8,128)(2,1)S(1)}, bf16[64,4608]{1,0:T(8,128)(2,1)S(1)}, u32[]{:S(2)}, u32[]{:S(2)}) collective-permute-start(bf16[64,4608]{1,0:T(8,128)(2,1)S(1)} %column.3.refs_0_), channel_id=1, source_target_pairs={{0,4},{1,5},{2,6},{3,7},{4,0},{5,1},{6,2},{7,3},{8,12},{9,13},{10,... | collective-permute-start | bytes 1769480 | tf_op jit(solution)/shard_map/ppermute | solution.py:72
  55.8 2.2 %collective-permute-start.17 = (bf16[64,4608]{1,0:T(8,128)(2,1)S(1)}, bf16[64,4608]{1,0:T(8,128)(2,1)S(1)}, u32[]{:S(2)}, u32[]{:S(2)}) collective-permute-start(bf16[64,4608]{1,0:T(8,128)(2,1)S(1)} %collective-permute-done.13.refs_1_), channel_id=1, source_target_pairs={{0,4},{1,5},{2,6},{3,7},{4,0},{5,1},{6,2},{7,3},{8,12},{9,13},{10,... | collective-permute-start | bytes 1769480 | tf_op jit(solution)/shard_map/ppermute | solution.py:72
  56.4 2.5 %collective-permute-start.18 = (bf16[64,4608]{1,0:T(8,128)(2,1)S(1)}, bf16[64,4608]{1,0:T(8,128)(2,1)S(1)}, u32[]{:S(2)}, u32[]{:S(2)}) collective-permute-start(bf16[64,4608]{1,0:T(8,128)(2,1)S(1)} %collective-permute-done.14.refs_2_), channel_id=1, source_target_pairs={{0,4},{1,5},{2,6},{3,7},{4,0},{5,1},{6,2},{7,3},{8,12},{9,13},{10,... | collective-permute-start | bytes 1769480 | tf_op jit(solution)/shard_map/ppermute | solution.py:72
  56.4 3.3 %collective-permute-start.19 = (bf16[64,4608]{1,0:T(8,128)(2,1)S(1)}, bf16[64,4608]{1,0:T(8,128)(2,1)S(1)}, u32[]{:S(2)}, u32[]{:S(2)}) collective-permute-start(bf16[64,4608]{1,0:T(8,128)(2,1)S(1)} %collective-permute-done.15.refs_3_), channel_id=1, source_target_pairs={{0,4},{1,5},{2,6},{3,7},{4,0},{5,1},{6,2},{7,3},{8,12},{9,13},{10,... | collective-permute-start | bytes 1769480 | tf_op jit(solution)/shard_map/ppermute | solution.py:72
  78.0 4.6 %collective-permute-start.20 = (bf16[4,64,4608]{2,1,0:T(8,128)(2,1)S(1)}, bf16[4,64,4608]{2,1,0:T(8,128)(2,1)S(1)}, u32[]{:S(2)}, u32[]{:S(2)}) collective-permute-start(bf16[4,64,4608]{2,1,0:T(8,128)(2,1)S(1)} %get-tuple-element.151), channel_id=1, source_target_pairs={{0,4},{1,5},{2,6},{3,7},{4,0},{5,1},{6,2},{7,3},{8,12},{9,13},{10,... | collective-permute-start | bytes 7077896 | tf_op jit(solution)/shard_map/ppermute | solution.py:72
  83.2 29.5 %collective-permute-start.21 = (bf16[64,4608]{1,0:T(8,128)(2,1)S(1)}, bf16[64,4608]{1,0:T(8,128)(2,1)S(1)}, u32[]{:S(2)}, u32[]{:S(2)}) collective-permute-start(bf16[64,4608]{1,0:T(8,128)(2,1)S(1)} %get-tuple-element.154), channel_id=1, source_target_pairs={{0,8},{1,9},{2,10},{3,11},{4,5},{5,6},{6,7},{7,4},{8,0},{9,1},{10,... | collective-permute-start | bytes 1769480 | tf_op jit(solution)/shard_map/ppermute | solution.py:69
  84.7 27.9 %collective-permute-start.22 = (bf16[64,4608]{1,0:T(8,128)(2,1)S(1)}, bf16[64,4608]{1,0:T(8,128)(2,1)S(1)}, u32[]{:S(2)}, u32[]{:S(2)}) collective-permute-start(bf16[64,4608]{1,0:T(8,128)(2,1)S(1)} %get-tuple-element.155), channel_id=1, source_target_pairs={{0,16},{1,17},{2,18},{3,19},{4,6},{5,7},{6,4},{7,5},{8,24},{9,25},... | collective-permute-start | bytes 1769480 | tf_op jit(solution)/shard_map/ppermute | solution.py:69
  86.1 26.5 %collective-permute-start.23 = (bf16[64,4608]{1,0:T(8,128)(2,1)S(1)}, bf16[64,4608]{1,0:T(8,128)(2,1)S(1)}, u32[]{:S(2)}, u32[]{:S(2)}) collective-permute-start(bf16[64,4608]{1,0:T(8,128)(2,1)S(1)} %get-tuple-element.156), channel_id=1, source_target_pairs={{0,24},{1,25},{2,26},{3,27},{4,7},{5,4},{6,5},{7,6},{8,16},{9,17},... | collective-permute-start | bytes 1769480 | tf_op jit(solution)/shard_map/ppermute | solution.py:69
  112.6 2.8 %collective-permute-start.24 = (bf16[4,64,1664]{2,1,0:T(8,128)(2,1)S(1)}, bf16[4,64,1664]{2,1,0:T(8,128)(2,1)S(1)}, u32[]{:S(2)}, u32[]{:S(2)}) collective-permute-start(bf16[4,64,1664]{2,1,0:T(8,128)(2,1)S(1)} %get-tuple-element.164), channel_id=1, source_target_pairs={{0,4},{1,5},{2,6},{3,7},{4,0},{5,1},{6,2},{7,3},{8,12},{9,13},{10,... | collective-permute-start | bytes 2555912 | tf_op jit(solution)/shard_map/ppermute | solution.py:72
  115.7 8.2 %collective-permute-start.25 = (bf16[64,1664]{1,0:T(8,128)(2,1)S(1)}, bf16[64,1664]{1,0:T(8,128)(2,1)S(1)}, u32[]{:S(2)}, u32[]{:S(2)}) collective-permute-start(bf16[64,1664]{1,0:T(8,128)(2,1)S(1)} %get-tuple-element.165), channel_id=1, source_target_pairs={{0,8},{1,9},{2,10},{3,11},{4,12},{5,13},{6,14},{7,15},{8,0},{9,1},... | collective-permute-start | bytes 638984 | tf_op jit(solution)/shard_map/ppermute | solution.py:69
  117.2 12.7 %collective-permute-start.26 = (bf16[64,1664]{1,0:T(8,128)(2,1)S(1)}, bf16[64,1664]{1,0:T(8,128)(2,1)S(1)}, u32[]{:S(2)}, u32[]{:S(2)}) collective-permute-start(bf16[64,1664]{1,0:T(8,128)(2,1)S(1)} %get-tuple-element.166), channel_id=1, source_target_pairs={{0,16},{1,17},{2,18},{3,19},{4,20},{5,21},{6,22},{7,23},{8,24},{9,... | collective-permute-start | bytes 638984 | tf_op jit(solution)/shard_map/ppermute | solution.py:69
  118.4 11.5 %collective-permute-start.27 = (bf16[64,1664]{1,0:T(8,128)(2,1)S(1)}, bf16[64,1664]{1,0:T(8,128)(2,1)S(1)}, u32[]{:S(2)}, u32[]{:S(2)}) collective-permute-start(bf16[64,1664]{1,0:T(8,128)(2,1)S(1)} %get-tuple-element.167), channel_id=1, source_target_pairs={{0,24},{1,25},{2,26},{3,27},{4,28},{5,29},{6,30},{7,31},{8,16},{9,... | collective-permute-start | bytes 638984 | tf_op jit(solution)/shard_map/ppermute | solution.py:69
  119.7 13.0 %collective-permute-start.31 = (bf16[16,4608]{1,0:T(8,128)(2,1)S(1)}, bf16[16,4608]{1,0:T(8,128)(2,1)S(1)}, u32[]{:S(2)}, u32[]{:S(2)}) collective-permute-start(bf16[16,4608]{1,0:T(8,128)(2,1)S(1)} %get-tuple-element.188), channel_id=1, source_target_pairs={{0,1},{1,2},{2,3},{3,0},{4,12},{5,13},{6,14},{7,15},{8,9},{9,10},{... | collective-permute-start | bytes 442376 | tf_op jit(solution)/shard_map/ppermute | solution.py:69
  120.0 14.3 %collective-permute-start.32 = (bf16[16,4608]{1,0:T(8,128)(2,1)S(1)}, bf16[16,4608]{1,0:T(8,128)(2,1)S(1)}, u32[]{:S(2)}, u32[]{:S(2)}) collective-permute-start(bf16[16,4608]{1,0:T(8,128)(2,1)S(1)} %get-tuple-element.189), channel_id=1, source_target_pairs={{0,2},{1,3},{2,0},{3,1},{4,20},{5,21},{6,22},{7,23},{8,10},{9,11},... | collective-permute-start | bytes 442376 | tf_op jit(solution)/shard_map/ppermute | solution.py:69
  123.8 10.5 %collective-permute-start.33 = (bf16[16,4608]{1,0:T(8,128)(2,1)S(1)}, bf16[16,4608]{1,0:T(8,128)(2,1)S(1)}, u32[]{:S(2)}, u32[]{:S(2)}) collective-permute-start(bf16[16,4608]{1,0:T(8,128)(2,1)S(1)} %get-tuple-element.190), channel_id=1, source_target_pairs={{0,3},{1,0},{2,1},{3,2},{4,28},{5,29},{6,30},{7,31},{8,11},{9,8},{... | collective-permute-start | bytes 442376 | tf_op jit(solution)/shard_map/ppermute | solution.py:69
  130.1 6.1 %collective-permute-start.28 = (bf16[16,1664]{1,0:T(8,128)(2,1)S(1)}, bf16[16,1664]{1,0:T(8,128)(2,1)S(1)}, u32[]{:S(2)}, u32[]{:S(2)}) collective-permute-start(bf16[16,1664]{1,0:T(8,128)(2,1)S(1)} %get-tuple-element.180), channel_id=1, source_target_pairs={{0,1},{1,2},{2,3},{3,0},{4,5},{5,6},{6,7},{7,4},{8,9},{9,10},{10,1... | collective-permute-start | bytes 159752 | tf_op jit(solution)/shard_map/ppermute | solution.py:69
  130.5 6.5 %collective-permute-start.29 = (bf16[16,1664]{1,0:T(8,128)(2,1)S(1)}, bf16[16,1664]{1,0:T(8,128)(2,1)S(1)}, u32[]{:S(2)}, u32[]{:S(2)}) collective-permute-start(bf16[16,1664]{1,0:T(8,128)(2,1)S(1)} %get-tuple-element.181), channel_id=1, source_target_pairs={{0,2},{1,3},{2,0},{3,1},{4,6},{5,7},{6,4},{7,5},{8,10},{9,11},{10,... | collective-permute-start | bytes 159752 | tf_op jit(solution)/shard_map/ppermute | solution.py:69
  132.6 4.4 %collective-permute-start.30 = (bf16[16,1664]{1,0:T(8,128)(2,1)S(1)}, bf16[16,1664]{1,0:T(8,128)(2,1)S(1)}, u32[]{:S(2)}, u32[]{:S(2)}) collective-permute-start(bf16[16,1664]{1,0:T(8,128)(2,1)S(1)} %get-tuple-element.182), channel_id=1, source_target_pairs={{0,3},{1,0},{2,1},{3,2},{4,7},{5,4},{6,5},{7,6},{8,11},{9,8},{10,9... | collective-permute-start | bytes 159752 | tf_op jit(solution)/shard_map/ppermute | solution.py:69
  (22 other events, 132.1 us)

commit v10 on v9

--- a/solution.py
+++ b/solution.py
@@ -519,12 +519,13 @@
     gain, bias = gains[0:1], gains[1:2]
 
     def one_chunk(i, carry):
-        span = pl.ds(pl.multiple_of(i * CHUNK, CHUNK), CHUNK)
+        span = pl.ds(i * CHUNK, CHUNK)
         normed, _ = normalize(x[span].astype(jnp.float32))
         first[span] = (normed * gain + bias).astype(jnp.bfloat16)
         return carry
 
-    lax.fori_loop(0, rows // CHUNK, one_chunk, 0)
+    for i in range(rows // CHUNK):
+        one_chunk(i, 0)
 
     def one_block(i, carry):
         columns = pl.ds(pl.multiple_of(i * 512, 512), 512)
@@ -563,14 +564,17 @@
 
     def one_chunk(i, carry):
         gain_sum, bias_sum = carry
-        span = pl.ds(pl.multiple_of(i * CHUNK, CHUNK), CHUNK)
+        span = pl.ds(i * CHUNK, CHUNK)
         normed, scale = normalize(x[span].astype(jnp.float32))
         back = dot(packed[span], weight[:, : 3 * width], 1, 1)
         grad_in[span] = (middle_grad[span] + norm_back(back, normed, scale, gain)).astype(jnp.bfloat16)
         gain_sum = gain_sum + jnp.sum(back * normed, axis=0, keepdims=True)
         return gain_sum, bias_sum + jnp.sum(back, axis=0, keepdims=True)
 
-    gain_sum, bias_sum = lax.fori_loop(0, rows // CHUNK, one_chunk, (zero, zero))
+    sums = (zero, zero)
+    for i in range(rows // CHUNK):
+        sums = one_chunk(i, sums)
+    gain_sum, bias_sum = sums
     norm_grads[...] = jnp.concatenate([gain_sum, bias_sum, jnp.zeros((6, width), jnp.float32)], axis=0)
 
 

time: 152 us -> 151 us (level)
  no operation moved by 1% of the time
where the time goes in v10:
time: 151 us
  Pallas kernels  77.3 us (51%)
  starting transfers between devices  35 us (23%)
  waiting for transfers between devices  17.4 us (12%)
  blocking collectives  12.9 us (9%)
  local copies, waits for them, and re-layouts  4.81 us (3%)
  other arithmetic  2.59 us (2%)
    ppermute x24, starting transfers between devices, over(): return lax.ppermute(value, AXES, self.pairs(move))  31.6 us
    pallas_call x1, Pallas kernels, attend(): pl.pallas_call(partial(attend_kernel, lay, len(pieces)), out_shape=(wide,...  21.1 us
    pallas_call x1, Pallas kernels, attend_back(): pl.pallas_call(attend_back_kernel, out_shape=jax.ShapeDtypeStruct((rows,...  18.8 us
    pallas_call x1, Pallas kernels, feed(): pl.pallas_call(partial(feed_kernel, lay, len(pieces), len(deep_pieces)),...  18.3 us
    all_to_all x1, blocking collectives, exchange(): return lax.all_to_all(value, AXES, 0, 0)  12.9 us
    ppermute x24, waiting for transfers between devices, over(): return lax.ppermute(value, AXES, self.pairs(move))  9 us
    ppermute x10, waiting for transfers between devices, to_core(): return lax.ppermute(value, AXES, self.pairs(lambda p, c, z: (p, 1 - c, z)))  8.44 us
    unnamed x43, local copies, waits for them, and re-layouts  4.8 us
  transfers between devices with their start and end apart: 34, of which 16 were waited for; matrix products, arithmetic and copies ran while one was open for 2% of the time, Pallas kernels for 37%

profile of v10, /device:TPU:0, one launch (start us, length us, event | category | flops | bytes accessed | tf_op | source)
XLA Modules:
  0.0 151.1 jit_solution(5770498658178157533)
XLA Ops:
  2.3 5.0 %collective-permute-start.2 = (bf16[16,1664]{1,0:T(8,128)(2,1)S(1)}, bf16[16,1664]{1,0:T(8,128)(2,1)S(1)}, u32[]{:S(2)}, u32[]{:S(2)}) collective-permute-start(bf16[16,1664]{1,0:T(8,128)(2,1)S(1)} %pack.1.refs_0_), channel_id=1, source_target_pairs={{0,3},{1,0},{2,1},{3,2},{4,7},{5,4},{6,5},{7,6},{8,11},{9,8},{10,9... | collective-permute-start | bytes 159752 | tf_op jit(solution)/shard_map/ppermute | solution.py:69
  7.4 1.0 collective-permute-start
  11.0 1.4 collective-permute-done.1.refs_2_
  13.3 1.5 %collective-permute-start.12 = (bf16[16,4608]{1,0:T(8,128)(2,1)S(1)}, bf16[16,4608]{1,0:T(8,128)(2,1)S(1)}, u32[]{:S(2)}, u32[]{:S(2)}) collective-permute-start(bf16[16,4608]{1,0:T(8,128)(2,1)S(1)} %slice_dynamic-update-slice_fusion.refs_0_), channel_id=1, source_target_pairs={{0,3},{1,0},{2,1},{3,2},{4,28},{5,29},{6,30},{7,31},{8,11},{9,8},{... | collective-permute-start | bytes 442376 | tf_op jit(solution)/shard_map/ppermute | solution.py:69
  14.9 2.5 %collective-permute-start.5 = (bf16[64,1664]{1,0:T(8,128)(2,1)S(1)}, bf16[64,1664]{1,0:T(8,128)(2,1)S(1)}, u32[]{:S(2)}, u32[]{:S(2)}) collective-permute-start(bf16[64,1664]{1,0:T(8,128)(2,1)S(1)} %column.2.refs_0_), channel_id=1, source_target_pairs={{0,24},{1,25},{2,26},{3,27},{4,28},{5,29},{6,30},{7,31},{8,16},{9,... | collective-permute-start | bytes 638984 | tf_op jit(solution)/shard_map/ppermute | solution.py:69
  18.7 1.7 %collective-permute-start.10 = (bf16[16,4608]{1,0:T(8,128)(2,1)S(1)}, bf16[16,4608]{1,0:T(8,128)(2,1)S(1)}, u32[]{:S(2)}, u32[]{:S(2)}) collective-permute-start(bf16[16,4608]{1,0:T(8,128)(2,1)S(1)} %slice_dynamic-update-slice_fusion.refs_0_), channel_id=1, source_target_pairs={{0,1},{1,2},{2,3},{3,0},{4,12},{5,13},{6,14},{7,15},{8,9},{9,10},{... | collective-permute-start | bytes 442376 | tf_op jit(solution)/shard_map/ppermute | solution.py:69
  20.4 1.2 copy-done.2
  21.6 1.2 copy-done.3
  23.5 1.1 arrange.1
  24.6 3.0 %collective-permute-done.11.refs_2_ = bf16[16,4608]{1,0:T(8,128)(2,1)S(1)} collective-permute-done((bf16[16,4608]{1,0:T(8,128)(2,1)S(1)}, bf16[16,4608]{1,0:T(8,128)(2,1)S(1)}, u32[]{:S(2)}, u32[]{:S(2)}) %collective-permute-start.11) | collective-permute-done | bytes 147488 | tf_op jit(solution)/shard_map/ppermute | solution.py:69
  27.9 2.5 %collective-permute-start.15 = (bf16[64,4608]{1,0:T(8,128)(2,1)S(1)}, bf16[64,4608]{1,0:T(8,128)(2,1)S(1)}, u32[]{:S(2)}, u32[]{:S(2)}) collective-permute-start(bf16[64,4608]{1,0:T(8,128)(2,1)S(1)} %column.3.refs_0_), channel_id=1, source_target_pairs={{0,24},{1,25},{2,26},{3,27},{4,7},{5,4},{6,5},{7,6},{8,16},{9,17},... | collective-permute-start | bytes 1769480 | tf_op jit(solution)/shard_map/ppermute | solution.py:69
  34.7 21.1 %attend.1 = (bf16[1056,1024]{1,0:T(8,128)(2,1)S(1)}, bf16[1056,1024]{1,0:T(8,128)(2,1)S(1)}, bf16[1056,1024]{1,0:T(8,128)(2,1)S(1)}, bf16[1056,512]{1,0:T(8,128)(2,1)S(1)}, f32[8,512]{1,0:T(8,128)S(1)}) custom-call(bf16[1056,512]{1,0:T(8,128)(2,1)S(1)} %get-tuple-element.128.x, s32[1056,128]{1,0:T(8,128)S(1)} %get-tuple-element.129.labels, ...), custom_call_target="tpu_custom_call" | custom-call | tf_op jit(solution)/shard_map/attend/pallas_call | solution.py:303
  56.9 1.1 collective-permute-done.17.refs_5_
  59.7 18.3 %feed.1 = (f32[1056,512]{1,0:T(8,128)S(1)}, f32[1056,512]{1,0:T(8,128)S(1)}, bf16[1056,512]{1,0:T(8,128)(2,1)S(1)}, bf16[1056,2048]{1,0:T(8,128)(2,1)S(1)}, bf16...) custom-call(bf16[1056,512]{1,0:T(8,128)(2,1)S(1)} %get-tuple-element, ...), custom_call_target="tpu_custom_call" | custom-call | tf_op jit(solution)/shard_map/feed/pallas_call | solution.py:461
  78.5 2.7 %mixed_back.1.dox = bf16[1056,1024]{1,0:T(8,128)(2,1)S(1)} custom-call(bf16[1056,512]{1,0:T(8,128)(2,1)S(1)} %get-tuple-element.148.middle_low, bf16[1056,512]{1,0:T(8,128)(2,1)S(1)} %get-tuple-element.138.mixed, bf16[512,512]{1,0:T(8,128)(2,1)S(1)} %get-tuple-element.149.out_weight), custom_call_target="tpu_custom_call" | custom-call | tf_op jit(solution)/shard_map/mixed_back/pallas_call | solution.py:507
  81.2 1.5 collective-permute-done.20.got
  83.2 1.5 %collective-permute-start.21 = (bf16[64,4608]{1,0:T(8,128)(2,1)S(1)}, bf16[64,4608]{1,0:T(8,128)(2,1)S(1)}, u32[]{:S(2)}, u32[]{:S(2)}) collective-permute-start(bf16[64,4608]{1,0:T(8,128)(2,1)S(1)} %get-tuple-element.154), channel_id=1, source_target_pairs={{0,8},{1,9},{2,10},{3,11},{4,5},{5,6},{6,7},{7,4},{8,0},{9,1},{10,... | collective-permute-start | bytes 1769480 | tf_op jit(solution)/shard_map/ppermute | solution.py:69
  84.7 1.4 collective-permute-start.22
  86.7 18.8 %attend_back.1.packed = bf16[1056,1536]{1,0:T(8,128)(2,1)S(1)} custom-call(bf16[1056,1024]{1,0:T(8,128)(2,1)S(1)} %get-tuple-element.145.qx, bf16[1056,1024]{1,0:T(8,128)(2,1)S(1)} %get-tuple-element.146.kx, bf16[1056,1024]{1,0:T(8,128)(2,1)S(1)} %get-tuple-element.147.vx, bf16[1056,1024]{1,0:T(8,128)(2,1)S(1)} %mixed_back.1.dox), custom_call_target="tpu_custom_call" | custom-call | tf_op jit(solution)/shard_map/attend_back/pallas_call | solution.py:357
  105.5 2.6 %input_back.1 = (bf16[1056,512]{1,0:T(8,128)(2,1)S(1)}, f32[8,512]{1,0:T(8,128)S(1)}) custom-call(bf16[1056,512]{1,0:T(8,128)(2,1)S(1)} %get-tuple-element.128.x, bf16[1056,1536]{1,0:T(8,128)(2,1)S(1)} %attend_back.1.packed, f32[8,512]{1,0:T(8,128)S(1)} %get-tuple-element.140.gains, f32[1056,512]{1,0:T(8,128)S(1)} %get-tuple-element.158.middle_grad, ...), custom_call_target="tpu_custom_call" | custom-call | tf_op jit(solution)/shard_map/input_back/pallas_call | solution.py:583
  108.2 3.8 %project_back.1 = (bf16[4,64,1664]{2,1,0:T(8,128)(2,1)S(1)}, bf16[4,64,1664]{2,1,0:T(8,128)(2,1)S(1)}) custom-call(bf16[1056,512]{1,0:T(8,128)(2,1)S(1)} %get-tuple-element.128.x, bf16[1056,1536]{1,0:T(8,128)(2,1)S(1)} %attend_back.1.packed, f32[8,512]{1,0:T(8,128)S(1)} %get-tuple-element.140.gains, f32[8,512]{1,0:T(8,128)S(1)} %get-tuple-element.159.first_norms, ...), custom_call_target="tpu_custom_call" | custom-call | tf_op jit(solution)/shard_map/project_back/pallas_call | solution.py:546
  112.8 2.0 %collective-permute-done.24.got = bf16[4,64,1664]{2,1,0:T(8,128)(2,1)S(1)} collective-permute-done((bf16[4,64,1664]{2,1,0:T(8,128)(2,1)S(1)}, bf16[4,64,1664]{2,1,0:T(8,128)(2,1)S(1)}, u32[]{:S(2)}, u32[]{:S(2)}) %collective-permute-start.24) | collective-permute-done | bytes 852000 | tf_op jit(solution)/shard_map/ppermute | solution.py:72
  115.0 1.5 %collective-permute-start.25 = (bf16[64,1664]{1,0:T(8,128)(2,1)S(1)}, bf16[64,1664]{1,0:T(8,128)(2,1)S(1)}, u32[]{:S(2)}, u32[]{:S(2)}) collective-permute-start(bf16[64,1664]{1,0:T(8,128)(2,1)S(1)} %get-tuple-element.165), channel_id=1, source_target_pairs={{0,8},{1,9},{2,10},{3,11},{4,12},{5,13},{6,14},{7,15},{8,0},{9,1},... | collective-permute-start | bytes 638984 | tf_op jit(solution)/shard_map/ppermute | solution.py:69
  116.6 1.2 collective-permute-start.26
  119.4 1.8 %collective-permute-start.32 = (bf16[16,4608]{1,0:T(8,128)(2,1)S(1)}, bf16[16,4608]{1,0:T(8,128)(2,1)S(1)}, u32[]{:S(2)}, u32[]{:S(2)}) collective-permute-start(bf16[16,4608]{1,0:T(8,128)(2,1)S(1)} %get-tuple-element.189), channel_id=1, source_target_pairs={{0,2},{1,3},{2,0},{3,1},{4,20},{5,21},{6,22},{7,23},{8,10},{9,11},... | collective-permute-start | bytes 442376 | tf_op jit(solution)/shard_map/ppermute | solution.py:69
  121.1 2.0 %collective-permute-done.25.refs_0_ = bf16[64,1664]{1,0:T(8,128)(2,1)S(1)} collective-permute-done((bf16[64,1664]{1,0:T(8,128)(2,1)S(1)}, bf16[64,1664]{1,0:T(8,128)(2,1)S(1)}, u32[]{:S(2)}, u32[]{:S(2)}) %collective-permute-start.25) | collective-permute-done | bytes 213024 | tf_op jit(solution)/shard_map/ppermute | solution.py:69
  123.2 1.5 %collective-permute-start.33 = (bf16[16,4608]{1,0:T(8,128)(2,1)S(1)}, bf16[16,4608]{1,0:T(8,128)(2,1)S(1)}, u32[]{:S(2)}, u32[]{:S(2)}) collective-permute-start(bf16[16,4608]{1,0:T(8,128)(2,1)S(1)} %get-tuple-element.190), channel_id=1, source_target_pairs={{0,3},{1,0},{2,1},{3,2},{4,28},{5,29},{6,30},{7,31},{8,11},{9,8},{... | collective-permute-start | bytes 442376 | tf_op jit(solution)/shard_map/ppermute | solution.py:69
  124.8 4.3 %finish.1 = (bf16[1044,512]{1,0:T(8,128)(2,1)}, bf16[1044,512]{1,0:T(8,128)(2,1)}) custom-call(f32[8,128]{1,0:T(8,128)S(1)} %get-tuple-element.117.begin, f32[1056,512]{1,0:T(8,128)S(1)} %get-tuple-element.168.middle, bf16[1056,2048]{1,0:T(8,128)(2,1)S(1)} %get-tuple-element.169.active, bf16[2048,512]{1,0:T(8,128)(2,1)S(1)} %get-tuple-element.170.contract, ...), custom_call_target="tpu_custom_call" | custom-call | tf_op jit(solution)/shard_map/finish/pallas_call | solution.py:221
  129.9 2.1 %collective-permute-start.29 = (bf16[16,1664]{1,0:T(8,128)(2,1)S(1)}, bf16[16,1664]{1,0:T(8,128)(2,1)S(1)}, u32[]{:S(2)}, u32[]{:S(2)}) collective-permute-start(bf16[16,1664]{1,0:T(8,128)(2,1)S(1)} %get-tuple-element.181), channel_id=1, source_target_pairs={{0,2},{1,3},{2,0},{3,1},{4,6},{5,7},{6,4},{7,5},{8,10},{9,11},{10,... | collective-permute-start | bytes 159752 | tf_op jit(solution)/shard_map/ppermute | solution.py:69
  132.0 1.7 %collective-permute-start.30 = (bf16[16,1664]{1,0:T(8,128)(2,1)S(1)}, bf16[16,1664]{1,0:T(8,128)(2,1)S(1)}, u32[]{:S(2)}, u32[]{:S(2)}) collective-permute-start(bf16[16,1664]{1,0:T(8,128)(2,1)S(1)} %get-tuple-element.182), channel_id=1, source_target_pairs={{0,3},{1,0},{2,1},{3,2},{4,7},{5,4},{6,5},{7,6},{8,11},{9,8},{10,9... | collective-permute-start | bytes 159752 | tf_op jit(solution)/shard_map/ppermute | solution.py:69
  133.8 1.1 moments.2
  137.2 12.9 %all_to_all.5.sums = f32[32,1,128]{2,1,0:T(1,128)S(1)} all-to-all(f32[32,1,128]{2,1,0:T(1,128)S(1)} %get-tuple-element.192), channel_id=1, replica_groups=mesh['dp'=8,'rep'=4] {'dp','rep'}, dimensions={0} | all-to-all | bytes 32768 | tf_op jit(solution)/shard_map/all_to_all | solution.py:800
  (102 shorter events, 22.6 us)
Async XLA Ops:
  2.3 8.7 %collective-permute-start.2 = (bf16[16,1664]{1,0:T(8,128)(2,1)S(1)}, bf16[16,1664]{1,0:T(8,128)(2,1)S(1)}, u32[]{:S(2)}, u32[]{:S(2)}) collective-permute-start(bf16[16,1664]{1,0:T(8,128)(2,1)S(1)} %pack.1.refs_0_), channel_id=1, source_target_pairs={{0,3},{1,0},{2,1},{3,2},{4,7},{5,4},{6,5},{7,6},{8,11},{9,8},{10,9... | collective-permute-start | bytes 159752 | tf_op jit(solution)/shard_map/ppermute | solution.py:69
  7.4 5.1 %collective-permute-start.1 = (bf16[16,1664]{1,0:T(8,128)(2,1)S(1)}, bf16[16,1664]{1,0:T(8,128)(2,1)S(1)}, u32[]{:S(2)}, u32[]{:S(2)}) collective-permute-start(bf16[16,1664]{1,0:T(8,128)(2,1)S(1)} %pack.1.refs_0_), channel_id=1, source_target_pairs={{0,2},{1,3},{2,0},{3,1},{4,6},{5,7},{6,4},{7,5},{8,10},{9,11},{10,... | collective-permute-start | bytes 159752 | tf_op jit(solution)/shard_map/ppermute | solution.py:69
  7.4 5.9 %collective-permute-start = (bf16[16,1664]{1,0:T(8,128)(2,1)S(1)}, bf16[16,1664]{1,0:T(8,128)(2,1)S(1)}, u32[]{:S(2)}, u32[]{:S(2)}) collective-permute-start(bf16[16,1664]{1,0:T(8,128)(2,1)S(1)} %pack.1.refs_0_), channel_id=1, source_target_pairs={{0,1},{1,2},{2,3},{3,0},{4,5},{5,6},{6,7},{7,4},{8,9},{9,10},{10,1... | collective-permute-start | bytes 159752 | tf_op jit(solution)/shard_map/ppermute | solution.py:69
  13.3 5.4 %collective-permute-start.12 = (bf16[16,4608]{1,0:T(8,128)(2,1)S(1)}, bf16[16,4608]{1,0:T(8,128)(2,1)S(1)}, u32[]{:S(2)}, u32[]{:S(2)}) collective-permute-start(bf16[16,4608]{1,0:T(8,128)(2,1)S(1)} %slice_dynamic-update-slice_fusion.refs_0_), channel_id=1, source_target_pairs={{0,3},{1,0},{2,1},{3,2},{4,28},{5,29},{6,30},{7,31},{8,11},{9,8},{... | collective-permute-start | bytes 442376 | tf_op jit(solution)/shard_map/ppermute | solution.py:69
  14.9 12.7 %collective-permute-start.5 = (bf16[64,1664]{1,0:T(8,128)(2,1)S(1)}, bf16[64,1664]{1,0:T(8,128)(2,1)S(1)}, u32[]{:S(2)}, u32[]{:S(2)}) collective-permute-start(bf16[64,1664]{1,0:T(8,128)(2,1)S(1)} %column.2.refs_0_), channel_id=1, source_target_pairs={{0,24},{1,25},{2,26},{3,27},{4,28},{5,29},{6,30},{7,31},{8,16},{9,... | collective-permute-start | bytes 638984 | tf_op jit(solution)/shard_map/ppermute | solution.py:69
  17.5 10.2 %collective-permute-start.4 = (bf16[64,1664]{1,0:T(8,128)(2,1)S(1)}, bf16[64,1664]{1,0:T(8,128)(2,1)S(1)}, u32[]{:S(2)}, u32[]{:S(2)}) collective-permute-start(bf16[64,1664]{1,0:T(8,128)(2,1)S(1)} %column.2.refs_0_), channel_id=1, source_target_pairs={{0,16},{1,17},{2,18},{3,19},{4,20},{5,21},{6,22},{7,23},{8,24},{9,... | collective-permute-start | bytes 638984 | tf_op jit(solution)/shard_map/ppermute | solution.py:69
  18.0 9.7 %collective-permute-start.3 = (bf16[64,1664]{1,0:T(8,128)(2,1)S(1)}, bf16[64,1664]{1,0:T(8,128)(2,1)S(1)}, u32[]{:S(2)}, u32[]{:S(2)}) collective-permute-start(bf16[64,1664]{1,0:T(8,128)(2,1)S(1)} %column.2.refs_0_), channel_id=1, source_target_pairs={{0,8},{1,9},{2,10},{3,11},{4,12},{5,13},{6,14},{7,15},{8,0},{9,1},... | collective-permute-start | bytes 638984 | tf_op jit(solution)/shard_map/ppermute | solution.py:69
  18.5 9.1 %collective-permute-start.11 = (bf16[16,4608]{1,0:T(8,128)(2,1)S(1)}, bf16[16,4608]{1,0:T(8,128)(2,1)S(1)}, u32[]{:S(2)}, u32[]{:S(2)}) collective-permute-start(bf16[16,4608]{1,0:T(8,128)(2,1)S(1)} %slice_dynamic-update-slice_fusion.refs_0_), channel_id=1, source_target_pairs={{0,2},{1,3},{2,0},{3,1},{4,20},{5,21},{6,22},{7,23},{8,10},{9,11},... | collective-permute-start | bytes 442376 | tf_op jit(solution)/shard_map/ppermute | solution.py:69
  18.7 8.9 %collective-permute-start.10 = (bf16[16,4608]{1,0:T(8,128)(2,1)S(1)}, bf16[16,4608]{1,0:T(8,128)(2,1)S(1)}, u32[]{:S(2)}, u32[]{:S(2)}) collective-permute-start(bf16[16,4608]{1,0:T(8,128)(2,1)S(1)} %slice_dynamic-update-slice_fusion.refs_0_), channel_id=1, source_target_pairs={{0,1},{1,2},{2,3},{3,0},{4,12},{5,13},{6,14},{7,15},{8,9},{9,10},{... | collective-permute-start | bytes 442376 | tf_op jit(solution)/shard_map/ppermute | solution.py:69
  27.9 27.9 %collective-permute-start.15 = (bf16[64,4608]{1,0:T(8,128)(2,1)S(1)}, bf16[64,4608]{1,0:T(8,128)(2,1)S(1)}, u32[]{:S(2)}, u32[]{:S(2)}) collective-permute-start(bf16[64,4608]{1,0:T(8,128)(2,1)S(1)} %column.3.refs_0_), channel_id=1, source_target_pairs={{0,24},{1,25},{2,26},{3,27},{4,7},{5,4},{6,5},{7,6},{8,16},{9,17},... | collective-permute-start | bytes 1769480 | tf_op jit(solution)/shard_map/ppermute | solution.py:69
  30.4 25.4 %collective-permute-start.14 = (bf16[64,4608]{1,0:T(8,128)(2,1)S(1)}, bf16[64,4608]{1,0:T(8,128)(2,1)S(1)}, u32[]{:S(2)}, u32[]{:S(2)}) collective-permute-start(bf16[64,4608]{1,0:T(8,128)(2,1)S(1)} %column.3.refs_0_), channel_id=1, source_target_pairs={{0,16},{1,17},{2,18},{3,19},{4,6},{5,7},{6,4},{7,5},{8,24},{9,25},... | collective-permute-start | bytes 1769480 | tf_op jit(solution)/shard_map/ppermute | solution.py:69
  30.9 24.9 %collective-permute-start.13 = (bf16[64,4608]{1,0:T(8,128)(2,1)S(1)}, bf16[64,4608]{1,0:T(8,128)(2,1)S(1)}, u32[]{:S(2)}, u32[]{:S(2)}) collective-permute-start(bf16[64,4608]{1,0:T(8,128)(2,1)S(1)} %column.3.refs_0_), channel_id=1, source_target_pairs={{0,8},{1,9},{2,10},{3,11},{4,5},{5,6},{6,7},{7,4},{8,0},{9,1},{10,... | collective-permute-start | bytes 1769480 | tf_op jit(solution)/shard_map/ppermute | solution.py:69
  31.4 1.5 collective-permute-start.6
  31.6 1.6 %collective-permute-start.9 = (bf16[64,1664]{1,0:T(8,128)(2,1)S(1)}, bf16[64,1664]{1,0:T(8,128)(2,1)S(1)}, u32[]{:S(2)}, u32[]{:S(2)}) collective-permute-start(bf16[64,1664]{1,0:T(8,128)(2,1)S(1)} %collective-permute-done.5.refs_3_), channel_id=1, source_target_pairs={{0,4},{1,5},{2,6},{3,7},{4,0},{5,1},{6,2},{7,3},{8,12},{9,13},{10,... | collective-permute-start | bytes 638984 | tf_op jit(solution)/shard_map/ppermute | solution.py:72
  34.4 22.5 %collective-permute-start.16 = (bf16[64,4608]{1,0:T(8,128)(2,1)S(1)}, bf16[64,4608]{1,0:T(8,128)(2,1)S(1)}, u32[]{:S(2)}, u32[]{:S(2)}) collective-permute-start(bf16[64,4608]{1,0:T(8,128)(2,1)S(1)} %column.3.refs_0_), channel_id=1, source_target_pairs={{0,4},{1,5},{2,6},{3,7},{4,0},{5,1},{6,2},{7,3},{8,12},{9,13},{10,... | collective-permute-start | bytes 1769480 | tf_op jit(solution)/shard_map/ppermute | solution.py:72
  55.8 2.2 %collective-permute-start.17 = (bf16[64,4608]{1,0:T(8,128)(2,1)S(1)}, bf16[64,4608]{1,0:T(8,128)(2,1)S(1)}, u32[]{:S(2)}, u32[]{:S(2)}) collective-permute-start(bf16[64,4608]{1,0:T(8,128)(2,1)S(1)} %collective-permute-done.13.refs_1_), channel_id=1, source_target_pairs={{0,4},{1,5},{2,6},{3,7},{4,0},{5,1},{6,2},{7,3},{8,12},{9,13},{10,... | collective-permute-start | bytes 1769480 | tf_op jit(solution)/shard_map/ppermute | solution.py:72
  56.4 2.5 %collective-permute-start.18 = (bf16[64,4608]{1,0:T(8,128)(2,1)S(1)}, bf16[64,4608]{1,0:T(8,128)(2,1)S(1)}, u32[]{:S(2)}, u32[]{:S(2)}) collective-permute-start(bf16[64,4608]{1,0:T(8,128)(2,1)S(1)} %collective-permute-done.14.refs_2_), channel_id=1, source_target_pairs={{0,4},{1,5},{2,6},{3,7},{4,0},{5,1},{6,2},{7,3},{8,12},{9,13},{10,... | collective-permute-start | bytes 1769480 | tf_op jit(solution)/shard_map/ppermute | solution.py:72
  56.4 3.3 %collective-permute-start.19 = (bf16[64,4608]{1,0:T(8,128)(2,1)S(1)}, bf16[64,4608]{1,0:T(8,128)(2,1)S(1)}, u32[]{:S(2)}, u32[]{:S(2)}) collective-permute-start(bf16[64,4608]{1,0:T(8,128)(2,1)S(1)} %collective-permute-done.15.refs_3_), channel_id=1, source_target_pairs={{0,4},{1,5},{2,6},{3,7},{4,0},{5,1},{6,2},{7,3},{8,12},{9,13},{10,... | collective-permute-start | bytes 1769480 | tf_op jit(solution)/shard_map/ppermute | solution.py:72
  78.0 4.6 %collective-permute-start.20 = (bf16[4,64,4608]{2,1,0:T(8,128)(2,1)S(1)}, bf16[4,64,4608]{2,1,0:T(8,128)(2,1)S(1)}, u32[]{:S(2)}, u32[]{:S(2)}) collective-permute-start(bf16[4,64,4608]{2,1,0:T(8,128)(2,1)S(1)} %get-tuple-element.151), channel_id=1, source_target_pairs={{0,4},{1,5},{2,6},{3,7},{4,0},{5,1},{6,2},{7,3},{8,12},{9,13},{10,... | collective-permute-start | bytes 7077896 | tf_op jit(solution)/shard_map/ppermute | solution.py:72
  83.2 28.8 %collective-permute-start.21 = (bf16[64,4608]{1,0:T(8,128)(2,1)S(1)}, bf16[64,4608]{1,0:T(8,128)(2,1)S(1)}, u32[]{:S(2)}, u32[]{:S(2)}) collective-permute-start(bf16[64,4608]{1,0:T(8,128)(2,1)S(1)} %get-tuple-element.154), channel_id=1, source_target_pairs={{0,8},{1,9},{2,10},{3,11},{4,5},{5,6},{6,7},{7,4},{8,0},{9,1},{10,... | collective-permute-start | bytes 1769480 | tf_op jit(solution)/shard_map/ppermute | solution.py:69
  84.7 27.3 %collective-permute-start.22 = (bf16[64,4608]{1,0:T(8,128)(2,1)S(1)}, bf16[64,4608]{1,0:T(8,128)(2,1)S(1)}, u32[]{:S(2)}, u32[]{:S(2)}) collective-permute-start(bf16[64,4608]{1,0:T(8,128)(2,1)S(1)} %get-tuple-element.155), channel_id=1, source_target_pairs={{0,16},{1,17},{2,18},{3,19},{4,6},{5,7},{6,4},{7,5},{8,24},{9,25},... | collective-permute-start | bytes 1769480 | tf_op jit(solution)/shard_map/ppermute | solution.py:69
  86.1 25.9 %collective-permute-start.23 = (bf16[64,4608]{1,0:T(8,128)(2,1)S(1)}, bf16[64,4608]{1,0:T(8,128)(2,1)S(1)}, u32[]{:S(2)}, u32[]{:S(2)}) collective-permute-start(bf16[64,4608]{1,0:T(8,128)(2,1)S(1)} %get-tuple-element.156), channel_id=1, source_target_pairs={{0,24},{1,25},{2,26},{3,27},{4,7},{5,4},{6,5},{7,6},{8,16},{9,17},... | collective-permute-start | bytes 1769480 | tf_op jit(solution)/shard_map/ppermute | solution.py:69
  112.0 2.8 %collective-permute-start.24 = (bf16[4,64,1664]{2,1,0:T(8,128)(2,1)S(1)}, bf16[4,64,1664]{2,1,0:T(8,128)(2,1)S(1)}, u32[]{:S(2)}, u32[]{:S(2)}) collective-permute-start(bf16[4,64,1664]{2,1,0:T(8,128)(2,1)S(1)} %get-tuple-element.164), channel_id=1, source_target_pairs={{0,4},{1,5},{2,6},{3,7},{4,0},{5,1},{6,2},{7,3},{8,12},{9,13},{10,... | collective-permute-start | bytes 2555912 | tf_op jit(solution)/shard_map/ppermute | solution.py:72
  115.0 8.2 %collective-permute-start.25 = (bf16[64,1664]{1,0:T(8,128)(2,1)S(1)}, bf16[64,1664]{1,0:T(8,128)(2,1)S(1)}, u32[]{:S(2)}, u32[]{:S(2)}) collective-permute-start(bf16[64,1664]{1,0:T(8,128)(2,1)S(1)} %get-tuple-element.165), channel_id=1, source_target_pairs={{0,8},{1,9},{2,10},{3,11},{4,12},{5,13},{6,14},{7,15},{8,0},{9,1},... | collective-permute-start | bytes 638984 | tf_op jit(solution)/shard_map/ppermute | solution.py:69
  116.6 12.7 %collective-permute-start.26 = (bf16[64,1664]{1,0:T(8,128)(2,1)S(1)}, bf16[64,1664]{1,0:T(8,128)(2,1)S(1)}, u32[]{:S(2)}, u32[]{:S(2)}) collective-permute-start(bf16[64,1664]{1,0:T(8,128)(2,1)S(1)} %get-tuple-element.166), channel_id=1, source_target_pairs={{0,16},{1,17},{2,18},{3,19},{4,20},{5,21},{6,22},{7,23},{8,24},{9,... | collective-permute-start | bytes 638984 | tf_op jit(solution)/shard_map/ppermute | solution.py:69
  117.8 11.5 %collective-permute-start.27 = (bf16[64,1664]{1,0:T(8,128)(2,1)S(1)}, bf16[64,1664]{1,0:T(8,128)(2,1)S(1)}, u32[]{:S(2)}, u32[]{:S(2)}) collective-permute-start(bf16[64,1664]{1,0:T(8,128)(2,1)S(1)} %get-tuple-element.167), channel_id=1, source_target_pairs={{0,24},{1,25},{2,26},{3,27},{4,28},{5,29},{6,30},{7,31},{8,16},{9,... | collective-permute-start | bytes 638984 | tf_op jit(solution)/shard_map/ppermute | solution.py:69
  119.0 13.0 %collective-permute-start.31 = (bf16[16,4608]{1,0:T(8,128)(2,1)S(1)}, bf16[16,4608]{1,0:T(8,128)(2,1)S(1)}, u32[]{:S(2)}, u32[]{:S(2)}) collective-permute-start(bf16[16,4608]{1,0:T(8,128)(2,1)S(1)} %get-tuple-element.188), channel_id=1, source_target_pairs={{0,1},{1,2},{2,3},{3,0},{4,12},{5,13},{6,14},{7,15},{8,9},{9,10},{... | collective-permute-start | bytes 442376 | tf_op jit(solution)/shard_map/ppermute | solution.py:69
  119.4 14.3 %collective-permute-start.32 = (bf16[16,4608]{1,0:T(8,128)(2,1)S(1)}, bf16[16,4608]{1,0:T(8,128)(2,1)S(1)}, u32[]{:S(2)}, u32[]{:S(2)}) collective-permute-start(bf16[16,4608]{1,0:T(8,128)(2,1)S(1)} %get-tuple-element.189), channel_id=1, source_target_pairs={{0,2},{1,3},{2,0},{3,1},{4,20},{5,21},{6,22},{7,23},{8,10},{9,11},... | collective-permute-start | bytes 442376 | tf_op jit(solution)/shard_map/ppermute | solution.py:69
  123.2 10.5 %collective-permute-start.33 = (bf16[16,4608]{1,0:T(8,128)(2,1)S(1)}, bf16[16,4608]{1,0:T(8,128)(2,1)S(1)}, u32[]{:S(2)}, u32[]{:S(2)}) collective-permute-start(bf16[16,4608]{1,0:T(8,128)(2,1)S(1)} %get-tuple-element.190), channel_id=1, source_target_pairs={{0,3},{1,0},{2,1},{3,2},{4,28},{5,29},{6,30},{7,31},{8,11},{9,8},{... | collective-permute-start | bytes 442376 | tf_op jit(solution)/shard_map/ppermute | solution.py:69
  129.4 6.1 %collective-permute-start.28 = (bf16[16,1664]{1,0:T(8,128)(2,1)S(1)}, bf16[16,1664]{1,0:T(8,128)(2,1)S(1)}, u32[]{:S(2)}, u32[]{:S(2)}) collective-permute-start(bf16[16,1664]{1,0:T(8,128)(2,1)S(1)} %get-tuple-element.180), channel_id=1, source_target_pairs={{0,1},{1,2},{2,3},{3,0},{4,5},{5,6},{6,7},{7,4},{8,9},{9,10},{10,1... | collective-permute-start | bytes 159752 | tf_op jit(solution)/shard_map/ppermute | solution.py:69
  129.9 6.5 %collective-permute-start.29 = (bf16[16,1664]{1,0:T(8,128)(2,1)S(1)}, bf16[16,1664]{1,0:T(8,128)(2,1)S(1)}, u32[]{:S(2)}, u32[]{:S(2)}) collective-permute-start(bf16[16,1664]{1,0:T(8,128)(2,1)S(1)} %get-tuple-element.181), channel_id=1, source_target_pairs={{0,2},{1,3},{2,0},{3,1},{4,6},{5,7},{6,4},{7,5},{8,10},{9,11},{10,... | collective-permute-start | bytes 159752 | tf_op jit(solution)/shard_map/ppermute | solution.py:69
  132.0 4.4 %collective-permute-start.30 = (bf16[16,1664]{1,0:T(8,128)(2,1)S(1)}, bf16[16,1664]{1,0:T(8,128)(2,1)S(1)}, u32[]{:S(2)}, u32[]{:S(2)}) collective-permute-start(bf16[16,1664]{1,0:T(8,128)(2,1)S(1)} %get-tuple-element.182), channel_id=1, source_target_pairs={{0,3},{1,0},{2,1},{3,2},{4,7},{5,4},{6,5},{7,6},{8,11},{9,8},{10,9... | collective-permute-start | bytes 159752 | tf_op jit(solution)/shard_map/ppermute | solution.py:69
  (22 other events, 132.2 us)
